TPU v7x, 32 devices: a whole 2x2x4 slice. The times are simulated.
32 devices in a mesh: groups: 1, wide: 32 (over z, y, x, core).
Axes of the slice: x: 2, y: 2, z: 4, core: 2. Of those that a mesh axis runs over, the one named last changes fastest.
Arguments:
- queries: bfloat16 [256, 1152], P('groups'), may hold values from -4 to 4
- patch_keys: bfloat16 [4096, 1152], P(('groups', 'wide')), may hold values from -173 to 173
- patch_values: bfloat16 [4096, 2560], P(('groups', 'wide')), may hold values from -6 to 6
- norm_gain: float32 [2560], replicated, may hold values from 0.1 to 1.9
- route_experts: int32 [512, 6], P(('groups', 'wide')), may hold values from 0 to 15, all different within a row; in each aligned block of 16 rows (0 to 15, 16 to 31, ...) at most 16 rows name the same one
- route_weights: int32 [512, 6], P(('groups', 'wide')), may hold values from 1 to 16
- w_gate: bfloat16 [16384, 2560], P('wide'), may hold values from -0.125 to 0.125
- w_up: bfloat16 [16384, 2560], P('wide'), may hold values from -0.125 to 0.125
- w_down: bfloat16 [16384, 2560], P('wide'), may hold values from -0.1875 to 0.1875
Outputs:
- mixed_rows: bfloat16 [512, 2560], P(('groups', 'wide'))
Inputs may be any that keep to these rules, and one draw needn't show every extreme that they name: `route_experts`: each row names 6 different experts. In each aligned block of 16 rows (the rows of one device) no expert is named by more than 16 rows, a bound that some block reaches.
All inputs are finite; a program needn't handle non-finite values.
Results may differ from a plain program's by a relative error of at most 0.02.
Values may be sent and summed in bfloat16 or wider, within the bound.
No kernel may reach another device: no remote copies, remote signals or barrier semaphores. Data moves between devices by JAX's collectives and lax.ppermute only.
A program may use at most 128 MiB of HBM per device.

v0:
```python
import functools

import jax
import jax.numpy as jnp
from jax import lax
from jax.experimental import pallas as pl
from jax.experimental.pallas import tpu as pltpu
from jax.sharding import PartitionSpec as P


HEADS = 16
LANES = 128
TABLE_LANE = 64
UNITS = 256


def near(value):
    return pltpu.with_memory_space_constraint(value, pltpu.VMEM)


def far(value):
    return pltpu.with_memory_space_constraint(value, pltpu.HBM)


def near_shape(shape, dtype):
    return pltpu.VMEM(shape, dtype)


def partner(value, axis, stride):
    mask = 2**stride
    pairs = [(source, source ^ mask) for source in range(lax.axis_size(axis))]
    return lax.ppermute(value, axis, pairs)


def plan_orders(devices, group_size):
    near_bits = list(range(1, group_size.bit_length() - 1))
    all_bits = list(range(1, devices.bit_length() - 1))
    merge = (near_bits, near_bits[1:] + near_bits[:1])
    rest = [[bit for bit in all_bits if bit != order[-1]] for order in merge]
    gather = (rest[0][::-1], rest[1][2:][::-1] + rest[1][:2])
    scatter = [order[::-1] + kept[-1:] for order, kept in zip(gather, merge)]
    return merge, gather, scatter


def exchange(value, orders, stage):
    pairs = [
        (source, source ^ (1 << orders[source % 2][stage]))
        for source in range(lax.axis_size("wide"))
    ]
    return lax.ppermute(value, "wide", pairs)


def lane_iota(shape):
    return lax.broadcasted_iota(jnp.int32, shape, 1)


def expand_tile(columns, tile, value_size):
    first = tile * LANES // value_size
    last = (tile * LANES + LANES - 1) // value_size
    rows = columns[0].shape[0]
    out = jnp.broadcast_to(columns[first], (rows, LANES))
    for head in range(first + 1, last + 1):
        edge = head * value_size - tile * LANES
        out = jnp.where(lane_iota((rows, LANES)) < edge, out, columns[head])
    return out


def pack_stats(peak, total, head_count):
    lane = lane_iota(peak.shape)
    high = total.astype(jnp.bfloat16).astype(jnp.float32)
    low = total - high
    packed = jnp.where(lane < head_count, peak, 0.0)
    shifted = pltpu.roll(jnp.where(lane < head_count, high, 0.0), head_count, 1)
    shifted_low = pltpu.roll(jnp.where(lane < head_count, low, 0.0), 2 * head_count, 1)
    return packed + shifted + shifted_low


def total_of(stats, head_count):
    return pltpu.roll(stats, LANES - head_count, 1) + pltpu.roll(
        stats, LANES - 2 * head_count, 1
    )


def attend_kernel(
    head_count,
    row_count,
    blocks_ref,
    queries_ref,
    keys_a_ref,
    keys_b_ref,
    values_a_ref,
    values_b_ref,
    sent_ref,
    kept_ref,
    query_scratch,
):
    block_count = blocks_ref.shape[0]
    rows = block_count * row_count
    half = rows // 2
    vision_width = queries_ref.shape[1]
    model_width = values_a_ref.shape[1]
    key_size = vision_width // head_count
    value_size = model_width // head_count
    scale = key_size ** (-0.5)
    for slot in range(block_count):
        start = pl.multiple_of(blocks_ref[slot] * row_count, row_count)
        query_scratch[slot * row_count : (slot + 1) * row_count, :] = queries_ref[
            pl.ds(start, row_count), :
        ]
    peaks = jnp.zeros((rows, LANES), jnp.float32)
    totals = jnp.zeros((rows, LANES), jnp.float32)
    lane = lane_iota((rows, LANES))
    contract_last = (((1,), (1,)), ((), ()))
    contract_rows = (((1,), (0,)), ((), ()))
    waiting = None

    def put(tile, value):
        columns = slice(tile * LANES, (tile + 1) * LANES)
        kept_ref[:, columns] = value[:half]
        sent_ref[:, columns] = value[half:].astype(jnp.bfloat16)

    for head in range(head_count):
        low = head * key_size // LANES * LANES
        high = -(-(head + 1) * key_size // LANES) * LANES
        window = lane_iota((rows, high - low)) + low
        inside = (window >= head * key_size) & (window < (head + 1) * key_size)
        query = jnp.where(inside, query_scratch[:, low:high], jnp.zeros((), jnp.bfloat16))
        score_a = scale * lax.dot_general(
            query, keys_a_ref[:, low:high], contract_last, preferred_element_type=jnp.float32
        )
        score_b = scale * lax.dot_general(
            query, keys_b_ref[:, low:high], contract_last, preferred_element_type=jnp.float32
        )
        peak = jnp.maximum(
            jnp.max(score_a, axis=1, keepdims=True), jnp.max(score_b, axis=1, keepdims=True)
        )
        peak = peak.astype(jnp.bfloat16).astype(jnp.float32)
        raised_a = jnp.exp(score_a - peak)
        raised_b = jnp.exp(score_b - peak)
        total = jnp.sum(raised_a, axis=1, keepdims=True) + jnp.sum(
            raised_b, axis=1, keepdims=True
        )
        peaks = jnp.where(lane == head, peak, peaks)
        totals = jnp.where(lane == head, total, totals)
        low = head * value_size // LANES
        high = -(-(head + 1) * value_size // LANES)
        summed = lax.dot_general(
            raised_a.astype(jnp.bfloat16),
            values_a_ref[:, low * LANES : high * LANES],
            contract_rows,
            preferred_element_type=jnp.float32,
        ) + lax.dot_general(
            raised_b.astype(jnp.bfloat16),
            values_b_ref[:, low * LANES : high * LANES],
            contract_rows,
            preferred_element_type=jnp.float32,
        )
        for tile in range(low, high):
            value = summed[:, (tile - low) * LANES : (tile - low + 1) * LANES]
            edge = head * value_size - tile * LANES
            if edge > 0:
                value = jnp.where(lane < edge, waiting, value)
            if (tile + 1) * LANES > (head + 1) * value_size:
                waiting = value
            else:
                put(tile, value)
    put(model_width // LANES, pack_stats(peaks, totals, head_count))


def merged_parts(kept_ref, came_ref, head_count, model_width):
    stats_a = kept_ref[:, model_width:]
    stats_b = came_ref[:, model_width:].astype(jnp.float32)
    peak = jnp.maximum(stats_a, stats_b)
    factor_a = jnp.exp(stats_a - peak)
    factor_b = jnp.exp(stats_b - peak)
    total = total_of(stats_a, head_count) * factor_a + total_of(stats_b, head_count) * factor_b
    return peak, total, factor_a, factor_b


def head_columns(array, head_count):
    return [array[:, head : head + 1] for head in range(head_count)]


def merge_kernel(head_count, kept_ref, came_ref, sent_ref, next_ref):
    model_width = kept_ref.shape[1] - LANES
    half = kept_ref.shape[0] // 2
    peak, total, factor_a, factor_b = merged_parts(kept_ref, came_ref, head_count, model_width)
    columns_a = head_columns(factor_a, head_count)
    columns_b = head_columns(factor_b, head_count)
    for tile in range(model_width // LANES + 1):
        columns = slice(tile * LANES, (tile + 1) * LANES)
        if tile * LANES == model_width:
            value = pack_stats(peak, total, head_count)
        else:
            value = kept_ref[:, columns] * expand_tile(
                columns_a, tile, model_width // head_count
            ) + came_ref[:, columns].astype(jnp.float32) * expand_tile(
                columns_b, tile, model_width // head_count
            )
        next_ref[:, columns] = value[:half]
        sent_ref[:, columns] = value[half:].astype(jnp.bfloat16)


def last_merge_kernel(head_count, kept_ref, came_ref, table_ref, sent_ref, next_ref):
    model_width = kept_ref.shape[1] - LANES
    half = kept_ref.shape[0] // 2
    peak, total, factor_a, factor_b = merged_parts(kept_ref, came_ref, head_count, model_width)
    columns_a = head_columns(factor_a, head_count)
    columns_b = head_columns(factor_b, head_count)
    for tile in range(model_width // LANES + 1):
        columns = slice(tile * LANES, (tile + 1) * LANES)
        if tile * LANES == model_width:
            value = pack_stats(peak, total, head_count)
            own = value[:half] + table_ref[...].astype(jnp.float32)
        else:
            value = kept_ref[:, columns] * expand_tile(
                columns_a, tile, model_width // head_count
            ) + came_ref[:, columns].astype(jnp.float32) * expand_tile(
                columns_b, tile, model_width // head_count
            )
            own = value[:half]
        next_ref[:, columns] = value
        sent_ref[:half, columns] = value[half:].astype(jnp.bfloat16)
        sent_ref[half:, columns] = own.astype(jnp.bfloat16)


def finish_kernel(head_count, kept_ref, came_ref, gain_ref, table_ref, block_ref, projected_ref):
    model_width = kept_ref.shape[1] - LANES
    half = kept_ref.shape[0] // 2
    _, total, factor_a, factor_b = merged_parts(kept_ref, came_ref, head_count, model_width)
    columns_a = head_columns(factor_a / total, head_count)
    columns_b = head_columns(factor_b / total, head_count)
    square = jnp.zeros((kept_ref.shape[0], LANES), jnp.float32)
    for tile in range(model_width // LANES):
        columns = slice(tile * LANES, (tile + 1) * LANES)
        value = kept_ref[:, columns] * expand_tile(
            columns_a, tile, model_width // head_count
        ) + came_ref[:, columns].astype(jnp.float32) * expand_tile(
            columns_b, tile, model_width // head_count
        )
        rounded = value.astype(jnp.bfloat16)
        block_ref[:, columns] = rounded
        projected_ref[:, columns] = rounded[:half]
        residual = rounded.astype(jnp.float32)
        square = square + residual * residual
    mean = jnp.sum(square, axis=1, keepdims=True) / model_width
    inverse = lax.rsqrt(mean + 1e-06)
    normed = block_ref[:, :model_width].astype(jnp.float32) * inverse * gain_ref[...]
    block_ref[:, :model_width] = normed.astype(jnp.bfloat16)
    came_table = came_ref[half:, model_width:]
    lane = lane_iota(came_table.shape)
    block_ref[:half, model_width:] = table_ref[...]
    block_ref[half:, model_width:] = jnp.where(
        lane >= TABLE_LANE, came_table.astype(jnp.float32), 0.0
    ).astype(jnp.bfloat16)


def expert_math(expert_ref, rows_ref, gate_ref, up_ref, down_ref, out_ref, turned, hidden, ready):
    model_width = out_ref.shape[1]
    for low in range(0, rows_ref.shape[1], LANES):
        turned[low : low + LANES, :] = rows_ref[:, low : low + LANES].T
    scores = turned[model_width:, :].astype(jnp.float32)
    lane = lax.broadcasted_iota(jnp.int32, scores.shape, 0)
    chosen = jnp.where(lane == expert_ref[0] + TABLE_LANE, scores, 0.0)
    share = jnp.sum(chosen, axis=0, keepdims=True) / jnp.sum(scores, axis=0, keepdims=True)
    rows = turned[:model_width, :]
    for chunk in range(gate_ref.shape[0] // UNITS):
        ready(chunk)
        units = slice(chunk * UNITS, (chunk + 1) * UNITS)
        gate_part = jnp.dot(gate_ref[units, :], rows, preferred_element_type=jnp.float32)
        up_part = jnp.dot(up_ref[units, :], rows, preferred_element_type=jnp.float32)
        silu = gate_part / (1.0 + jnp.exp(-gate_part))
        hidden[:, units] = (silu * up_part * share).T.astype(jnp.bfloat16)
    ready(None)
    for low in range(0, model_width, 4 * LANES):
        columns = slice(low, low + 4 * LANES)
        out_ref[:, columns] = jnp.dot(
            hidden[...], down_ref[:, columns], preferred_element_type=jnp.float32
        ).astype(out_ref.dtype)


def first_expert_kernel(
    expert_ref,
    rows_ref,
    gate_a,
    gate_b,
    up_a,
    up_b,
    down_a,
    down_b,
    out_ref,
    gate_ref,
    up_ref,
    down_ref,
    turned,
    hidden,
    arrived,
):
    per_half = gate_a.shape[0] // UNITS
    chunks = 2 * per_half

    def copy_of(part, chunk):
        pair, target = ((gate_a, gate_b), (up_a, up_b), (down_a, down_b))[part], (
            gate_ref,
            up_ref,
            down_ref,
        )[part]
        low = chunk % per_half * UNITS
        return pltpu.make_async_copy(
            pair[chunk // per_half].at[low : low + UNITS, :],
            target.at[chunk * UNITS : (chunk + 1) * UNITS, :],
            arrived.at[part, chunk],
        )

    for chunk in range(chunks):
        for part in range(2):
            copy_of(part, chunk).start()
    for chunk in range(chunks):
        copy_of(2, chunk).start()

    def ready(chunk):
        if chunk is None:
            for piece in range(chunks):
                copy_of(2, piece).wait()
        else:
            copy_of(0, chunk).wait()
            copy_of(1, chunk).wait()

    expert_math(
        expert_ref, rows_ref, gate_ref, up_ref, down_ref, out_ref, turned, hidden, ready
    )


def second_expert_kernel(
    expert_ref, rows_ref, gate_ref, up_ref, down_ref, out_ref, turned, hidden
):
    expert_math(
        expert_ref,
        rows_ref,
        gate_ref,
        up_ref,
        down_ref,
        out_ref,
        turned,
        hidden,
        lambda chunk: None,
    )


def first_expert_rows(expert, rows, weights):
    units, model_width = weights[0].shape
    row_count, packed_width = rows.shape
    whole = pl.BlockSpec(memory_space=pltpu.VMEM)
    anywhere = pl.BlockSpec(memory_space=pltpu.HBM)
    chunks = 2 * units // UNITS
    return pl.pallas_call(
        first_expert_kernel,
        name="expert_first",
        compiler_params=pltpu.CompilerParams(vmem_limit_bytes=12 << 20),
        out_shape=(near_shape((row_count, model_width), jnp.float32),)
        + (near_shape((2 * units, model_width), jnp.bfloat16),) * 3,
        in_specs=[pl.BlockSpec(memory_space=pltpu.SMEM), whole] + [anywhere] * 6,
        out_specs=(whole,) * 4,
        scratch_shapes=[
            pltpu.VMEM((packed_width, row_count), jnp.bfloat16),
            pltpu.VMEM((row_count, 2 * units), jnp.bfloat16),
            pltpu.SemaphoreType.DMA((3, chunks)),
        ],
        cost_estimate=pl.CostEstimate(
            flops=12 * row_count * model_width * units,
            transcendentals=0,
            bytes_accessed=12 * units * model_width,
        ),
    )(expert, near(rows), *[far(weight) for weight in weights])


def second_expert_rows(expert, rows, weights):
    units, model_width = weights[0].shape
    row_count, packed_width = rows.shape
    whole = pl.BlockSpec(memory_space=pltpu.VMEM)
    return pl.pallas_call(
        second_expert_kernel,
        name="expert_second",
        compiler_params=pltpu.CompilerParams(vmem_limit_bytes=12 << 20),
        out_shape=near_shape((row_count, model_width), jnp.bfloat16),
        in_specs=[pl.BlockSpec(memory_space=pltpu.SMEM)] + [whole] * 4,
        out_specs=whole,
        scratch_shapes=[
            pltpu.VMEM((packed_width, row_count), jnp.bfloat16),
            pltpu.VMEM((row_count, units), jnp.bfloat16),
        ],
    )(expert, near(rows), *[near(weight) for weight in weights])


def attention_rows(
    queries, patch_keys, patch_values, other_keys, other_values, norm_gain, table, row_count, orders
):
    model_width = patch_values.shape[1]
    packed_width = model_width + LANES
    group_size = queries.shape[0] // row_count
    stages = len(orders[0])
    device_index = lax.axis_index("wide")
    masks = [
        [
            sum(
                (1 << order[stage])
                for stage in range(stages)
                if slot >> (stages - 1 - stage) & 1
            )
            for slot in range(1 << stages)
        ]
        for order in orders
    ]
    masks = jnp.array(masks, jnp.int32)
    blocks = (device_index % group_size) ^ jnp.where(device_index % 2 == 1, masks[1], masks[0])
    rows = row_count << stages
    whole = pl.BlockSpec(memory_space=pltpu.VMEM)

    def pair_shapes(rows):
        return (
            near_shape((rows, packed_width), jnp.bfloat16),
            near_shape((rows, packed_width), jnp.float32),
        )

    sent, kept = pl.pallas_call(
        functools.partial(attend_kernel, HEADS, row_count),
        name="attend",
        compiler_params=pltpu.CompilerParams(vmem_limit_bytes=12 << 20),
        out_shape=pair_shapes(rows // 2),
        in_specs=[pl.BlockSpec(memory_space=pltpu.SMEM)] + [whole] * 5,
        out_specs=(whole, whole),
        scratch_shapes=[pltpu.VMEM((rows, queries.shape[1]), jnp.bfloat16)],
    )(
        blocks,
        far(queries),
        far(patch_keys),
        near(other_keys),
        far(patch_values),
        near(other_values),
    )
    for stage in range(stages - 1):
        came = exchange(sent, orders, stage)
        rows = kept.shape[0]
        if stage < stages - 2:
            sent, kept = pl.pallas_call(
                functools.partial(merge_kernel, HEADS),
                name="merge",
                compiler_params=pltpu.CompilerParams(vmem_limit_bytes=6 << 20),
                out_shape=pair_shapes(rows // 2),
                in_specs=[whole] * 2,
                out_specs=(whole, whole),
            )(near(kept), near(came))
        else:
            sent, kept = pl.pallas_call(
                functools.partial(last_merge_kernel, HEADS),
                name="last_merge",
                compiler_params=pltpu.CompilerParams(vmem_limit_bytes=6 << 20),
                out_shape=pair_shapes(rows),
                in_specs=[whole] * 3,
                out_specs=(whole, whole),
            )(near(kept), near(came), near(table))
    came = exchange(sent, orders, stages - 1)
    rows = kept.shape[0]
    return pl.pallas_call(
        functools.partial(finish_kernel, HEADS),
        name="finish",
        compiler_params=pltpu.CompilerParams(vmem_limit_bytes=6 << 20),
        out_shape=(
            near_shape((rows, packed_width), jnp.bfloat16),
            near_shape((row_count, model_width), jnp.bfloat16),
        ),
        in_specs=[whole] * 4,
        out_specs=(whole, whole),
    )(near(kept), near(came), near(norm_gain.reshape(1, model_width)), near(table))


def on_device(
    queries, patch_keys, patch_values, norm_gain, route_experts, route_weights, w_gate, w_up, w_down
):
    row_count = route_experts.shape[0]
    devices = lax.axis_size("wide")
    device_index = lax.axis_index("wide")
    score_table = jnp.sum(
        jnp.where(
            route_experts[:, :, None] == jnp.arange(-TABLE_LANE, LANES - TABLE_LANE, dtype=jnp.int32),
            route_weights[:, :, None],
            0,
        ),
        axis=1,
    ).astype(jnp.bfloat16)
    merge_order, gather_order, scatter_order = plan_orders(
        devices, queries.shape[0] // row_count
    )
    other_keys = partner(patch_keys, "wide", 0)
    other_values = partner(patch_values, "wide", 0)
    halves, other_keys, other_values = lax.optimization_barrier(
        ((w_gate, w_up, w_down), other_keys, other_values)
    )
    weights = []
    for own in halves:
        weights += [own, partner(own, "wide", 0)]
    block, projected = attention_rows(
        queries,
        patch_keys,
        patch_values,
        other_keys,
        other_values,
        norm_gain,
        score_table,
        row_count,
        merge_order,
    )
    stages = len(gather_order[0])
    for stage in range(stages - 1):
        block = jnp.concatenate([block, exchange(block, gather_order, stage)], axis=0)
    came = exchange(block, gather_order, stages - 1)
    expert = (device_index // 2).reshape(1)
    total, *weights = first_expert_rows(expert, block, weights)
    sent = second_expert_rows(expert, came, weights)
    total = total + exchange(sent, scatter_order, 0).astype(jnp.float32)
    for stage in range(1, len(scatter_order[0])):
        half_rows = total.shape[0] // 2
        total = total[:half_rows] + exchange(
            total[half_rows:].astype(jnp.bfloat16), scatter_order, stage
        ).astype(jnp.float32)
    return (projected.astype(jnp.float32) + total).astype(jnp.bfloat16)


def solution(mesh):
    return mapped(mesh)


def mapped(mesh):
    return jax.shard_map(
        on_device,
        mesh=mesh,
        in_specs=(
            P("groups", None),
            P(("groups", "wide"), None),
            P(("groups", "wide"), None),
            P(),
            P(("groups", "wide"), None),
            P(("groups", "wide"), None),
            P("wide", None),
            P("wide", None),
            P("wide", None),
        ),
        out_specs=P(("groups", "wide"), None),
        check_vma=False,
    )
```

profile of v0, /device:TPU:0, one launch (start us, length us, event | category | flops | bytes accessed | tf_op | source)
XLA Modules:
  0.0 88.4 jit_solution(17027971839585110504)
XLA Ops:
  0.0 0.6 collective-permute-start.1
  0.6 0.7 fusion.3.blocks_ref
  1.3 1.6 %collective-permute-done.keys_b_ref = bf16[128,1152]{1,0:T(8,128)(2,1)S(1)} collective-permute-done((bf16[128,1152]{1,0:T(8,128)(2,1)}, bf16[128,1152]{1,0:T(8,128)(2,1)S(1)}, u32[]{:S(2)}, u32[]{:S(2)}) %collective-permute-start) | collective-permute-done | bytes 294944 | tf_op jit(solution)/shard_map/ppermute | solution.py:32
  2.9 3.0 %attend.1 = (bf16[64,2688]{1,0:T(8,128)(2,1)S(1)}, f32[64,2688]{1,0:T(8,128)S(1)}) custom-call(s32[8]{0:T(128)S(1)} %fusion.3.blocks_ref, bf16[256,1152]{1,0:T(8,128)(2,1)} %queries_ref.1, bf16[128,1152]{1,0:T(8,128)(2,1)} %keys_a_ref.1, bf16[128,1152]{1,0:T(8,128)(2,1)S(1)} %collective-permute-done.keys_b_ref, bf16[128,2560]{1,0:T(8,128)(2,1)} %values_a_ref.1, ...), custom_call_target="tpu_custom_call" | custom-call | tf_op jit(solution)/shard_map/attend/pallas_call | solution.py:425
  5.9 2.9 %collective-permute-start.2 = (bf16[64,2688]{1,0:T(8,128)(2,1)S(1)}, bf16[64,2688]{1,0:T(8,128)(2,1)S(1)}, u32[]{:S(2)}, u32[]{:S(2)}) collective-permute-start(bf16[64,2688]{1,0:T(8,128)(2,1)S(1)} %get-tuple-element.25), channel_id=1, source_target_pairs={{0,2},{1,5},{2,0},{3,7},{4,6},{5,1},{6,4},{7,3},{8,10},{9,13},{10,... | collective-permute-start | bytes 1032200 | tf_op jit(solution)/shard_map/ppermute | solution.py:50
  8.8 0.5 collective-permute-start.8
  9.4 4.7 %collective-permute-done.2.came_ref = bf16[64,2688]{1,0:T(8,128)(2,1)S(1)} collective-permute-done((bf16[64,2688]{1,0:T(8,128)(2,1)S(1)}, bf16[64,2688]{1,0:T(8,128)(2,1)S(1)}, u32[]{:S(2)}, u32[]{:S(2)}) %collective-permute-start.2) | collective-permute-done | bytes 344096 | tf_op jit(solution)/shard_map/ppermute | solution.py:50
  14.1 0.4 merge.1
  14.5 2.1 %collective-permute-start.3 = (bf16[32,2688]{1,0:T(8,128)(2,1)S(1)}, bf16[32,2688]{1,0:T(8,128)(2,1)S(1)}, u32[]{:S(2)}, u32[]{:S(2)}) collective-permute-start(bf16[32,2688]{1,0:T(8,128)(2,1)S(1)} %get-tuple-element.27), channel_id=1, source_target_pairs={{0,4},{1,9},{2,6},{3,11},{4,0},{5,13},{6,2},{7,15},{8,12},{9,1},{1... | collective-permute-start | bytes 516104 | tf_op jit(solution)/shard_map/ppermute | solution.py:50
  16.6 0.1 select_reduce_fusion
  16.7 3.3 %collective-permute-done.3.came_ref = bf16[32,2688]{1,0:T(8,128)(2,1)S(1)} collective-permute-done((bf16[32,2688]{1,0:T(8,128)(2,1)S(1)}, bf16[32,2688]{1,0:T(8,128)(2,1)S(1)}, u32[]{:S(2)}, u32[]{:S(2)}) %collective-permute-start.3) | collective-permute-done | bytes 172064 | tf_op jit(solution)/shard_map/ppermute | solution.py:50
  20.0 0.2 last_merge.1
  20.2 2.1 %collective-permute-start.4 = (bf16[32,2688]{1,0:T(8,128)(2,1)S(1)}, bf16[32,2688]{1,0:T(8,128)(2,1)S(1)}, u32[]{:S(2)}, u32[]{:S(2)}) collective-permute-start(bf16[32,2688]{1,0:T(8,128)(2,1)S(1)} %get-tuple-element.29), channel_id=1, source_target_pairs={{0,8},{1,3},{2,10},{3,1},{4,12},{5,7},{6,14},{7,5},{8,0},{9,11},{1... | collective-permute-start | bytes 516104 | tf_op jit(solution)/shard_map/ppermute | solution.py:50
  22.4 3.4 %collective-permute-done.4.came_ref = bf16[32,2688]{1,0:T(8,128)(2,1)S(1)} collective-permute-done((bf16[32,2688]{1,0:T(8,128)(2,1)S(1)}, bf16[32,2688]{1,0:T(8,128)(2,1)S(1)}, u32[]{:S(2)}, u32[]{:S(2)}) %collective-permute-start.4) | collective-permute-done | bytes 172064 | tf_op jit(solution)/shard_map/ppermute | solution.py:50
  25.8 0.4 finish.1
  26.2 3.1 %collective-permute-start.5 = (bf16[32,2688]{1,0:T(8,128)(2,1)S(1)}, bf16[32,2688]{1,0:T(8,128)(2,1)S(1)}, u32[]{:S(2)}, u32[]{:S(2)}) collective-permute-start(bf16[32,2688]{1,0:T(8,128)(2,1)S(1)} %get-tuple-element.31), channel_id=1, source_target_pairs={{0,16},{1,17},{2,18},{3,19},{4,20},{5,21},{6,22},{7,23},{8,24},{9,... | collective-permute-start | bytes 516104 | tf_op jit(solution)/shard_map/ppermute | solution.py:50
  29.3 5.5 %collective-permute-done.5 = bf16[32,2688]{1,0:T(8,128)(2,1)S(1)} collective-permute-done((bf16[32,2688]{1,0:T(8,128)(2,1)S(1)}, bf16[32,2688]{1,0:T(8,128)(2,1)S(1)}, u32[]{:S(2)}, u32[]{:S(2)}) %collective-permute-start.5) | collective-permute-done | bytes 172064 | tf_op jit(solution)/shard_map/ppermute | solution.py:50
  34.8 1.7 %collective-permute-start.6 = (bf16[64,2688]{1,0:T(8,128)(2,1)S(1)}, bf16[64,2688]{1,0:T(8,128)(2,1)S(1)}, u32[]{:S(2)}, u32[]{:S(2)}) collective-permute-start(bf16[64,2688]{1,0:T(8,128)(2,1)S(1)} %pad_maximum_fusion), channel_id=1, source_target_pairs={{0,4},{1,5},{2,6},{3,7},{4,0},{5,1},{6,2},{7,3},{8,12},{9,13},{10,... | collective-permute-start | bytes 1032200 | tf_op jit(solution)/shard_map/ppermute | solution.py:50
  36.5 5.6 %collective-permute-done.6 = bf16[64,2688]{1,0:T(8,128)(2,1)S(1)} collective-permute-done((bf16[64,2688]{1,0:T(8,128)(2,1)S(1)}, bf16[64,2688]{1,0:T(8,128)(2,1)S(1)}, u32[]{:S(2)}, u32[]{:S(2)}) %collective-permute-start.6) | collective-permute-done | bytes 344096 | tf_op jit(solution)/shard_map/ppermute | solution.py:50
  42.2 1.6 %collective-permute-start.10 = (bf16[128,2688]{1,0:T(8,128)(2,1)S(1)}, bf16[128,2688]{1,0:T(8,128)(2,1)S(1)}, u32[]{:S(2)}, u32[]{:S(2)}) collective-permute-start(bf16[128,2688]{1,0:T(8,128)(2,1)S(1)} %constant_dynamic-update-slice_fusion.rows_ref), channel_id=1, source_target_pairs={{0,2},{1,9},{2,0},{3,11},{4,6},{5,13},{6,4},{7,15},{8,10},{9,1},{1... | collective-permute-start | bytes 2064392 | tf_op jit(solution)/shard_map/ppermute | solution.py:50
  43.8 6.5 %expert_first.1 = (f32[128,2560]{1,0:T(8,128)S(1)}, bf16[1024,2560]{1,0:T(8,128)(2,1)S(1)}, bf16[1024,2560]{1,0:T(8,128)(2,1)S(1)}, bf16[1024,2560]{1,0:T(8,128)(2,1)S(1)}) custom-call(s32[1]{0:T(128)} %bitcast.1.expert_ref, bf16[128,2688]{1,0:T(8,128)(2,1)S(1)} %constant_dynamic-update-slice_fusion.rows_ref, bf16[512,2560]{1,0:T(8,128)(2,1)} %gate_a, ...), custom_call_target="tpu_custom_call" | custom-call | flops 2013265920 | bytes 15728640 | tf_op jit(solution)/shard_map/expert_first/pallas_call | solution.py:356
  50.3 2.9 %collective-permute-done.10.rows_ref = bf16[128,2688]{1,0:T(8,128)(2,1)S(1)} collective-permute-done((bf16[128,2688]{1,0:T(8,128)(2,1)S(1)}, bf16[128,2688]{1,0:T(8,128)(2,1)S(1)}, u32[]{:S(2)}, u32[]{:S(2)}) %collective-permute-start.10) | collective-permute-done | bytes 688160 | tf_op jit(solution)/shard_map/ppermute | solution.py:50
  53.2 3.9 %expert_second.1 = bf16[128,2560]{1,0:T(8,128)(2,1)S(1)} custom-call(s32[1]{0:T(128)} %bitcast.1.expert_ref, bf16[128,2688]{1,0:T(8,128)(2,1)S(1)} %collective-permute-done.10.rows_ref, bf16[1024,2560]{1,0:T(8,128)(2,1)S(1)} %get-tuple-element.36.gate_ref, bf16[1024,2560]{1,0:T(8,128)(2,1)S(1)} %get-tuple-element.37.up_ref, ...), custom_call_target="tpu_custom_call" | custom-call | tf_op jit(solution)/shard_map/expert_second/pallas_call | solution.py:381
  57.1 1.6 %collective-permute-start.11 = (bf16[128,2560]{1,0:T(8,128)(2,1)S(1)}, bf16[128,2560]{1,0:T(8,128)(2,1)S(1)}, u32[]{:S(2)}, u32[]{:S(2)}) collective-permute-start(bf16[128,2560]{1,0:T(8,128)(2,1)S(1)} %expert_second.1), channel_id=1, source_target_pairs={{0,2},{1,9},{2,0},{3,11},{4,6},{5,13},{6,4},{7,15},{8,10},{9,1},{1... | collective-permute-start | bytes 1966088 | tf_op jit(solution)/shard_map/ppermute | solution.py:50
  58.7 9.0 %collective-permute-done.11 = bf16[128,2560]{1,0:T(8,128)(2,1)S(1)} collective-permute-done((bf16[128,2560]{1,0:T(8,128)(2,1)S(1)}, bf16[128,2560]{1,0:T(8,128)(2,1)S(1)}, u32[]{:S(2)}, u32[]{:S(2)}) %collective-permute-start.11) | collective-permute-done | bytes 655392 | tf_op jit(solution)/shard_map/ppermute | solution.py:50
  67.7 0.1 convert_add_fusion
  67.9 1.7 %collective-permute-start.12 = (bf16[64,2560]{1,0:T(8,128)(2,1)S(1)}, bf16[64,2560]{1,0:T(8,128)(2,1)S(1)}, u32[]{:S(2)}, u32[]{:S(2)}) collective-permute-start(bf16[64,2560]{1,0:T(8,128)(2,1)S(1)} %slice.51), channel_id=1, source_target_pairs={{0,4},{1,5},{2,6},{3,7},{4,0},{5,1},{6,2},{7,3},{8,12},{9,13},{10,... | collective-permute-start | bytes 983048 | tf_op jit(solution)/shard_map/ppermute | solution.py:50
  69.6 5.5 %collective-permute-done.12 = bf16[64,2560]{1,0:T(8,128)(2,1)S(1)} collective-permute-done((bf16[64,2560]{1,0:T(8,128)(2,1)S(1)}, bf16[64,2560]{1,0:T(8,128)(2,1)S(1)}, u32[]{:S(2)}, u32[]{:S(2)}) %collective-permute-start.12) | collective-permute-done | bytes 327712 | tf_op jit(solution)/shard_map/ppermute | solution.py:50
  75.2 1.0 %collective-permute-start.13 = (bf16[32,2560]{1,0:T(8,128)(2,1)S(1)}, bf16[32,2560]{1,0:T(8,128)(2,1)S(1)}, u32[]{:S(2)}, u32[]{:S(2)}) collective-permute-start(bf16[32,2560]{1,0:T(8,128)(2,1)S(1)} %slice.52), channel_id=1, source_target_pairs={{0,16},{1,17},{2,18},{3,19},{4,20},{5,21},{6,22},{7,23},{8,24},{9,... | collective-permute-start | bytes 491528 | tf_op jit(solution)/shard_map/ppermute | solution.py:50
  76.1 7.1 %collective-permute-done.13 = bf16[32,2560]{1,0:T(8,128)(2,1)S(1)} collective-permute-done((bf16[32,2560]{1,0:T(8,128)(2,1)S(1)}, bf16[32,2560]{1,0:T(8,128)(2,1)S(1)}, u32[]{:S(2)}, u32[]{:S(2)}) %collective-permute-start.13) | collective-permute-done | bytes 163872 | tf_op jit(solution)/shard_map/ppermute | solution.py:50
  83.3 4.4 %collective-permute-done.14 = bf16[16,2560]{1,0:T(8,128)(2,1)S(1)} collective-permute-done((bf16[16,2560]{1,0:T(8,128)(2,1)S(1)}, bf16[16,2560]{1,0:T(8,128)(2,1)S(1)}, u32[]{:S(2)}, u32[]{:S(2)}) %collective-permute-start.14) | collective-permute-done | bytes 81952 | tf_op jit(solution)/shard_map/ppermute | solution.py:50
  87.8 0.7 fusion.1
  (26 shorter events, 0.5 us)
Async XLA Ops:
  0.0 16.6 %copy-start.2 = (s32[16,6]{0,1:T(8,128)S(1)}, s32[16,6]{0,1:T(8,128)}, u32[]{:S(2)}) copy-start(s32[16,6]{0,1:T(8,128)} %param.14) | copy-start | bytes 1156
  0.0 16.6 %copy-start.1 = (s32[16,6]{0,1:T(8,128)S(1)}, s32[16,6]{0,1:T(8,128)}, u32[]{:S(2)}) copy-start(s32[16,6]{0,1:T(8,128)} %param.15) | copy-start | bytes 1156
  0.0 22.4 %copy-start = (f32[2560]{0:T(1024)S(1)}, f32[2560]{0:T(1024)}, u32[]{:S(2)}) copy-start(f32[2560]{0:T(1024)} %param.13) | copy-start | bytes 30724
  0.0 2.9 %collective-permute-start.1 = (bf16[128,2560]{1,0:T(8,128)(2,1)}, bf16[128,2560]{1,0:T(8,128)(2,1)S(1)}, u32[]{:S(2)}, u32[]{:S(2)}) collective-permute-start(bf16[128,2560]{1,0:T(8,128)(2,1)} %values_a_ref.1), channel_id=1, source_target_pairs={{0,1},{1,0},{2,3},{3,2},{4,5},{5,4},{6,7},{7,6},{8,9},{9,8},{10,11... | collective-permute-start | bytes 1966088 | tf_op jit(solution)/shard_map/ppermute | solution.py:32
  0.6 2.4 %collective-permute-start = (bf16[128,1152]{1,0:T(8,128)(2,1)}, bf16[128,1152]{1,0:T(8,128)(2,1)S(1)}, u32[]{:S(2)}, u32[]{:S(2)}) collective-permute-start(bf16[128,1152]{1,0:T(8,128)(2,1)} %keys_a_ref.1), channel_id=1, source_target_pairs={{0,1},{1,0},{2,3},{3,2},{4,5},{5,4},{6,7},{7,6},{8,9},{9,8},{10,11... | collective-permute-start | bytes 884744 | tf_op jit(solution)/shard_map/ppermute | solution.py:32
  5.9 8.1 %collective-permute-start.2 = (bf16[64,2688]{1,0:T(8,128)(2,1)S(1)}, bf16[64,2688]{1,0:T(8,128)(2,1)S(1)}, u32[]{:S(2)}, u32[]{:S(2)}) collective-permute-start(bf16[64,2688]{1,0:T(8,128)(2,1)S(1)} %get-tuple-element.25), channel_id=1, source_target_pairs={{0,2},{1,5},{2,0},{3,7},{4,6},{5,1},{6,4},{7,3},{8,10},{9,13},{10,... | collective-permute-start | bytes 1032200 | tf_op jit(solution)/shard_map/ppermute | solution.py:50
  8.8 35.0 %collective-permute-start.7 = (bf16[512,2560]{1,0:T(8,128)(2,1)}, bf16[512,2560]{1,0:T(8,128)(2,1)}, u32[]{:S(2)}, u32[]{:S(2)}) collective-permute-start(bf16[512,2560]{1,0:T(8,128)(2,1)} %gate_a), channel_id=1, source_target_pairs={{0,1},{1,0},{2,3},{3,2},{4,5},{5,4},{6,7},{7,6},{8,9},{9,8},{10,11... | collective-permute-start | bytes 7864328 | tf_op jit(solution)/shard_map/ppermute | solution.py:32
  8.8 35.0 %collective-permute-start.8 = (bf16[512,2560]{1,0:T(8,128)(2,1)}, bf16[512,2560]{1,0:T(8,128)(2,1)}, u32[]{:S(2)}, u32[]{:S(2)}) collective-permute-start(bf16[512,2560]{1,0:T(8,128)(2,1)} %up_a), channel_id=1, source_target_pairs={{0,1},{1,0},{2,3},{3,2},{4,5},{5,4},{6,7},{7,6},{8,9},{9,8},{10,11... | collective-permute-start | bytes 7864328 | tf_op jit(solution)/shard_map/ppermute | solution.py:32
  9.4 34.5 %collective-permute-start.9 = (bf16[512,2560]{1,0:T(8,128)(2,1)}, bf16[512,2560]{1,0:T(8,128)(2,1)}, u32[]{:S(2)}, u32[]{:S(2)}) collective-permute-start(bf16[512,2560]{1,0:T(8,128)(2,1)} %down_a), channel_id=1, source_target_pairs={{0,1},{1,0},{2,3},{3,2},{4,5},{5,4},{6,7},{7,6},{8,9},{9,8},{10,11... | collective-permute-start | bytes 7864328 | tf_op jit(solution)/shard_map/ppermute | solution.py:32
  14.5 5.5 %collective-permute-start.3 = (bf16[32,2688]{1,0:T(8,128)(2,1)S(1)}, bf16[32,2688]{1,0:T(8,128)(2,1)S(1)}, u32[]{:S(2)}, u32[]{:S(2)}) collective-permute-start(bf16[32,2688]{1,0:T(8,128)(2,1)S(1)} %get-tuple-element.27), channel_id=1, source_target_pairs={{0,4},{1,9},{2,6},{3,11},{4,0},{5,13},{6,2},{7,15},{8,12},{9,1},{1... | collective-permute-start | bytes 516104 | tf_op jit(solution)/shard_map/ppermute | solution.py:50
  20.2 5.5 %collective-permute-start.4 = (bf16[32,2688]{1,0:T(8,128)(2,1)S(1)}, bf16[32,2688]{1,0:T(8,128)(2,1)S(1)}, u32[]{:S(2)}, u32[]{:S(2)}) collective-permute-start(bf16[32,2688]{1,0:T(8,128)(2,1)S(1)} %get-tuple-element.29), channel_id=1, source_target_pairs={{0,8},{1,3},{2,10},{3,1},{4,12},{5,7},{6,14},{7,5},{8,0},{9,11},{1... | collective-permute-start | bytes 516104 | tf_op jit(solution)/shard_map/ppermute | solution.py:50
  26.2 8.6 %collective-permute-start.5 = (bf16[32,2688]{1,0:T(8,128)(2,1)S(1)}, bf16[32,2688]{1,0:T(8,128)(2,1)S(1)}, u32[]{:S(2)}, u32[]{:S(2)}) collective-permute-start(bf16[32,2688]{1,0:T(8,128)(2,1)S(1)} %get-tuple-element.31), channel_id=1, source_target_pairs={{0,16},{1,17},{2,18},{3,19},{4,20},{5,21},{6,22},{7,23},{8,24},{9,... | collective-permute-start | bytes 516104 | tf_op jit(solution)/shard_map/ppermute | solution.py:50
  34.8 7.3 %collective-permute-start.6 = (bf16[64,2688]{1,0:T(8,128)(2,1)S(1)}, bf16[64,2688]{1,0:T(8,128)(2,1)S(1)}, u32[]{:S(2)}, u32[]{:S(2)}) collective-permute-start(bf16[64,2688]{1,0:T(8,128)(2,1)S(1)} %pad_maximum_fusion), channel_id=1, source_target_pairs={{0,4},{1,5},{2,6},{3,7},{4,0},{5,1},{6,2},{7,3},{8,12},{9,13},{10,... | collective-permute-start | bytes 1032200 | tf_op jit(solution)/shard_map/ppermute | solution.py:50
  42.2 11.0 %collective-permute-start.10 = (bf16[128,2688]{1,0:T(8,128)(2,1)S(1)}, bf16[128,2688]{1,0:T(8,128)(2,1)S(1)}, u32[]{:S(2)}, u32[]{:S(2)}) collective-permute-start(bf16[128,2688]{1,0:T(8,128)(2,1)S(1)} %constant_dynamic-update-slice_fusion.rows_ref), channel_id=1, source_target_pairs={{0,2},{1,9},{2,0},{3,11},{4,6},{5,13},{6,4},{7,15},{8,10},{9,1},{1... | collective-permute-start | bytes 2064392 | tf_op jit(solution)/shard_map/ppermute | solution.py:50
  57.1 10.7 %collective-permute-start.11 = (bf16[128,2560]{1,0:T(8,128)(2,1)S(1)}, bf16[128,2560]{1,0:T(8,128)(2,1)S(1)}, u32[]{:S(2)}, u32[]{:S(2)}) collective-permute-start(bf16[128,2560]{1,0:T(8,128)(2,1)S(1)} %expert_second.1), channel_id=1, source_target_pairs={{0,2},{1,9},{2,0},{3,11},{4,6},{5,13},{6,4},{7,15},{8,10},{9,1},{1... | collective-permute-start | bytes 1966088 | tf_op jit(solution)/shard_map/ppermute | solution.py:50
  67.9 7.1 %collective-permute-start.12 = (bf16[64,2560]{1,0:T(8,128)(2,1)S(1)}, bf16[64,2560]{1,0:T(8,128)(2,1)S(1)}, u32[]{:S(2)}, u32[]{:S(2)}) collective-permute-start(bf16[64,2560]{1,0:T(8,128)(2,1)S(1)} %slice.51), channel_id=1, source_target_pairs={{0,4},{1,5},{2,6},{3,7},{4,0},{5,1},{6,2},{7,3},{8,12},{9,13},{10,... | collective-permute-start | bytes 983048 | tf_op jit(solution)/shard_map/ppermute | solution.py:50
  75.2 8.0 %collective-permute-start.13 = (bf16[32,2560]{1,0:T(8,128)(2,1)S(1)}, bf16[32,2560]{1,0:T(8,128)(2,1)S(1)}, u32[]{:S(2)}, u32[]{:S(2)}) collective-permute-start(bf16[32,2560]{1,0:T(8,128)(2,1)S(1)} %slice.52), channel_id=1, source_target_pairs={{0,16},{1,17},{2,18},{3,19},{4,20},{5,21},{6,22},{7,23},{8,24},{9,... | collective-permute-start | bytes 491528 | tf_op jit(solution)/shard_map/ppermute | solution.py:50
  83.3 4.5 %collective-permute-start.14 = (bf16[16,2560]{1,0:T(8,128)(2,1)S(1)}, bf16[16,2560]{1,0:T(8,128)(2,1)S(1)}, u32[]{:S(2)}, u32[]{:S(2)}) collective-permute-start(bf16[16,2560]{1,0:T(8,128)(2,1)S(1)} %slice.53), channel_id=1, source_target_pairs={{0,8},{1,3},{2,10},{3,1},{4,12},{5,7},{6,14},{7,5},{8,0},{9,11},{1... | collective-permute-start | bytes 245768 | tf_op jit(solution)/shard_map/ppermute | solution.py:50
where the time goes:
time: 88.6 us; the launch traced here: 88.4 us
  waiting for transfers between devices  53 us (60%)
  starting transfers between devices  19 us (21%)
  Pallas kernels  14.5 us (16%)
  other arithmetic  1.69 us (2%)
    ppermute x10, waiting for transfers between devices, exchange(): return lax.ppermute(value, 'wide', pairs)  51.4 us
    ppermute x10, starting transfers between devices, exchange(): return lax.ppermute(value, 'wide', pairs)  17.9 us
    pallas_call x1, Pallas kernels, first_expert_rows(): pl.pallas_call(first_expert_kernel, name='expert_first', compiler_params=...  6.49 us
    pallas_call x1, Pallas kernels, second_expert_rows(): pl.pallas_call(second_expert_kernel, name='expert_second', compiler_param...  3.88 us
    pallas_call x1, Pallas kernels, attention_rows(): pl.pallas_call(functools.partial(attend_kernel, HEADS, row_count), name='...  3 us
  transfers between devices with their start and end apart: 15, of which 11 were waited for; matrix products, arithmetic and copies ran while one was open for 1% of the time, Pallas kernels for 9%

commit v1 on v0

--- a/solution.py
+++ b/solution.py
@@ -12,6 +12,7 @@
 LANES = 128
 TABLE_LANE = 64
 UNITS = 256
+PARTS = 2
 
 
 def near(value):
@@ -90,10 +91,11 @@
     keys_b_ref,
     values_a_ref,
     values_b_ref,
-    sent_ref,
-    kept_ref,
-    query_scratch,
+    *rest,
 ):
+    outputs, query_scratch = rest[:-1], rest[-1]
+    parts = len(outputs) // 2
+    part_heads = head_count // parts
     block_count = blocks_ref.shape[0]
     rows = block_count * row_count
     half = rows // 2
@@ -107,19 +109,22 @@
         query_scratch[slot * row_count : (slot + 1) * row_count, :] = queries_ref[
             pl.ds(start, row_count), :
         ]
-    peaks = jnp.zeros((rows, LANES), jnp.float32)
-    totals = jnp.zeros((rows, LANES), jnp.float32)
     lane = lane_iota((rows, LANES))
     contract_last = (((1,), (1,)), ((), ()))
     contract_rows = (((1,), (0,)), ((), ()))
     waiting = None
 
-    def put(tile, value):
+    def put(part, tile, value):
         columns = slice(tile * LANES, (tile + 1) * LANES)
-        kept_ref[:, columns] = value[:half]
-        sent_ref[:, columns] = value[half:].astype(jnp.bfloat16)
+        outputs[2 * part + 1][:, columns] = value[:half]
+        outputs[2 * part][:, columns] = value[half:].astype(jnp.bfloat16)
 
     for head in range(head_count):
+        part = head // part_heads
+        part_tiles = model_width // parts // LANES
+        if head % part_heads == 0:
+            peaks = jnp.zeros((rows, LANES), jnp.float32)
+            totals = jnp.zeros((rows, LANES), jnp.float32)
         low = head * key_size // LANES * LANES
         high = -(-(head + 1) * key_size // LANES) * LANES
         window = lane_iota((rows, high - low)) + low
@@ -140,8 +145,8 @@
         total = jnp.sum(raised_a, axis=1, keepdims=True) + jnp.sum(
             raised_b, axis=1, keepdims=True
         )
-        peaks = jnp.where(lane == head, peak, peaks)
-        totals = jnp.where(lane == head, total, totals)
+        peaks = jnp.where(lane == head % part_heads, peak, peaks)
+        totals = jnp.where(lane == head % part_heads, total, totals)
         low = head * value_size // LANES
         high = -(-(head + 1) * value_size // LANES)
         summed = lax.dot_general(
@@ -163,8 +168,9 @@
             if (tile + 1) * LANES > (head + 1) * value_size:
                 waiting = value
             else:
-                put(tile, value)
-    put(model_width // LANES, pack_stats(peaks, totals, head_count))
+                put(part, tile - part * part_tiles, value)
+        if (head + 1) % part_heads == 0:
+            put(part, part_tiles, pack_stats(peaks, totals, part_heads))
 
 
 def merged_parts(kept_ref, came_ref, head_count, model_width):
@@ -201,7 +207,8 @@
         sent_ref[:, columns] = value[half:].astype(jnp.bfloat16)
 
 
-def last_merge_kernel(head_count, kept_ref, came_ref, table_ref, sent_ref, next_ref):
+def last_merge_kernel(head_count, kept_ref, came_ref, *rest):
+    tables, (sent_ref, next_ref) = rest[:-2], rest[-2:]
     model_width = kept_ref.shape[1] - LANES
     half = kept_ref.shape[0] // 2
     peak, total, factor_a, factor_b = merged_parts(kept_ref, came_ref, head_count, model_width)
@@ -211,7 +218,9 @@
         columns = slice(tile * LANES, (tile + 1) * LANES)
         if tile * LANES == model_width:
             value = pack_stats(peak, total, head_count)
-            own = value[:half] + table_ref[...].astype(jnp.float32)
+            own = value[:half]
+            for table_ref in tables:
+                own = own + table_ref[...].astype(jnp.float32)
         else:
             value = kept_ref[:, columns] * expand_tile(
                 columns_a, tile, model_width // head_count
@@ -224,41 +233,54 @@
         sent_ref[half:, columns] = own.astype(jnp.bfloat16)
 
 
-def finish_kernel(head_count, kept_ref, came_ref, gain_ref, table_ref, block_ref, projected_ref):
-    model_width = kept_ref.shape[1] - LANES
-    half = kept_ref.shape[0] // 2
-    _, total, factor_a, factor_b = merged_parts(kept_ref, came_ref, head_count, model_width)
-    columns_a = head_columns(factor_a / total, head_count)
-    columns_b = head_columns(factor_b / total, head_count)
-    square = jnp.zeros((kept_ref.shape[0], LANES), jnp.float32)
-    for tile in range(model_width // LANES):
-        columns = slice(tile * LANES, (tile + 1) * LANES)
-        value = kept_ref[:, columns] * expand_tile(
-            columns_a, tile, model_width // head_count
-        ) + came_ref[:, columns].astype(jnp.float32) * expand_tile(
-            columns_b, tile, model_width // head_count
-        )
-        rounded = value.astype(jnp.bfloat16)
-        block_ref[:, columns] = rounded
-        projected_ref[:, columns] = rounded[:half]
-        residual = rounded.astype(jnp.float32)
-        square = square + residual * residual
-    mean = jnp.sum(square, axis=1, keepdims=True) / model_width
+def finish_kernel(head_count, gain_ref, table_ref, *rest):
+    parts = (len(rest) - 1) // 3
+    pairs, blocks, projected_ref = rest[: 2 * parts], rest[2 * parts : 3 * parts], rest[-1]
+    part_heads = head_count // parts
+    rows = pairs[0].shape[0]
+    half = rows // 2
+    width = pairs[0].shape[1] - LANES
+    square = jnp.zeros((rows, LANES), jnp.float32)
+    for part in range(parts):
+        kept_ref, came_ref = pairs[2 * part : 2 * part + 2]
+        _, total, factor_a, factor_b = merged_parts(kept_ref, came_ref, part_heads, width)
+        columns_a = head_columns(factor_a / total, part_heads)
+        columns_b = head_columns(factor_b / total, part_heads)
+        for tile in range(width // LANES):
+            columns = slice(tile * LANES, (tile + 1) * LANES)
+            value = kept_ref[:, columns] * expand_tile(
+                columns_a, tile, width // part_heads
+            ) + came_ref[:, columns].astype(jnp.float32) * expand_tile(
+                columns_b, tile, width // part_heads
+            )
+            rounded = value.astype(jnp.bfloat16)
+            blocks[part][:, columns] = rounded
+            low = part * width + tile * LANES
+            projected_ref[:, low : low + LANES] = rounded[:half]
+            residual = rounded.astype(jnp.float32)
+            square = square + residual * residual
+    mean = jnp.sum(square, axis=1, keepdims=True) / (parts * width)
     inverse = lax.rsqrt(mean + 1e-06)
-    normed = block_ref[:, :model_width].astype(jnp.float32) * inverse * gain_ref[...]
-    block_ref[:, :model_width] = normed.astype(jnp.bfloat16)
-    came_table = came_ref[half:, model_width:]
+    for part in range(parts):
+        gain = gain_ref[:, part * width : (part + 1) * width]
+        normed = blocks[part][:, :width].astype(jnp.float32) * inverse * gain
+        blocks[part][:, :width] = normed.astype(jnp.bfloat16)
+    came_table = pairs[1][half:, width:]
     lane = lane_iota(came_table.shape)
-    block_ref[:half, model_width:] = table_ref[...]
-    block_ref[half:, model_width:] = jnp.where(
+    blocks[0][:half, width:] = table_ref[...]
+    blocks[0][half:, width:] = jnp.where(
         lane >= TABLE_LANE, came_table.astype(jnp.float32), 0.0
     ).astype(jnp.bfloat16)
 
 
-def expert_math(expert_ref, rows_ref, gate_ref, up_ref, down_ref, out_ref, turned, hidden, ready):
-    model_width = out_ref.shape[1]
-    for low in range(0, rows_ref.shape[1], LANES):
-        turned[low : low + LANES, :] = rows_ref[:, low : low + LANES].T
+def hidden_units(expert_ref, row_refs, gate_ref, up_ref, turned, hidden, ready):
+    width = row_refs[1].shape[1]
+    model_width = width * len(row_refs)
+    for part, rows_ref in enumerate(row_refs):
+        for low in range(0, width, LANES):
+            at = part * width + low
+            turned[at : at + LANES, :] = rows_ref[:, low : low + LANES].T
+    turned[model_width:, :] = row_refs[0][:, width:].T
     scores = turned[model_width:, :].astype(jnp.float32)
     lane = lax.broadcasted_iota(jnp.int32, scores.shape, 0)
     chosen = jnp.where(lane == expert_ref[0] + TABLE_LANE, scores, 0.0)
@@ -271,24 +293,31 @@
         up_part = jnp.dot(up_ref[units, :], rows, preferred_element_type=jnp.float32)
         silu = gate_part / (1.0 + jnp.exp(-gate_part))
         hidden[:, units] = (silu * up_part * share).T.astype(jnp.bfloat16)
-    ready(None)
-    for low in range(0, model_width, 4 * LANES):
-        columns = slice(low, low + 4 * LANES)
-        out_ref[:, columns] = jnp.dot(
-            hidden[...], down_ref[:, columns], preferred_element_type=jnp.float32
+
+
+def down_product(hidden_ref, down_ref, out_ref, start):
+    width = out_ref.shape[1]
+    step = width // 2 if width % (4 * LANES) else 4 * LANES
+    for low in range(0, width, step):
+        out_ref[:, low : low + step] = jnp.dot(
+            hidden_ref[...],
+            down_ref[:, start + low : start + low + step],
+            preferred_element_type=jnp.float32,
         ).astype(out_ref.dtype)
 
 
 def first_expert_kernel(
     expert_ref,
-    rows_ref,
+    rows_a,
+    rows_b,
     gate_a,
     gate_b,
     up_a,
     up_b,
     down_a,
     down_b,
-    out_ref,
+    out_a,
+    out_b,
     gate_ref,
     up_ref,
     down_ref,
@@ -298,17 +327,14 @@
 ):
     per_half = gate_a.shape[0] // UNITS
     chunks = 2 * per_half
+    pairs = ((gate_a, gate_b), (up_a, up_b), (down_a, down_b))
+    targets = (gate_ref, up_ref, down_ref)
 
     def copy_of(part, chunk):
-        pair, target = ((gate_a, gate_b), (up_a, up_b), (down_a, down_b))[part], (
-            gate_ref,
-            up_ref,
-            down_ref,
-        )[part]
         low = chunk % per_half * UNITS
         return pltpu.make_async_copy(
-            pair[chunk // per_half].at[low : low + UNITS, :],
-            target.at[chunk * UNITS : (chunk + 1) * UNITS, :],
+            pairs[part][chunk // per_half].at[low : low + UNITS, :],
+            targets[part].at[chunk * UNITS : (chunk + 1) * UNITS, :],
             arrived.at[part, chunk],
         )
 
@@ -319,37 +345,32 @@
         copy_of(2, chunk).start()
 
     def ready(chunk):
-        if chunk is None:
-            for piece in range(chunks):
-                copy_of(2, piece).wait()
-        else:
-            copy_of(0, chunk).wait()
-            copy_of(1, chunk).wait()
-
-    expert_math(
-        expert_ref, rows_ref, gate_ref, up_ref, down_ref, out_ref, turned, hidden, ready
-    )
+        copy_of(0, chunk).wait()
+        copy_of(1, chunk).wait()
+
+    hidden_units(expert_ref, (rows_a, rows_b), gate_ref, up_ref, turned, hidden, ready)
+    for chunk in range(chunks):
+        copy_of(2, chunk).wait()
+    down_product(hidden, down_ref, out_a, 0)
+    down_product(hidden, down_ref, out_b, out_a.shape[1])
 
 
 def second_expert_kernel(
-    expert_ref, rows_ref, gate_ref, up_ref, down_ref, out_ref, turned, hidden
+    expert_ref, rows_a, rows_b, gate_ref, up_ref, down_ref, out_ref, hidden, turned
 ):
-    expert_math(
-        expert_ref,
-        rows_ref,
-        gate_ref,
-        up_ref,
-        down_ref,
-        out_ref,
-        turned,
-        hidden,
-        lambda chunk: None,
-    )
-
-
-def first_expert_rows(expert, rows, weights):
+    hidden_units(
+        expert_ref, (rows_a, rows_b), gate_ref, up_ref, turned, hidden, lambda chunk: None
+    )
+    down_product(hidden, down_ref, out_ref, 0)
+
+
+def rest_expert_kernel(start, hidden_ref, down_ref, out_ref):
+    down_product(hidden_ref, down_ref, out_ref, start)
+
+
+def first_expert_rows(expert, halves, weights):
     units, model_width = weights[0].shape
-    row_count, packed_width = rows.shape
+    row_count = halves[0].shape[0]
     whole = pl.BlockSpec(memory_space=pltpu.VMEM)
     anywhere = pl.BlockSpec(memory_space=pltpu.HBM)
     chunks = 2 * units // UNITS
@@ -357,12 +378,12 @@
         first_expert_kernel,
         name="expert_first",
         compiler_params=pltpu.CompilerParams(vmem_limit_bytes=12 << 20),
-        out_shape=(near_shape((row_count, model_width), jnp.float32),)
+        out_shape=(near_shape((row_count, model_width // 2), jnp.float32),) * 2
         + (near_shape((2 * units, model_width), jnp.bfloat16),) * 3,
-        in_specs=[pl.BlockSpec(memory_space=pltpu.SMEM), whole] + [anywhere] * 6,
-        out_specs=(whole,) * 4,
+        in_specs=[pl.BlockSpec(memory_space=pltpu.SMEM)] + [whole] * 2 + [anywhere] * 6,
+        out_specs=(whole,) * 5,
         scratch_shapes=[
-            pltpu.VMEM((packed_width, row_count), jnp.bfloat16),
+            pltpu.VMEM((model_width + LANES, row_count), jnp.bfloat16),
             pltpu.VMEM((row_count, 2 * units), jnp.bfloat16),
             pltpu.SemaphoreType.DMA((3, chunks)),
         ],
@@ -371,32 +392,43 @@
             transcendentals=0,
             bytes_accessed=12 * units * model_width,
         ),
-    )(expert, near(rows), *[far(weight) for weight in weights])
-
-
-def second_expert_rows(expert, rows, weights):
+    )(expert, *[near(half) for half in halves], *[far(weight) for weight in weights])
+
+
+def second_expert_rows(expert, halves, weights):
     units, model_width = weights[0].shape
-    row_count, packed_width = rows.shape
+    row_count = halves[0].shape[0]
+    width = model_width // 2
     whole = pl.BlockSpec(memory_space=pltpu.VMEM)
-    return pl.pallas_call(
+    first, hidden = pl.pallas_call(
         second_expert_kernel,
         name="expert_second",
         compiler_params=pltpu.CompilerParams(vmem_limit_bytes=12 << 20),
-        out_shape=near_shape((row_count, model_width), jnp.bfloat16),
-        in_specs=[pl.BlockSpec(memory_space=pltpu.SMEM)] + [whole] * 4,
+        out_shape=(
+            near_shape((row_count, width), jnp.bfloat16),
+            near_shape((row_count, units), jnp.bfloat16),
+        ),
+        in_specs=[pl.BlockSpec(memory_space=pltpu.SMEM)] + [whole] * 5,
+        out_specs=(whole, whole),
+        scratch_shapes=[pltpu.VMEM((model_width + LANES, row_count), jnp.bfloat16)],
+    )(expert, *[near(half) for half in halves], *[near(weight) for weight in weights])
+    second = pl.pallas_call(
+        functools.partial(rest_expert_kernel, width),
+        name="expert_rest",
+        compiler_params=pltpu.CompilerParams(vmem_limit_bytes=12 << 20),
+        out_shape=near_shape((row_count, width), jnp.bfloat16),
+        in_specs=[whole] * 2,
         out_specs=whole,
-        scratch_shapes=[
-            pltpu.VMEM((packed_width, row_count), jnp.bfloat16),
-            pltpu.VMEM((row_count, units), jnp.bfloat16),
-        ],
-    )(expert, near(rows), *[near(weight) for weight in weights])
+    )(near(hidden), near(weights[2]))
+    return [first, second]
 
 
 def attention_rows(
     queries, patch_keys, patch_values, other_keys, other_values, norm_gain, table, row_count, orders
 ):
     model_width = patch_values.shape[1]
-    packed_width = model_width + LANES
+    part_width = model_width // PARTS + LANES
+    part_heads = HEADS // PARTS
     group_size = queries.shape[0] // row_count
     stages = len(orders[0])
     device_index = lax.axis_index("wide")
@@ -418,17 +450,17 @@
 
     def pair_shapes(rows):
         return (
-            near_shape((rows, packed_width), jnp.bfloat16),
-            near_shape((rows, packed_width), jnp.float32),
-        )
-
-    sent, kept = pl.pallas_call(
+            near_shape((rows, part_width), jnp.bfloat16),
+            near_shape((rows, part_width), jnp.float32),
+        )
+
+    chains = pl.pallas_call(
         functools.partial(attend_kernel, HEADS, row_count),
         name="attend",
         compiler_params=pltpu.CompilerParams(vmem_limit_bytes=12 << 20),
-        out_shape=pair_shapes(rows // 2),
+        out_shape=pair_shapes(rows // 2) * PARTS,
         in_specs=[pl.BlockSpec(memory_space=pltpu.SMEM)] + [whole] * 5,
-        out_specs=(whole, whole),
+        out_specs=(whole,) * (2 * PARTS),
         scratch_shapes=[pltpu.VMEM((rows, queries.shape[1]), jnp.bfloat16)],
     )(
         blocks,
@@ -438,40 +470,39 @@
         far(patch_values),
         near(other_values),
     )
-    for stage in range(stages - 1):
-        came = exchange(sent, orders, stage)
-        rows = kept.shape[0]
-        if stage < stages - 2:
+    finished = []
+    for part in range(PARTS):
+        sent, kept = chains[2 * part : 2 * part + 2]
+        for stage in range(stages - 1):
+            came = exchange(sent, orders, stage)
+            rows = kept.shape[0]
+            last = stage == stages - 2
+            operands = [near(kept), near(came)]
+            if last and part == 0:
+                operands.append(near(table))
             sent, kept = pl.pallas_call(
-                functools.partial(merge_kernel, HEADS),
-                name="merge",
+                functools.partial(last_merge_kernel if last else merge_kernel, part_heads),
                 compiler_params=pltpu.CompilerParams(vmem_limit_bytes=6 << 20),
-                out_shape=pair_shapes(rows // 2),
-                in_specs=[whole] * 2,
+                out_shape=pair_shapes(rows if last else rows // 2),
+                in_specs=[whole] * len(operands),
                 out_specs=(whole, whole),
-            )(near(kept), near(came))
-        else:
-            sent, kept = pl.pallas_call(
-                functools.partial(last_merge_kernel, HEADS),
-                name="last_merge",
-                compiler_params=pltpu.CompilerParams(vmem_limit_bytes=6 << 20),
-                out_shape=pair_shapes(rows),
-                in_specs=[whole] * 3,
-                out_specs=(whole, whole),
-            )(near(kept), near(came), near(table))
-    came = exchange(sent, orders, stages - 1)
+            )(*operands)
+        came = exchange(sent, orders, stages - 1)
+        finished += [near(kept), near(came)]
     rows = kept.shape[0]
-    return pl.pallas_call(
+    *blocks, projected = pl.pallas_call(
         functools.partial(finish_kernel, HEADS),
         name="finish",
         compiler_params=pltpu.CompilerParams(vmem_limit_bytes=6 << 20),
-        out_shape=(
-            near_shape((rows, packed_width), jnp.bfloat16),
-            near_shape((row_count, model_width), jnp.bfloat16),
-        ),
-        in_specs=[whole] * 4,
-        out_specs=(whole, whole),
-    )(near(kept), near(came), near(norm_gain.reshape(1, model_width)), near(table))
+        out_shape=tuple(
+            near_shape((rows, model_width // PARTS + (LANES if part == 0 else 0)), jnp.bfloat16)
+            for part in range(PARTS)
+        )
+        + (near_shape((row_count, model_width), jnp.bfloat16),),
+        in_specs=[whole] * (2 + 2 * PARTS),
+        out_specs=(whole,) * (PARTS + 1),
+    )(near(norm_gain.reshape(1, model_width)), near(table), *finished)
+    return blocks, projected
 
 
 def on_device(
@@ -499,7 +530,7 @@
     weights = []
     for own in halves:
         weights += [own, partner(own, "wide", 0)]
-    block, projected = attention_rows(
+    blocks, projected = attention_rows(
         queries,
         patch_keys,
         patch_values,
@@ -511,18 +542,26 @@
         merge_order,
     )
     stages = len(gather_order[0])
-    for stage in range(stages - 1):
-        block = jnp.concatenate([block, exchange(block, gather_order, stage)], axis=0)
-    came = exchange(block, gather_order, stages - 1)
+    came = []
+    for part in range(PARTS):
+        for stage in range(stages - 1):
+            arrived = exchange(blocks[part], gather_order, stage)
+            blocks[part] = jnp.concatenate([blocks[part], arrived], axis=0)
+        came.append(exchange(blocks[part], gather_order, stages - 1))
     expert = (device_index // 2).reshape(1)
-    total, *weights = first_expert_rows(expert, block, weights)
-    sent = second_expert_rows(expert, came, weights)
-    total = total + exchange(sent, scatter_order, 0).astype(jnp.float32)
-    for stage in range(1, len(scatter_order[0])):
-        half_rows = total.shape[0] // 2
-        total = total[:half_rows] + exchange(
-            total[half_rows:].astype(jnp.bfloat16), scatter_order, stage
-        ).astype(jnp.float32)
+    *totals, gate, up, down = first_expert_rows(expert, blocks, weights)
+    outputs = []
+    for part, sent in enumerate(second_expert_rows(expert, came, (gate, up, down))):
+        kept = totals[part]
+        for stage in range(len(scatter_order[0])):
+            arrived = exchange(sent, scatter_order, stage)
+            kept = kept + arrived.astype(jnp.float32)
+            half_rows = kept.shape[0] // 2
+            if stage < len(scatter_order[0]) - 1:
+                sent = kept[half_rows:].astype(jnp.bfloat16)
+                kept = kept[:half_rows]
+        outputs.append(kept)
+    total = jnp.concatenate(outputs, axis=1)
     return (projected.astype(jnp.float32) + total).astype(jnp.bfloat16)
 
 

time: 88.6 us -> 82.1 us (0.927)
  waiting for transfers between devices: 53 us -> 31.2 us
  starting transfers between devices: 19 us -> 33.2 us
  Pallas kernels: 14.5 us -> 15.4 us
    ppermute x10 -> x20, waiting for transfers between devices: 51.4 us -> 28.9 us  [exchange(): return lax.ppermute(value, 'wide', pairs)]
    ppermute x10 -> x20, starting transfers between devices: 17.9 us -> 31.7 us  [exchange(): return lax.ppermute(value, 'wide', pairs)]
  transfers between devices with their start and end apart: 15 -> 25, of which waited for: 11 -> 15; matrix products, arithmetic and copies ran while one was open for 1% -> 1% of each run, Pallas kernels for 9% -> 14%
where the time goes in v1:
time: 82.1 us; the launch traced here: 81.9 us
  starting transfers between devices  33.2 us (40%)
  waiting for transfers between devices  31.2 us (38%)
  Pallas kernels  15.4 us (19%)
  other arithmetic  1.7 us (2%)
    ppermute x20, starting transfers between devices, exchange(): return lax.ppermute(value, 'wide', pairs)  31.7 us
    ppermute x20, waiting for transfers between devices, exchange(): return lax.ppermute(value, 'wide', pairs)  28.9 us
    pallas_call x1, Pallas kernels, first_expert_rows(): pl.pallas_call(first_expert_kernel, name='expert_first', compiler_params=...  6.64 us
    pallas_call x1, Pallas kernels, second_expert_rows(): pl.pallas_call(second_expert_kernel, name='expert_second', compiler_param...  3.6 us
    pallas_call x1, Pallas kernels, attention_rows(): pl.pallas_call(functools.partial(attend_kernel, HEADS, row_count), name='...  3.21 us
    ppermute x5, waiting for transfers between devices, partner(): return lax.ppermute(value, axis, pairs)  2.29 us
  transfers between devices with their start and end apart: 25, of which 15 were waited for; matrix products, arithmetic and copies ran while one was open for 1% of the time, Pallas kernels for 14%

profile of v1, /device:TPU:0, one launch (start us, length us, event | category | flops | bytes accessed | tf_op | source)
XLA Modules:
  0.0 81.9 jit_solution(2369134264940293959)
XLA Ops:
  0.6 2.3 %collective-permute-done.keys_b_ref = bf16[128,1152]{1,0:T(8,128)(2,1)S(1)} collective-permute-done((bf16[128,1152]{1,0:T(8,128)(2,1)}, bf16[128,1152]{1,0:T(8,128)(2,1)S(1)}, u32[]{:S(2)}, u32[]{:S(2)}) %collective-permute-start) | collective-permute-done | bytes 294944 | tf_op jit(solution)/shard_map/ppermute | solution.py:33
  3.8 0.7 fusion.2.blocks_ref
  4.5 3.2 %attend.1 = (bf16[64,1408]{1,0:T(8,128)(2,1)S(1)}, f32[64,1408]{1,0:T(8,128)S(1)}, bf16[64,1408]{1,0:T(8,128)(2,1)S(1)}, f32[64,1408]{1,0:T(8,128)S(1)}) custom-call(s32[8]{0:T(128)S(1)} %fusion.2.blocks_ref, bf16[256,1152]{1,0:T(8,128)(2,1)} %queries_ref.1, bf16[128,1152]{1,0:T(8,128)(2,1)} %keys_a_ref.1, ...), custom_call_target="tpu_custom_call" | custom-call | tf_op jit(solution)/shard_map/attend/pallas_call | solution.py:457
  7.7 2.7 %collective-permute-start.5 = (bf16[64,1408]{1,0:T(8,128)(2,1)S(1)}, bf16[64,1408]{1,0:T(8,128)(2,1)S(1)}, u32[]{:S(2)}, u32[]{:S(2)}) collective-permute-start(bf16[64,1408]{1,0:T(8,128)(2,1)S(1)} %get-tuple-element.41), channel_id=1, source_target_pairs={{0,2},{1,5},{2,0},{3,7},{4,6},{5,1},{6,4},{7,3},{8,10},{9,13},{10,... | collective-permute-start | bytes 540680 | tf_op jit(solution)/shard_map/ppermute | solution.py:51
  10.5 3.4 %collective-permute-done.5.came_ref = bf16[64,1408]{1,0:T(8,128)(2,1)S(1)} collective-permute-done((bf16[64,1408]{1,0:T(8,128)(2,1)S(1)}, bf16[64,1408]{1,0:T(8,128)(2,1)S(1)}, u32[]{:S(2)}, u32[]{:S(2)}) %collective-permute-start.5) | collective-permute-done | bytes 180256 | tf_op jit(solution)/shard_map/ppermute | solution.py:51
  14.1 2.1 %collective-permute-start.6 = (bf16[32,1408]{1,0:T(8,128)(2,1)S(1)}, bf16[32,1408]{1,0:T(8,128)(2,1)S(1)}, u32[]{:S(2)}, u32[]{:S(2)}) collective-permute-start(bf16[32,1408]{1,0:T(8,128)(2,1)S(1)} %get-tuple-element.43), channel_id=1, source_target_pairs={{0,4},{1,9},{2,6},{3,11},{4,0},{5,13},{6,2},{7,15},{8,12},{9,1},{1... | collective-permute-start | bytes 270344 | tf_op jit(solution)/shard_map/ppermute | solution.py:51
  16.5 1.7 %collective-permute-start.3 = (bf16[32,1408]{1,0:T(8,128)(2,1)S(1)}, bf16[32,1408]{1,0:T(8,128)(2,1)S(1)}, u32[]{:S(2)}, u32[]{:S(2)}) collective-permute-start(bf16[32,1408]{1,0:T(8,128)(2,1)S(1)} %get-tuple-element.37), channel_id=1, source_target_pairs={{0,4},{1,9},{2,6},{3,11},{4,0},{5,13},{6,2},{7,15},{8,12},{9,1},{1... | collective-permute-start | bytes 270344 | tf_op jit(solution)/shard_map/ppermute | solution.py:51
  18.9 2.1 %collective-permute-start.7 = (bf16[32,1408]{1,0:T(8,128)(2,1)S(1)}, bf16[32,1408]{1,0:T(8,128)(2,1)S(1)}, u32[]{:S(2)}, u32[]{:S(2)}) collective-permute-start(bf16[32,1408]{1,0:T(8,128)(2,1)S(1)} %get-tuple-element.45), channel_id=1, source_target_pairs={{0,8},{1,3},{2,10},{3,1},{4,12},{5,7},{6,14},{7,5},{8,0},{9,11},{1... | collective-permute-start | bytes 270344 | tf_op jit(solution)/shard_map/ppermute | solution.py:51
  21.2 1.7 %collective-permute-start.4 = (bf16[32,1408]{1,0:T(8,128)(2,1)S(1)}, bf16[32,1408]{1,0:T(8,128)(2,1)S(1)}, u32[]{:S(2)}, u32[]{:S(2)}) collective-permute-start(bf16[32,1408]{1,0:T(8,128)(2,1)S(1)} %get-tuple-element.39), channel_id=1, source_target_pairs={{0,8},{1,3},{2,10},{3,1},{4,12},{5,7},{6,14},{7,5},{8,0},{9,11},{1... | collective-permute-start | bytes 270344 | tf_op jit(solution)/shard_map/ppermute | solution.py:51
  23.5 2.3 %collective-permute-done.4.rest_1_ = bf16[32,1408]{1,0:T(8,128)(2,1)S(1)} collective-permute-done((bf16[32,1408]{1,0:T(8,128)(2,1)S(1)}, bf16[32,1408]{1,0:T(8,128)(2,1)S(1)}, u32[]{:S(2)}, u32[]{:S(2)}) %collective-permute-start.4) | collective-permute-done | bytes 90144 | tf_op jit(solution)/shard_map/ppermute | solution.py:51
  26.4 2.7 %collective-permute-start.10 = (bf16[32,1280]{1,0:T(8,128)(2,1)S(1)}, bf16[32,1280]{1,0:T(8,128)(2,1)S(1)}, u32[]{:S(2)}, u32[]{:S(2)}) collective-permute-start(bf16[32,1280]{1,0:T(8,128)(2,1)S(1)} %get-tuple-element.48), channel_id=1, source_target_pairs={{0,16},{1,17},{2,18},{3,19},{4,20},{5,21},{6,22},{7,23},{8,24},{9,... | collective-permute-start | bytes 245768 | tf_op jit(solution)/shard_map/ppermute | solution.py:51
  29.4 4.2 %collective-permute-done.10 = bf16[32,1280]{1,0:T(8,128)(2,1)S(1)} collective-permute-done((bf16[32,1280]{1,0:T(8,128)(2,1)S(1)}, bf16[32,1280]{1,0:T(8,128)(2,1)S(1)}, u32[]{:S(2)}, u32[]{:S(2)}) %collective-permute-start.10) | collective-permute-done | bytes 81952 | tf_op jit(solution)/shard_map/ppermute | solution.py:51
  33.6 1.6 %collective-permute-start.11 = (bf16[64,1280]{1,0:T(8,128)(2,1)S(1)}, bf16[64,1280]{1,0:T(8,128)(2,1)S(1)}, u32[]{:S(2)}, u32[]{:S(2)}) collective-permute-start(bf16[64,1280]{1,0:T(8,128)(2,1)S(1)} %pad_maximum_fusion.1), channel_id=1, source_target_pairs={{0,4},{1,5},{2,6},{3,7},{4,0},{5,1},{6,2},{7,3},{8,12},{9,13},{10,... | collective-permute-start | bytes 491528 | tf_op jit(solution)/shard_map/ppermute | solution.py:51
  35.3 0.9 %collective-permute-start.9 = (bf16[64,1408]{1,0:T(8,128)(2,1)S(1)}, bf16[64,1408]{1,0:T(8,128)(2,1)S(1)}, u32[]{:S(2)}, u32[]{:S(2)}) collective-permute-start(bf16[64,1408]{1,0:T(8,128)(2,1)S(1)} %pad_maximum_fusion), channel_id=1, source_target_pairs={{0,4},{1,5},{2,6},{3,7},{4,0},{5,1},{6,2},{7,3},{8,12},{9,13},{10,... | collective-permute-start | bytes 540680 | tf_op jit(solution)/shard_map/ppermute | solution.py:51
  36.2 4.7 %collective-permute-done.9 = bf16[64,1408]{1,0:T(8,128)(2,1)S(1)} collective-permute-done((bf16[64,1408]{1,0:T(8,128)(2,1)S(1)}, bf16[64,1408]{1,0:T(8,128)(2,1)S(1)}, u32[]{:S(2)}, u32[]{:S(2)}) %collective-permute-start.9) | collective-permute-done | bytes 180256 | tf_op jit(solution)/shard_map/ppermute | solution.py:51
  41.0 1.5 %collective-permute-start.15 = (bf16[128,1408]{1,0:T(8,128)(2,1)S(1)}, bf16[128,1408]{1,0:T(8,128)(2,1)S(1)}, u32[]{:S(2)}, u32[]{:S(2)}) collective-permute-start(bf16[128,1408]{1,0:T(8,128)(2,1)S(1)} %constant_dynamic-update-slice_fusion.rows_a), channel_id=1, source_target_pairs={{0,2},{1,9},{2,0},{3,11},{4,6},{5,13},{6,4},{7,15},{8,10},{9,1},{1... | collective-permute-start | bytes 1081352 | tf_op jit(solution)/shard_map/ppermute | solution.py:51
  43.2 6.6 %expert_first.1 = (f32[128,1280]{1,0:T(8,128)S(1)}, f32[128,1280]{1,0:T(8,128)S(1)}, bf16[1024,2560]{1,0:T(8,128)(2,1)S(1)}, bf16[1024,2560]{1,0:T(8,128)(2,1)S(1)}, bf16[1024,2560]{1,0:T(8,128)(2,1)S(1)}) custom-call(s32[1]{0:T(128)} %bitcast.1.expert_ref, bf16[128,1408]{1,0:T(8,128)(2,1)S(1)} %constant_dynamic-update-slice_fusion.rows_a, ...), custom_call_target="tpu_custom_call" | custom-call | flops 2013265920 | bytes 15728640 | tf_op jit(solution)/shard_map/expert_first/pallas_call | solution.py:377
  49.8 2.2 %collective-permute-done.16.rows_b = bf16[128,1280]{1,0:T(8,128)(2,1)S(1)} collective-permute-done((bf16[128,1280]{1,0:T(8,128)(2,1)S(1)}, bf16[128,1280]{1,0:T(8,128)(2,1)S(1)}, u32[]{:S(2)}, u32[]{:S(2)}) %collective-permute-start.16) | collective-permute-done | bytes 327712 | tf_op jit(solution)/shard_map/ppermute | solution.py:51
  52.0 3.6 %expert_second.1 = (bf16[128,1280]{1,0:T(8,128)(2,1)S(1)}, bf16[128,1024]{1,0:T(8,128)(2,1)S(1)}) custom-call(s32[1]{0:T(128)} %bitcast.1.expert_ref, bf16[128,1408]{1,0:T(8,128)(2,1)S(1)} %collective-permute-done.15.rows_a, bf16[128,1280]{1,0:T(8,128)(2,1)S(1)} %collective-permute-done.16.rows_b, bf16[1024,2560]{1,0:T(8,128)(2,1)S(1)} %get-tuple-element.53.gate_ref, ...), custom_call_target="tpu_custom_call" | custom-call | tf_op jit(solution)/shard_map/expert_second/pallas_call | solution.py:403
  55.6 1.5 %collective-permute-start.17 = (bf16[128,1280]{1,0:T(8,128)(2,1)S(1)}, bf16[128,1280]{1,0:T(8,128)(2,1)S(1)}, u32[]{:S(2)}, u32[]{:S(2)}) collective-permute-start(bf16[128,1280]{1,0:T(8,128)(2,1)S(1)} %get-tuple-element.56), channel_id=1, source_target_pairs={{0,2},{1,9},{2,0},{3,11},{4,6},{5,13},{6,4},{7,15},{8,10},{9,1},{1... | collective-permute-start | bytes 983048 | tf_op jit(solution)/shard_map/ppermute | solution.py:51
  58.3 4.4 %collective-permute-done.17 = bf16[128,1280]{1,0:T(8,128)(2,1)S(1)} collective-permute-done((bf16[128,1280]{1,0:T(8,128)(2,1)S(1)}, bf16[128,1280]{1,0:T(8,128)(2,1)S(1)}, u32[]{:S(2)}, u32[]{:S(2)}) %collective-permute-start.17) | collective-permute-done | bytes 327712 | tf_op jit(solution)/shard_map/ppermute | solution.py:51
  62.8 1.6 %collective-permute-start.18 = (bf16[64,1280]{1,0:T(8,128)(2,1)S(1)}, bf16[64,1280]{1,0:T(8,128)(2,1)S(1)}, u32[]{:S(2)}, u32[]{:S(2)}) collective-permute-start(bf16[64,1280]{1,0:T(8,128)(2,1)S(1)} %slice.87), channel_id=1, source_target_pairs={{0,4},{1,5},{2,6},{3,7},{4,0},{5,1},{6,2},{7,3},{8,12},{9,13},{10,... | collective-permute-start | bytes 491528 | tf_op jit(solution)/shard_map/ppermute | solution.py:51
  64.4 1.8 %collective-permute-done.21 = bf16[128,1280]{1,0:T(8,128)(2,1)S(1)} collective-permute-done((bf16[128,1280]{1,0:T(8,128)(2,1)S(1)}, bf16[128,1280]{1,0:T(8,128)(2,1)S(1)}, u32[]{:S(2)}, u32[]{:S(2)}) %collective-permute-start.21) | collective-permute-done | bytes 327712 | tf_op jit(solution)/shard_map/ppermute | solution.py:51
  66.3 1.6 %collective-permute-start.22 = (bf16[64,1280]{1,0:T(8,128)(2,1)S(1)}, bf16[64,1280]{1,0:T(8,128)(2,1)S(1)}, u32[]{:S(2)}, u32[]{:S(2)}) collective-permute-start(bf16[64,1280]{1,0:T(8,128)(2,1)S(1)} %slice.86), channel_id=1, source_target_pairs={{0,4},{1,5},{2,6},{3,7},{4,0},{5,1},{6,2},{7,3},{8,12},{9,13},{10,... | collective-permute-start | bytes 491528 | tf_op jit(solution)/shard_map/ppermute | solution.py:51
  68.3 2.4 %collective-permute-start.19 = (bf16[32,1280]{1,0:T(8,128)(2,1)S(1)}, bf16[32,1280]{1,0:T(8,128)(2,1)S(1)}, u32[]{:S(2)}, u32[]{:S(2)}) collective-permute-start(bf16[32,1280]{1,0:T(8,128)(2,1)S(1)} %slice.89), channel_id=1, source_target_pairs={{0,16},{1,17},{2,18},{3,19},{4,20},{5,21},{6,22},{7,23},{8,24},{9,... | collective-permute-start | bytes 245768 | tf_op jit(solution)/shard_map/ppermute | solution.py:51
  70.7 1.0 %collective-permute-done.22 = bf16[64,1280]{1,0:T(8,128)(2,1)S(1)} collective-permute-done((bf16[64,1280]{1,0:T(8,128)(2,1)S(1)}, bf16[64,1280]{1,0:T(8,128)(2,1)S(1)}, u32[]{:S(2)}, u32[]{:S(2)}) %collective-permute-start.22) | collective-permute-done | bytes 163872 | tf_op jit(solution)/shard_map/ppermute | solution.py:51
  71.8 1.0 %collective-permute-start.23 = (bf16[32,1280]{1,0:T(8,128)(2,1)S(1)}, bf16[32,1280]{1,0:T(8,128)(2,1)S(1)}, u32[]{:S(2)}, u32[]{:S(2)}) collective-permute-start(bf16[32,1280]{1,0:T(8,128)(2,1)S(1)} %slice.88), channel_id=1, source_target_pairs={{0,16},{1,17},{2,18},{3,19},{4,20},{5,21},{6,22},{7,23},{8,24},{9,... | collective-permute-start | bytes 245768 | tf_op jit(solution)/shard_map/ppermute | solution.py:51
  72.8 0.9 %collective-permute-done.19 = bf16[32,1280]{1,0:T(8,128)(2,1)S(1)} collective-permute-done((bf16[32,1280]{1,0:T(8,128)(2,1)S(1)}, bf16[32,1280]{1,0:T(8,128)(2,1)S(1)}, u32[]{:S(2)}, u32[]{:S(2)}) %collective-permute-start.19) | collective-permute-done | bytes 81952 | tf_op jit(solution)/shard_map/ppermute | solution.py:51
  73.7 2.9 %collective-permute-start.20 = (bf16[16,1280]{1,0:T(8,128)(2,1)S(1)}, bf16[16,1280]{1,0:T(8,128)(2,1)S(1)}, u32[]{:S(2)}, u32[]{:S(2)}) collective-permute-start(bf16[16,1280]{1,0:T(8,128)(2,1)S(1)} %slice.91), channel_id=1, source_target_pairs={{0,8},{1,3},{2,10},{3,1},{4,12},{5,7},{6,14},{7,5},{8,0},{9,11},{1... | collective-permute-start | bytes 122888 | tf_op jit(solution)/shard_map/ppermute | solution.py:51
  77.2 1.9 %collective-permute-start.24 = (bf16[16,1280]{1,0:T(8,128)(2,1)S(1)}, bf16[16,1280]{1,0:T(8,128)(2,1)S(1)}, u32[]{:S(2)}, u32[]{:S(2)}) collective-permute-start(bf16[16,1280]{1,0:T(8,128)(2,1)S(1)} %slice.90), channel_id=1, source_target_pairs={{0,8},{1,3},{2,10},{3,1},{4,12},{5,7},{6,14},{7,5},{8,0},{9,11},{1... | collective-permute-start | bytes 122888 | tf_op jit(solution)/shard_map/ppermute | solution.py:51
  79.1 2.1 %collective-permute-done.24 = bf16[16,1280]{1,0:T(8,128)(2,1)S(1)} collective-permute-done((bf16[16,1280]{1,0:T(8,128)(2,1)S(1)}, bf16[16,1280]{1,0:T(8,128)(2,1)S(1)}, u32[]{:S(2)}, u32[]{:S(2)}) %collective-permute-start.24) | collective-permute-done | bytes 40992 | tf_op jit(solution)/shard_map/ppermute | solution.py:51
  81.3 0.7 fusion
  (61 shorter events, 7.4 us)
Async XLA Ops:
  0.0 18.1 %copy-start.2 = (s32[16,6]{0,1:T(8,128)S(1)}, s32[16,6]{0,1:T(8,128)}, u32[]{:S(2)}) copy-start(s32[16,6]{0,1:T(8,128)} %param.14) | copy-start | bytes 1156
  0.0 18.1 %copy-start.1 = (s32[16,6]{0,1:T(8,128)S(1)}, s32[16,6]{0,1:T(8,128)}, u32[]{:S(2)}) copy-start(s32[16,6]{0,1:T(8,128)} %param.15) | copy-start | bytes 1156
  0.0 23.0 %copy-start = (f32[2560]{0:T(1024)S(1)}, f32[2560]{0:T(1024)}, u32[]{:S(2)}) copy-start(f32[2560]{0:T(1024)} %param.13) | copy-start | bytes 30724
  0.0 2.9 %collective-permute-start.1 = (bf16[128,2560]{1,0:T(8,128)(2,1)}, bf16[128,2560]{1,0:T(8,128)(2,1)S(1)}, u32[]{:S(2)}, u32[]{:S(2)}) collective-permute-start(bf16[128,2560]{1,0:T(8,128)(2,1)} %values_a_ref.1), channel_id=1, source_target_pairs={{0,1},{1,0},{2,3},{3,2},{4,5},{5,4},{6,7},{7,6},{8,9},{9,8},{10,11... | collective-permute-start | bytes 1966088 | tf_op jit(solution)/shard_map/ppermute | solution.py:33
  0.6 2.4 %collective-permute-start = (bf16[128,1152]{1,0:T(8,128)(2,1)}, bf16[128,1152]{1,0:T(8,128)(2,1)S(1)}, u32[]{:S(2)}, u32[]{:S(2)}) collective-permute-start(bf16[128,1152]{1,0:T(8,128)(2,1)} %keys_a_ref.1), channel_id=1, source_target_pairs={{0,1},{1,0},{2,3},{3,2},{4,5},{5,4},{6,7},{7,6},{8,9},{9,8},{10,11... | collective-permute-start | bytes 884744 | tf_op jit(solution)/shard_map/ppermute | solution.py:33
  2.9 40.2 %collective-permute-start.12 = (bf16[512,2560]{1,0:T(8,128)(2,1)}, bf16[512,2560]{1,0:T(8,128)(2,1)}, u32[]{:S(2)}, u32[]{:S(2)}) collective-permute-start(bf16[512,2560]{1,0:T(8,128)(2,1)} %gate_a), channel_id=1, source_target_pairs={{0,1},{1,0},{2,3},{3,2},{4,5},{5,4},{6,7},{7,6},{8,9},{9,8},{10,11... | collective-permute-start | bytes 7864328 | tf_op jit(solution)/shard_map/ppermute | solution.py:33
  3.3 39.8 %collective-permute-start.13 = (bf16[512,2560]{1,0:T(8,128)(2,1)}, bf16[512,2560]{1,0:T(8,128)(2,1)}, u32[]{:S(2)}, u32[]{:S(2)}) collective-permute-start(bf16[512,2560]{1,0:T(8,128)(2,1)} %up_a), channel_id=1, source_target_pairs={{0,1},{1,0},{2,3},{3,2},{4,5},{5,4},{6,7},{7,6},{8,9},{9,8},{10,11... | collective-permute-start | bytes 7864328 | tf_op jit(solution)/shard_map/ppermute | solution.py:33
  3.4 39.7 %collective-permute-start.14 = (bf16[512,2560]{1,0:T(8,128)(2,1)}, bf16[512,2560]{1,0:T(8,128)(2,1)}, u32[]{:S(2)}, u32[]{:S(2)}) collective-permute-start(bf16[512,2560]{1,0:T(8,128)(2,1)} %down_a), channel_id=1, source_target_pairs={{0,1},{1,0},{2,3},{3,2},{4,5},{5,4},{6,7},{7,6},{8,9},{9,8},{10,11... | collective-permute-start | bytes 7864328 | tf_op jit(solution)/shard_map/ppermute | solution.py:33
  7.7 6.2 %collective-permute-start.5 = (bf16[64,1408]{1,0:T(8,128)(2,1)S(1)}, bf16[64,1408]{1,0:T(8,128)(2,1)S(1)}, u32[]{:S(2)}, u32[]{:S(2)}) collective-permute-start(bf16[64,1408]{1,0:T(8,128)(2,1)S(1)} %get-tuple-element.41), channel_id=1, source_target_pairs={{0,2},{1,5},{2,0},{3,7},{4,6},{5,1},{6,4},{7,3},{8,10},{9,13},{10,... | collective-permute-start | bytes 540680 | tf_op jit(solution)/shard_map/ppermute | solution.py:51
  10.4 5.8 %collective-permute-start.2 = (bf16[64,1408]{1,0:T(8,128)(2,1)S(1)}, bf16[64,1408]{1,0:T(8,128)(2,1)S(1)}, u32[]{:S(2)}, u32[]{:S(2)}) collective-permute-start(bf16[64,1408]{1,0:T(8,128)(2,1)S(1)} %get-tuple-element.35), channel_id=1, source_target_pairs={{0,2},{1,5},{2,0},{3,7},{4,6},{5,1},{6,4},{7,3},{8,10},{9,13},{10,... | collective-permute-start | bytes 540680 | tf_op jit(solution)/shard_map/ppermute | solution.py:51
  14.1 4.6 %collective-permute-start.6 = (bf16[32,1408]{1,0:T(8,128)(2,1)S(1)}, bf16[32,1408]{1,0:T(8,128)(2,1)S(1)}, u32[]{:S(2)}, u32[]{:S(2)}) collective-permute-start(bf16[32,1408]{1,0:T(8,128)(2,1)S(1)} %get-tuple-element.43), channel_id=1, source_target_pairs={{0,4},{1,9},{2,6},{3,11},{4,0},{5,13},{6,2},{7,15},{8,12},{9,1},{1... | collective-permute-start | bytes 270344 | tf_op jit(solution)/shard_map/ppermute | solution.py:51
  16.5 4.6 %collective-permute-start.3 = (bf16[32,1408]{1,0:T(8,128)(2,1)S(1)}, bf16[32,1408]{1,0:T(8,128)(2,1)S(1)}, u32[]{:S(2)}, u32[]{:S(2)}) collective-permute-start(bf16[32,1408]{1,0:T(8,128)(2,1)S(1)} %get-tuple-element.37), channel_id=1, source_target_pairs={{0,4},{1,9},{2,6},{3,11},{4,0},{5,13},{6,2},{7,15},{8,12},{9,1},{1... | collective-permute-start | bytes 270344 | tf_op jit(solution)/shard_map/ppermute | solution.py:51
  18.9 4.7 %collective-permute-start.7 = (bf16[32,1408]{1,0:T(8,128)(2,1)S(1)}, bf16[32,1408]{1,0:T(8,128)(2,1)S(1)}, u32[]{:S(2)}, u32[]{:S(2)}) collective-permute-start(bf16[32,1408]{1,0:T(8,128)(2,1)S(1)} %get-tuple-element.45), channel_id=1, source_target_pairs={{0,8},{1,3},{2,10},{3,1},{4,12},{5,7},{6,14},{7,5},{8,0},{9,11},{1... | collective-permute-start | bytes 270344 | tf_op jit(solution)/shard_map/ppermute | solution.py:51
  21.2 4.6 %collective-permute-start.4 = (bf16[32,1408]{1,0:T(8,128)(2,1)S(1)}, bf16[32,1408]{1,0:T(8,128)(2,1)S(1)}, u32[]{:S(2)}, u32[]{:S(2)}) collective-permute-start(bf16[32,1408]{1,0:T(8,128)(2,1)S(1)} %get-tuple-element.39), channel_id=1, source_target_pairs={{0,8},{1,3},{2,10},{3,1},{4,12},{5,7},{6,14},{7,5},{8,0},{9,11},{1... | collective-permute-start | bytes 270344 | tf_op jit(solution)/shard_map/ppermute | solution.py:51
  26.4 7.2 %collective-permute-start.10 = (bf16[32,1280]{1,0:T(8,128)(2,1)S(1)}, bf16[32,1280]{1,0:T(8,128)(2,1)S(1)}, u32[]{:S(2)}, u32[]{:S(2)}) collective-permute-start(bf16[32,1280]{1,0:T(8,128)(2,1)S(1)} %get-tuple-element.48), channel_id=1, source_target_pairs={{0,16},{1,17},{2,18},{3,19},{4,20},{5,21},{6,22},{7,23},{8,24},{9,... | collective-permute-start | bytes 245768 | tf_op jit(solution)/shard_map/ppermute | solution.py:51
  29.1 6.1 %collective-permute-start.8 = (bf16[32,1408]{1,0:T(8,128)(2,1)S(1)}, bf16[32,1408]{1,0:T(8,128)(2,1)S(1)}, u32[]{:S(2)}, u32[]{:S(2)}) collective-permute-start(bf16[32,1408]{1,0:T(8,128)(2,1)S(1)} %get-tuple-element.47), channel_id=1, source_target_pairs={{0,16},{1,17},{2,18},{3,19},{4,20},{5,21},{6,22},{7,23},{8,24},{9,... | collective-permute-start | bytes 270344 | tf_op jit(solution)/shard_map/ppermute | solution.py:51
  33.6 8.9 %collective-permute-start.11 = (bf16[64,1280]{1,0:T(8,128)(2,1)S(1)}, bf16[64,1280]{1,0:T(8,128)(2,1)S(1)}, u32[]{:S(2)}, u32[]{:S(2)}) collective-permute-start(bf16[64,1280]{1,0:T(8,128)(2,1)S(1)} %pad_maximum_fusion.1), channel_id=1, source_target_pairs={{0,4},{1,5},{2,6},{3,7},{4,0},{5,1},{6,2},{7,3},{8,12},{9,13},{10,... | collective-permute-start | bytes 491528 | tf_op jit(solution)/shard_map/ppermute | solution.py:51
  35.3 5.7 %collective-permute-start.9 = (bf16[64,1408]{1,0:T(8,128)(2,1)S(1)}, bf16[64,1408]{1,0:T(8,128)(2,1)S(1)}, u32[]{:S(2)}, u32[]{:S(2)}) collective-permute-start(bf16[64,1408]{1,0:T(8,128)(2,1)S(1)} %pad_maximum_fusion), channel_id=1, source_target_pairs={{0,4},{1,5},{2,6},{3,7},{4,0},{5,1},{6,2},{7,3},{8,12},{9,13},{10,... | collective-permute-start | bytes 540680 | tf_op jit(solution)/shard_map/ppermute | solution.py:51
  41.0 11.0 %collective-permute-start.15 = (bf16[128,1408]{1,0:T(8,128)(2,1)S(1)}, bf16[128,1408]{1,0:T(8,128)(2,1)S(1)}, u32[]{:S(2)}, u32[]{:S(2)}) collective-permute-start(bf16[128,1408]{1,0:T(8,128)(2,1)S(1)} %constant_dynamic-update-slice_fusion.rows_a), channel_id=1, source_target_pairs={{0,2},{1,9},{2,0},{3,11},{4,6},{5,13},{6,4},{7,15},{8,10},{9,1},{1... | collective-permute-start | bytes 1081352 | tf_op jit(solution)/shard_map/ppermute | solution.py:51
  42.5 9.4 %collective-permute-start.16 = (bf16[128,1280]{1,0:T(8,128)(2,1)S(1)}, bf16[128,1280]{1,0:T(8,128)(2,1)S(1)}, u32[]{:S(2)}, u32[]{:S(2)}) collective-permute-start(bf16[128,1280]{1,0:T(8,128)(2,1)S(1)} %constant_dynamic-update-slice_fusion.3.rows_b), channel_id=1, source_target_pairs={{0,2},{1,9},{2,0},{3,11},{4,6},{5,13},{6,4},{7,15},{8,10},{9,1},{1... | collective-permute-start | bytes 983048 | tf_op jit(solution)/shard_map/ppermute | solution.py:51
  55.6 7.1 %collective-permute-start.17 = (bf16[128,1280]{1,0:T(8,128)(2,1)S(1)}, bf16[128,1280]{1,0:T(8,128)(2,1)S(1)}, u32[]{:S(2)}, u32[]{:S(2)}) collective-permute-start(bf16[128,1280]{1,0:T(8,128)(2,1)S(1)} %get-tuple-element.56), channel_id=1, source_target_pairs={{0,2},{1,9},{2,0},{3,11},{4,6},{5,13},{6,4},{7,15},{8,10},{9,1},{1... | collective-permute-start | bytes 983048 | tf_op jit(solution)/shard_map/ppermute | solution.py:51
  57.7 8.5 %collective-permute-start.21 = (bf16[128,1280]{1,0:T(8,128)(2,1)S(1)}, bf16[128,1280]{1,0:T(8,128)(2,1)S(1)}, u32[]{:S(2)}, u32[]{:S(2)}) collective-permute-start(bf16[128,1280]{1,0:T(8,128)(2,1)S(1)} %expert_rest.1), channel_id=1, source_target_pairs={{0,2},{1,9},{2,0},{3,11},{4,6},{5,13},{6,4},{7,15},{8,10},{9,1},{1... | collective-permute-start | bytes 983048 | tf_op jit(solution)/shard_map/ppermute | solution.py:51
  62.8 5.4 %collective-permute-start.18 = (bf16[64,1280]{1,0:T(8,128)(2,1)S(1)}, bf16[64,1280]{1,0:T(8,128)(2,1)S(1)}, u32[]{:S(2)}, u32[]{:S(2)}) collective-permute-start(bf16[64,1280]{1,0:T(8,128)(2,1)S(1)} %slice.87), channel_id=1, source_target_pairs={{0,4},{1,5},{2,6},{3,7},{4,0},{5,1},{6,2},{7,3},{8,12},{9,13},{10,... | collective-permute-start | bytes 491528 | tf_op jit(solution)/shard_map/ppermute | solution.py:51
  66.3 5.4 %collective-permute-start.22 = (bf16[64,1280]{1,0:T(8,128)(2,1)S(1)}, bf16[64,1280]{1,0:T(8,128)(2,1)S(1)}, u32[]{:S(2)}, u32[]{:S(2)}) collective-permute-start(bf16[64,1280]{1,0:T(8,128)(2,1)S(1)} %slice.86), channel_id=1, source_target_pairs={{0,4},{1,5},{2,6},{3,7},{4,0},{5,1},{6,2},{7,3},{8,12},{9,13},{10,... | collective-permute-start | bytes 491528 | tf_op jit(solution)/shard_map/ppermute | solution.py:51
  68.3 5.5 %collective-permute-start.19 = (bf16[32,1280]{1,0:T(8,128)(2,1)S(1)}, bf16[32,1280]{1,0:T(8,128)(2,1)S(1)}, u32[]{:S(2)}, u32[]{:S(2)}) collective-permute-start(bf16[32,1280]{1,0:T(8,128)(2,1)S(1)} %slice.89), channel_id=1, source_target_pairs={{0,16},{1,17},{2,18},{3,19},{4,20},{5,21},{6,22},{7,23},{8,24},{9,... | collective-permute-start | bytes 245768 | tf_op jit(solution)/shard_map/ppermute | solution.py:51
  71.8 5.4 %collective-permute-start.23 = (bf16[32,1280]{1,0:T(8,128)(2,1)S(1)}, bf16[32,1280]{1,0:T(8,128)(2,1)S(1)}, u32[]{:S(2)}, u32[]{:S(2)}) collective-permute-start(bf16[32,1280]{1,0:T(8,128)(2,1)S(1)} %slice.88), channel_id=1, source_target_pairs={{0,16},{1,17},{2,18},{3,19},{4,20},{5,21},{6,22},{7,23},{8,24},{9,... | collective-permute-start | bytes 245768 | tf_op jit(solution)/shard_map/ppermute | solution.py:51
  73.7 5.4 %collective-permute-start.20 = (bf16[16,1280]{1,0:T(8,128)(2,1)S(1)}, bf16[16,1280]{1,0:T(8,128)(2,1)S(1)}, u32[]{:S(2)}, u32[]{:S(2)}) collective-permute-start(bf16[16,1280]{1,0:T(8,128)(2,1)S(1)} %slice.91), channel_id=1, source_target_pairs={{0,8},{1,3},{2,10},{3,1},{4,12},{5,7},{6,14},{7,5},{8,0},{9,11},{1... | collective-permute-start | bytes 122888 | tf_op jit(solution)/shard_map/ppermute | solution.py:51
  77.2 4.1 %collective-permute-start.24 = (bf16[16,1280]{1,0:T(8,128)(2,1)S(1)}, bf16[16,1280]{1,0:T(8,128)(2,1)S(1)}, u32[]{:S(2)}, u32[]{:S(2)}) collective-permute-start(bf16[16,1280]{1,0:T(8,128)(2,1)S(1)} %slice.90), channel_id=1, source_target_pairs={{0,8},{1,3},{2,10},{3,1},{4,12},{5,7},{6,14},{7,5},{8,0},{9,11},{1... | collective-permute-start | bytes 122888 | tf_op jit(solution)/shard_map/ppermute | solution.py:51

commit v2 on v1

--- a/solution.py
+++ b/solution.py
@@ -40,7 +40,8 @@
     rest = [[bit for bit in all_bits if bit != order[-1]] for order in merge]
     gather = (rest[0][::-1], rest[1][2:][::-1] + rest[1][:2])
     scatter = [order[::-1] + kept[-1:] for order, kept in zip(gather, merge)]
-    return merge, gather, scatter
+    crossed = [order[1::-1] + order[2:] for order in scatter]
+    return merge, gather, (scatter, crossed)
 
 
 def exchange(value, orders, stage):
@@ -82,94 +83,126 @@
     )
 
 
-def attend_kernel(
-    head_count,
-    row_count,
-    blocks_ref,
-    queries_ref,
-    keys_a_ref,
-    keys_b_ref,
-    values_a_ref,
-    values_b_ref,
-    *rest,
+def head_windows(head, size):
+    return head * size // LANES, -(-(head + 1) * size // LANES)
+
+
+def head_scores(head, head_count, query_ref, keys_ref):
+    key_size = query_ref.shape[1] // head_count
+    low, high = [LANES * tile for tile in head_windows(head, key_size)]
+    window = lane_iota((query_ref.shape[0], high - low)) + low
+    inside = (window >= head * key_size) & (window < (head + 1) * key_size)
+    query = jnp.where(inside, query_ref[:, low:high], jnp.zeros((), jnp.bfloat16))
+    return key_size ** (-0.5) * lax.dot_general(
+        query,
+        keys_ref[:, low:high],
+        (((1,), (1,)), ((), ())),
+        preferred_element_type=jnp.float32,
+    )
+
+
+def rounded_peak(scores):
+    peak = jnp.max(scores, axis=1, keepdims=True)
+    return peak.astype(jnp.bfloat16).astype(jnp.float32)
+
+
+def head_sums(head, value_size, raised, values_ref):
+    low, high = head_windows(head, value_size)
+    return jnp.dot(
+        raised.astype(jnp.bfloat16),
+        values_ref[:, low * LANES : high * LANES],
+        preferred_element_type=jnp.float32,
+    )
+
+
+def attend_own_kernel(
+    head_count, row_count, masks, device_ref, queries_ref, keys_ref, values_ref, query_ref, *parts
 ):
-    outputs, query_scratch = rest[:-1], rest[-1]
-    parts = len(outputs) // 2
-    part_heads = head_count // parts
-    block_count = blocks_ref.shape[0]
-    rows = block_count * row_count
-    half = rows // 2
-    vision_width = queries_ref.shape[1]
-    model_width = values_a_ref.shape[1]
-    key_size = vision_width // head_count
-    value_size = model_width // head_count
-    scale = key_size ** (-0.5)
-    for slot in range(block_count):
-        start = pl.multiple_of(blocks_ref[slot] * row_count, row_count)
-        query_scratch[slot * row_count : (slot + 1) * row_count, :] = queries_ref[
+    group_size = queries_ref.shape[0] // row_count
+    device = device_ref[0]
+    odd = lax.rem(device, 2) == 1
+    own_block = lax.rem(device, group_size)
+    for slot, (even_mask, odd_mask) in enumerate(zip(*masks)):
+        block = own_block ^ jnp.where(odd, odd_mask, even_mask)
+        start = pl.multiple_of(block * row_count, row_count)
+        query_ref[slot * row_count : (slot + 1) * row_count, :] = queries_ref[
             pl.ds(start, row_count), :
         ]
+    rows = query_ref.shape[0]
+    value_size = values_ref.shape[1] // head_count
+    part_heads = head_count // len(parts)
+    part_tiles = values_ref.shape[1] // len(parts) // LANES
     lane = lane_iota((rows, LANES))
-    contract_last = (((1,), (1,)), ((), ()))
-    contract_rows = (((1,), (0,)), ((), ()))
-    waiting = None
-
-    def put(part, tile, value):
-        columns = slice(tile * LANES, (tile + 1) * LANES)
-        outputs[2 * part + 1][:, columns] = value[:half]
-        outputs[2 * part][:, columns] = value[half:].astype(jnp.bfloat16)
-
     for head in range(head_count):
-        part = head // part_heads
-        part_tiles = model_width // parts // LANES
+        part_ref = parts[head // part_heads]
+        base = head // part_heads * part_tiles
         if head % part_heads == 0:
-            peaks = jnp.zeros((rows, LANES), jnp.float32)
-            totals = jnp.zeros((rows, LANES), jnp.float32)
-        low = head * key_size // LANES * LANES
-        high = -(-(head + 1) * key_size // LANES) * LANES
-        window = lane_iota((rows, high - low)) + low
-        inside = (window >= head * key_size) & (window < (head + 1) * key_size)
-        query = jnp.where(inside, query_scratch[:, low:high], jnp.zeros((), jnp.bfloat16))
-        score_a = scale * lax.dot_general(
-            query, keys_a_ref[:, low:high], contract_last, preferred_element_type=jnp.float32
-        )
-        score_b = scale * lax.dot_general(
-            query, keys_b_ref[:, low:high], contract_last, preferred_element_type=jnp.float32
-        )
-        peak = jnp.maximum(
-            jnp.max(score_a, axis=1, keepdims=True), jnp.max(score_b, axis=1, keepdims=True)
-        )
-        peak = peak.astype(jnp.bfloat16).astype(jnp.float32)
-        raised_a = jnp.exp(score_a - peak)
-        raised_b = jnp.exp(score_b - peak)
-        total = jnp.sum(raised_a, axis=1, keepdims=True) + jnp.sum(
-            raised_b, axis=1, keepdims=True
-        )
-        peaks = jnp.where(lane == head % part_heads, peak, peaks)
-        totals = jnp.where(lane == head % part_heads, total, totals)
-        low = head * value_size // LANES
-        high = -(-(head + 1) * value_size // LANES)
-        summed = lax.dot_general(
-            raised_a.astype(jnp.bfloat16),
-            values_a_ref[:, low * LANES : high * LANES],
-            contract_rows,
-            preferred_element_type=jnp.float32,
-        ) + lax.dot_general(
-            raised_b.astype(jnp.bfloat16),
-            values_b_ref[:, low * LANES : high * LANES],
-            contract_rows,
-            preferred_element_type=jnp.float32,
-        )
+            stats = jnp.zeros((rows, LANES), jnp.float32)
+        scores = head_scores(head, head_count, query_ref, keys_ref)
+        peak = rounded_peak(scores)
+        raised = jnp.exp(scores - peak)
+        total = jnp.sum(raised, axis=1, keepdims=True)
+        stats = jnp.where(lane == head % part_heads, peak, stats)
+        stats = jnp.where(lane == head % part_heads + part_heads, total, stats)
+        summed = head_sums(head, value_size, raised, values_ref)
+        low, high = head_windows(head, value_size)
         for tile in range(low, high):
             value = summed[:, (tile - low) * LANES : (tile - low + 1) * LANES]
             edge = head * value_size - tile * LANES
             if edge > 0:
                 value = jnp.where(lane < edge, waiting, value)
-            if (tile + 1) * LANES > (head + 1) * value_size:
-                waiting = value
-            else:
-                put(part, tile - part * part_tiles, value)
+            waiting = value
+            if (tile + 1) * LANES <= (head + 1) * value_size:
+                part_ref[:, (tile - base) * LANES : (tile - base + 1) * LANES] = value
         if (head + 1) % part_heads == 0:
+            part_ref[:, part_tiles * LANES :] = stats
+
+
+def attend_other_kernel(head_count, query_ref, keys_ref, values_ref, *rest):
+    part_count = len(rest) // 3
+    parts, outputs = rest[:part_count], rest[part_count:]
+    rows = query_ref.shape[0]
+    half = rows // 2
+    value_size = values_ref.shape[1] // head_count
+    part_heads = head_count // part_count
+    part_tiles = values_ref.shape[1] // part_count // LANES
+    lane = lane_iota((rows, LANES))
+
+    def put(part, tile, value):
+        columns = slice(tile * LANES, (tile + 1) * LANES)
+        outputs[2 * part + 1][:, columns] = value[:half]
+        outputs[2 * part][:, columns] = value[half:].astype(jnp.bfloat16)
+
+    for head in range(head_count):
+        part = head // part_heads
+        at = head % part_heads
+        base = part * part_tiles
+        if at == 0:
+            stats = parts[part][:, part_tiles * LANES :]
+            peaks = jnp.zeros((rows, LANES), jnp.float32)
+            totals = jnp.zeros((rows, LANES), jnp.float32)
+        scores = head_scores(head, head_count, query_ref, keys_ref)
+        old_peak = stats[:, at : at + 1]
+        peak = jnp.maximum(rounded_peak(scores), old_peak)
+        factor = jnp.exp(old_peak - peak)
+        raised = jnp.exp(scores - peak)
+        total = jnp.sum(raised, axis=1, keepdims=True)
+        total = total + stats[:, part_heads + at : part_heads + at + 1] * factor
+        peaks = jnp.where(lane == at, peak, peaks)
+        totals = jnp.where(lane == at, total, totals)
+        summed = head_sums(head, value_size, raised, values_ref)
+        low, high = head_windows(head, value_size)
+        for tile in range(low, high):
+            value = summed[:, (tile - low) * LANES : (tile - low + 1) * LANES]
+            old = parts[part][:, (tile - base) * LANES : (tile - base + 1) * LANES]
+            value = value + old * factor
+            edge = head * value_size - tile * LANES
+            if edge > 0:
+                value = jnp.where(lane < edge, waiting, value)
+            waiting = value
+            if (tile + 1) * LANES <= (head + 1) * value_size:
+                put(part, tile - base, value)
+        if at == part_heads - 1:
             put(part, part_tiles, pack_stats(peaks, totals, part_heads))
 
 
@@ -364,8 +397,13 @@
     down_product(hidden, down_ref, out_ref, 0)
 
 
-def rest_expert_kernel(start, hidden_ref, down_ref, out_ref):
-    down_product(hidden_ref, down_ref, out_ref, start)
+def rest_expert_kernel(start, hidden_ref, down_ref, first_ref, sent_ref, kept_ref, value_ref):
+    down_product(hidden_ref, down_ref, value_ref, start)
+    half = first_ref.shape[0] // 2
+    sent_ref[:half, :] = first_ref[half:, :].astype(sent_ref.dtype)
+    sent_ref[half:, :] = value_ref[half:, :].astype(sent_ref.dtype)
+    kept_ref[:half, :] = first_ref[:half, :]
+    kept_ref[half:, :] = value_ref[:half, :]
 
 
 def first_expert_rows(expert, halves, weights):
@@ -395,7 +433,7 @@
     )(expert, *[near(half) for half in halves], *[far(weight) for weight in weights])
 
 
-def second_expert_rows(expert, halves, weights):
+def second_expert_rows(expert, halves, weights, totals):
     units, model_width = weights[0].shape
     row_count = halves[0].shape[0]
     width = model_width // 2
@@ -412,15 +450,19 @@
         out_specs=(whole, whole),
         scratch_shapes=[pltpu.VMEM((model_width + LANES, row_count), jnp.bfloat16)],
     )(expert, *[near(half) for half in halves], *[near(weight) for weight in weights])
-    second = pl.pallas_call(
+    sent, kept = pl.pallas_call(
         functools.partial(rest_expert_kernel, width),
         name="expert_rest",
         compiler_params=pltpu.CompilerParams(vmem_limit_bytes=12 << 20),
-        out_shape=near_shape((row_count, width), jnp.bfloat16),
-        in_specs=[whole] * 2,
-        out_specs=whole,
-    )(near(hidden), near(weights[2]))
-    return [first, second]
+        out_shape=(
+            near_shape((row_count, width), jnp.bfloat16),
+            near_shape((row_count, width), jnp.float32),
+        ),
+        in_specs=[whole] * 3,
+        out_specs=(whole, whole),
+        scratch_shapes=[pltpu.VMEM((row_count, width), jnp.float32)],
+    )(near(hidden), near(weights[2]), near(totals[1]))
+    return [(first, totals[0]), (sent, kept)]
 
 
 def attention_rows(
@@ -429,7 +471,6 @@
     model_width = patch_values.shape[1]
     part_width = model_width // PARTS + LANES
     part_heads = HEADS // PARTS
-    group_size = queries.shape[0] // row_count
     stages = len(orders[0])
     device_index = lax.axis_index("wide")
     masks = [
@@ -443,8 +484,6 @@
         ]
         for order in orders
     ]
-    masks = jnp.array(masks, jnp.int32)
-    blocks = (device_index % group_size) ^ jnp.where(device_index % 2 == 1, masks[1], masks[0])
     rows = row_count << stages
     whole = pl.BlockSpec(memory_space=pltpu.VMEM)
 
@@ -454,21 +493,27 @@
             near_shape((rows, part_width), jnp.float32),
         )
 
+    query_rows, *partials = pl.pallas_call(
+        functools.partial(attend_own_kernel, HEADS, row_count, masks),
+        name="attend_own",
+        compiler_params=pltpu.CompilerParams(vmem_limit_bytes=12 << 20),
+        out_shape=(near_shape((rows, queries.shape[1]), jnp.bfloat16),)
+        + (near_shape((rows, part_width), jnp.float32),) * PARTS,
+        in_specs=[pl.BlockSpec(memory_space=pltpu.SMEM)] + [whole] * 3,
+        out_specs=(whole,) * (PARTS + 1),
+    )(device_index.reshape(1), far(queries), far(patch_keys), far(patch_values))
     chains = pl.pallas_call(
-        functools.partial(attend_kernel, HEADS, row_count),
-        name="attend",
+        functools.partial(attend_other_kernel, HEADS),
+        name="attend_other",
         compiler_params=pltpu.CompilerParams(vmem_limit_bytes=12 << 20),
         out_shape=pair_shapes(rows // 2) * PARTS,
-        in_specs=[pl.BlockSpec(memory_space=pltpu.SMEM)] + [whole] * 5,
+        in_specs=[whole] * (3 + PARTS),
         out_specs=(whole,) * (2 * PARTS),
-        scratch_shapes=[pltpu.VMEM((rows, queries.shape[1]), jnp.bfloat16)],
     )(
-        blocks,
-        far(queries),
-        far(patch_keys),
+        near(query_rows),
         near(other_keys),
-        far(patch_values),
         near(other_values),
+        *[near(partial) for partial in partials],
     )
     finished = []
     for part in range(PARTS):
@@ -551,13 +596,14 @@
     expert = (device_index // 2).reshape(1)
     *totals, gate, up, down = first_expert_rows(expert, blocks, weights)
     outputs = []
-    for part, sent in enumerate(second_expert_rows(expert, came, (gate, up, down))):
-        kept = totals[part]
-        for stage in range(len(scatter_order[0])):
-            arrived = exchange(sent, scatter_order, stage)
+    for part, (sent, kept) in enumerate(
+        second_expert_rows(expert, came, (gate, up, down), totals)
+    ):
+        for stage in range(stages + 1):
+            arrived = exchange(sent, scatter_order[part], stage)
             kept = kept + arrived.astype(jnp.float32)
             half_rows = kept.shape[0] // 2
-            if stage < len(scatter_order[0]) - 1:
+            if stage < stages:
                 sent = kept[half_rows:].astype(jnp.bfloat16)
                 kept = kept[:half_rows]
         outputs.append(kept)

time: 82.1 us -> 86.1 us (1.049)
  Pallas kernels: 15.4 us -> 20.7 us
  waiting for transfers between devices: 31.2 us -> 28.7 us
  starting transfers between devices: 33.2 us -> 35.2 us
    pallas_call x1 -> x2, Pallas kernels: 3.21 us -> 8.26 us  [the longest x1 5.51 us: attention_rows(): pl.pallas_call(functools.partial(attend_other_kernel, HEADS), name='atten...]
    ppermute x20, waiting for transfers between devices: 28.9 us -> 26.3 us  [exchange(): return lax.ppermute(value, 'wide', pairs)]
    ppermute x20, starting transfers between devices: 31.7 us -> 33.8 us  [exchange(): return lax.ppermute(value, 'wide', pairs)]
  transfers between devices with their start and end apart: 25 -> 25, of which waited for: 15 -> 13; matrix products, arithmetic and copies ran while one was open for 1% -> 1% of each run, Pallas kernels for 14% -> 20%
where the time goes in v2:
time: 86.1 us; the launch traced here: 86 us
  starting transfers between devices  35.2 us (41%)
  waiting for transfers between devices  28.7 us (33%)
  Pallas kernels  20.7 us (24%)
  other arithmetic  1.02 us (1%)
    ppermute x20, starting transfers between devices, exchange(): return lax.ppermute(value, 'wide', pairs)  33.8 us
    ppermute x20, waiting for transfers between devices, exchange(): return lax.ppermute(value, 'wide', pairs)  26.3 us
    pallas_call x1, Pallas kernels, first_expert_rows(): pl.pallas_call(first_expert_kernel, name='expert_first', compiler_params=...  6.64 us
    pallas_call x1, Pallas kernels, attention_rows(): pl.pallas_call(functools.partial(attend_other_kernel, HEADS), name='atten...  5.51 us
    pallas_call x1, Pallas kernels, second_expert_rows(): pl.pallas_call(second_expert_kernel, name='expert_second', compiler_param...  3.81 us
    pallas_call x1, Pallas kernels, attention_rows(): pl.pallas_call(functools.partial(attend_own_kernel, HEADS, row_count, mas...  2.75 us
    ppermute x5, waiting for transfers between devices, partner(): return lax.ppermute(value, axis, pairs)  2.35 us
  transfers between devices with their start and end apart: 25, of which 13 were waited for; matrix products, arithmetic and copies ran while one was open for 1% of the time, Pallas kernels for 20%

profile of v2, /device:TPU:0, one launch (start us, length us, event | category | flops | bytes accessed | tf_op | source)
XLA Modules:
  0.0 86.0 jit_solution(12907837783505418070)
XLA Ops:
  0.5 2.3 %collective-permute-done.keys_ref = bf16[128,1152]{1,0:T(8,128)(2,1)S(1)} collective-permute-done((bf16[128,1152]{1,0:T(8,128)(2,1)}, bf16[128,1152]{1,0:T(8,128)(2,1)S(1)}, u32[]{:S(2)}, u32[]{:S(2)}) %collective-permute-start) | collective-permute-done | bytes 294944 | tf_op jit(solution)/shard_map/ppermute | solution.py:33
  3.7 2.7 %attend_own.1 = (bf16[128,1152]{1,0:T(8,128)(2,1)S(1)}, f32[128,1408]{1,0:T(8,128)S(1)}, f32[128,1408]{1,0:T(8,128)S(1)}) custom-call(s32[1]{0:T(128)} %bitcast.device_ref, bf16[256,1152]{1,0:T(8,128)(2,1)} %queries_ref.1, bf16[128,1152]{1,0:T(8,128)(2,1)} %keys_ref.1, bf16[128,2560]{1,0:T(8,128)(2,1)} %values_ref.1), custom_call_target="tpu_custom_call" | custom-call | tf_op jit(solution)/shard_map/attend_own/pallas_call | solution.py:496
  6.5 5.5 %attend_other.1 = (bf16[64,1408]{1,0:T(8,128)(2,1)S(1)}, f32[64,1408]{1,0:T(8,128)S(1)}, bf16[64,1408]{1,0:T(8,128)(2,1)S(1)}, f32[64,1408]{1,0:T(8,128)S(1)}) custom-call(bf16[128,1152]{1,0:T(8,128)(2,1)S(1)} %get-tuple-element.37.query_ref, bf16[128,1152]{1,0:T(8,128)(2,1)S(1)} %collective-permute-done.keys_ref, ...), custom_call_target="tpu_custom_call" | custom-call | tf_op jit(solution)/shard_map/attend_other/pallas_call | solution.py:505
  12.0 2.7 %collective-permute-start.2 = (bf16[64,1408]{1,0:T(8,128)(2,1)S(1)}, bf16[64,1408]{1,0:T(8,128)(2,1)S(1)}, u32[]{:S(2)}, u32[]{:S(2)}) collective-permute-start(bf16[64,1408]{1,0:T(8,128)(2,1)S(1)} %get-tuple-element.43), channel_id=1, source_target_pairs={{0,2},{1,5},{2,0},{3,7},{4,6},{5,1},{6,4},{7,3},{8,10},{9,13},{10,... | collective-permute-start | bytes 540680 | tf_op jit(solution)/shard_map/ppermute | solution.py:52
  14.8 3.4 %collective-permute-done.2.came_ref = bf16[64,1408]{1,0:T(8,128)(2,1)S(1)} collective-permute-done((bf16[64,1408]{1,0:T(8,128)(2,1)S(1)}, bf16[64,1408]{1,0:T(8,128)(2,1)S(1)}, u32[]{:S(2)}, u32[]{:S(2)}) %collective-permute-start.2) | collective-permute-done | bytes 180256 | tf_op jit(solution)/shard_map/ppermute | solution.py:52
  18.4 2.1 %collective-permute-start.3 = (bf16[32,1408]{1,0:T(8,128)(2,1)S(1)}, bf16[32,1408]{1,0:T(8,128)(2,1)S(1)}, u32[]{:S(2)}, u32[]{:S(2)}) collective-permute-start(bf16[32,1408]{1,0:T(8,128)(2,1)S(1)} %get-tuple-element.45), channel_id=1, source_target_pairs={{0,4},{1,9},{2,6},{3,11},{4,0},{5,13},{6,2},{7,15},{8,12},{9,1},{1... | collective-permute-start | bytes 270344 | tf_op jit(solution)/shard_map/ppermute | solution.py:52
  20.8 1.7 %collective-permute-start.6 = (bf16[32,1408]{1,0:T(8,128)(2,1)S(1)}, bf16[32,1408]{1,0:T(8,128)(2,1)S(1)}, u32[]{:S(2)}, u32[]{:S(2)}) collective-permute-start(bf16[32,1408]{1,0:T(8,128)(2,1)S(1)} %get-tuple-element.51), channel_id=1, source_target_pairs={{0,4},{1,9},{2,6},{3,11},{4,0},{5,13},{6,2},{7,15},{8,12},{9,1},{1... | collective-permute-start | bytes 270344 | tf_op jit(solution)/shard_map/ppermute | solution.py:52
  23.2 2.1 %collective-permute-start.4 = (bf16[32,1408]{1,0:T(8,128)(2,1)S(1)}, bf16[32,1408]{1,0:T(8,128)(2,1)S(1)}, u32[]{:S(2)}, u32[]{:S(2)}) collective-permute-start(bf16[32,1408]{1,0:T(8,128)(2,1)S(1)} %get-tuple-element.47), channel_id=1, source_target_pairs={{0,8},{1,3},{2,10},{3,1},{4,12},{5,7},{6,14},{7,5},{8,0},{9,11},{1... | collective-permute-start | bytes 270344 | tf_op jit(solution)/shard_map/ppermute | solution.py:52
  25.6 1.7 %collective-permute-start.7 = (bf16[32,1408]{1,0:T(8,128)(2,1)S(1)}, bf16[32,1408]{1,0:T(8,128)(2,1)S(1)}, u32[]{:S(2)}, u32[]{:S(2)}) collective-permute-start(bf16[32,1408]{1,0:T(8,128)(2,1)S(1)} %get-tuple-element.53), channel_id=1, source_target_pairs={{0,8},{1,3},{2,10},{3,1},{4,12},{5,7},{6,14},{7,5},{8,0},{9,11},{1... | collective-permute-start | bytes 270344 | tf_op jit(solution)/shard_map/ppermute | solution.py:52
  27.9 2.3 %collective-permute-done.7.rest_3_ = bf16[32,1408]{1,0:T(8,128)(2,1)S(1)} collective-permute-done((bf16[32,1408]{1,0:T(8,128)(2,1)S(1)}, bf16[32,1408]{1,0:T(8,128)(2,1)S(1)}, u32[]{:S(2)}, u32[]{:S(2)}) %collective-permute-start.7) | collective-permute-done | bytes 90144 | tf_op jit(solution)/shard_map/ppermute | solution.py:52
  30.7 2.7 %collective-permute-start.10 = (bf16[32,1280]{1,0:T(8,128)(2,1)S(1)}, bf16[32,1280]{1,0:T(8,128)(2,1)S(1)}, u32[]{:S(2)}, u32[]{:S(2)}) collective-permute-start(bf16[32,1280]{1,0:T(8,128)(2,1)S(1)} %get-tuple-element.56), channel_id=1, source_target_pairs={{0,16},{1,17},{2,18},{3,19},{4,20},{5,21},{6,22},{7,23},{8,24},{9,... | collective-permute-start | bytes 245768 | tf_op jit(solution)/shard_map/ppermute | solution.py:52
  33.7 4.2 %collective-permute-done.10 = bf16[32,1280]{1,0:T(8,128)(2,1)S(1)} collective-permute-done((bf16[32,1280]{1,0:T(8,128)(2,1)S(1)}, bf16[32,1280]{1,0:T(8,128)(2,1)S(1)}, u32[]{:S(2)}, u32[]{:S(2)}) %collective-permute-start.10) | collective-permute-done | bytes 81952 | tf_op jit(solution)/shard_map/ppermute | solution.py:52
  37.9 1.6 %collective-permute-start.11 = (bf16[64,1280]{1,0:T(8,128)(2,1)S(1)}, bf16[64,1280]{1,0:T(8,128)(2,1)S(1)}, u32[]{:S(2)}, u32[]{:S(2)}) collective-permute-start(bf16[64,1280]{1,0:T(8,128)(2,1)S(1)} %pad_maximum_fusion.1), channel_id=1, source_target_pairs={{0,4},{1,5},{2,6},{3,7},{4,0},{5,1},{6,2},{7,3},{8,12},{9,13},{10,... | collective-permute-start | bytes 491528 | tf_op jit(solution)/shard_map/ppermute | solution.py:52
  39.6 0.9 %collective-permute-start.9 = (bf16[64,1408]{1,0:T(8,128)(2,1)S(1)}, bf16[64,1408]{1,0:T(8,128)(2,1)S(1)}, u32[]{:S(2)}, u32[]{:S(2)}) collective-permute-start(bf16[64,1408]{1,0:T(8,128)(2,1)S(1)} %pad_maximum_fusion), channel_id=1, source_target_pairs={{0,4},{1,5},{2,6},{3,7},{4,0},{5,1},{6,2},{7,3},{8,12},{9,13},{10,... | collective-permute-start | bytes 540680 | tf_op jit(solution)/shard_map/ppermute | solution.py:52
  40.5 4.7 %collective-permute-done.9 = bf16[64,1408]{1,0:T(8,128)(2,1)S(1)} collective-permute-done((bf16[64,1408]{1,0:T(8,128)(2,1)S(1)}, bf16[64,1408]{1,0:T(8,128)(2,1)S(1)}, u32[]{:S(2)}, u32[]{:S(2)}) %collective-permute-start.9) | collective-permute-done | bytes 180256 | tf_op jit(solution)/shard_map/ppermute | solution.py:52
  45.3 1.6 %collective-permute-start.15 = (bf16[128,1408]{1,0:T(8,128)(2,1)S(1)}, bf16[128,1408]{1,0:T(8,128)(2,1)S(1)}, u32[]{:S(2)}, u32[]{:S(2)}) collective-permute-start(bf16[128,1408]{1,0:T(8,128)(2,1)S(1)} %constant_dynamic-update-slice_fusion.rows_a), channel_id=1, source_target_pairs={{0,2},{1,9},{2,0},{3,11},{4,6},{5,13},{6,4},{7,15},{8,10},{9,1},{1... | collective-permute-start | bytes 1081352 | tf_op jit(solution)/shard_map/ppermute | solution.py:52
  46.9 0.6 collective-permute-start.16
  47.5 6.6 %expert_first.1 = (f32[128,1280]{1,0:T(8,128)S(1)}, f32[128,1280]{1,0:T(8,128)S(1)}, bf16[1024,2560]{1,0:T(8,128)(2,1)S(1)}, bf16[1024,2560]{1,0:T(8,128)(2,1)S(1)}, bf16[1024,2560]{1,0:T(8,128)(2,1)S(1)}) custom-call(s32[1]{0:T(128)} %bitcast.1.expert_ref, bf16[128,1408]{1,0:T(8,128)(2,1)S(1)} %constant_dynamic-update-slice_fusion.rows_a, ...), custom_call_target="tpu_custom_call" | custom-call | flops 2013265920 | bytes 15728640 | tf_op jit(solution)/shard_map/expert_first/pallas_call | solution.py:415
  54.1 2.2 %collective-permute-done.16.rows_b = bf16[128,1280]{1,0:T(8,128)(2,1)S(1)} collective-permute-done((bf16[128,1280]{1,0:T(8,128)(2,1)S(1)}, bf16[128,1280]{1,0:T(8,128)(2,1)S(1)}, u32[]{:S(2)}, u32[]{:S(2)}) %collective-permute-start.16) | collective-permute-done | bytes 327712 | tf_op jit(solution)/shard_map/ppermute | solution.py:52
  56.3 3.8 %expert_second.1 = (bf16[128,1280]{1,0:T(8,128)(2,1)S(1)}, bf16[128,1024]{1,0:T(8,128)(2,1)S(1)}) custom-call(s32[1]{0:T(128)} %bitcast.1.expert_ref, bf16[128,1408]{1,0:T(8,128)(2,1)S(1)} %collective-permute-done.15.rows_a, bf16[128,1280]{1,0:T(8,128)(2,1)S(1)} %collective-permute-done.16.rows_b, bf16[1024,2560]{1,0:T(8,128)(2,1)S(1)} %get-tuple-element.61.gate_ref, ...), custom_call_target="tpu_custom_call" | custom-call | tf_op jit(solution)/shard_map/expert_second/pallas_call | solution.py:441
  60.1 1.6 %collective-permute-start.17 = (bf16[128,1280]{1,0:T(8,128)(2,1)S(1)}, bf16[128,1280]{1,0:T(8,128)(2,1)S(1)}, u32[]{:S(2)}, u32[]{:S(2)}) collective-permute-start(bf16[128,1280]{1,0:T(8,128)(2,1)S(1)} %get-tuple-element.64), channel_id=1, source_target_pairs={{0,2},{1,9},{2,0},{3,11},{4,6},{5,13},{6,4},{7,15},{8,10},{9,1},{1... | collective-permute-start | bytes 983048 | tf_op jit(solution)/shard_map/ppermute | solution.py:52
  62.2 1.6 %collective-permute-start.21 = (bf16[128,1280]{1,0:T(8,128)(2,1)S(1)}, bf16[128,1280]{1,0:T(8,128)(2,1)S(1)}, u32[]{:S(2)}, u32[]{:S(2)}) collective-permute-start(bf16[128,1280]{1,0:T(8,128)(2,1)S(1)} %get-tuple-element.68), channel_id=1, source_target_pairs={{0,4},{1,5},{2,6},{3,7},{4,0},{5,1},{6,2},{7,3},{8,12},{9,13},{10,... | collective-permute-start | bytes 983048 | tf_op jit(solution)/shard_map/ppermute | solution.py:52
  63.8 3.4 %collective-permute-done.17 = bf16[128,1280]{1,0:T(8,128)(2,1)S(1)} collective-permute-done((bf16[128,1280]{1,0:T(8,128)(2,1)S(1)}, bf16[128,1280]{1,0:T(8,128)(2,1)S(1)}, u32[]{:S(2)}, u32[]{:S(2)}) %collective-permute-start.17) | collective-permute-done | bytes 327712 | tf_op jit(solution)/shard_map/ppermute | solution.py:52
  67.3 1.6 %collective-permute-start.18 = (bf16[64,1280]{1,0:T(8,128)(2,1)S(1)}, bf16[64,1280]{1,0:T(8,128)(2,1)S(1)}, u32[]{:S(2)}, u32[]{:S(2)}) collective-permute-start(bf16[64,1280]{1,0:T(8,128)(2,1)S(1)} %slice.79), channel_id=1, source_target_pairs={{0,4},{1,5},{2,6},{3,7},{4,0},{5,1},{6,2},{7,3},{8,12},{9,13},{10,... | collective-permute-start | bytes 491528 | tf_op jit(solution)/shard_map/ppermute | solution.py:52
  69.5 1.1 %collective-permute-start.22 = (bf16[64,1280]{1,0:T(8,128)(2,1)S(1)}, bf16[64,1280]{1,0:T(8,128)(2,1)S(1)}, u32[]{:S(2)}, u32[]{:S(2)}) collective-permute-start(bf16[64,1280]{1,0:T(8,128)(2,1)S(1)} %slice.78), channel_id=1, source_target_pairs={{0,2},{1,9},{2,0},{3,11},{4,6},{5,13},{6,4},{7,15},{8,10},{9,1},{1... | collective-permute-start | bytes 491528 | tf_op jit(solution)/shard_map/ppermute | solution.py:52
  70.6 2.2 %collective-permute-done.18 = bf16[64,1280]{1,0:T(8,128)(2,1)S(1)} collective-permute-done((bf16[64,1280]{1,0:T(8,128)(2,1)S(1)}, bf16[64,1280]{1,0:T(8,128)(2,1)S(1)}, u32[]{:S(2)}, u32[]{:S(2)}) %collective-permute-start.18) | collective-permute-done | bytes 163872 | tf_op jit(solution)/shard_map/ppermute | solution.py:52
  72.8 1.6 %collective-permute-start.19 = (bf16[32,1280]{1,0:T(8,128)(2,1)S(1)}, bf16[32,1280]{1,0:T(8,128)(2,1)S(1)}, u32[]{:S(2)}, u32[]{:S(2)}) collective-permute-start(bf16[32,1280]{1,0:T(8,128)(2,1)S(1)} %slice.81), channel_id=1, source_target_pairs={{0,16},{1,17},{2,18},{3,19},{4,20},{5,21},{6,22},{7,23},{8,24},{9,... | collective-permute-start | bytes 245768 | tf_op jit(solution)/shard_map/ppermute | solution.py:52
  74.9 3.2 %collective-permute-start.23 = (bf16[32,1280]{1,0:T(8,128)(2,1)S(1)}, bf16[32,1280]{1,0:T(8,128)(2,1)S(1)}, u32[]{:S(2)}, u32[]{:S(2)}) collective-permute-start(bf16[32,1280]{1,0:T(8,128)(2,1)S(1)} %slice.80), channel_id=1, source_target_pairs={{0,16},{1,17},{2,18},{3,19},{4,20},{5,21},{6,22},{7,23},{8,24},{9,... | collective-permute-start | bytes 245768 | tf_op jit(solution)/shard_map/ppermute | solution.py:52
  78.2 2.7 %collective-permute-start.20 = (bf16[16,1280]{1,0:T(8,128)(2,1)S(1)}, bf16[16,1280]{1,0:T(8,128)(2,1)S(1)}, u32[]{:S(2)}, u32[]{:S(2)}) collective-permute-start(bf16[16,1280]{1,0:T(8,128)(2,1)S(1)} %slice.83), channel_id=1, source_target_pairs={{0,8},{1,3},{2,10},{3,1},{4,12},{5,7},{6,14},{7,5},{8,0},{9,11},{1... | collective-permute-start | bytes 122888 | tf_op jit(solution)/shard_map/ppermute | solution.py:52
  80.9 2.4 %collective-permute-start.24 = (bf16[16,1280]{1,0:T(8,128)(2,1)S(1)}, bf16[16,1280]{1,0:T(8,128)(2,1)S(1)}, u32[]{:S(2)}, u32[]{:S(2)}) collective-permute-start(bf16[16,1280]{1,0:T(8,128)(2,1)S(1)} %slice.82), channel_id=1, source_target_pairs={{0,8},{1,3},{2,10},{3,1},{4,12},{5,7},{6,14},{7,5},{8,0},{9,11},{1... | collective-permute-start | bytes 122888 | tf_op jit(solution)/shard_map/ppermute | solution.py:52
  83.3 2.0 %collective-permute-done.24 = bf16[16,1280]{1,0:T(8,128)(2,1)S(1)} collective-permute-done((bf16[16,1280]{1,0:T(8,128)(2,1)S(1)}, bf16[16,1280]{1,0:T(8,128)(2,1)S(1)}, u32[]{:S(2)}, u32[]{:S(2)}) %collective-permute-start.24) | collective-permute-done | bytes 40992 | tf_op jit(solution)/shard_map/ppermute | solution.py:52
  85.3 0.7 fusion
  (61 shorter events, 6.2 us)
Async XLA Ops:
  0.0 2.9 %collective-permute-start.1 = (bf16[128,2560]{1,0:T(8,128)(2,1)}, bf16[128,2560]{1,0:T(8,128)(2,1)S(1)}, u32[]{:S(2)}, u32[]{:S(2)}) collective-permute-start(bf16[128,2560]{1,0:T(8,128)(2,1)} %values_ref.1), channel_id=1, source_target_pairs={{0,1},{1,0},{2,3},{3,2},{4,5},{5,4},{6,7},{7,6},{8,9},{9,8},{10,11... | collective-permute-start | bytes 1966088 | tf_op jit(solution)/shard_map/ppermute | solution.py:33
  0.5 2.4 %collective-permute-start = (bf16[128,1152]{1,0:T(8,128)(2,1)}, bf16[128,1152]{1,0:T(8,128)(2,1)S(1)}, u32[]{:S(2)}, u32[]{:S(2)}) collective-permute-start(bf16[128,1152]{1,0:T(8,128)(2,1)} %keys_ref.1), channel_id=1, source_target_pairs={{0,1},{1,0},{2,3},{3,2},{4,5},{5,4},{6,7},{7,6},{8,9},{9,8},{10,11... | collective-permute-start | bytes 884744 | tf_op jit(solution)/shard_map/ppermute | solution.py:33
  2.9 44.6 %collective-permute-start.12 = (bf16[512,2560]{1,0:T(8,128)(2,1)}, bf16[512,2560]{1,0:T(8,128)(2,1)}, u32[]{:S(2)}, u32[]{:S(2)}) collective-permute-start(bf16[512,2560]{1,0:T(8,128)(2,1)} %gate_a), channel_id=1, source_target_pairs={{0,1},{1,0},{2,3},{3,2},{4,5},{5,4},{6,7},{7,6},{8,9},{9,8},{10,11... | collective-permute-start | bytes 7864328 | tf_op jit(solution)/shard_map/ppermute | solution.py:33
  3.2 44.2 %collective-permute-start.13 = (bf16[512,2560]{1,0:T(8,128)(2,1)}, bf16[512,2560]{1,0:T(8,128)(2,1)}, u32[]{:S(2)}, u32[]{:S(2)}) collective-permute-start(bf16[512,2560]{1,0:T(8,128)(2,1)} %up_a), channel_id=1, source_target_pairs={{0,1},{1,0},{2,3},{3,2},{4,5},{5,4},{6,7},{7,6},{8,9},{9,8},{10,11... | collective-permute-start | bytes 7864328 | tf_op jit(solution)/shard_map/ppermute | solution.py:33
  3.4 44.1 %collective-permute-start.14 = (bf16[512,2560]{1,0:T(8,128)(2,1)}, bf16[512,2560]{1,0:T(8,128)(2,1)}, u32[]{:S(2)}, u32[]{:S(2)}) collective-permute-start(bf16[512,2560]{1,0:T(8,128)(2,1)} %down_a), channel_id=1, source_target_pairs={{0,1},{1,0},{2,3},{3,2},{4,5},{5,4},{6,7},{7,6},{8,9},{9,8},{10,11... | collective-permute-start | bytes 7864328 | tf_op jit(solution)/shard_map/ppermute | solution.py:33
  3.7 18.7 %copy-start.1 = (s32[16,6]{0,1:T(8,128)S(1)}, s32[16,6]{0,1:T(8,128)}, u32[]{:S(2)}) copy-start(s32[16,6]{0,1:T(8,128)} %param.14) | copy-start | bytes 1156
  3.7 18.7 %copy-start.2 = (s32[16,6]{0,1:T(8,128)S(1)}, s32[16,6]{0,1:T(8,128)}, u32[]{:S(2)}) copy-start(s32[16,6]{0,1:T(8,128)} %param.13) | copy-start | bytes 1156
  3.7 23.6 %copy-start = (f32[2560]{0:T(1024)S(1)}, f32[2560]{0:T(1024)}, u32[]{:S(2)}) copy-start(f32[2560]{0:T(1024)} %param.12) | copy-start | bytes 30724
  12.0 6.1 %collective-permute-start.2 = (bf16[64,1408]{1,0:T(8,128)(2,1)S(1)}, bf16[64,1408]{1,0:T(8,128)(2,1)S(1)}, u32[]{:S(2)}, u32[]{:S(2)}) collective-permute-start(bf16[64,1408]{1,0:T(8,128)(2,1)S(1)} %get-tuple-element.43), channel_id=1, source_target_pairs={{0,2},{1,5},{2,0},{3,7},{4,6},{5,1},{6,4},{7,3},{8,10},{9,13},{10,... | collective-permute-start | bytes 540680 | tf_op jit(solution)/shard_map/ppermute | solution.py:52
  14.7 5.8 %collective-permute-start.5 = (bf16[64,1408]{1,0:T(8,128)(2,1)S(1)}, bf16[64,1408]{1,0:T(8,128)(2,1)S(1)}, u32[]{:S(2)}, u32[]{:S(2)}) collective-permute-start(bf16[64,1408]{1,0:T(8,128)(2,1)S(1)} %get-tuple-element.49), channel_id=1, source_target_pairs={{0,2},{1,5},{2,0},{3,7},{4,6},{5,1},{6,4},{7,3},{8,10},{9,13},{10,... | collective-permute-start | bytes 540680 | tf_op jit(solution)/shard_map/ppermute | solution.py:52
  18.4 4.6 %collective-permute-start.3 = (bf16[32,1408]{1,0:T(8,128)(2,1)S(1)}, bf16[32,1408]{1,0:T(8,128)(2,1)S(1)}, u32[]{:S(2)}, u32[]{:S(2)}) collective-permute-start(bf16[32,1408]{1,0:T(8,128)(2,1)S(1)} %get-tuple-element.45), channel_id=1, source_target_pairs={{0,4},{1,9},{2,6},{3,11},{4,0},{5,13},{6,2},{7,15},{8,12},{9,1},{1... | collective-permute-start | bytes 270344 | tf_op jit(solution)/shard_map/ppermute | solution.py:52
  20.8 4.6 %collective-permute-start.6 = (bf16[32,1408]{1,0:T(8,128)(2,1)S(1)}, bf16[32,1408]{1,0:T(8,128)(2,1)S(1)}, u32[]{:S(2)}, u32[]{:S(2)}) collective-permute-start(bf16[32,1408]{1,0:T(8,128)(2,1)S(1)} %get-tuple-element.51), channel_id=1, source_target_pairs={{0,4},{1,9},{2,6},{3,11},{4,0},{5,13},{6,2},{7,15},{8,12},{9,1},{1... | collective-permute-start | bytes 270344 | tf_op jit(solution)/shard_map/ppermute | solution.py:52
  23.2 4.7 %collective-permute-start.4 = (bf16[32,1408]{1,0:T(8,128)(2,1)S(1)}, bf16[32,1408]{1,0:T(8,128)(2,1)S(1)}, u32[]{:S(2)}, u32[]{:S(2)}) collective-permute-start(bf16[32,1408]{1,0:T(8,128)(2,1)S(1)} %get-tuple-element.47), channel_id=1, source_target_pairs={{0,8},{1,3},{2,10},{3,1},{4,12},{5,7},{6,14},{7,5},{8,0},{9,11},{1... | collective-permute-start | bytes 270344 | tf_op jit(solution)/shard_map/ppermute | solution.py:52
  25.6 4.6 %collective-permute-start.7 = (bf16[32,1408]{1,0:T(8,128)(2,1)S(1)}, bf16[32,1408]{1,0:T(8,128)(2,1)S(1)}, u32[]{:S(2)}, u32[]{:S(2)}) collective-permute-start(bf16[32,1408]{1,0:T(8,128)(2,1)S(1)} %get-tuple-element.53), channel_id=1, source_target_pairs={{0,8},{1,3},{2,10},{3,1},{4,12},{5,7},{6,14},{7,5},{8,0},{9,11},{1... | collective-permute-start | bytes 270344 | tf_op jit(solution)/shard_map/ppermute | solution.py:52
  30.7 7.2 %collective-permute-start.10 = (bf16[32,1280]{1,0:T(8,128)(2,1)S(1)}, bf16[32,1280]{1,0:T(8,128)(2,1)S(1)}, u32[]{:S(2)}, u32[]{:S(2)}) collective-permute-start(bf16[32,1280]{1,0:T(8,128)(2,1)S(1)} %get-tuple-element.56), channel_id=1, source_target_pairs={{0,16},{1,17},{2,18},{3,19},{4,20},{5,21},{6,22},{7,23},{8,24},{9,... | collective-permute-start | bytes 245768 | tf_op jit(solution)/shard_map/ppermute | solution.py:52
  33.5 6.1 %collective-permute-start.8 = (bf16[32,1408]{1,0:T(8,128)(2,1)S(1)}, bf16[32,1408]{1,0:T(8,128)(2,1)S(1)}, u32[]{:S(2)}, u32[]{:S(2)}) collective-permute-start(bf16[32,1408]{1,0:T(8,128)(2,1)S(1)} %get-tuple-element.55), channel_id=1, source_target_pairs={{0,16},{1,17},{2,18},{3,19},{4,20},{5,21},{6,22},{7,23},{8,24},{9,... | collective-permute-start | bytes 270344 | tf_op jit(solution)/shard_map/ppermute | solution.py:52
  37.9 8.9 %collective-permute-start.11 = (bf16[64,1280]{1,0:T(8,128)(2,1)S(1)}, bf16[64,1280]{1,0:T(8,128)(2,1)S(1)}, u32[]{:S(2)}, u32[]{:S(2)}) collective-permute-start(bf16[64,1280]{1,0:T(8,128)(2,1)S(1)} %pad_maximum_fusion.1), channel_id=1, source_target_pairs={{0,4},{1,5},{2,6},{3,7},{4,0},{5,1},{6,2},{7,3},{8,12},{9,13},{10,... | collective-permute-start | bytes 491528 | tf_op jit(solution)/shard_map/ppermute | solution.py:52
  39.6 5.7 %collective-permute-start.9 = (bf16[64,1408]{1,0:T(8,128)(2,1)S(1)}, bf16[64,1408]{1,0:T(8,128)(2,1)S(1)}, u32[]{:S(2)}, u32[]{:S(2)}) collective-permute-start(bf16[64,1408]{1,0:T(8,128)(2,1)S(1)} %pad_maximum_fusion), channel_id=1, source_target_pairs={{0,4},{1,5},{2,6},{3,7},{4,0},{5,1},{6,2},{7,3},{8,12},{9,13},{10,... | collective-permute-start | bytes 540680 | tf_op jit(solution)/shard_map/ppermute | solution.py:52
  45.3 11.0 %collective-permute-start.15 = (bf16[128,1408]{1,0:T(8,128)(2,1)S(1)}, bf16[128,1408]{1,0:T(8,128)(2,1)S(1)}, u32[]{:S(2)}, u32[]{:S(2)}) collective-permute-start(bf16[128,1408]{1,0:T(8,128)(2,1)S(1)} %constant_dynamic-update-slice_fusion.rows_a), channel_id=1, source_target_pairs={{0,2},{1,9},{2,0},{3,11},{4,6},{5,13},{6,4},{7,15},{8,10},{9,1},{1... | collective-permute-start | bytes 1081352 | tf_op jit(solution)/shard_map/ppermute | solution.py:52
  46.9 9.4 %collective-permute-start.16 = (bf16[128,1280]{1,0:T(8,128)(2,1)S(1)}, bf16[128,1280]{1,0:T(8,128)(2,1)S(1)}, u32[]{:S(2)}, u32[]{:S(2)}) collective-permute-start(bf16[128,1280]{1,0:T(8,128)(2,1)S(1)} %constant_dynamic-update-slice_fusion.3.rows_b), channel_id=1, source_target_pairs={{0,2},{1,9},{2,0},{3,11},{4,6},{5,13},{6,4},{7,15},{8,10},{9,1},{1... | collective-permute-start | bytes 983048 | tf_op jit(solution)/shard_map/ppermute | solution.py:52
  60.1 7.1 %collective-permute-start.17 = (bf16[128,1280]{1,0:T(8,128)(2,1)S(1)}, bf16[128,1280]{1,0:T(8,128)(2,1)S(1)}, u32[]{:S(2)}, u32[]{:S(2)}) collective-permute-start(bf16[128,1280]{1,0:T(8,128)(2,1)S(1)} %get-tuple-element.64), channel_id=1, source_target_pairs={{0,2},{1,9},{2,0},{3,11},{4,6},{5,13},{6,4},{7,15},{8,10},{9,1},{1... | collective-permute-start | bytes 983048 | tf_op jit(solution)/shard_map/ppermute | solution.py:52
  62.2 7.1 %collective-permute-start.21 = (bf16[128,1280]{1,0:T(8,128)(2,1)S(1)}, bf16[128,1280]{1,0:T(8,128)(2,1)S(1)}, u32[]{:S(2)}, u32[]{:S(2)}) collective-permute-start(bf16[128,1280]{1,0:T(8,128)(2,1)S(1)} %get-tuple-element.68), channel_id=1, source_target_pairs={{0,4},{1,5},{2,6},{3,7},{4,0},{5,1},{6,2},{7,3},{8,12},{9,13},{10,... | collective-permute-start | bytes 983048 | tf_op jit(solution)/shard_map/ppermute | solution.py:52
  67.3 5.4 %collective-permute-start.18 = (bf16[64,1280]{1,0:T(8,128)(2,1)S(1)}, bf16[64,1280]{1,0:T(8,128)(2,1)S(1)}, u32[]{:S(2)}, u32[]{:S(2)}) collective-permute-start(bf16[64,1280]{1,0:T(8,128)(2,1)S(1)} %slice.79), channel_id=1, source_target_pairs={{0,4},{1,5},{2,6},{3,7},{4,0},{5,1},{6,2},{7,3},{8,12},{9,13},{10,... | collective-permute-start | bytes 491528 | tf_op jit(solution)/shard_map/ppermute | solution.py:52
  69.5 5.4 %collective-permute-start.22 = (bf16[64,1280]{1,0:T(8,128)(2,1)S(1)}, bf16[64,1280]{1,0:T(8,128)(2,1)S(1)}, u32[]{:S(2)}, u32[]{:S(2)}) collective-permute-start(bf16[64,1280]{1,0:T(8,128)(2,1)S(1)} %slice.78), channel_id=1, source_target_pairs={{0,2},{1,9},{2,0},{3,11},{4,6},{5,13},{6,4},{7,15},{8,10},{9,1},{1... | collective-permute-start | bytes 491528 | tf_op jit(solution)/shard_map/ppermute | solution.py:52
  72.8 5.4 %collective-permute-start.19 = (bf16[32,1280]{1,0:T(8,128)(2,1)S(1)}, bf16[32,1280]{1,0:T(8,128)(2,1)S(1)}, u32[]{:S(2)}, u32[]{:S(2)}) collective-permute-start(bf16[32,1280]{1,0:T(8,128)(2,1)S(1)} %slice.81), channel_id=1, source_target_pairs={{0,16},{1,17},{2,18},{3,19},{4,20},{5,21},{6,22},{7,23},{8,24},{9,... | collective-permute-start | bytes 245768 | tf_op jit(solution)/shard_map/ppermute | solution.py:52
  74.9 6.0 %collective-permute-start.23 = (bf16[32,1280]{1,0:T(8,128)(2,1)S(1)}, bf16[32,1280]{1,0:T(8,128)(2,1)S(1)}, u32[]{:S(2)}, u32[]{:S(2)}) collective-permute-start(bf16[32,1280]{1,0:T(8,128)(2,1)S(1)} %slice.80), channel_id=1, source_target_pairs={{0,16},{1,17},{2,18},{3,19},{4,20},{5,21},{6,22},{7,23},{8,24},{9,... | collective-permute-start | bytes 245768 | tf_op jit(solution)/shard_map/ppermute | solution.py:52
  78.2 5.1 %collective-permute-start.20 = (bf16[16,1280]{1,0:T(8,128)(2,1)S(1)}, bf16[16,1280]{1,0:T(8,128)(2,1)S(1)}, u32[]{:S(2)}, u32[]{:S(2)}) collective-permute-start(bf16[16,1280]{1,0:T(8,128)(2,1)S(1)} %slice.83), channel_id=1, source_target_pairs={{0,8},{1,3},{2,10},{3,1},{4,12},{5,7},{6,14},{7,5},{8,0},{9,11},{1... | collective-permute-start | bytes 122888 | tf_op jit(solution)/shard_map/ppermute | solution.py:52
  80.9 4.4 %collective-permute-start.24 = (bf16[16,1280]{1,0:T(8,128)(2,1)S(1)}, bf16[16,1280]{1,0:T(8,128)(2,1)S(1)}, u32[]{:S(2)}, u32[]{:S(2)}) collective-permute-start(bf16[16,1280]{1,0:T(8,128)(2,1)S(1)} %slice.82), channel_id=1, source_target_pairs={{0,8},{1,3},{2,10},{3,1},{4,12},{5,7},{6,14},{7,5},{8,0},{9,11},{1... | collective-permute-start | bytes 122888 | tf_op jit(solution)/shard_map/ppermute | solution.py:52

commit v3 on v2

--- a/solution.py
+++ b/solution.py
@@ -115,36 +115,72 @@
     )
 
 
-def attend_own_kernel(
-    head_count, row_count, masks, device_ref, queries_ref, keys_ref, values_ref, query_ref, *parts
+def stage_kernel(
+    row_count,
+    masks,
+    device_ref,
+    queries_ref,
+    keys_ref,
+    values_ref,
+    query_ref,
+    near_keys_ref,
+    near_values_ref,
+    arrived,
 ):
     group_size = queries_ref.shape[0] // row_count
     device = device_ref[0]
     odd = lax.rem(device, 2) == 1
     own_block = lax.rem(device, group_size)
+    copies = [
+        pltpu.make_async_copy(keys_ref, near_keys_ref, arrived.at[0]),
+        pltpu.make_async_copy(values_ref, near_values_ref, arrived.at[1]),
+    ]
     for slot, (even_mask, odd_mask) in enumerate(zip(*masks)):
         block = own_block ^ jnp.where(odd, odd_mask, even_mask)
         start = pl.multiple_of(block * row_count, row_count)
-        query_ref[slot * row_count : (slot + 1) * row_count, :] = queries_ref[
-            pl.ds(start, row_count), :
-        ]
+        copies.append(
+            pltpu.make_async_copy(
+                queries_ref.at[pl.ds(start, row_count), :],
+                query_ref.at[slot * row_count : (slot + 1) * row_count, :],
+                arrived.at[2 + slot],
+            )
+        )
+    for copy in copies:
+        copy.start()
+    for copy in copies:
+        copy.wait()
+
+
+def attend_kernel(
+    head_count, part, part_heads, query_ref, keys_a, keys_b, values_a, values_b, sent_ref, kept_ref
+):
     rows = query_ref.shape[0]
-    value_size = values_ref.shape[1] // head_count
-    part_heads = head_count // len(parts)
-    part_tiles = values_ref.shape[1] // len(parts) // LANES
+    half = rows // 2
+    value_size = values_a.shape[1] // head_count
+    part_tiles = part_heads * value_size // LANES
+    base = part * part_tiles
     lane = lane_iota((rows, LANES))
-    for head in range(head_count):
-        part_ref = parts[head // part_heads]
-        base = head // part_heads * part_tiles
-        if head % part_heads == 0:
-            stats = jnp.zeros((rows, LANES), jnp.float32)
-        scores = head_scores(head, head_count, query_ref, keys_ref)
-        peak = rounded_peak(scores)
-        raised = jnp.exp(scores - peak)
-        total = jnp.sum(raised, axis=1, keepdims=True)
-        stats = jnp.where(lane == head % part_heads, peak, stats)
-        stats = jnp.where(lane == head % part_heads + part_heads, total, stats)
-        summed = head_sums(head, value_size, raised, values_ref)
+    peaks = jnp.zeros((rows, LANES), jnp.float32)
+    totals = jnp.zeros((rows, LANES), jnp.float32)
+
+    def put(tile, value):
+        columns = slice(tile * LANES, (tile + 1) * LANES)
+        kept_ref[:, columns] = value[:half]
+        sent_ref[:, columns] = value[half:].astype(jnp.bfloat16)
+
+    for at in range(part_heads):
+        head = part * part_heads + at
+        scores_a = head_scores(head, head_count, query_ref, keys_a)
+        scores_b = head_scores(head, head_count, query_ref, keys_b)
+        peak = jnp.maximum(rounded_peak(scores_a), rounded_peak(scores_b))
+        raised_a = jnp.exp(scores_a - peak)
+        raised_b = jnp.exp(scores_b - peak)
+        total = jnp.sum(raised_a + raised_b, axis=1, keepdims=True)
+        peaks = jnp.where(lane == at, peak, peaks)
+        totals = jnp.where(lane == at, total, totals)
+        summed = head_sums(head, value_size, raised_a, values_a) + head_sums(
+            head, value_size, raised_b, values_b
+        )
         low, high = head_windows(head, value_size)
         for tile in range(low, high):
             value = summed[:, (tile - low) * LANES : (tile - low + 1) * LANES]
@@ -153,57 +189,8 @@
                 value = jnp.where(lane < edge, waiting, value)
             waiting = value
             if (tile + 1) * LANES <= (head + 1) * value_size:
-                part_ref[:, (tile - base) * LANES : (tile - base + 1) * LANES] = value
-        if (head + 1) % part_heads == 0:
-            part_ref[:, part_tiles * LANES :] = stats
-
-
-def attend_other_kernel(head_count, query_ref, keys_ref, values_ref, *rest):
-    part_count = len(rest) // 3
-    parts, outputs = rest[:part_count], rest[part_count:]
-    rows = query_ref.shape[0]
-    half = rows // 2
-    value_size = values_ref.shape[1] // head_count
-    part_heads = head_count // part_count
-    part_tiles = values_ref.shape[1] // part_count // LANES
-    lane = lane_iota((rows, LANES))
-
-    def put(part, tile, value):
-        columns = slice(tile * LANES, (tile + 1) * LANES)
-        outputs[2 * part + 1][:, columns] = value[:half]
-        outputs[2 * part][:, columns] = value[half:].astype(jnp.bfloat16)
-
-    for head in range(head_count):
-        part = head // part_heads
-        at = head % part_heads
-        base = part * part_tiles
-        if at == 0:
-            stats = parts[part][:, part_tiles * LANES :]
-            peaks = jnp.zeros((rows, LANES), jnp.float32)
-            totals = jnp.zeros((rows, LANES), jnp.float32)
-        scores = head_scores(head, head_count, query_ref, keys_ref)
-        old_peak = stats[:, at : at + 1]
-        peak = jnp.maximum(rounded_peak(scores), old_peak)
-        factor = jnp.exp(old_peak - peak)
-        raised = jnp.exp(scores - peak)
-        total = jnp.sum(raised, axis=1, keepdims=True)
-        total = total + stats[:, part_heads + at : part_heads + at + 1] * factor
-        peaks = jnp.where(lane == at, peak, peaks)
-        totals = jnp.where(lane == at, total, totals)
-        summed = head_sums(head, value_size, raised, values_ref)
-        low, high = head_windows(head, value_size)
-        for tile in range(low, high):
-            value = summed[:, (tile - low) * LANES : (tile - low + 1) * LANES]
-            old = parts[part][:, (tile - base) * LANES : (tile - base + 1) * LANES]
-            value = value + old * factor
-            edge = head * value_size - tile * LANES
-            if edge > 0:
-                value = jnp.where(lane < edge, waiting, value)
-            waiting = value
-            if (tile + 1) * LANES <= (head + 1) * value_size:
-                put(part, tile - base, value)
-        if at == part_heads - 1:
-            put(part, part_tiles, pack_stats(peaks, totals, part_heads))
+                put(tile - base, value)
+    put(part_tiles, pack_stats(peaks, totals, part_heads))
 
 
 def merged_parts(kept_ref, came_ref, head_count, model_width):
@@ -493,28 +480,30 @@
             near_shape((rows, part_width), jnp.float32),
         )
 
-    query_rows, *partials = pl.pallas_call(
-        functools.partial(attend_own_kernel, HEADS, row_count, masks),
-        name="attend_own",
-        compiler_params=pltpu.CompilerParams(vmem_limit_bytes=12 << 20),
-        out_shape=(near_shape((rows, queries.shape[1]), jnp.bfloat16),)
-        + (near_shape((rows, part_width), jnp.float32),) * PARTS,
-        in_specs=[pl.BlockSpec(memory_space=pltpu.SMEM)] + [whole] * 3,
-        out_specs=(whole,) * (PARTS + 1),
+    anywhere = pl.BlockSpec(memory_space=pltpu.HBM)
+    query_rows, own_keys, own_values = pl.pallas_call(
+        functools.partial(stage_kernel, row_count, masks),
+        name="stage_in",
+        compiler_params=pltpu.CompilerParams(vmem_limit_bytes=4 << 20),
+        out_shape=(
+            near_shape((rows, queries.shape[1]), jnp.bfloat16),
+            near_shape(patch_keys.shape, jnp.bfloat16),
+            near_shape(patch_values.shape, jnp.bfloat16),
+        ),
+        in_specs=[pl.BlockSpec(memory_space=pltpu.SMEM)] + [anywhere] * 3,
+        out_specs=(whole,) * 3,
+        scratch_shapes=[pltpu.SemaphoreType.DMA((2 + (1 << stages),))],
     )(device_index.reshape(1), far(queries), far(patch_keys), far(patch_values))
-    chains = pl.pallas_call(
-        functools.partial(attend_other_kernel, HEADS),
-        name="attend_other",
-        compiler_params=pltpu.CompilerParams(vmem_limit_bytes=12 << 20),
-        out_shape=pair_shapes(rows // 2) * PARTS,
-        in_specs=[whole] * (3 + PARTS),
-        out_specs=(whole,) * (2 * PARTS),
-    )(
-        near(query_rows),
-        near(other_keys),
-        near(other_values),
-        *[near(partial) for partial in partials],
-    )
+    operands = (query_rows, own_keys, other_keys, own_values, other_values)
+    chains = []
+    for part in range(PARTS):
+        chains += pl.pallas_call(
+            functools.partial(attend_kernel, HEADS, part, part_heads),
+            compiler_params=pltpu.CompilerParams(vmem_limit_bytes=8 << 20),
+            out_shape=pair_shapes(rows // 2),
+            in_specs=[whole] * 5,
+            out_specs=(whole, whole),
+        )(*[near(operand) for operand in operands])
     finished = []
     for part in range(PARTS):
         sent, kept = chains[2 * part : 2 * part + 2]

time: 86.1 us -> 80.9 us (0.940)
  Pallas kernels: 20.7 us -> 16.2 us
  starting transfers between devices: 35.2 us -> 34 us
    pallas_call x2 -> x3, Pallas kernels: 8.26 us -> 4.02 us  [the longest x2 2.74 us: attention_rows(): pl.pallas_call(functools.partial(attend_kernel, HEADS, part, part_heads),...]
    ppermute x20, starting transfers between devices: 33.8 us -> 32.6 us  [exchange(): return lax.ppermute(value, 'wide', pairs)]
  transfers between devices with their start and end apart: 25 -> 25, of which waited for: 13 -> 18; matrix products, arithmetic and copies ran while one was open for 1% -> 1% of each run, Pallas kernels for 20% -> 16%
where the time goes in v3:
time: 80.9 us; the launch traced here: 80.8 us
  starting transfers between devices  34 us (42%)
  waiting for transfers between devices  29.1 us (36%)
  Pallas kernels  16.2 us (20%)
  other arithmetic  1.01 us (1%)
    ppermute x20, starting transfers between devices, exchange(): return lax.ppermute(value, 'wide', pairs)  32.6 us
    ppermute x20, waiting for transfers between devices, exchange(): return lax.ppermute(value, 'wide', pairs)  26.8 us
    pallas_call x1, Pallas kernels, first_expert_rows(): pl.pallas_call(first_expert_kernel, name='expert_first', compiler_params=...  6.64 us
    pallas_call x1, Pallas kernels, second_expert_rows(): pl.pallas_call(second_expert_kernel, name='expert_second', compiler_param...  3.59 us
    pallas_call x2, Pallas kernels, attention_rows(): pl.pallas_call(functools.partial(attend_kernel, HEADS, part, part_heads),...  2.74 us
    ppermute x5, waiting for transfers between devices, partner(): return lax.ppermute(value, axis, pairs)  2.35 us
  transfers between devices with their start and end apart: 25, of which 18 were waited for; matrix products, arithmetic and copies ran while one was open for 1% of the time, Pallas kernels for 16%

profile of v3, /device:TPU:0, one launch (start us, length us, event | category | flops | bytes accessed | tf_op | source)
XLA Modules:
  0.0 80.8 jit_solution(4471516008679061536)
XLA Ops:
  0.5 2.3 %collective-permute-done.keys_b = bf16[128,1152]{1,0:T(8,128)(2,1)S(1)} collective-permute-done((bf16[128,1152]{1,0:T(8,128)(2,1)}, bf16[128,1152]{1,0:T(8,128)(2,1)S(1)}, u32[]{:S(2)}, u32[]{:S(2)}) %collective-permute-start) | collective-permute-done | bytes 294944 | tf_op jit(solution)/shard_map/ppermute | solution.py:33
  3.7 1.3 %stage_in.1 = (bf16[128,1152]{1,0:T(8,128)(2,1)S(1)}, bf16[128,1152]{1,0:T(8,128)(2,1)S(1)}, bf16[128,2560]{1,0:T(8,128)(2,1)S(1)}) custom-call(s32[1]{0:T(128)} %bitcast.device_ref, bf16[256,1152]{1,0:T(8,128)(2,1)} %queries_ref.1, bf16[128,1152]{1,0:T(8,128)(2,1)} %keys_ref.1, bf16[128,2560]{1,0:T(8,128)(2,1)} %values_ref.1), custom_call_target="tpu_custom_call" | custom-call | tf_op jit(solution)/shard_map/stage_in/pallas_call | solution.py:484
  5.1 1.2 %shard_map.91 = (bf16[64,1408]{1,0:T(8,128)(2,1)S(1)}, f32[64,1408]{1,0:T(8,128)S(1)}) custom-call(bf16[128,1152]{1,0:T(8,128)(2,1)S(1)} %get-tuple-element.37.query_ref, bf16[128,1152]{1,0:T(8,128)(2,1)S(1)} %get-tuple-element.38.keys_a, bf16[128,1152]{1,0:T(8,128)(2,1)S(1)} %collective-permute-done.keys_b, ...), custom_call_target="tpu_custom_call" | custom-call | tf_op jit(solution)/shard_map/pallas_call | solution.py:500
  6.3 2.7 %collective-permute-start.2 = (bf16[64,1408]{1,0:T(8,128)(2,1)S(1)}, bf16[64,1408]{1,0:T(8,128)(2,1)S(1)}, u32[]{:S(2)}, u32[]{:S(2)}) collective-permute-start(bf16[64,1408]{1,0:T(8,128)(2,1)S(1)} %get-tuple-element.43), channel_id=1, source_target_pairs={{0,2},{1,5},{2,0},{3,7},{4,6},{5,1},{6,4},{7,3},{8,10},{9,13},{10,... | collective-permute-start | bytes 540680 | tf_op jit(solution)/shard_map/ppermute | solution.py:52
  9.0 1.5 %shard_map.94 = (bf16[64,1408]{1,0:T(8,128)(2,1)S(1)}, f32[64,1408]{1,0:T(8,128)S(1)}) custom-call(bf16[128,1152]{1,0:T(8,128)(2,1)S(1)} %get-tuple-element.37.query_ref, bf16[128,1152]{1,0:T(8,128)(2,1)S(1)} %get-tuple-element.38.keys_a, bf16[128,1152]{1,0:T(8,128)(2,1)S(1)} %collective-permute-done.keys_b, ...), custom_call_target="tpu_custom_call" | custom-call | tf_op jit(solution)/shard_map/pallas_call | solution.py:500
  10.6 1.8 %collective-permute-done.2.came_ref = bf16[64,1408]{1,0:T(8,128)(2,1)S(1)} collective-permute-done((bf16[64,1408]{1,0:T(8,128)(2,1)S(1)}, bf16[64,1408]{1,0:T(8,128)(2,1)S(1)}, u32[]{:S(2)}, u32[]{:S(2)}) %collective-permute-start.2) | collective-permute-done | bytes 180256 | tf_op jit(solution)/shard_map/ppermute | solution.py:52
  12.7 2.1 %collective-permute-start.3 = (bf16[32,1408]{1,0:T(8,128)(2,1)S(1)}, bf16[32,1408]{1,0:T(8,128)(2,1)S(1)}, u32[]{:S(2)}, u32[]{:S(2)}) collective-permute-start(bf16[32,1408]{1,0:T(8,128)(2,1)S(1)} %get-tuple-element.45), channel_id=1, source_target_pairs={{0,4},{1,9},{2,6},{3,11},{4,0},{5,13},{6,2},{7,15},{8,12},{9,1},{1... | collective-permute-start | bytes 270344 | tf_op jit(solution)/shard_map/ppermute | solution.py:52
  14.8 1.3 %collective-permute-done.5.came_ref = bf16[64,1408]{1,0:T(8,128)(2,1)S(1)} collective-permute-done((bf16[64,1408]{1,0:T(8,128)(2,1)S(1)}, bf16[64,1408]{1,0:T(8,128)(2,1)S(1)}, u32[]{:S(2)}, u32[]{:S(2)}) %collective-permute-start.5) | collective-permute-done | bytes 180256 | tf_op jit(solution)/shard_map/ppermute | solution.py:52
  16.3 1.6 %collective-permute-start.6 = (bf16[32,1408]{1,0:T(8,128)(2,1)S(1)}, bf16[32,1408]{1,0:T(8,128)(2,1)S(1)}, u32[]{:S(2)}, u32[]{:S(2)}) collective-permute-start(bf16[32,1408]{1,0:T(8,128)(2,1)S(1)} %get-tuple-element.51), channel_id=1, source_target_pairs={{0,4},{1,9},{2,6},{3,11},{4,0},{5,13},{6,2},{7,15},{8,12},{9,1},{1... | collective-permute-start | bytes 270344 | tf_op jit(solution)/shard_map/ppermute | solution.py:52
  18.2 1.6 %collective-permute-start.4 = (bf16[32,1408]{1,0:T(8,128)(2,1)S(1)}, bf16[32,1408]{1,0:T(8,128)(2,1)S(1)}, u32[]{:S(2)}, u32[]{:S(2)}) collective-permute-start(bf16[32,1408]{1,0:T(8,128)(2,1)S(1)} %get-tuple-element.47), channel_id=1, source_target_pairs={{0,8},{1,3},{2,10},{3,1},{4,12},{5,7},{6,14},{7,5},{8,0},{9,11},{1... | collective-permute-start | bytes 270344 | tf_op jit(solution)/shard_map/ppermute | solution.py:52
  19.8 1.1 %collective-permute-done.6.came_ref = bf16[32,1408]{1,0:T(8,128)(2,1)S(1)} collective-permute-done((bf16[32,1408]{1,0:T(8,128)(2,1)S(1)}, bf16[32,1408]{1,0:T(8,128)(2,1)S(1)}, u32[]{:S(2)}, u32[]{:S(2)}) %collective-permute-start.6) | collective-permute-done | bytes 90144 | tf_op jit(solution)/shard_map/ppermute | solution.py:52
  21.1 1.6 %collective-permute-start.7 = (bf16[32,1408]{1,0:T(8,128)(2,1)S(1)}, bf16[32,1408]{1,0:T(8,128)(2,1)S(1)}, u32[]{:S(2)}, u32[]{:S(2)}) collective-permute-start(bf16[32,1408]{1,0:T(8,128)(2,1)S(1)} %get-tuple-element.53), channel_id=1, source_target_pairs={{0,8},{1,3},{2,10},{3,1},{4,12},{5,7},{6,14},{7,5},{8,0},{9,11},{1... | collective-permute-start | bytes 270344 | tf_op jit(solution)/shard_map/ppermute | solution.py:52
  22.8 2.9 %collective-permute-done.7.rest_3_ = bf16[32,1408]{1,0:T(8,128)(2,1)S(1)} collective-permute-done((bf16[32,1408]{1,0:T(8,128)(2,1)S(1)}, bf16[32,1408]{1,0:T(8,128)(2,1)S(1)}, u32[]{:S(2)}, u32[]{:S(2)}) %collective-permute-start.7) | collective-permute-done | bytes 90144 | tf_op jit(solution)/shard_map/ppermute | solution.py:52
  26.2 2.7 %collective-permute-start.10 = (bf16[32,1280]{1,0:T(8,128)(2,1)S(1)}, bf16[32,1280]{1,0:T(8,128)(2,1)S(1)}, u32[]{:S(2)}, u32[]{:S(2)}) collective-permute-start(bf16[32,1280]{1,0:T(8,128)(2,1)S(1)} %get-tuple-element.56), channel_id=1, source_target_pairs={{0,16},{1,17},{2,18},{3,19},{4,20},{5,21},{6,22},{7,23},{8,24},{9,... | collective-permute-start | bytes 245768 | tf_op jit(solution)/shard_map/ppermute | solution.py:52
  29.2 3.8 %collective-permute-done.10 = bf16[32,1280]{1,0:T(8,128)(2,1)S(1)} collective-permute-done((bf16[32,1280]{1,0:T(8,128)(2,1)S(1)}, bf16[32,1280]{1,0:T(8,128)(2,1)S(1)}, u32[]{:S(2)}, u32[]{:S(2)}) %collective-permute-start.10) | collective-permute-done | bytes 81952 | tf_op jit(solution)/shard_map/ppermute | solution.py:52
  33.5 0.9 %collective-permute-done.8 = bf16[32,1408]{1,0:T(8,128)(2,1)S(1)} collective-permute-done((bf16[32,1408]{1,0:T(8,128)(2,1)S(1)}, bf16[32,1408]{1,0:T(8,128)(2,1)S(1)}, u32[]{:S(2)}, u32[]{:S(2)}) %collective-permute-start.8) | collective-permute-done | bytes 90144 | tf_op jit(solution)/shard_map/ppermute | solution.py:52
  34.3 3.1 %collective-permute-start.9 = (bf16[64,1408]{1,0:T(8,128)(2,1)S(1)}, bf16[64,1408]{1,0:T(8,128)(2,1)S(1)}, u32[]{:S(2)}, u32[]{:S(2)}) collective-permute-start(bf16[64,1408]{1,0:T(8,128)(2,1)S(1)} %pad_maximum_fusion), channel_id=1, source_target_pairs={{0,4},{1,5},{2,6},{3,7},{4,0},{5,1},{6,2},{7,3},{8,12},{9,13},{10,... | collective-permute-start | bytes 540680 | tf_op jit(solution)/shard_map/ppermute | solution.py:52
  37.4 3.5 %collective-permute-done.9 = bf16[64,1408]{1,0:T(8,128)(2,1)S(1)} collective-permute-done((bf16[64,1408]{1,0:T(8,128)(2,1)S(1)}, bf16[64,1408]{1,0:T(8,128)(2,1)S(1)}, u32[]{:S(2)}, u32[]{:S(2)}) %collective-permute-start.9) | collective-permute-done | bytes 180256 | tf_op jit(solution)/shard_map/ppermute | solution.py:52
  40.9 1.8 %collective-permute-start.15 = (bf16[128,1408]{1,0:T(8,128)(2,1)S(1)}, bf16[128,1408]{1,0:T(8,128)(2,1)S(1)}, u32[]{:S(2)}, u32[]{:S(2)}) collective-permute-start(bf16[128,1408]{1,0:T(8,128)(2,1)S(1)} %constant_dynamic-update-slice_fusion.rows_a), channel_id=1, source_target_pairs={{0,2},{1,9},{2,0},{3,11},{4,6},{5,13},{6,4},{7,15},{8,10},{9,1},{1... | collective-permute-start | bytes 1081352 | tf_op jit(solution)/shard_map/ppermute | solution.py:52
  43.1 6.6 %expert_first.1 = (f32[128,1280]{1,0:T(8,128)S(1)}, f32[128,1280]{1,0:T(8,128)S(1)}, bf16[1024,2560]{1,0:T(8,128)(2,1)S(1)}, bf16[1024,2560]{1,0:T(8,128)(2,1)S(1)}, bf16[1024,2560]{1,0:T(8,128)(2,1)S(1)}) custom-call(s32[1]{0:T(128)} %bitcast.1.expert_ref, bf16[128,1408]{1,0:T(8,128)(2,1)S(1)} %constant_dynamic-update-slice_fusion.rows_a, ...), custom_call_target="tpu_custom_call" | custom-call | flops 2013265920 | bytes 15728640 | tf_op jit(solution)/shard_map/expert_first/pallas_call | solution.py:402
  49.8 2.2 %collective-permute-done.16.rows_b = bf16[128,1280]{1,0:T(8,128)(2,1)S(1)} collective-permute-done((bf16[128,1280]{1,0:T(8,128)(2,1)S(1)}, bf16[128,1280]{1,0:T(8,128)(2,1)S(1)}, u32[]{:S(2)}, u32[]{:S(2)}) %collective-permute-start.16) | collective-permute-done | bytes 327712 | tf_op jit(solution)/shard_map/ppermute | solution.py:52
  51.9 3.6 %expert_second.1 = (bf16[128,1280]{1,0:T(8,128)(2,1)S(1)}, bf16[128,1024]{1,0:T(8,128)(2,1)S(1)}) custom-call(s32[1]{0:T(128)} %bitcast.1.expert_ref, bf16[128,1408]{1,0:T(8,128)(2,1)S(1)} %collective-permute-done.15.rows_a, bf16[128,1280]{1,0:T(8,128)(2,1)S(1)} %collective-permute-done.16.rows_b, bf16[1024,2560]{1,0:T(8,128)(2,1)S(1)} %get-tuple-element.61.gate_ref, ...), custom_call_target="tpu_custom_call" | custom-call | tf_op jit(solution)/shard_map/expert_second/pallas_call | solution.py:428
  55.5 1.8 %collective-permute-start.17 = (bf16[128,1280]{1,0:T(8,128)(2,1)S(1)}, bf16[128,1280]{1,0:T(8,128)(2,1)S(1)}, u32[]{:S(2)}, u32[]{:S(2)}) collective-permute-start(bf16[128,1280]{1,0:T(8,128)(2,1)S(1)} %get-tuple-element.64), channel_id=1, source_target_pairs={{0,2},{1,9},{2,0},{3,11},{4,6},{5,13},{6,4},{7,15},{8,10},{9,1},{1... | collective-permute-start | bytes 983048 | tf_op jit(solution)/shard_map/ppermute | solution.py:52
  58.3 4.4 %collective-permute-done.17 = bf16[128,1280]{1,0:T(8,128)(2,1)S(1)} collective-permute-done((bf16[128,1280]{1,0:T(8,128)(2,1)S(1)}, bf16[128,1280]{1,0:T(8,128)(2,1)S(1)}, u32[]{:S(2)}, u32[]{:S(2)}) %collective-permute-start.17) | collective-permute-done | bytes 327712 | tf_op jit(solution)/shard_map/ppermute | solution.py:52
  62.8 2.1 %collective-permute-start.18 = (bf16[64,1280]{1,0:T(8,128)(2,1)S(1)}, bf16[64,1280]{1,0:T(8,128)(2,1)S(1)}, u32[]{:S(2)}, u32[]{:S(2)}) collective-permute-start(bf16[64,1280]{1,0:T(8,128)(2,1)S(1)} %slice.79), channel_id=1, source_target_pairs={{0,4},{1,5},{2,6},{3,7},{4,0},{5,1},{6,2},{7,3},{8,12},{9,13},{10,... | collective-permute-start | bytes 491528 | tf_op jit(solution)/shard_map/ppermute | solution.py:52
  65.1 2.2 %collective-permute-start.22 = (bf16[64,1280]{1,0:T(8,128)(2,1)S(1)}, bf16[64,1280]{1,0:T(8,128)(2,1)S(1)}, u32[]{:S(2)}, u32[]{:S(2)}) collective-permute-start(bf16[64,1280]{1,0:T(8,128)(2,1)S(1)} %slice.78), channel_id=1, source_target_pairs={{0,2},{1,9},{2,0},{3,11},{4,6},{5,13},{6,4},{7,15},{8,10},{9,1},{1... | collective-permute-start | bytes 491528 | tf_op jit(solution)/shard_map/ppermute | solution.py:52
  67.3 0.9 %collective-permute-done.18 = bf16[64,1280]{1,0:T(8,128)(2,1)S(1)} collective-permute-done((bf16[64,1280]{1,0:T(8,128)(2,1)S(1)}, bf16[64,1280]{1,0:T(8,128)(2,1)S(1)}, u32[]{:S(2)}, u32[]{:S(2)}) %collective-permute-start.18) | collective-permute-done | bytes 163872 | tf_op jit(solution)/shard_map/ppermute | solution.py:52
  68.2 2.1 %collective-permute-start.19 = (bf16[32,1280]{1,0:T(8,128)(2,1)S(1)}, bf16[32,1280]{1,0:T(8,128)(2,1)S(1)}, u32[]{:S(2)}, u32[]{:S(2)}) collective-permute-start(bf16[32,1280]{1,0:T(8,128)(2,1)S(1)} %slice.81), channel_id=1, source_target_pairs={{0,16},{1,17},{2,18},{3,19},{4,20},{5,21},{6,22},{7,23},{8,24},{9,... | collective-permute-start | bytes 245768 | tf_op jit(solution)/shard_map/ppermute | solution.py:52
  70.6 3.0 %collective-permute-start.23 = (bf16[32,1280]{1,0:T(8,128)(2,1)S(1)}, bf16[32,1280]{1,0:T(8,128)(2,1)S(1)}, u32[]{:S(2)}, u32[]{:S(2)}) collective-permute-start(bf16[32,1280]{1,0:T(8,128)(2,1)S(1)} %slice.80), channel_id=1, source_target_pairs={{0,16},{1,17},{2,18},{3,19},{4,20},{5,21},{6,22},{7,23},{8,24},{9,... | collective-permute-start | bytes 245768 | tf_op jit(solution)/shard_map/ppermute | solution.py:52
  73.6 0.9 %collective-permute-done.19 = bf16[32,1280]{1,0:T(8,128)(2,1)S(1)} collective-permute-done((bf16[32,1280]{1,0:T(8,128)(2,1)S(1)}, bf16[32,1280]{1,0:T(8,128)(2,1)S(1)}, u32[]{:S(2)}, u32[]{:S(2)}) %collective-permute-start.19) | collective-permute-done | bytes 81952 | tf_op jit(solution)/shard_map/ppermute | solution.py:52
  76.0 2.0 %collective-permute-start.24 = (bf16[16,1280]{1,0:T(8,128)(2,1)S(1)}, bf16[16,1280]{1,0:T(8,128)(2,1)S(1)}, u32[]{:S(2)}, u32[]{:S(2)}) collective-permute-start(bf16[16,1280]{1,0:T(8,128)(2,1)S(1)} %slice.82), channel_id=1, source_target_pairs={{0,8},{1,3},{2,10},{3,1},{4,12},{5,7},{6,14},{7,5},{8,0},{9,11},{1... | collective-permute-start | bytes 122888 | tf_op jit(solution)/shard_map/ppermute | solution.py:52
  78.6 1.5 %collective-permute-done.24 = bf16[16,1280]{1,0:T(8,128)(2,1)S(1)} collective-permute-done((bf16[16,1280]{1,0:T(8,128)(2,1)S(1)}, bf16[16,1280]{1,0:T(8,128)(2,1)S(1)}, u32[]{:S(2)}, u32[]{:S(2)}) %collective-permute-start.24) | collective-permute-done | bytes 40992 | tf_op jit(solution)/shard_map/ppermute | solution.py:52
  (62 shorter events, 8.7 us)
Async XLA Ops:
  0.0 2.9 %collective-permute-start.1 = (bf16[128,2560]{1,0:T(8,128)(2,1)}, bf16[128,2560]{1,0:T(8,128)(2,1)S(1)}, u32[]{:S(2)}, u32[]{:S(2)}) collective-permute-start(bf16[128,2560]{1,0:T(8,128)(2,1)} %values_ref.1), channel_id=1, source_target_pairs={{0,1},{1,0},{2,3},{3,2},{4,5},{5,4},{6,7},{7,6},{8,9},{9,8},{10,11... | collective-permute-start | bytes 1966088 | tf_op jit(solution)/shard_map/ppermute | solution.py:33
  0.5 2.4 %collective-permute-start = (bf16[128,1152]{1,0:T(8,128)(2,1)}, bf16[128,1152]{1,0:T(8,128)(2,1)S(1)}, u32[]{:S(2)}, u32[]{:S(2)}) collective-permute-start(bf16[128,1152]{1,0:T(8,128)(2,1)} %keys_ref.1), channel_id=1, source_target_pairs={{0,1},{1,0},{2,3},{3,2},{4,5},{5,4},{6,7},{7,6},{8,9},{9,8},{10,11... | collective-permute-start | bytes 884744 | tf_op jit(solution)/shard_map/ppermute | solution.py:33
  2.9 40.3 %collective-permute-start.12 = (bf16[512,2560]{1,0:T(8,128)(2,1)}, bf16[512,2560]{1,0:T(8,128)(2,1)}, u32[]{:S(2)}, u32[]{:S(2)}) collective-permute-start(bf16[512,2560]{1,0:T(8,128)(2,1)} %gate_a), channel_id=1, source_target_pairs={{0,1},{1,0},{2,3},{3,2},{4,5},{5,4},{6,7},{7,6},{8,9},{9,8},{10,11... | collective-permute-start | bytes 7864328 | tf_op jit(solution)/shard_map/ppermute | solution.py:33
  3.2 39.9 %collective-permute-start.13 = (bf16[512,2560]{1,0:T(8,128)(2,1)}, bf16[512,2560]{1,0:T(8,128)(2,1)}, u32[]{:S(2)}, u32[]{:S(2)}) collective-permute-start(bf16[512,2560]{1,0:T(8,128)(2,1)} %up_a), channel_id=1, source_target_pairs={{0,1},{1,0},{2,3},{3,2},{4,5},{5,4},{6,7},{7,6},{8,9},{9,8},{10,11... | collective-permute-start | bytes 7864328 | tf_op jit(solution)/shard_map/ppermute | solution.py:33
  3.4 39.7 %collective-permute-start.14 = (bf16[512,2560]{1,0:T(8,128)(2,1)}, bf16[512,2560]{1,0:T(8,128)(2,1)}, u32[]{:S(2)}, u32[]{:S(2)}) collective-permute-start(bf16[512,2560]{1,0:T(8,128)(2,1)} %down_a), channel_id=1, source_target_pairs={{0,1},{1,0},{2,3},{3,2},{4,5},{5,4},{6,7},{7,6},{8,9},{9,8},{10,11... | collective-permute-start | bytes 7864328 | tf_op jit(solution)/shard_map/ppermute | solution.py:33
  5.0 12.9 %copy-start.1 = (s32[16,6]{0,1:T(8,128)S(1)}, s32[16,6]{0,1:T(8,128)}, u32[]{:S(2)}) copy-start(s32[16,6]{0,1:T(8,128)} %param.14) | copy-start | bytes 1156
  5.0 12.9 %copy-start.2 = (s32[16,6]{0,1:T(8,128)S(1)}, s32[16,6]{0,1:T(8,128)}, u32[]{:S(2)}) copy-start(s32[16,6]{0,1:T(8,128)} %param.13) | copy-start | bytes 1156
  5.1 17.7 %copy-start = (f32[2560]{0:T(1024)S(1)}, f32[2560]{0:T(1024)}, u32[]{:S(2)}) copy-start(f32[2560]{0:T(1024)} %param.12) | copy-start | bytes 30724
  6.3 6.2 %collective-permute-start.2 = (bf16[64,1408]{1,0:T(8,128)(2,1)S(1)}, bf16[64,1408]{1,0:T(8,128)(2,1)S(1)}, u32[]{:S(2)}, u32[]{:S(2)}) collective-permute-start(bf16[64,1408]{1,0:T(8,128)(2,1)S(1)} %get-tuple-element.43), channel_id=1, source_target_pairs={{0,2},{1,5},{2,0},{3,7},{4,6},{5,1},{6,4},{7,3},{8,10},{9,13},{10,... | collective-permute-start | bytes 540680 | tf_op jit(solution)/shard_map/ppermute | solution.py:52
  10.5 5.6 %collective-permute-start.5 = (bf16[64,1408]{1,0:T(8,128)(2,1)S(1)}, bf16[64,1408]{1,0:T(8,128)(2,1)S(1)}, u32[]{:S(2)}, u32[]{:S(2)}) collective-permute-start(bf16[64,1408]{1,0:T(8,128)(2,1)S(1)} %get-tuple-element.49), channel_id=1, source_target_pairs={{0,2},{1,5},{2,0},{3,7},{4,6},{5,1},{6,4},{7,3},{8,10},{9,13},{10,... | collective-permute-start | bytes 540680 | tf_op jit(solution)/shard_map/ppermute | solution.py:52
  12.7 5.3 %collective-permute-start.3 = (bf16[32,1408]{1,0:T(8,128)(2,1)S(1)}, bf16[32,1408]{1,0:T(8,128)(2,1)S(1)}, u32[]{:S(2)}, u32[]{:S(2)}) collective-permute-start(bf16[32,1408]{1,0:T(8,128)(2,1)S(1)} %get-tuple-element.45), channel_id=1, source_target_pairs={{0,4},{1,9},{2,6},{3,11},{4,0},{5,13},{6,2},{7,15},{8,12},{9,1},{1... | collective-permute-start | bytes 270344 | tf_op jit(solution)/shard_map/ppermute | solution.py:52
  16.3 4.6 %collective-permute-start.6 = (bf16[32,1408]{1,0:T(8,128)(2,1)S(1)}, bf16[32,1408]{1,0:T(8,128)(2,1)S(1)}, u32[]{:S(2)}, u32[]{:S(2)}) collective-permute-start(bf16[32,1408]{1,0:T(8,128)(2,1)S(1)} %get-tuple-element.51), channel_id=1, source_target_pairs={{0,4},{1,9},{2,6},{3,11},{4,0},{5,13},{6,2},{7,15},{8,12},{9,1},{1... | collective-permute-start | bytes 270344 | tf_op jit(solution)/shard_map/ppermute | solution.py:52
  18.2 4.6 %collective-permute-start.4 = (bf16[32,1408]{1,0:T(8,128)(2,1)S(1)}, bf16[32,1408]{1,0:T(8,128)(2,1)S(1)}, u32[]{:S(2)}, u32[]{:S(2)}) collective-permute-start(bf16[32,1408]{1,0:T(8,128)(2,1)S(1)} %get-tuple-element.47), channel_id=1, source_target_pairs={{0,8},{1,3},{2,10},{3,1},{4,12},{5,7},{6,14},{7,5},{8,0},{9,11},{1... | collective-permute-start | bytes 270344 | tf_op jit(solution)/shard_map/ppermute | solution.py:52
  21.1 4.6 %collective-permute-start.7 = (bf16[32,1408]{1,0:T(8,128)(2,1)S(1)}, bf16[32,1408]{1,0:T(8,128)(2,1)S(1)}, u32[]{:S(2)}, u32[]{:S(2)}) collective-permute-start(bf16[32,1408]{1,0:T(8,128)(2,1)S(1)} %get-tuple-element.53), channel_id=1, source_target_pairs={{0,8},{1,3},{2,10},{3,1},{4,12},{5,7},{6,14},{7,5},{8,0},{9,11},{1... | collective-permute-start | bytes 270344 | tf_op jit(solution)/shard_map/ppermute | solution.py:52
  26.2 6.8 %collective-permute-start.10 = (bf16[32,1280]{1,0:T(8,128)(2,1)S(1)}, bf16[32,1280]{1,0:T(8,128)(2,1)S(1)}, u32[]{:S(2)}, u32[]{:S(2)}) collective-permute-start(bf16[32,1280]{1,0:T(8,128)(2,1)S(1)} %get-tuple-element.56), channel_id=1, source_target_pairs={{0,16},{1,17},{2,18},{3,19},{4,20},{5,21},{6,22},{7,23},{8,24},{9,... | collective-permute-start | bytes 245768 | tf_op jit(solution)/shard_map/ppermute | solution.py:52
  28.9 5.4 %collective-permute-start.8 = (bf16[32,1408]{1,0:T(8,128)(2,1)S(1)}, bf16[32,1408]{1,0:T(8,128)(2,1)S(1)}, u32[]{:S(2)}, u32[]{:S(2)}) collective-permute-start(bf16[32,1408]{1,0:T(8,128)(2,1)S(1)} %get-tuple-element.55), channel_id=1, source_target_pairs={{0,16},{1,17},{2,18},{3,19},{4,20},{5,21},{6,22},{7,23},{8,24},{9,... | collective-permute-start | bytes 270344 | tf_op jit(solution)/shard_map/ppermute | solution.py:52
  33.1 9.6 %collective-permute-start.11 = (bf16[64,1280]{1,0:T(8,128)(2,1)S(1)}, bf16[64,1280]{1,0:T(8,128)(2,1)S(1)}, u32[]{:S(2)}, u32[]{:S(2)}) collective-permute-start(bf16[64,1280]{1,0:T(8,128)(2,1)S(1)} %pad_maximum_fusion.1), channel_id=1, source_target_pairs={{0,4},{1,5},{2,6},{3,7},{4,0},{5,1},{6,2},{7,3},{8,12},{9,13},{10,... | collective-permute-start | bytes 491528 | tf_op jit(solution)/shard_map/ppermute | solution.py:52
  34.3 6.6 %collective-permute-start.9 = (bf16[64,1408]{1,0:T(8,128)(2,1)S(1)}, bf16[64,1408]{1,0:T(8,128)(2,1)S(1)}, u32[]{:S(2)}, u32[]{:S(2)}) collective-permute-start(bf16[64,1408]{1,0:T(8,128)(2,1)S(1)} %pad_maximum_fusion), channel_id=1, source_target_pairs={{0,4},{1,5},{2,6},{3,7},{4,0},{5,1},{6,2},{7,3},{8,12},{9,13},{10,... | collective-permute-start | bytes 540680 | tf_op jit(solution)/shard_map/ppermute | solution.py:52
  40.9 11.0 %collective-permute-start.15 = (bf16[128,1408]{1,0:T(8,128)(2,1)S(1)}, bf16[128,1408]{1,0:T(8,128)(2,1)S(1)}, u32[]{:S(2)}, u32[]{:S(2)}) collective-permute-start(bf16[128,1408]{1,0:T(8,128)(2,1)S(1)} %constant_dynamic-update-slice_fusion.rows_a), channel_id=1, source_target_pairs={{0,2},{1,9},{2,0},{3,11},{4,6},{5,13},{6,4},{7,15},{8,10},{9,1},{1... | collective-permute-start | bytes 1081352 | tf_op jit(solution)/shard_map/ppermute | solution.py:52
  42.7 9.2 %collective-permute-start.16 = (bf16[128,1280]{1,0:T(8,128)(2,1)S(1)}, bf16[128,1280]{1,0:T(8,128)(2,1)S(1)}, u32[]{:S(2)}, u32[]{:S(2)}) collective-permute-start(bf16[128,1280]{1,0:T(8,128)(2,1)S(1)} %constant_dynamic-update-slice_fusion.3.rows_b), channel_id=1, source_target_pairs={{0,2},{1,9},{2,0},{3,11},{4,6},{5,13},{6,4},{7,15},{8,10},{9,1},{1... | collective-permute-start | bytes 983048 | tf_op jit(solution)/shard_map/ppermute | solution.py:52
  55.5 7.1 %collective-permute-start.17 = (bf16[128,1280]{1,0:T(8,128)(2,1)S(1)}, bf16[128,1280]{1,0:T(8,128)(2,1)S(1)}, u32[]{:S(2)}, u32[]{:S(2)}) collective-permute-start(bf16[128,1280]{1,0:T(8,128)(2,1)S(1)} %get-tuple-element.64), channel_id=1, source_target_pairs={{0,2},{1,9},{2,0},{3,11},{4,6},{5,13},{6,4},{7,15},{8,10},{9,1},{1... | collective-permute-start | bytes 983048 | tf_op jit(solution)/shard_map/ppermute | solution.py:52
  57.9 7.1 %collective-permute-start.21 = (bf16[128,1280]{1,0:T(8,128)(2,1)S(1)}, bf16[128,1280]{1,0:T(8,128)(2,1)S(1)}, u32[]{:S(2)}, u32[]{:S(2)}) collective-permute-start(bf16[128,1280]{1,0:T(8,128)(2,1)S(1)} %get-tuple-element.68), channel_id=1, source_target_pairs={{0,4},{1,5},{2,6},{3,7},{4,0},{5,1},{6,2},{7,3},{8,12},{9,13},{10,... | collective-permute-start | bytes 983048 | tf_op jit(solution)/shard_map/ppermute | solution.py:52
  62.8 5.4 %collective-permute-start.18 = (bf16[64,1280]{1,0:T(8,128)(2,1)S(1)}, bf16[64,1280]{1,0:T(8,128)(2,1)S(1)}, u32[]{:S(2)}, u32[]{:S(2)}) collective-permute-start(bf16[64,1280]{1,0:T(8,128)(2,1)S(1)} %slice.79), channel_id=1, source_target_pairs={{0,4},{1,5},{2,6},{3,7},{4,0},{5,1},{6,2},{7,3},{8,12},{9,13},{10,... | collective-permute-start | bytes 491528 | tf_op jit(solution)/shard_map/ppermute | solution.py:52
  65.1 5.5 %collective-permute-start.22 = (bf16[64,1280]{1,0:T(8,128)(2,1)S(1)}, bf16[64,1280]{1,0:T(8,128)(2,1)S(1)}, u32[]{:S(2)}, u32[]{:S(2)}) collective-permute-start(bf16[64,1280]{1,0:T(8,128)(2,1)S(1)} %slice.78), channel_id=1, source_target_pairs={{0,2},{1,9},{2,0},{3,11},{4,6},{5,13},{6,4},{7,15},{8,10},{9,1},{1... | collective-permute-start | bytes 491528 | tf_op jit(solution)/shard_map/ppermute | solution.py:52
  68.2 6.3 %collective-permute-start.19 = (bf16[32,1280]{1,0:T(8,128)(2,1)S(1)}, bf16[32,1280]{1,0:T(8,128)(2,1)S(1)}, u32[]{:S(2)}, u32[]{:S(2)}) collective-permute-start(bf16[32,1280]{1,0:T(8,128)(2,1)S(1)} %slice.81), channel_id=1, source_target_pairs={{0,16},{1,17},{2,18},{3,19},{4,20},{5,21},{6,22},{7,23},{8,24},{9,... | collective-permute-start | bytes 245768 | tf_op jit(solution)/shard_map/ppermute | solution.py:52
  70.6 5.4 %collective-permute-start.23 = (bf16[32,1280]{1,0:T(8,128)(2,1)S(1)}, bf16[32,1280]{1,0:T(8,128)(2,1)S(1)}, u32[]{:S(2)}, u32[]{:S(2)}) collective-permute-start(bf16[32,1280]{1,0:T(8,128)(2,1)S(1)} %slice.80), channel_id=1, source_target_pairs={{0,16},{1,17},{2,18},{3,19},{4,20},{5,21},{6,22},{7,23},{8,24},{9,... | collective-permute-start | bytes 245768 | tf_op jit(solution)/shard_map/ppermute | solution.py:52
  74.5 4.1 %collective-permute-start.20 = (bf16[16,1280]{1,0:T(8,128)(2,1)S(1)}, bf16[16,1280]{1,0:T(8,128)(2,1)S(1)}, u32[]{:S(2)}, u32[]{:S(2)}) collective-permute-start(bf16[16,1280]{1,0:T(8,128)(2,1)S(1)} %slice.83), channel_id=1, source_target_pairs={{0,8},{1,3},{2,10},{3,1},{4,12},{5,7},{6,14},{7,5},{8,0},{9,11},{1... | collective-permute-start | bytes 122888 | tf_op jit(solution)/shard_map/ppermute | solution.py:52
  76.0 4.1 %collective-permute-start.24 = (bf16[16,1280]{1,0:T(8,128)(2,1)S(1)}, bf16[16,1280]{1,0:T(8,128)(2,1)S(1)}, u32[]{:S(2)}, u32[]{:S(2)}) collective-permute-start(bf16[16,1280]{1,0:T(8,128)(2,1)S(1)} %slice.82), channel_id=1, source_target_pairs={{0,8},{1,3},{2,10},{3,1},{4,12},{5,7},{6,14},{7,5},{8,0},{9,11},{1... | collective-permute-start | bytes 122888 | tf_op jit(solution)/shard_map/ppermute | solution.py:52

commit v4 on v3

--- a/solution.py
+++ b/solution.py
@@ -253,53 +253,48 @@
         sent_ref[half:, columns] = own.astype(jnp.bfloat16)
 
 
-def finish_kernel(head_count, gain_ref, table_ref, *rest):
-    parts = (len(rest) - 1) // 3
-    pairs, blocks, projected_ref = rest[: 2 * parts], rest[2 * parts : 3 * parts], rest[-1]
-    part_heads = head_count // parts
-    rows = pairs[0].shape[0]
-    half = rows // 2
-    width = pairs[0].shape[1] - LANES
-    square = jnp.zeros((rows, LANES), jnp.float32)
-    for part in range(parts):
-        kept_ref, came_ref = pairs[2 * part : 2 * part + 2]
-        _, total, factor_a, factor_b = merged_parts(kept_ref, came_ref, part_heads, width)
-        columns_a = head_columns(factor_a / total, part_heads)
-        columns_b = head_columns(factor_b / total, part_heads)
-        for tile in range(width // LANES):
-            columns = slice(tile * LANES, (tile + 1) * LANES)
-            value = kept_ref[:, columns] * expand_tile(
-                columns_a, tile, width // part_heads
-            ) + came_ref[:, columns].astype(jnp.float32) * expand_tile(
-                columns_b, tile, width // part_heads
-            )
-            rounded = value.astype(jnp.bfloat16)
-            blocks[part][:, columns] = rounded
-            low = part * width + tile * LANES
-            projected_ref[:, low : low + LANES] = rounded[:half]
-            residual = rounded.astype(jnp.float32)
-            square = square + residual * residual
-    mean = jnp.sum(square, axis=1, keepdims=True) / (parts * width)
-    inverse = lax.rsqrt(mean + 1e-06)
-    for part in range(parts):
-        gain = gain_ref[:, part * width : (part + 1) * width]
-        normed = blocks[part][:, :width].astype(jnp.float32) * inverse * gain
-        blocks[part][:, :width] = normed.astype(jnp.bfloat16)
-    came_table = pairs[1][half:, width:]
-    lane = lane_iota(came_table.shape)
-    blocks[0][:half, width:] = table_ref[...]
-    blocks[0][half:, width:] = jnp.where(
-        lane >= TABLE_LANE, came_table.astype(jnp.float32), 0.0
-    ).astype(jnp.bfloat16)
-
-
-def hidden_units(expert_ref, row_refs, gate_ref, up_ref, turned, hidden, ready):
+def finish_kernel(part_heads, kept_ref, came_ref, *rest):
+    tables, (block_ref, projected_ref) = rest[:-2], rest[-2:]
+    half = kept_ref.shape[0] // 2
+    width = kept_ref.shape[1] - LANES
+    _, total, factor_a, factor_b = merged_parts(kept_ref, came_ref, part_heads, width)
+    columns_a = head_columns(factor_a / total, part_heads)
+    columns_b = head_columns(factor_b / total, part_heads)
+    for tile in range(width // LANES):
+        columns = slice(tile * LANES, (tile + 1) * LANES)
+        value = kept_ref[:, columns] * expand_tile(
+            columns_a, tile, width // part_heads
+        ) + came_ref[:, columns].astype(jnp.float32) * expand_tile(
+            columns_b, tile, width // part_heads
+        )
+        rounded = value.astype(jnp.bfloat16)
+        block_ref[:, columns] = rounded
+        projected_ref[:, columns] = rounded[:half]
+    for table_ref in tables:
+        came_table = came_ref[half:, width:]
+        lane = lane_iota(came_table.shape)
+        block_ref[:half, width:] = table_ref[...]
+        block_ref[half:, width:] = jnp.where(
+            lane >= TABLE_LANE, came_table.astype(jnp.float32), 0.0
+        ).astype(jnp.bfloat16)
+
+
+def hidden_units(expert_ref, gain_ref, row_refs, gate_ref, up_ref, turned, hidden, ready):
     width = row_refs[1].shape[1]
     model_width = width * len(row_refs)
+    square = jnp.zeros((row_refs[0].shape[0], LANES), jnp.float32)
+    for rows_ref in row_refs:
+        for low in range(0, width, LANES):
+            residual = rows_ref[:, low : low + LANES].astype(jnp.float32)
+            square = square + residual * residual
+    mean = jnp.sum(square, axis=1, keepdims=True) / model_width
+    inverse = jnp.broadcast_to(lax.rsqrt(mean + 1e-06), square.shape)
     for part, rows_ref in enumerate(row_refs):
         for low in range(0, width, LANES):
             at = part * width + low
-            turned[at : at + LANES, :] = rows_ref[:, low : low + LANES].T
+            residual = rows_ref[:, low : low + LANES].astype(jnp.float32)
+            normed = residual * inverse * gain_ref[:, at : at + LANES]
+            turned[at : at + LANES, :] = normed.astype(jnp.bfloat16).T
     turned[model_width:, :] = row_refs[0][:, width:].T
     scores = turned[model_width:, :].astype(jnp.float32)
     lane = lax.broadcasted_iota(jnp.int32, scores.shape, 0)
@@ -328,6 +323,7 @@
 
 def first_expert_kernel(
     expert_ref,
+    gain_ref,
     rows_a,
     rows_b,
     gate_a,
@@ -368,7 +364,9 @@
         copy_of(0, chunk).wait()
         copy_of(1, chunk).wait()
 
-    hidden_units(expert_ref, (rows_a, rows_b), gate_ref, up_ref, turned, hidden, ready)
+    hidden_units(
+        expert_ref, gain_ref, (rows_a, rows_b), gate_ref, up_ref, turned, hidden, ready
+    )
     for chunk in range(chunks):
         copy_of(2, chunk).wait()
     down_product(hidden, down_ref, out_a, 0)
@@ -376,10 +374,17 @@
 
 
 def second_expert_kernel(
-    expert_ref, rows_a, rows_b, gate_ref, up_ref, down_ref, out_ref, hidden, turned
+    expert_ref, gain_ref, rows_a, rows_b, gate_ref, up_ref, down_ref, out_ref, hidden, turned
 ):
     hidden_units(
-        expert_ref, (rows_a, rows_b), gate_ref, up_ref, turned, hidden, lambda chunk: None
+        expert_ref,
+        gain_ref,
+        (rows_a, rows_b),
+        gate_ref,
+        up_ref,
+        turned,
+        hidden,
+        lambda chunk: None,
     )
     down_product(hidden, down_ref, out_ref, 0)
 
@@ -393,7 +398,7 @@
     kept_ref[half:, :] = value_ref[:half, :]
 
 
-def first_expert_rows(expert, halves, weights):
+def first_expert_rows(expert, gain, halves, weights):
     units, model_width = weights[0].shape
     row_count = halves[0].shape[0]
     whole = pl.BlockSpec(memory_space=pltpu.VMEM)
@@ -405,7 +410,7 @@
         compiler_params=pltpu.CompilerParams(vmem_limit_bytes=12 << 20),
         out_shape=(near_shape((row_count, model_width // 2), jnp.float32),) * 2
         + (near_shape((2 * units, model_width), jnp.bfloat16),) * 3,
-        in_specs=[pl.BlockSpec(memory_space=pltpu.SMEM)] + [whole] * 2 + [anywhere] * 6,
+        in_specs=[pl.BlockSpec(memory_space=pltpu.SMEM)] + [whole] * 3 + [anywhere] * 6,
         out_specs=(whole,) * 5,
         scratch_shapes=[
             pltpu.VMEM((model_width + LANES, row_count), jnp.bfloat16),
@@ -417,10 +422,15 @@
             transcendentals=0,
             bytes_accessed=12 * units * model_width,
         ),
-    )(expert, *[near(half) for half in halves], *[far(weight) for weight in weights])
-
-
-def second_expert_rows(expert, halves, weights, totals):
+    )(
+        expert,
+        near(gain),
+        *[near(half) for half in halves],
+        *[far(weight) for weight in weights],
+    )
+
+
+def second_expert_rows(expert, gain, halves, weights, totals):
     units, model_width = weights[0].shape
     row_count = halves[0].shape[0]
     width = model_width // 2
@@ -433,10 +443,15 @@
             near_shape((row_count, width), jnp.bfloat16),
             near_shape((row_count, units), jnp.bfloat16),
         ),
-        in_specs=[pl.BlockSpec(memory_space=pltpu.SMEM)] + [whole] * 5,
+        in_specs=[pl.BlockSpec(memory_space=pltpu.SMEM)] + [whole] * 6,
         out_specs=(whole, whole),
         scratch_shapes=[pltpu.VMEM((model_width + LANES, row_count), jnp.bfloat16)],
-    )(expert, *[near(half) for half in halves], *[near(weight) for weight in weights])
+    )(
+        expert,
+        near(gain),
+        *[near(half) for half in halves],
+        *[near(weight) for weight in weights],
+    )
     sent, kept = pl.pallas_call(
         functools.partial(rest_expert_kernel, width),
         name="expert_rest",
@@ -453,7 +468,7 @@
 
 
 def attention_rows(
-    queries, patch_keys, patch_values, other_keys, other_values, norm_gain, table, row_count, orders
+    queries, patch_keys, patch_values, other_keys, other_values, table, row_count, orders
 ):
     model_width = patch_values.shape[1]
     part_width = model_width // PARTS + LANES
@@ -522,27 +537,28 @@
                 out_specs=(whole, whole),
             )(*operands)
         came = exchange(sent, orders, stages - 1)
-        finished += [near(kept), near(came)]
-    rows = kept.shape[0]
-    *blocks, projected = pl.pallas_call(
-        functools.partial(finish_kernel, HEADS),
-        name="finish",
-        compiler_params=pltpu.CompilerParams(vmem_limit_bytes=6 << 20),
-        out_shape=tuple(
-            near_shape((rows, model_width // PARTS + (LANES if part == 0 else 0)), jnp.bfloat16)
-            for part in range(PARTS)
-        )
-        + (near_shape((row_count, model_width), jnp.bfloat16),),
-        in_specs=[whole] * (2 + 2 * PARTS),
-        out_specs=(whole,) * (PARTS + 1),
-    )(near(norm_gain.reshape(1, model_width)), near(table), *finished)
-    return blocks, projected
+        rows = kept.shape[0]
+        width = model_width // PARTS
+        operands = [near(kept), near(came)] + ([near(table)] if part == 0 else [])
+        block, projected = pl.pallas_call(
+            functools.partial(finish_kernel, part_heads),
+            compiler_params=pltpu.CompilerParams(vmem_limit_bytes=6 << 20),
+            out_shape=(
+                near_shape((rows, width + (LANES if part == 0 else 0)), jnp.bfloat16),
+                near_shape((row_count, width), jnp.bfloat16),
+            ),
+            in_specs=[whole] * len(operands),
+            out_specs=(whole, whole),
+        )(*operands)
+        finished.append((block, projected))
+    return finished
 
 
 def on_device(
     queries, patch_keys, patch_values, norm_gain, route_experts, route_weights, w_gate, w_up, w_down
 ):
     row_count = route_experts.shape[0]
+    model_width = patch_values.shape[1]
     devices = lax.axis_size("wide")
     device_index = lax.axis_index("wide")
     score_table = jnp.sum(
@@ -564,17 +580,18 @@
     weights = []
     for own in halves:
         weights += [own, partner(own, "wide", 0)]
-    blocks, projected = attention_rows(
+    finished = attention_rows(
         queries,
         patch_keys,
         patch_values,
         other_keys,
         other_values,
-        norm_gain,
         score_table,
         row_count,
         merge_order,
     )
+    blocks = [block for block, _ in finished]
+    gain = norm_gain.reshape(1, model_width)
     stages = len(gather_order[0])
     came = []
     for part in range(PARTS):
@@ -583,10 +600,10 @@
             blocks[part] = jnp.concatenate([blocks[part], arrived], axis=0)
         came.append(exchange(blocks[part], gather_order, stages - 1))
     expert = (device_index // 2).reshape(1)
-    *totals, gate, up, down = first_expert_rows(expert, blocks, weights)
+    *totals, gate, up, down = first_expert_rows(expert, gain, blocks, weights)
     outputs = []
     for part, (sent, kept) in enumerate(
-        second_expert_rows(expert, came, (gate, up, down), totals)
+        second_expert_rows(expert, gain, came, (gate, up, down), totals)
     ):
         for stage in range(stages + 1):
             arrived = exchange(sent, scatter_order[part], stage)
@@ -595,9 +612,8 @@
             if stage < stages:
                 sent = kept[half_rows:].astype(jnp.bfloat16)
                 kept = kept[:half_rows]
-        outputs.append(kept)
-    total = jnp.concatenate(outputs, axis=1)
-    return (projected.astype(jnp.float32) + total).astype(jnp.bfloat16)
+        outputs.append((finished[part][1].astype(jnp.float32) + kept).astype(jnp.bfloat16))
+    return jnp.concatenate(outputs, axis=1)
 
 
 def solution(mesh):

time: 80.9 us -> 81.2 us (level)
  waiting for transfers between devices: 29.1 us -> 36.3 us
  starting transfers between devices: 34 us -> 27 us
    ppermute x20, waiting for transfers between devices: 26.8 us -> 33.9 us  [exchange(): return lax.ppermute(value, 'wide', pairs)]
    ppermute x20, starting transfers between devices: 32.6 us -> 25.6 us  [exchange(): return lax.ppermute(value, 'wide', pairs)]
where the time goes in v4:
time: 81.2 us; the launch traced here: 81 us
  waiting for transfers between devices  36.3 us (45%)
  starting transfers between devices  27 us (33%)
  Pallas kernels  16.3 us (20%)
  other arithmetic  1 us (1%)
    ppermute x20, waiting for transfers between devices, exchange(): return lax.ppermute(value, 'wide', pairs)  33.9 us
    ppermute x20, starting transfers between devices, exchange(): return lax.ppermute(value, 'wide', pairs)  25.6 us
    pallas_call x1, Pallas kernels, first_expert_rows(): pl.pallas_call(first_expert_kernel, name='expert_first', compiler_params=...  6.73 us
    pallas_call x1, Pallas kernels, second_expert_rows(): pl.pallas_call(second_expert_kernel, name='expert_second', compiler_param...  3.68 us
    pallas_call x2, Pallas kernels, attention_rows(): pl.pallas_call(functools.partial(attend_kernel, HEADS, part, part_heads),...  2.75 us
    ppermute x5, waiting for transfers between devices, partner(): return lax.ppermute(value, axis, pairs)  2.35 us
  transfers between devices with their start and end apart: 25, of which 18 were waited for; matrix products, arithmetic and copies ran while one was open for 1% of the time, Pallas kernels for 16%

profile of v4, /device:TPU:0, one launch (start us, length us, event | category | flops | bytes accessed | tf_op | source)
XLA Modules:
  0.0 81.0 jit_solution(8202001932211303588)
XLA Ops:
  0.5 2.3 %collective-permute-done.keys_b = bf16[128,1152]{1,0:T(8,128)(2,1)S(1)} collective-permute-done((bf16[128,1152]{1,0:T(8,128)(2,1)}, bf16[128,1152]{1,0:T(8,128)(2,1)S(1)}, u32[]{:S(2)}, u32[]{:S(2)}) %collective-permute-start) | collective-permute-done | bytes 294944 | tf_op jit(solution)/shard_map/ppermute | solution.py:33
  3.7 1.3 %stage_in.1 = (bf16[128,1152]{1,0:T(8,128)(2,1)S(1)}, bf16[128,1152]{1,0:T(8,128)(2,1)S(1)}, bf16[128,2560]{1,0:T(8,128)(2,1)S(1)}) custom-call(s32[1]{0:T(128)} %bitcast.device_ref, bf16[256,1152]{1,0:T(8,128)(2,1)} %queries_ref.1, bf16[128,1152]{1,0:T(8,128)(2,1)} %keys_ref.1, bf16[128,2560]{1,0:T(8,128)(2,1)} %values_ref.1), custom_call_target="tpu_custom_call" | custom-call | tf_op jit(solution)/shard_map/stage_in/pallas_call | solution.py:499
  5.1 1.5 %shard_map.95 = (bf16[64,1408]{1,0:T(8,128)(2,1)S(1)}, f32[64,1408]{1,0:T(8,128)S(1)}) custom-call(bf16[128,1152]{1,0:T(8,128)(2,1)S(1)} %get-tuple-element.38.query_ref, bf16[128,1152]{1,0:T(8,128)(2,1)S(1)} %get-tuple-element.39.keys_a, bf16[128,1152]{1,0:T(8,128)(2,1)S(1)} %collective-permute-done.keys_b, ...), custom_call_target="tpu_custom_call" | custom-call | tf_op jit(solution)/shard_map/pallas_call | solution.py:515
  6.6 2.7 %collective-permute-start.7 = (bf16[64,1408]{1,0:T(8,128)(2,1)S(1)}, bf16[64,1408]{1,0:T(8,128)(2,1)S(1)}, u32[]{:S(2)}, u32[]{:S(2)}) collective-permute-start(bf16[64,1408]{1,0:T(8,128)(2,1)S(1)} %get-tuple-element.52), channel_id=1, source_target_pairs={{0,2},{1,5},{2,0},{3,7},{4,6},{5,1},{6,4},{7,3},{8,10},{9,13},{10,... | collective-permute-start | bytes 540680 | tf_op jit(solution)/shard_map/ppermute | solution.py:52
  9.3 1.2 %shard_map.91 = (bf16[64,1408]{1,0:T(8,128)(2,1)S(1)}, f32[64,1408]{1,0:T(8,128)S(1)}) custom-call(bf16[128,1152]{1,0:T(8,128)(2,1)S(1)} %get-tuple-element.38.query_ref, bf16[128,1152]{1,0:T(8,128)(2,1)S(1)} %get-tuple-element.39.keys_a, bf16[128,1152]{1,0:T(8,128)(2,1)S(1)} %collective-permute-done.keys_b, ...), custom_call_target="tpu_custom_call" | custom-call | tf_op jit(solution)/shard_map/pallas_call | solution.py:515
  10.6 2.2 %collective-permute-done.7.came_ref = bf16[64,1408]{1,0:T(8,128)(2,1)S(1)} collective-permute-done((bf16[64,1408]{1,0:T(8,128)(2,1)S(1)}, bf16[64,1408]{1,0:T(8,128)(2,1)S(1)}, u32[]{:S(2)}, u32[]{:S(2)}) %collective-permute-start.7) | collective-permute-done | bytes 180256 | tf_op jit(solution)/shard_map/ppermute | solution.py:52
  13.0 2.1 %collective-permute-start.8 = (bf16[32,1408]{1,0:T(8,128)(2,1)S(1)}, bf16[32,1408]{1,0:T(8,128)(2,1)S(1)}, u32[]{:S(2)}, u32[]{:S(2)}) collective-permute-start(bf16[32,1408]{1,0:T(8,128)(2,1)S(1)} %get-tuple-element.54), channel_id=1, source_target_pairs={{0,4},{1,9},{2,6},{3,11},{4,0},{5,13},{6,2},{7,15},{8,12},{9,1},{1... | collective-permute-start | bytes 270344 | tf_op jit(solution)/shard_map/ppermute | solution.py:52
  15.1 0.9 %collective-permute-done.2.came_ref = bf16[64,1408]{1,0:T(8,128)(2,1)S(1)} collective-permute-done((bf16[64,1408]{1,0:T(8,128)(2,1)S(1)}, bf16[64,1408]{1,0:T(8,128)(2,1)S(1)}, u32[]{:S(2)}, u32[]{:S(2)}) %collective-permute-start.2) | collective-permute-done | bytes 180256 | tf_op jit(solution)/shard_map/ppermute | solution.py:52
  16.3 1.6 %collective-permute-start.3 = (bf16[32,1408]{1,0:T(8,128)(2,1)S(1)}, bf16[32,1408]{1,0:T(8,128)(2,1)S(1)}, u32[]{:S(2)}, u32[]{:S(2)}) collective-permute-start(bf16[32,1408]{1,0:T(8,128)(2,1)S(1)} %get-tuple-element.46), channel_id=1, source_target_pairs={{0,4},{1,9},{2,6},{3,11},{4,0},{5,13},{6,2},{7,15},{8,12},{9,1},{1... | collective-permute-start | bytes 270344 | tf_op jit(solution)/shard_map/ppermute | solution.py:52
  18.2 1.7 %collective-permute-start.9 = (bf16[32,1408]{1,0:T(8,128)(2,1)S(1)}, bf16[32,1408]{1,0:T(8,128)(2,1)S(1)}, u32[]{:S(2)}, u32[]{:S(2)}) collective-permute-start(bf16[32,1408]{1,0:T(8,128)(2,1)S(1)} %get-tuple-element.56), channel_id=1, source_target_pairs={{0,8},{1,3},{2,10},{3,1},{4,12},{5,7},{6,14},{7,5},{8,0},{9,11},{1... | collective-permute-start | bytes 270344 | tf_op jit(solution)/shard_map/ppermute | solution.py:52
  19.9 1.0 %collective-permute-done.3.came_ref = bf16[32,1408]{1,0:T(8,128)(2,1)S(1)} collective-permute-done((bf16[32,1408]{1,0:T(8,128)(2,1)S(1)}, bf16[32,1408]{1,0:T(8,128)(2,1)S(1)}, u32[]{:S(2)}, u32[]{:S(2)}) %collective-permute-start.3) | collective-permute-done | bytes 90144 | tf_op jit(solution)/shard_map/ppermute | solution.py:52
  21.1 1.6 %collective-permute-start.4 = (bf16[32,1408]{1,0:T(8,128)(2,1)S(1)}, bf16[32,1408]{1,0:T(8,128)(2,1)S(1)}, u32[]{:S(2)}, u32[]{:S(2)}) collective-permute-start(bf16[32,1408]{1,0:T(8,128)(2,1)S(1)} %get-tuple-element.48), channel_id=1, source_target_pairs={{0,8},{1,3},{2,10},{3,1},{4,12},{5,7},{6,14},{7,5},{8,0},{9,11},{1... | collective-permute-start | bytes 270344 | tf_op jit(solution)/shard_map/ppermute | solution.py:52
  23.0 2.8 %collective-permute-start.10 = (bf16[32,1280]{1,0:T(8,128)(2,1)S(1)}, bf16[32,1280]{1,0:T(8,128)(2,1)S(1)}, u32[]{:S(2)}, u32[]{:S(2)}) collective-permute-start(bf16[32,1280]{1,0:T(8,128)(2,1)S(1)} %get-tuple-element.57), channel_id=1, source_target_pairs={{0,16},{1,17},{2,18},{3,19},{4,20},{5,21},{6,22},{7,23},{8,24},{9,... | collective-permute-start | bytes 245768 | tf_op jit(solution)/shard_map/ppermute | solution.py:52
  26.8 1.8 %collective-permute-start.5 = (bf16[32,1408]{1,0:T(8,128)(2,1)S(1)}, bf16[32,1408]{1,0:T(8,128)(2,1)S(1)}, u32[]{:S(2)}, u32[]{:S(2)}) collective-permute-start(bf16[32,1408]{1,0:T(8,128)(2,1)S(1)} %get-tuple-element.50), channel_id=1, source_target_pairs={{0,16},{1,17},{2,18},{3,19},{4,20},{5,21},{6,22},{7,23},{8,24},{9,... | collective-permute-start | bytes 270344 | tf_op jit(solution)/shard_map/ppermute | solution.py:52
  28.6 2.5 %collective-permute-done.10 = bf16[32,1280]{1,0:T(8,128)(2,1)S(1)} collective-permute-done((bf16[32,1280]{1,0:T(8,128)(2,1)S(1)}, bf16[32,1280]{1,0:T(8,128)(2,1)S(1)}, u32[]{:S(2)}, u32[]{:S(2)}) %collective-permute-start.10) | collective-permute-done | bytes 81952 | tf_op jit(solution)/shard_map/ppermute | solution.py:52
  31.1 1.0 %collective-permute-start.11 = (bf16[64,1280]{1,0:T(8,128)(2,1)S(1)}, bf16[64,1280]{1,0:T(8,128)(2,1)S(1)}, u32[]{:S(2)}, u32[]{:S(2)}) collective-permute-start(bf16[64,1280]{1,0:T(8,128)(2,1)S(1)} %pad_maximum_fusion.1), channel_id=1, source_target_pairs={{0,4},{1,5},{2,6},{3,7},{4,0},{5,1},{6,2},{7,3},{8,12},{9,13},{10,... | collective-permute-start | bytes 491528 | tf_op jit(solution)/shard_map/ppermute | solution.py:52
  32.3 1.1 %collective-permute-start.6 = (bf16[64,1408]{1,0:T(8,128)(2,1)S(1)}, bf16[64,1408]{1,0:T(8,128)(2,1)S(1)}, u32[]{:S(2)}, u32[]{:S(2)}) collective-permute-start(bf16[64,1408]{1,0:T(8,128)(2,1)S(1)} %pad_maximum_fusion), channel_id=1, source_target_pairs={{0,4},{1,5},{2,6},{3,7},{4,0},{5,1},{6,2},{7,3},{8,12},{9,13},{10,... | collective-permute-start | bytes 540680 | tf_op jit(solution)/shard_map/ppermute | solution.py:52
  33.4 6.0 %collective-permute-done.6 = bf16[64,1408]{1,0:T(8,128)(2,1)S(1)} collective-permute-done((bf16[64,1408]{1,0:T(8,128)(2,1)S(1)}, bf16[64,1408]{1,0:T(8,128)(2,1)S(1)}, u32[]{:S(2)}, u32[]{:S(2)}) %collective-permute-start.6) | collective-permute-done | bytes 180256 | tf_op jit(solution)/shard_map/ppermute | solution.py:52
  40.3 1.3 %collective-permute-start.16 = (bf16[128,1280]{1,0:T(8,128)(2,1)S(1)}, bf16[128,1280]{1,0:T(8,128)(2,1)S(1)}, u32[]{:S(2)}, u32[]{:S(2)}) collective-permute-start(bf16[128,1280]{1,0:T(8,128)(2,1)S(1)} %constant_dynamic-update-slice_fusion.3.rows_b), channel_id=1, source_target_pairs={{0,2},{1,9},{2,0},{3,11},{4,6},{5,13},{6,4},{7,15},{8,10},{9,1},{1... | collective-permute-start | bytes 983048 | tf_op jit(solution)/shard_map/ppermute | solution.py:52
  41.7 6.7 %expert_first.1 = (f32[128,1280]{1,0:T(8,128)S(1)}, f32[128,1280]{1,0:T(8,128)S(1)}, bf16[1024,2560]{1,0:T(8,128)(2,1)S(1)}, bf16[1024,2560]{1,0:T(8,128)(2,1)S(1)}, bf16[1024,2560]{1,0:T(8,128)(2,1)S(1)}) custom-call(s32[1]{0:T(128)} %bitcast.1.expert_ref, f32[1,2560]{1,0:T(1,128)S(1)} %reshape.17.gain_ref, ...), custom_call_target="tpu_custom_call" | custom-call | flops 2013265920 | bytes 15728640 | tf_op jit(solution)/shard_map/expert_first/pallas_call | solution.py:407
  48.4 2.0 %collective-permute-done.16.rows_b = bf16[128,1280]{1,0:T(8,128)(2,1)S(1)} collective-permute-done((bf16[128,1280]{1,0:T(8,128)(2,1)S(1)}, bf16[128,1280]{1,0:T(8,128)(2,1)S(1)}, u32[]{:S(2)}, u32[]{:S(2)}) %collective-permute-start.16) | collective-permute-done | bytes 327712 | tf_op jit(solution)/shard_map/ppermute | solution.py:52
  50.5 3.7 %expert_second.1 = (bf16[128,1280]{1,0:T(8,128)(2,1)S(1)}, bf16[128,1024]{1,0:T(8,128)(2,1)S(1)}) custom-call(s32[1]{0:T(128)} %bitcast.1.expert_ref, f32[1,2560]{1,0:T(1,128)S(1)} %reshape.17.gain_ref, bf16[128,1408]{1,0:T(8,128)(2,1)S(1)} %collective-permute-done.15.rows_a, bf16[128,1280]{1,0:T(8,128)(2,1)S(1)} %collective-permute-done.16.rows_b, ...), custom_call_target="tpu_custom_call" | custom-call | tf_op jit(solution)/shard_map/expert_second/pallas_call | solution.py:438
  56.1 5.2 %collective-permute-done.17 = bf16[128,1280]{1,0:T(8,128)(2,1)S(1)} collective-permute-done((bf16[128,1280]{1,0:T(8,128)(2,1)S(1)}, bf16[128,1280]{1,0:T(8,128)(2,1)S(1)}, u32[]{:S(2)}, u32[]{:S(2)}) %collective-permute-start.17) | collective-permute-done | bytes 327712 | tf_op jit(solution)/shard_map/ppermute | solution.py:52
  61.7 2.7 %collective-permute-done.21 = bf16[128,1280]{1,0:T(8,128)(2,1)S(1)} collective-permute-done((bf16[128,1280]{1,0:T(8,128)(2,1)S(1)}, bf16[128,1280]{1,0:T(8,128)(2,1)S(1)}, u32[]{:S(2)}, u32[]{:S(2)}) %collective-permute-start.21) | collective-permute-done | bytes 327712 | tf_op jit(solution)/shard_map/ppermute | solution.py:52
  64.6 1.3 %collective-permute-start.22 = (bf16[64,1280]{1,0:T(8,128)(2,1)S(1)}, bf16[64,1280]{1,0:T(8,128)(2,1)S(1)}, u32[]{:S(2)}, u32[]{:S(2)}) collective-permute-start(bf16[64,1280]{1,0:T(8,128)(2,1)S(1)} %slice.86), channel_id=1, source_target_pairs={{0,2},{1,9},{2,0},{3,11},{4,6},{5,13},{6,4},{7,15},{8,10},{9,1},{1... | collective-permute-start | bytes 491528 | tf_op jit(solution)/shard_map/ppermute | solution.py:52
  65.9 0.9 %collective-permute-done.18 = bf16[64,1280]{1,0:T(8,128)(2,1)S(1)} collective-permute-done((bf16[64,1280]{1,0:T(8,128)(2,1)S(1)}, bf16[64,1280]{1,0:T(8,128)(2,1)S(1)}, u32[]{:S(2)}, u32[]{:S(2)}) %collective-permute-start.18) | collective-permute-done | bytes 163872 | tf_op jit(solution)/shard_map/ppermute | solution.py:52
  66.8 1.2 %collective-permute-start.19 = (bf16[32,1280]{1,0:T(8,128)(2,1)S(1)}, bf16[32,1280]{1,0:T(8,128)(2,1)S(1)}, u32[]{:S(2)}, u32[]{:S(2)}) collective-permute-start(bf16[32,1280]{1,0:T(8,128)(2,1)S(1)} %slice.89), channel_id=1, source_target_pairs={{0,16},{1,17},{2,18},{3,19},{4,20},{5,21},{6,22},{7,23},{8,24},{9,... | collective-permute-start | bytes 245768 | tf_op jit(solution)/shard_map/ppermute | solution.py:52
  68.0 2.0 %collective-permute-done.22 = bf16[64,1280]{1,0:T(8,128)(2,1)S(1)} collective-permute-done((bf16[64,1280]{1,0:T(8,128)(2,1)S(1)}, bf16[64,1280]{1,0:T(8,128)(2,1)S(1)}, u32[]{:S(2)}, u32[]{:S(2)}) %collective-permute-start.22) | collective-permute-done | bytes 163872 | tf_op jit(solution)/shard_map/ppermute | solution.py:52
  70.0 1.7 %collective-permute-start.23 = (bf16[32,1280]{1,0:T(8,128)(2,1)S(1)}, bf16[32,1280]{1,0:T(8,128)(2,1)S(1)}, u32[]{:S(2)}, u32[]{:S(2)}) collective-permute-start(bf16[32,1280]{1,0:T(8,128)(2,1)S(1)} %slice.88), channel_id=1, source_target_pairs={{0,16},{1,17},{2,18},{3,19},{4,20},{5,21},{6,22},{7,23},{8,24},{9,... | collective-permute-start | bytes 245768 | tf_op jit(solution)/shard_map/ppermute | solution.py:52
  71.7 1.4 %collective-permute-done.19 = bf16[32,1280]{1,0:T(8,128)(2,1)S(1)} collective-permute-done((bf16[32,1280]{1,0:T(8,128)(2,1)S(1)}, bf16[32,1280]{1,0:T(8,128)(2,1)S(1)}, u32[]{:S(2)}, u32[]{:S(2)}) %collective-permute-start.19) | collective-permute-done | bytes 81952 | tf_op jit(solution)/shard_map/ppermute | solution.py:52
  74.0 2.3 %collective-permute-done.23 = bf16[32,1280]{1,0:T(8,128)(2,1)S(1)} collective-permute-done((bf16[32,1280]{1,0:T(8,128)(2,1)S(1)}, bf16[32,1280]{1,0:T(8,128)(2,1)S(1)}, u32[]{:S(2)}, u32[]{:S(2)}) %collective-permute-start.23) | collective-permute-done | bytes 81952 | tf_op jit(solution)/shard_map/ppermute | solution.py:52
  77.2 3.2 %collective-permute-done.24 = bf16[16,1280]{1,0:T(8,128)(2,1)S(1)} collective-permute-done((bf16[16,1280]{1,0:T(8,128)(2,1)S(1)}, bf16[16,1280]{1,0:T(8,128)(2,1)S(1)}, u32[]{:S(2)}, u32[]{:S(2)}) %collective-permute-start.24) | collective-permute-done | bytes 40992 | tf_op jit(solution)/shard_map/ppermute | solution.py:52
  (63 shorter events, 9.9 us)
Async XLA Ops:
  0.0 2.9 %collective-permute-start.1 = (bf16[128,2560]{1,0:T(8,128)(2,1)}, bf16[128,2560]{1,0:T(8,128)(2,1)S(1)}, u32[]{:S(2)}, u32[]{:S(2)}) collective-permute-start(bf16[128,2560]{1,0:T(8,128)(2,1)} %values_ref.1), channel_id=1, source_target_pairs={{0,1},{1,0},{2,3},{3,2},{4,5},{5,4},{6,7},{7,6},{8,9},{9,8},{10,11... | collective-permute-start | bytes 1966088 | tf_op jit(solution)/shard_map/ppermute | solution.py:33
  0.5 2.4 %collective-permute-start = (bf16[128,1152]{1,0:T(8,128)(2,1)}, bf16[128,1152]{1,0:T(8,128)(2,1)S(1)}, u32[]{:S(2)}, u32[]{:S(2)}) collective-permute-start(bf16[128,1152]{1,0:T(8,128)(2,1)} %keys_ref.1), channel_id=1, source_target_pairs={{0,1},{1,0},{2,3},{3,2},{4,5},{5,4},{6,7},{7,6},{8,9},{9,8},{10,11... | collective-permute-start | bytes 884744 | tf_op jit(solution)/shard_map/ppermute | solution.py:33
  2.9 38.8 %collective-permute-start.12 = (bf16[512,2560]{1,0:T(8,128)(2,1)}, bf16[512,2560]{1,0:T(8,128)(2,1)}, u32[]{:S(2)}, u32[]{:S(2)}) collective-permute-start(bf16[512,2560]{1,0:T(8,128)(2,1)} %gate_a), channel_id=1, source_target_pairs={{0,1},{1,0},{2,3},{3,2},{4,5},{5,4},{6,7},{7,6},{8,9},{9,8},{10,11... | collective-permute-start | bytes 7864328 | tf_op jit(solution)/shard_map/ppermute | solution.py:33
  3.2 38.4 %collective-permute-start.13 = (bf16[512,2560]{1,0:T(8,128)(2,1)}, bf16[512,2560]{1,0:T(8,128)(2,1)}, u32[]{:S(2)}, u32[]{:S(2)}) collective-permute-start(bf16[512,2560]{1,0:T(8,128)(2,1)} %up_a), channel_id=1, source_target_pairs={{0,1},{1,0},{2,3},{3,2},{4,5},{5,4},{6,7},{7,6},{8,9},{9,8},{10,11... | collective-permute-start | bytes 7864328 | tf_op jit(solution)/shard_map/ppermute | solution.py:33
  3.4 38.3 %collective-permute-start.14 = (bf16[512,2560]{1,0:T(8,128)(2,1)}, bf16[512,2560]{1,0:T(8,128)(2,1)}, u32[]{:S(2)}, u32[]{:S(2)}) collective-permute-start(bf16[512,2560]{1,0:T(8,128)(2,1)} %down_a), channel_id=1, source_target_pairs={{0,1},{1,0},{2,3},{3,2},{4,5},{5,4},{6,7},{7,6},{8,9},{9,8},{10,11... | collective-permute-start | bytes 7864328 | tf_op jit(solution)/shard_map/ppermute | solution.py:33
  5.0 12.9 %copy-start.1 = (s32[16,6]{0,1:T(8,128)S(1)}, s32[16,6]{0,1:T(8,128)}, u32[]{:S(2)}) copy-start(s32[16,6]{0,1:T(8,128)} %param.14) | copy-start | bytes 1156
  5.0 12.9 %copy-start.2 = (s32[16,6]{0,1:T(8,128)S(1)}, s32[16,6]{0,1:T(8,128)}, u32[]{:S(2)}) copy-start(s32[16,6]{0,1:T(8,128)} %param.13) | copy-start | bytes 1156
  6.6 6.1 %collective-permute-start.7 = (bf16[64,1408]{1,0:T(8,128)(2,1)S(1)}, bf16[64,1408]{1,0:T(8,128)(2,1)S(1)}, u32[]{:S(2)}, u32[]{:S(2)}) collective-permute-start(bf16[64,1408]{1,0:T(8,128)(2,1)S(1)} %get-tuple-element.52), channel_id=1, source_target_pairs={{0,2},{1,5},{2,0},{3,7},{4,6},{5,1},{6,4},{7,3},{8,10},{9,13},{10,... | collective-permute-start | bytes 540680 | tf_op jit(solution)/shard_map/ppermute | solution.py:52
  10.5 31.1 %copy-start = (f32[2560]{0:T(1024)S(1)}, f32[2560]{0:T(1024)}, u32[]{:S(2)}) copy-start(f32[2560]{0:T(1024)} %param.12) | copy-start | bytes 30724
  10.5 5.6 %collective-permute-start.2 = (bf16[64,1408]{1,0:T(8,128)(2,1)S(1)}, bf16[64,1408]{1,0:T(8,128)(2,1)S(1)}, u32[]{:S(2)}, u32[]{:S(2)}) collective-permute-start(bf16[64,1408]{1,0:T(8,128)(2,1)S(1)} %get-tuple-element.44), channel_id=1, source_target_pairs={{0,2},{1,5},{2,0},{3,7},{4,6},{5,1},{6,4},{7,3},{8,10},{9,13},{10,... | collective-permute-start | bytes 540680 | tf_op jit(solution)/shard_map/ppermute | solution.py:52
  13.0 5.0 %collective-permute-start.8 = (bf16[32,1408]{1,0:T(8,128)(2,1)S(1)}, bf16[32,1408]{1,0:T(8,128)(2,1)S(1)}, u32[]{:S(2)}, u32[]{:S(2)}) collective-permute-start(bf16[32,1408]{1,0:T(8,128)(2,1)S(1)} %get-tuple-element.54), channel_id=1, source_target_pairs={{0,4},{1,9},{2,6},{3,11},{4,0},{5,13},{6,2},{7,15},{8,12},{9,1},{1... | collective-permute-start | bytes 270344 | tf_op jit(solution)/shard_map/ppermute | solution.py:52
  16.3 4.6 %collective-permute-start.3 = (bf16[32,1408]{1,0:T(8,128)(2,1)S(1)}, bf16[32,1408]{1,0:T(8,128)(2,1)S(1)}, u32[]{:S(2)}, u32[]{:S(2)}) collective-permute-start(bf16[32,1408]{1,0:T(8,128)(2,1)S(1)} %get-tuple-element.46), channel_id=1, source_target_pairs={{0,4},{1,9},{2,6},{3,11},{4,0},{5,13},{6,2},{7,15},{8,12},{9,1},{1... | collective-permute-start | bytes 270344 | tf_op jit(solution)/shard_map/ppermute | solution.py:52
  18.2 4.6 %collective-permute-start.9 = (bf16[32,1408]{1,0:T(8,128)(2,1)S(1)}, bf16[32,1408]{1,0:T(8,128)(2,1)S(1)}, u32[]{:S(2)}, u32[]{:S(2)}) collective-permute-start(bf16[32,1408]{1,0:T(8,128)(2,1)S(1)} %get-tuple-element.56), channel_id=1, source_target_pairs={{0,8},{1,3},{2,10},{3,1},{4,12},{5,7},{6,14},{7,5},{8,0},{9,11},{1... | collective-permute-start | bytes 270344 | tf_op jit(solution)/shard_map/ppermute | solution.py:52
  21.1 5.5 %collective-permute-start.4 = (bf16[32,1408]{1,0:T(8,128)(2,1)S(1)}, bf16[32,1408]{1,0:T(8,128)(2,1)S(1)}, u32[]{:S(2)}, u32[]{:S(2)}) collective-permute-start(bf16[32,1408]{1,0:T(8,128)(2,1)S(1)} %get-tuple-element.48), channel_id=1, source_target_pairs={{0,8},{1,3},{2,10},{3,1},{4,12},{5,7},{6,14},{7,5},{8,0},{9,11},{1... | collective-permute-start | bytes 270344 | tf_op jit(solution)/shard_map/ppermute | solution.py:52
  23.0 8.1 %collective-permute-start.10 = (bf16[32,1280]{1,0:T(8,128)(2,1)S(1)}, bf16[32,1280]{1,0:T(8,128)(2,1)S(1)}, u32[]{:S(2)}, u32[]{:S(2)}) collective-permute-start(bf16[32,1280]{1,0:T(8,128)(2,1)S(1)} %get-tuple-element.57), channel_id=1, source_target_pairs={{0,16},{1,17},{2,18},{3,19},{4,20},{5,21},{6,22},{7,23},{8,24},{9,... | collective-permute-start | bytes 245768 | tf_op jit(solution)/shard_map/ppermute | solution.py:52
  26.8 5.5 %collective-permute-start.5 = (bf16[32,1408]{1,0:T(8,128)(2,1)S(1)}, bf16[32,1408]{1,0:T(8,128)(2,1)S(1)}, u32[]{:S(2)}, u32[]{:S(2)}) collective-permute-start(bf16[32,1408]{1,0:T(8,128)(2,1)S(1)} %get-tuple-element.50), channel_id=1, source_target_pairs={{0,16},{1,17},{2,18},{3,19},{4,20},{5,21},{6,22},{7,23},{8,24},{9,... | collective-permute-start | bytes 270344 | tf_op jit(solution)/shard_map/ppermute | solution.py:52
  31.1 9.2 %collective-permute-start.11 = (bf16[64,1280]{1,0:T(8,128)(2,1)S(1)}, bf16[64,1280]{1,0:T(8,128)(2,1)S(1)}, u32[]{:S(2)}, u32[]{:S(2)}) collective-permute-start(bf16[64,1280]{1,0:T(8,128)(2,1)S(1)} %pad_maximum_fusion.1), channel_id=1, source_target_pairs={{0,4},{1,5},{2,6},{3,7},{4,0},{5,1},{6,2},{7,3},{8,12},{9,13},{10,... | collective-permute-start | bytes 491528 | tf_op jit(solution)/shard_map/ppermute | solution.py:52
  32.3 7.1 %collective-permute-start.6 = (bf16[64,1408]{1,0:T(8,128)(2,1)S(1)}, bf16[64,1408]{1,0:T(8,128)(2,1)S(1)}, u32[]{:S(2)}, u32[]{:S(2)}) collective-permute-start(bf16[64,1408]{1,0:T(8,128)(2,1)S(1)} %pad_maximum_fusion), channel_id=1, source_target_pairs={{0,4},{1,5},{2,6},{3,7},{4,0},{5,1},{6,2},{7,3},{8,12},{9,13},{10,... | collective-permute-start | bytes 540680 | tf_op jit(solution)/shard_map/ppermute | solution.py:52
  39.5 11.0 %collective-permute-start.15 = (bf16[128,1408]{1,0:T(8,128)(2,1)S(1)}, bf16[128,1408]{1,0:T(8,128)(2,1)S(1)}, u32[]{:S(2)}, u32[]{:S(2)}) collective-permute-start(bf16[128,1408]{1,0:T(8,128)(2,1)S(1)} %constant_dynamic-update-slice_fusion.rows_a), channel_id=1, source_target_pairs={{0,2},{1,9},{2,0},{3,11},{4,6},{5,13},{6,4},{7,15},{8,10},{9,1},{1... | collective-permute-start | bytes 1081352 | tf_op jit(solution)/shard_map/ppermute | solution.py:52
  40.3 10.1 %collective-permute-start.16 = (bf16[128,1280]{1,0:T(8,128)(2,1)S(1)}, bf16[128,1280]{1,0:T(8,128)(2,1)S(1)}, u32[]{:S(2)}, u32[]{:S(2)}) collective-permute-start(bf16[128,1280]{1,0:T(8,128)(2,1)S(1)} %constant_dynamic-update-slice_fusion.3.rows_b), channel_id=1, source_target_pairs={{0,2},{1,9},{2,0},{3,11},{4,6},{5,13},{6,4},{7,15},{8,10},{9,1},{1... | collective-permute-start | bytes 983048 | tf_op jit(solution)/shard_map/ppermute | solution.py:52
  54.1 7.1 %collective-permute-start.17 = (bf16[128,1280]{1,0:T(8,128)(2,1)S(1)}, bf16[128,1280]{1,0:T(8,128)(2,1)S(1)}, u32[]{:S(2)}, u32[]{:S(2)}) collective-permute-start(bf16[128,1280]{1,0:T(8,128)(2,1)S(1)} %get-tuple-element.65), channel_id=1, source_target_pairs={{0,2},{1,9},{2,0},{3,11},{4,6},{5,13},{6,4},{7,15},{8,10},{9,1},{1... | collective-permute-start | bytes 983048 | tf_op jit(solution)/shard_map/ppermute | solution.py:52
  55.6 8.9 %collective-permute-start.21 = (bf16[128,1280]{1,0:T(8,128)(2,1)S(1)}, bf16[128,1280]{1,0:T(8,128)(2,1)S(1)}, u32[]{:S(2)}, u32[]{:S(2)}) collective-permute-start(bf16[128,1280]{1,0:T(8,128)(2,1)S(1)} %get-tuple-element.70), channel_id=1, source_target_pairs={{0,4},{1,5},{2,6},{3,7},{4,0},{5,1},{6,2},{7,3},{8,12},{9,13},{10,... | collective-permute-start | bytes 983048 | tf_op jit(solution)/shard_map/ppermute | solution.py:52
  61.4 5.4 %collective-permute-start.18 = (bf16[64,1280]{1,0:T(8,128)(2,1)S(1)}, bf16[64,1280]{1,0:T(8,128)(2,1)S(1)}, u32[]{:S(2)}, u32[]{:S(2)}) collective-permute-start(bf16[64,1280]{1,0:T(8,128)(2,1)S(1)} %slice.87), channel_id=1, source_target_pairs={{0,4},{1,5},{2,6},{3,7},{4,0},{5,1},{6,2},{7,3},{8,12},{9,13},{10,... | collective-permute-start | bytes 491528 | tf_op jit(solution)/shard_map/ppermute | solution.py:52
  64.6 5.4 %collective-permute-start.22 = (bf16[64,1280]{1,0:T(8,128)(2,1)S(1)}, bf16[64,1280]{1,0:T(8,128)(2,1)S(1)}, u32[]{:S(2)}, u32[]{:S(2)}) collective-permute-start(bf16[64,1280]{1,0:T(8,128)(2,1)S(1)} %slice.86), channel_id=1, source_target_pairs={{0,2},{1,9},{2,0},{3,11},{4,6},{5,13},{6,4},{7,15},{8,10},{9,1},{1... | collective-permute-start | bytes 491528 | tf_op jit(solution)/shard_map/ppermute | solution.py:52
  66.8 6.3 %collective-permute-start.19 = (bf16[32,1280]{1,0:T(8,128)(2,1)S(1)}, bf16[32,1280]{1,0:T(8,128)(2,1)S(1)}, u32[]{:S(2)}, u32[]{:S(2)}) collective-permute-start(bf16[32,1280]{1,0:T(8,128)(2,1)S(1)} %slice.89), channel_id=1, source_target_pairs={{0,16},{1,17},{2,18},{3,19},{4,20},{5,21},{6,22},{7,23},{8,24},{9,... | collective-permute-start | bytes 245768 | tf_op jit(solution)/shard_map/ppermute | solution.py:52
  70.0 6.3 %collective-permute-start.23 = (bf16[32,1280]{1,0:T(8,128)(2,1)S(1)}, bf16[32,1280]{1,0:T(8,128)(2,1)S(1)}, u32[]{:S(2)}, u32[]{:S(2)}) collective-permute-start(bf16[32,1280]{1,0:T(8,128)(2,1)S(1)} %slice.88), channel_id=1, source_target_pairs={{0,16},{1,17},{2,18},{3,19},{4,20},{5,21},{6,22},{7,23},{8,24},{9,... | collective-permute-start | bytes 245768 | tf_op jit(solution)/shard_map/ppermute | solution.py:52
  73.1 4.1 %collective-permute-start.20 = (bf16[16,1280]{1,0:T(8,128)(2,1)S(1)}, bf16[16,1280]{1,0:T(8,128)(2,1)S(1)}, u32[]{:S(2)}, u32[]{:S(2)}) collective-permute-start(bf16[16,1280]{1,0:T(8,128)(2,1)S(1)} %slice.91), channel_id=1, source_target_pairs={{0,8},{1,3},{2,10},{3,1},{4,12},{5,7},{6,14},{7,5},{8,0},{9,11},{1... | collective-permute-start | bytes 122888 | tf_op jit(solution)/shard_map/ppermute | solution.py:52
  76.3 4.1 %collective-permute-start.24 = (bf16[16,1280]{1,0:T(8,128)(2,1)S(1)}, bf16[16,1280]{1,0:T(8,128)(2,1)S(1)}, u32[]{:S(2)}, u32[]{:S(2)}) collective-permute-start(bf16[16,1280]{1,0:T(8,128)(2,1)S(1)} %slice.90), channel_id=1, source_target_pairs={{0,8},{1,3},{2,10},{3,1},{4,12},{5,7},{6,14},{7,5},{8,0},{9,11},{1... | collective-permute-start | bytes 122888 | tf_op jit(solution)/shard_map/ppermute | solution.py:52

commit v5 on v4

--- a/solution.py
+++ b/solution.py
@@ -373,19 +373,62 @@
     down_product(hidden, down_ref, out_b, out_a.shape[1])
 
 
+def turned_half(rows_ref, gain_ref, start, width, turned):
+    square = jnp.zeros((rows_ref.shape[0], LANES), jnp.float32)
+    for low in range(0, width, LANES):
+        residual = rows_ref[:, low : low + LANES].astype(jnp.float32)
+        square = square + residual * residual
+        gained = residual * gain_ref[:, start + low : start + low + LANES]
+        turned[low : low + LANES, :] = gained.astype(jnp.bfloat16).T
+    return jnp.sum(square.T, axis=0, keepdims=True)
+
+
+def half_expert_kernel(
+    expert_ref, gain_ref, rows_ref, gate_ref, up_ref, gates_ref, ups_ref, stats_ref, turned
+):
+    width = turned.shape[0]
+    stats_ref[0:1, :] = turned_half(rows_ref, gain_ref, 0, width, turned)
+    scores = rows_ref[:, width:].astype(jnp.float32).T
+    lane = lax.broadcasted_iota(jnp.int32, scores.shape, 0)
+    chosen = jnp.where(lane == expert_ref[0] + TABLE_LANE, scores, 0.0)
+    stats_ref[1:2, :] = jnp.sum(chosen, axis=0, keepdims=True) / jnp.sum(
+        scores, axis=0, keepdims=True
+    )
+    rows = turned[...]
+    gates_ref[...] = jnp.dot(gate_ref[:, :width], rows, preferred_element_type=jnp.float32)
+    ups_ref[...] = jnp.dot(up_ref[:, :width], rows, preferred_element_type=jnp.float32)
+
+
 def second_expert_kernel(
-    expert_ref, gain_ref, rows_a, rows_b, gate_ref, up_ref, down_ref, out_ref, hidden, turned
+    gain_ref,
+    rows_ref,
+    gates_ref,
+    ups_ref,
+    stats_ref,
+    gate_ref,
+    up_ref,
+    down_ref,
+    out_ref,
+    hidden,
+    turned,
 ):
-    hidden_units(
-        expert_ref,
-        gain_ref,
-        (rows_a, rows_b),
-        gate_ref,
-        up_ref,
-        turned,
-        hidden,
-        lambda chunk: None,
-    )
+    width = turned.shape[0]
+    square = stats_ref[0:1, :] + turned_half(rows_ref, gain_ref, width, width, turned)
+    inverse = lax.rsqrt(square / (2 * width) + 1e-06)
+    share = stats_ref[1:2, :]
+    rows = turned[...]
+    for low in range(0, gate_ref.shape[0], UNITS):
+        units = slice(low, low + UNITS)
+        gate_part = inverse * (
+            gates_ref[units, :]
+            + jnp.dot(gate_ref[units, width:], rows, preferred_element_type=jnp.float32)
+        )
+        up_part = inverse * (
+            ups_ref[units, :]
+            + jnp.dot(up_ref[units, width:], rows, preferred_element_type=jnp.float32)
+        )
+        silu = gate_part / (1.0 + jnp.exp(-gate_part))
+        hidden[:, units] = (silu * up_part * share).T.astype(jnp.bfloat16)
     down_product(hidden, down_ref, out_ref, 0)
 
 
@@ -435,6 +478,17 @@
     row_count = halves[0].shape[0]
     width = model_width // 2
     whole = pl.BlockSpec(memory_space=pltpu.VMEM)
+    gate, up, down = weights
+    gates, ups, stats = pl.pallas_call(
+        half_expert_kernel,
+        name="expert_half",
+        compiler_params=pltpu.CompilerParams(vmem_limit_bytes=12 << 20),
+        out_shape=(near_shape((units, row_count), jnp.float32),) * 2
+        + (near_shape((8, row_count), jnp.float32),),
+        in_specs=[pl.BlockSpec(memory_space=pltpu.SMEM)] + [whole] * 4,
+        out_specs=(whole,) * 3,
+        scratch_shapes=[pltpu.VMEM((width, row_count), jnp.bfloat16)],
+    )(expert, near(gain), near(halves[0]), near(gate), near(up))
     first, hidden = pl.pallas_call(
         second_expert_kernel,
         name="expert_second",
@@ -443,15 +497,10 @@
             near_shape((row_count, width), jnp.bfloat16),
             near_shape((row_count, units), jnp.bfloat16),
         ),
-        in_specs=[pl.BlockSpec(memory_space=pltpu.SMEM)] + [whole] * 6,
+        in_specs=[whole] * 8,
         out_specs=(whole, whole),
-        scratch_shapes=[pltpu.VMEM((model_width + LANES, row_count), jnp.bfloat16)],
-    )(
-        expert,
-        near(gain),
-        *[near(half) for half in halves],
-        *[near(weight) for weight in weights],
-    )
+        scratch_shapes=[pltpu.VMEM((width, row_count), jnp.bfloat16)],
+    )(near(gain), near(halves[1]), near(gates), near(ups), near(stats), near(gate), near(up), near(down))
     sent, kept = pl.pallas_call(
         functools.partial(rest_expert_kernel, width),
         name="expert_rest",

time: 81.2 us -> 81.3 us (level)
  waiting for transfers between devices: 36.3 us -> 37.2 us
    pallas_call x0 -> x1, Pallas kernels: none -> 1.6 us  [second_expert_rows(): pl.pallas_call(half_expert_kernel, name='expert_half', compiler_params=pl...]
    pallas_call x1, Pallas kernels: 3.68 us -> 2.1 us  [second_expert_rows(): pl.pallas_call(second_expert_kernel, name='expert_second', compiler_param...]
    ppermute x20, waiting for transfers between devices: 33.9 us -> 34.8 us  [exchange(): return lax.ppermute(value, 'wide', pairs)]
  transfers between devices with their start and end apart: 25 -> 25, of which waited for: 18 -> 17; matrix products, arithmetic and copies ran while one was open for 1% -> 1% of each run, Pallas kernels for 16% -> 18%
where the time goes in v5:
time: 81.3 us; the launch traced here: 81.2 us
  waiting for transfers between devices  37.2 us (46%)
  starting transfers between devices  26.2 us (32%)
  Pallas kernels  16.3 us (20%)
  other arithmetic  1.01 us (1%)
    ppermute x20, waiting for transfers between devices, exchange(): return lax.ppermute(value, 'wide', pairs)  34.8 us
    ppermute x20, starting transfers between devices, exchange(): return lax.ppermute(value, 'wide', pairs)  24.8 us
    pallas_call x1, Pallas kernels, first_expert_rows(): pl.pallas_call(first_expert_kernel, name='expert_first', compiler_params=...  6.74 us
    pallas_call x2, Pallas kernels, attention_rows(): pl.pallas_call(functools.partial(attend_kernel, HEADS, part, part_heads),...  2.75 us
    ppermute x5, waiting for transfers between devices, partner(): return lax.ppermute(value, axis, pairs)  2.35 us
    pallas_call x1, Pallas kernels, second_expert_rows(): pl.pallas_call(second_expert_kernel, name='expert_second', compiler_param...  2.1 us
  transfers between devices with their start and end apart: 25, of which 17 were waited for; matrix products, arithmetic and copies ran while one was open for 1% of the time, Pallas kernels for 18%

profile of v5, /device:TPU:0, one launch (start us, length us, event | category | flops | bytes accessed | tf_op | source)
XLA Modules:
  0.0 81.2 jit_solution(15424873023259778976)
XLA Ops:
  0.5 2.3 %collective-permute-done.keys_b = bf16[128,1152]{1,0:T(8,128)(2,1)S(1)} collective-permute-done((bf16[128,1152]{1,0:T(8,128)(2,1)}, bf16[128,1152]{1,0:T(8,128)(2,1)S(1)}, u32[]{:S(2)}, u32[]{:S(2)}) %collective-permute-start) | collective-permute-done | bytes 294944 | tf_op jit(solution)/shard_map/ppermute | solution.py:33
  3.7 1.3 %stage_in.1 = (bf16[128,1152]{1,0:T(8,128)(2,1)S(1)}, bf16[128,1152]{1,0:T(8,128)(2,1)S(1)}, bf16[128,2560]{1,0:T(8,128)(2,1)S(1)}) custom-call(s32[1]{0:T(128)} %bitcast.device_ref, bf16[256,1152]{1,0:T(8,128)(2,1)} %queries_ref.1, bf16[128,1152]{1,0:T(8,128)(2,1)} %keys_ref.1, bf16[128,2560]{1,0:T(8,128)(2,1)} %values_ref.1), custom_call_target="tpu_custom_call" | custom-call | tf_op jit(solution)/shard_map/stage_in/pallas_call | solution.py:548
  5.1 1.2 %shard_map.91 = (bf16[64,1408]{1,0:T(8,128)(2,1)S(1)}, f32[64,1408]{1,0:T(8,128)S(1)}) custom-call(bf16[128,1152]{1,0:T(8,128)(2,1)S(1)} %get-tuple-element.41.query_ref, bf16[128,1152]{1,0:T(8,128)(2,1)S(1)} %get-tuple-element.42.keys_a, bf16[128,1152]{1,0:T(8,128)(2,1)S(1)} %collective-permute-done.keys_b, ...), custom_call_target="tpu_custom_call" | custom-call | tf_op jit(solution)/shard_map/pallas_call | solution.py:564
  6.3 2.7 %collective-permute-start.2 = (bf16[64,1408]{1,0:T(8,128)(2,1)S(1)}, bf16[64,1408]{1,0:T(8,128)(2,1)S(1)}, u32[]{:S(2)}, u32[]{:S(2)}) collective-permute-start(bf16[64,1408]{1,0:T(8,128)(2,1)S(1)} %get-tuple-element.47), channel_id=1, source_target_pairs={{0,2},{1,5},{2,0},{3,7},{4,6},{5,1},{6,4},{7,3},{8,10},{9,13},{10,... | collective-permute-start | bytes 540680 | tf_op jit(solution)/shard_map/ppermute | solution.py:52
  9.0 1.5 %shard_map.95 = (bf16[64,1408]{1,0:T(8,128)(2,1)S(1)}, f32[64,1408]{1,0:T(8,128)S(1)}) custom-call(bf16[128,1152]{1,0:T(8,128)(2,1)S(1)} %get-tuple-element.41.query_ref, bf16[128,1152]{1,0:T(8,128)(2,1)S(1)} %get-tuple-element.42.keys_a, bf16[128,1152]{1,0:T(8,128)(2,1)S(1)} %collective-permute-done.keys_b, ...), custom_call_target="tpu_custom_call" | custom-call | tf_op jit(solution)/shard_map/pallas_call | solution.py:564
  10.6 1.8 %collective-permute-done.2.came_ref = bf16[64,1408]{1,0:T(8,128)(2,1)S(1)} collective-permute-done((bf16[64,1408]{1,0:T(8,128)(2,1)S(1)}, bf16[64,1408]{1,0:T(8,128)(2,1)S(1)}, u32[]{:S(2)}, u32[]{:S(2)}) %collective-permute-start.2) | collective-permute-done | bytes 180256 | tf_op jit(solution)/shard_map/ppermute | solution.py:52
  12.7 2.1 %collective-permute-start.3 = (bf16[32,1408]{1,0:T(8,128)(2,1)S(1)}, bf16[32,1408]{1,0:T(8,128)(2,1)S(1)}, u32[]{:S(2)}, u32[]{:S(2)}) collective-permute-start(bf16[32,1408]{1,0:T(8,128)(2,1)S(1)} %get-tuple-element.49), channel_id=1, source_target_pairs={{0,4},{1,9},{2,6},{3,11},{4,0},{5,13},{6,2},{7,15},{8,12},{9,1},{1... | collective-permute-start | bytes 270344 | tf_op jit(solution)/shard_map/ppermute | solution.py:52
  14.8 1.3 %collective-permute-done.7.came_ref = bf16[64,1408]{1,0:T(8,128)(2,1)S(1)} collective-permute-done((bf16[64,1408]{1,0:T(8,128)(2,1)S(1)}, bf16[64,1408]{1,0:T(8,128)(2,1)S(1)}, u32[]{:S(2)}, u32[]{:S(2)}) %collective-permute-start.7) | collective-permute-done | bytes 180256 | tf_op jit(solution)/shard_map/ppermute | solution.py:52
  16.3 1.6 %collective-permute-start.8 = (bf16[32,1408]{1,0:T(8,128)(2,1)S(1)}, bf16[32,1408]{1,0:T(8,128)(2,1)S(1)}, u32[]{:S(2)}, u32[]{:S(2)}) collective-permute-start(bf16[32,1408]{1,0:T(8,128)(2,1)S(1)} %get-tuple-element.57), channel_id=1, source_target_pairs={{0,4},{1,9},{2,6},{3,11},{4,0},{5,13},{6,2},{7,15},{8,12},{9,1},{1... | collective-permute-start | bytes 270344 | tf_op jit(solution)/shard_map/ppermute | solution.py:52
  18.2 1.6 %collective-permute-start.4 = (bf16[32,1408]{1,0:T(8,128)(2,1)S(1)}, bf16[32,1408]{1,0:T(8,128)(2,1)S(1)}, u32[]{:S(2)}, u32[]{:S(2)}) collective-permute-start(bf16[32,1408]{1,0:T(8,128)(2,1)S(1)} %get-tuple-element.51), channel_id=1, source_target_pairs={{0,8},{1,3},{2,10},{3,1},{4,12},{5,7},{6,14},{7,5},{8,0},{9,11},{1... | collective-permute-start | bytes 270344 | tf_op jit(solution)/shard_map/ppermute | solution.py:52
  19.8 1.1 %collective-permute-done.8.came_ref = bf16[32,1408]{1,0:T(8,128)(2,1)S(1)} collective-permute-done((bf16[32,1408]{1,0:T(8,128)(2,1)S(1)}, bf16[32,1408]{1,0:T(8,128)(2,1)S(1)}, u32[]{:S(2)}, u32[]{:S(2)}) %collective-permute-start.8) | collective-permute-done | bytes 90144 | tf_op jit(solution)/shard_map/ppermute | solution.py:52
  21.1 1.6 %collective-permute-start.9 = (bf16[32,1408]{1,0:T(8,128)(2,1)S(1)}, bf16[32,1408]{1,0:T(8,128)(2,1)S(1)}, u32[]{:S(2)}, u32[]{:S(2)}) collective-permute-start(bf16[32,1408]{1,0:T(8,128)(2,1)S(1)} %get-tuple-element.59), channel_id=1, source_target_pairs={{0,8},{1,3},{2,10},{3,1},{4,12},{5,7},{6,14},{7,5},{8,0},{9,11},{1... | collective-permute-start | bytes 270344 | tf_op jit(solution)/shard_map/ppermute | solution.py:52
  23.0 2.7 %collective-permute-start.5 = (bf16[32,1408]{1,0:T(8,128)(2,1)S(1)}, bf16[32,1408]{1,0:T(8,128)(2,1)S(1)}, u32[]{:S(2)}, u32[]{:S(2)}) collective-permute-start(bf16[32,1408]{1,0:T(8,128)(2,1)S(1)} %get-tuple-element.53), channel_id=1, source_target_pairs={{0,16},{1,17},{2,18},{3,19},{4,20},{5,21},{6,22},{7,23},{8,24},{9,... | collective-permute-start | bytes 270344 | tf_op jit(solution)/shard_map/ppermute | solution.py:52
  26.7 1.9 %collective-permute-start.10 = (bf16[32,1280]{1,0:T(8,128)(2,1)S(1)}, bf16[32,1280]{1,0:T(8,128)(2,1)S(1)}, u32[]{:S(2)}, u32[]{:S(2)}) collective-permute-start(bf16[32,1280]{1,0:T(8,128)(2,1)S(1)} %get-tuple-element.60), channel_id=1, source_target_pairs={{0,16},{1,17},{2,18},{3,19},{4,20},{5,21},{6,22},{7,23},{8,24},{9,... | collective-permute-start | bytes 245768 | tf_op jit(solution)/shard_map/ppermute | solution.py:52
  28.6 3.5 %collective-permute-done.10 = bf16[32,1280]{1,0:T(8,128)(2,1)S(1)} collective-permute-done((bf16[32,1280]{1,0:T(8,128)(2,1)S(1)}, bf16[32,1280]{1,0:T(8,128)(2,1)S(1)}, u32[]{:S(2)}, u32[]{:S(2)}) %collective-permute-start.10) | collective-permute-done | bytes 81952 | tf_op jit(solution)/shard_map/ppermute | solution.py:52
  33.1 1.2 %collective-permute-start.6 = (bf16[64,1408]{1,0:T(8,128)(2,1)S(1)}, bf16[64,1408]{1,0:T(8,128)(2,1)S(1)}, u32[]{:S(2)}, u32[]{:S(2)}) collective-permute-start(bf16[64,1408]{1,0:T(8,128)(2,1)S(1)} %pad_maximum_fusion), channel_id=1, source_target_pairs={{0,4},{1,5},{2,6},{3,7},{4,0},{5,1},{6,2},{7,3},{8,12},{9,13},{10,... | collective-permute-start | bytes 540680 | tf_op jit(solution)/shard_map/ppermute | solution.py:52
  34.3 6.7 %collective-permute-done.6 = bf16[64,1408]{1,0:T(8,128)(2,1)S(1)} collective-permute-done((bf16[64,1408]{1,0:T(8,128)(2,1)S(1)}, bf16[64,1408]{1,0:T(8,128)(2,1)S(1)}, u32[]{:S(2)}, u32[]{:S(2)}) %collective-permute-start.6) | collective-permute-done | bytes 180256 | tf_op jit(solution)/shard_map/ppermute | solution.py:52
  41.0 1.0 %collective-permute-start.16 = (bf16[128,1408]{1,0:T(8,128)(2,1)S(1)}, bf16[128,1408]{1,0:T(8,128)(2,1)S(1)}, u32[]{:S(2)}, u32[]{:S(2)}) collective-permute-start(bf16[128,1408]{1,0:T(8,128)(2,1)S(1)} %constant_dynamic-update-slice_fusion.rows_a), channel_id=1, source_target_pairs={{0,2},{1,9},{2,0},{3,11},{4,6},{5,13},{6,4},{7,15},{8,10},{9,1},{1... | collective-permute-start | bytes 1081352 | tf_op jit(solution)/shard_map/ppermute | solution.py:52
  42.0 1.2 %collective-permute-start.15 = (bf16[128,1280]{1,0:T(8,128)(2,1)S(1)}, bf16[128,1280]{1,0:T(8,128)(2,1)S(1)}, u32[]{:S(2)}, u32[]{:S(2)}) collective-permute-start(bf16[128,1280]{1,0:T(8,128)(2,1)S(1)} %constant_dynamic-update-slice_fusion.3.rows_b), channel_id=1, source_target_pairs={{0,2},{1,9},{2,0},{3,11},{4,6},{5,13},{6,4},{7,15},{8,10},{9,1},{1... | collective-permute-start | bytes 983048 | tf_op jit(solution)/shard_map/ppermute | solution.py:52
  43.3 6.7 %expert_first.1 = (f32[128,1280]{1,0:T(8,128)S(1)}, f32[128,1280]{1,0:T(8,128)S(1)}, bf16[1024,2560]{1,0:T(8,128)(2,1)S(1)}, bf16[1024,2560]{1,0:T(8,128)(2,1)S(1)}, bf16[1024,2560]{1,0:T(8,128)(2,1)S(1)}) custom-call(s32[1]{0:T(128)} %bitcast.1.expert_ref, f32[1,2560]{1,0:T(1,128)S(1)} %reshape.17.gain_ref, ...), custom_call_target="tpu_custom_call" | custom-call | flops 2013265920 | bytes 15728640 | tf_op jit(solution)/shard_map/expert_first/pallas_call | solution.py:450
  50.0 1.6 %expert_half.1 = (f32[1024,128]{1,0:T(8,128)S(1)}, f32[1024,128]{1,0:T(8,128)S(1)}, f32[8,128]{1,0:T(8,128)S(1)}) custom-call(s32[1]{0:T(128)} %bitcast.1.expert_ref, f32[1,2560]{1,0:T(1,128)S(1)} %reshape.17.gain_ref, bf16[128,1408]{1,0:T(8,128)(2,1)S(1)} %collective-permute-done.16.rows_ref, bf16[1024,2560]{1,0:T(8,128)(2,1)S(1)} %get-tuple-element.65.gate_ref, ...), custom_call_target="tpu_custom_call" | custom-call | tf_op jit(solution)/shard_map/expert_half/pallas_call | solution.py:482
  52.0 2.1 %expert_second.1 = (bf16[128,1280]{1,0:T(8,128)(2,1)S(1)}, bf16[128,1024]{1,0:T(8,128)(2,1)S(1)}) custom-call(f32[1,2560]{1,0:T(1,128)S(1)} %reshape.17.gain_ref, bf16[128,1280]{1,0:T(8,128)(2,1)S(1)} %collective-permute-done.15.rows_ref, f32[1024,128]{1,0:T(8,128)S(1)} %get-tuple-element.67.gates_ref, f32[1024,128]{1,0:T(8,128)S(1)} %get-tuple-element.68.ups_ref, ...), custom_call_target="tpu_custom_call" | custom-call | tf_op jit(solution)/shard_map/expert_second/pallas_call | solution.py:492
  54.1 1.0 %collective-permute-start.17 = (bf16[128,1280]{1,0:T(8,128)(2,1)S(1)}, bf16[128,1280]{1,0:T(8,128)(2,1)S(1)}, u32[]{:S(2)}, u32[]{:S(2)}) collective-permute-start(bf16[128,1280]{1,0:T(8,128)(2,1)S(1)} %get-tuple-element.71), channel_id=1, source_target_pairs={{0,2},{1,9},{2,0},{3,11},{4,6},{5,13},{6,4},{7,15},{8,10},{9,1},{1... | collective-permute-start | bytes 983048 | tf_op jit(solution)/shard_map/ppermute | solution.py:52
  56.1 5.2 %collective-permute-done.17 = bf16[128,1280]{1,0:T(8,128)(2,1)S(1)} collective-permute-done((bf16[128,1280]{1,0:T(8,128)(2,1)S(1)}, bf16[128,1280]{1,0:T(8,128)(2,1)S(1)}, u32[]{:S(2)}, u32[]{:S(2)}) %collective-permute-start.17) | collective-permute-done | bytes 327712 | tf_op jit(solution)/shard_map/ppermute | solution.py:52
  61.7 2.9 %collective-permute-done.21 = bf16[128,1280]{1,0:T(8,128)(2,1)S(1)} collective-permute-done((bf16[128,1280]{1,0:T(8,128)(2,1)S(1)}, bf16[128,1280]{1,0:T(8,128)(2,1)S(1)}, u32[]{:S(2)}, u32[]{:S(2)}) %collective-permute-start.21) | collective-permute-done | bytes 327712 | tf_op jit(solution)/shard_map/ppermute | solution.py:52
  64.7 1.2 %collective-permute-start.22 = (bf16[64,1280]{1,0:T(8,128)(2,1)S(1)}, bf16[64,1280]{1,0:T(8,128)(2,1)S(1)}, u32[]{:S(2)}, u32[]{:S(2)}) collective-permute-start(bf16[64,1280]{1,0:T(8,128)(2,1)S(1)} %slice.86), channel_id=1, source_target_pairs={{0,2},{1,9},{2,0},{3,11},{4,6},{5,13},{6,4},{7,15},{8,10},{9,1},{1... | collective-permute-start | bytes 491528 | tf_op jit(solution)/shard_map/ppermute | solution.py:52
  66.8 1.2 %collective-permute-start.19 = (bf16[32,1280]{1,0:T(8,128)(2,1)S(1)}, bf16[32,1280]{1,0:T(8,128)(2,1)S(1)}, u32[]{:S(2)}, u32[]{:S(2)}) collective-permute-start(bf16[32,1280]{1,0:T(8,128)(2,1)S(1)} %slice.89), channel_id=1, source_target_pairs={{0,16},{1,17},{2,18},{3,19},{4,20},{5,21},{6,22},{7,23},{8,24},{9,... | collective-permute-start | bytes 245768 | tf_op jit(solution)/shard_map/ppermute | solution.py:52
  68.0 2.0 %collective-permute-done.22 = bf16[64,1280]{1,0:T(8,128)(2,1)S(1)} collective-permute-done((bf16[64,1280]{1,0:T(8,128)(2,1)S(1)}, bf16[64,1280]{1,0:T(8,128)(2,1)S(1)}, u32[]{:S(2)}, u32[]{:S(2)}) %collective-permute-start.22) | collective-permute-done | bytes 163872 | tf_op jit(solution)/shard_map/ppermute | solution.py:52
  70.1 1.3 %collective-permute-start.23 = (bf16[32,1280]{1,0:T(8,128)(2,1)S(1)}, bf16[32,1280]{1,0:T(8,128)(2,1)S(1)}, u32[]{:S(2)}, u32[]{:S(2)}) collective-permute-start(bf16[32,1280]{1,0:T(8,128)(2,1)S(1)} %slice.88), channel_id=1, source_target_pairs={{0,16},{1,17},{2,18},{3,19},{4,20},{5,21},{6,22},{7,23},{8,24},{9,... | collective-permute-start | bytes 245768 | tf_op jit(solution)/shard_map/ppermute | solution.py:52
  71.4 1.7 %collective-permute-done.19 = bf16[32,1280]{1,0:T(8,128)(2,1)S(1)} collective-permute-done((bf16[32,1280]{1,0:T(8,128)(2,1)S(1)}, bf16[32,1280]{1,0:T(8,128)(2,1)S(1)}, u32[]{:S(2)}, u32[]{:S(2)}) %collective-permute-start.19) | collective-permute-done | bytes 81952 | tf_op jit(solution)/shard_map/ppermute | solution.py:52
  73.7 2.7 %collective-permute-done.23 = bf16[32,1280]{1,0:T(8,128)(2,1)S(1)} collective-permute-done((bf16[32,1280]{1,0:T(8,128)(2,1)S(1)}, bf16[32,1280]{1,0:T(8,128)(2,1)S(1)}, u32[]{:S(2)}, u32[]{:S(2)}) %collective-permute-start.23) | collective-permute-done | bytes 81952 | tf_op jit(solution)/shard_map/ppermute | solution.py:52
  77.2 3.3 %collective-permute-done.24 = bf16[16,1280]{1,0:T(8,128)(2,1)S(1)} collective-permute-done((bf16[16,1280]{1,0:T(8,128)(2,1)S(1)}, bf16[16,1280]{1,0:T(8,128)(2,1)S(1)}, u32[]{:S(2)}, u32[]{:S(2)}) %collective-permute-start.24) | collective-permute-done | bytes 40992 | tf_op jit(solution)/shard_map/ppermute | solution.py:52
  (64 shorter events, 9.7 us)
Async XLA Ops:
  0.0 2.9 %collective-permute-start.1 = (bf16[128,2560]{1,0:T(8,128)(2,1)}, bf16[128,2560]{1,0:T(8,128)(2,1)S(1)}, u32[]{:S(2)}, u32[]{:S(2)}) collective-permute-start(bf16[128,2560]{1,0:T(8,128)(2,1)} %values_ref.1), channel_id=1, source_target_pairs={{0,1},{1,0},{2,3},{3,2},{4,5},{5,4},{6,7},{7,6},{8,9},{9,8},{10,11... | collective-permute-start | bytes 1966088 | tf_op jit(solution)/shard_map/ppermute | solution.py:33
  0.5 2.4 %collective-permute-start = (bf16[128,1152]{1,0:T(8,128)(2,1)}, bf16[128,1152]{1,0:T(8,128)(2,1)S(1)}, u32[]{:S(2)}, u32[]{:S(2)}) collective-permute-start(bf16[128,1152]{1,0:T(8,128)(2,1)} %keys_ref.1), channel_id=1, source_target_pairs={{0,1},{1,0},{2,3},{3,2},{4,5},{5,4},{6,7},{7,6},{8,9},{9,8},{10,11... | collective-permute-start | bytes 884744 | tf_op jit(solution)/shard_map/ppermute | solution.py:33
  2.9 40.4 %collective-permute-start.12 = (bf16[512,2560]{1,0:T(8,128)(2,1)}, bf16[512,2560]{1,0:T(8,128)(2,1)}, u32[]{:S(2)}, u32[]{:S(2)}) collective-permute-start(bf16[512,2560]{1,0:T(8,128)(2,1)} %gate_a), channel_id=1, source_target_pairs={{0,1},{1,0},{2,3},{3,2},{4,5},{5,4},{6,7},{7,6},{8,9},{9,8},{10,11... | collective-permute-start | bytes 7864328 | tf_op jit(solution)/shard_map/ppermute | solution.py:33
  3.2 40.0 %collective-permute-start.13 = (bf16[512,2560]{1,0:T(8,128)(2,1)}, bf16[512,2560]{1,0:T(8,128)(2,1)}, u32[]{:S(2)}, u32[]{:S(2)}) collective-permute-start(bf16[512,2560]{1,0:T(8,128)(2,1)} %up_a), channel_id=1, source_target_pairs={{0,1},{1,0},{2,3},{3,2},{4,5},{5,4},{6,7},{7,6},{8,9},{9,8},{10,11... | collective-permute-start | bytes 7864328 | tf_op jit(solution)/shard_map/ppermute | solution.py:33
  3.4 39.9 %collective-permute-start.14 = (bf16[512,2560]{1,0:T(8,128)(2,1)}, bf16[512,2560]{1,0:T(8,128)(2,1)}, u32[]{:S(2)}, u32[]{:S(2)}) collective-permute-start(bf16[512,2560]{1,0:T(8,128)(2,1)} %down_a), channel_id=1, source_target_pairs={{0,1},{1,0},{2,3},{3,2},{4,5},{5,4},{6,7},{7,6},{8,9},{9,8},{10,11... | collective-permute-start | bytes 7864328 | tf_op jit(solution)/shard_map/ppermute | solution.py:33
  5.0 12.9 %copy-start.1 = (s32[16,6]{0,1:T(8,128)S(1)}, s32[16,6]{0,1:T(8,128)}, u32[]{:S(2)}) copy-start(s32[16,6]{0,1:T(8,128)} %param.14) | copy-start | bytes 1156
  5.0 12.9 %copy-start.2 = (s32[16,6]{0,1:T(8,128)S(1)}, s32[16,6]{0,1:T(8,128)}, u32[]{:S(2)}) copy-start(s32[16,6]{0,1:T(8,128)} %param.13) | copy-start | bytes 1156
  6.3 6.2 %collective-permute-start.2 = (bf16[64,1408]{1,0:T(8,128)(2,1)S(1)}, bf16[64,1408]{1,0:T(8,128)(2,1)S(1)}, u32[]{:S(2)}, u32[]{:S(2)}) collective-permute-start(bf16[64,1408]{1,0:T(8,128)(2,1)S(1)} %get-tuple-element.47), channel_id=1, source_target_pairs={{0,2},{1,5},{2,0},{3,7},{4,6},{5,1},{6,4},{7,3},{8,10},{9,13},{10,... | collective-permute-start | bytes 540680 | tf_op jit(solution)/shard_map/ppermute | solution.py:52
  10.5 32.7 %copy-start = (f32[2560]{0:T(1024)S(1)}, f32[2560]{0:T(1024)}, u32[]{:S(2)}) copy-start(f32[2560]{0:T(1024)} %param.12) | copy-start | bytes 30724
  10.5 5.6 %collective-permute-start.7 = (bf16[64,1408]{1,0:T(8,128)(2,1)S(1)}, bf16[64,1408]{1,0:T(8,128)(2,1)S(1)}, u32[]{:S(2)}, u32[]{:S(2)}) collective-permute-start(bf16[64,1408]{1,0:T(8,128)(2,1)S(1)} %get-tuple-element.55), channel_id=1, source_target_pairs={{0,2},{1,5},{2,0},{3,7},{4,6},{5,1},{6,4},{7,3},{8,10},{9,13},{10,... | collective-permute-start | bytes 540680 | tf_op jit(solution)/shard_map/ppermute | solution.py:52
  12.7 5.3 %collective-permute-start.3 = (bf16[32,1408]{1,0:T(8,128)(2,1)S(1)}, bf16[32,1408]{1,0:T(8,128)(2,1)S(1)}, u32[]{:S(2)}, u32[]{:S(2)}) collective-permute-start(bf16[32,1408]{1,0:T(8,128)(2,1)S(1)} %get-tuple-element.49), channel_id=1, source_target_pairs={{0,4},{1,9},{2,6},{3,11},{4,0},{5,13},{6,2},{7,15},{8,12},{9,1},{1... | collective-permute-start | bytes 270344 | tf_op jit(solution)/shard_map/ppermute | solution.py:52
  16.3 4.6 %collective-permute-start.8 = (bf16[32,1408]{1,0:T(8,128)(2,1)S(1)}, bf16[32,1408]{1,0:T(8,128)(2,1)S(1)}, u32[]{:S(2)}, u32[]{:S(2)}) collective-permute-start(bf16[32,1408]{1,0:T(8,128)(2,1)S(1)} %get-tuple-element.57), channel_id=1, source_target_pairs={{0,4},{1,9},{2,6},{3,11},{4,0},{5,13},{6,2},{7,15},{8,12},{9,1},{1... | collective-permute-start | bytes 270344 | tf_op jit(solution)/shard_map/ppermute | solution.py:52
  18.2 4.6 %collective-permute-start.4 = (bf16[32,1408]{1,0:T(8,128)(2,1)S(1)}, bf16[32,1408]{1,0:T(8,128)(2,1)S(1)}, u32[]{:S(2)}, u32[]{:S(2)}) collective-permute-start(bf16[32,1408]{1,0:T(8,128)(2,1)S(1)} %get-tuple-element.51), channel_id=1, source_target_pairs={{0,8},{1,3},{2,10},{3,1},{4,12},{5,7},{6,14},{7,5},{8,0},{9,11},{1... | collective-permute-start | bytes 270344 | tf_op jit(solution)/shard_map/ppermute | solution.py:52
  21.1 5.4 %collective-permute-start.9 = (bf16[32,1408]{1,0:T(8,128)(2,1)S(1)}, bf16[32,1408]{1,0:T(8,128)(2,1)S(1)}, u32[]{:S(2)}, u32[]{:S(2)}) collective-permute-start(bf16[32,1408]{1,0:T(8,128)(2,1)S(1)} %get-tuple-element.59), channel_id=1, source_target_pairs={{0,8},{1,3},{2,10},{3,1},{4,12},{5,7},{6,14},{7,5},{8,0},{9,11},{1... | collective-permute-start | bytes 270344 | tf_op jit(solution)/shard_map/ppermute | solution.py:52
  23.0 10.0 %collective-permute-start.5 = (bf16[32,1408]{1,0:T(8,128)(2,1)S(1)}, bf16[32,1408]{1,0:T(8,128)(2,1)S(1)}, u32[]{:S(2)}, u32[]{:S(2)}) collective-permute-start(bf16[32,1408]{1,0:T(8,128)(2,1)S(1)} %get-tuple-element.53), channel_id=1, source_target_pairs={{0,16},{1,17},{2,18},{3,19},{4,20},{5,21},{6,22},{7,23},{8,24},{9,... | collective-permute-start | bytes 270344 | tf_op jit(solution)/shard_map/ppermute | solution.py:52
  26.7 5.4 %collective-permute-start.10 = (bf16[32,1280]{1,0:T(8,128)(2,1)S(1)}, bf16[32,1280]{1,0:T(8,128)(2,1)S(1)}, u32[]{:S(2)}, u32[]{:S(2)}) collective-permute-start(bf16[32,1280]{1,0:T(8,128)(2,1)S(1)} %get-tuple-element.60), channel_id=1, source_target_pairs={{0,16},{1,17},{2,18},{3,19},{4,20},{5,21},{6,22},{7,23},{8,24},{9,... | collective-permute-start | bytes 245768 | tf_op jit(solution)/shard_map/ppermute | solution.py:52
  32.1 9.9 %collective-permute-start.11 = (bf16[64,1280]{1,0:T(8,128)(2,1)S(1)}, bf16[64,1280]{1,0:T(8,128)(2,1)S(1)}, u32[]{:S(2)}, u32[]{:S(2)}) collective-permute-start(bf16[64,1280]{1,0:T(8,128)(2,1)S(1)} %pad_maximum_fusion.1), channel_id=1, source_target_pairs={{0,4},{1,5},{2,6},{3,7},{4,0},{5,1},{6,2},{7,3},{8,12},{9,13},{10,... | collective-permute-start | bytes 491528 | tf_op jit(solution)/shard_map/ppermute | solution.py:52
  33.1 7.9 %collective-permute-start.6 = (bf16[64,1408]{1,0:T(8,128)(2,1)S(1)}, bf16[64,1408]{1,0:T(8,128)(2,1)S(1)}, u32[]{:S(2)}, u32[]{:S(2)}) collective-permute-start(bf16[64,1408]{1,0:T(8,128)(2,1)S(1)} %pad_maximum_fusion), channel_id=1, source_target_pairs={{0,4},{1,5},{2,6},{3,7},{4,0},{5,1},{6,2},{7,3},{8,12},{9,13},{10,... | collective-permute-start | bytes 540680 | tf_op jit(solution)/shard_map/ppermute | solution.py:52
  41.0 9.0 %collective-permute-start.16 = (bf16[128,1408]{1,0:T(8,128)(2,1)S(1)}, bf16[128,1408]{1,0:T(8,128)(2,1)S(1)}, u32[]{:S(2)}, u32[]{:S(2)}) collective-permute-start(bf16[128,1408]{1,0:T(8,128)(2,1)S(1)} %constant_dynamic-update-slice_fusion.rows_a), channel_id=1, source_target_pairs={{0,2},{1,9},{2,0},{3,11},{4,6},{5,13},{6,4},{7,15},{8,10},{9,1},{1... | collective-permute-start | bytes 1081352 | tf_op jit(solution)/shard_map/ppermute | solution.py:52
  42.0 10.0 %collective-permute-start.15 = (bf16[128,1280]{1,0:T(8,128)(2,1)S(1)}, bf16[128,1280]{1,0:T(8,128)(2,1)S(1)}, u32[]{:S(2)}, u32[]{:S(2)}) collective-permute-start(bf16[128,1280]{1,0:T(8,128)(2,1)S(1)} %constant_dynamic-update-slice_fusion.3.rows_b), channel_id=1, source_target_pairs={{0,2},{1,9},{2,0},{3,11},{4,6},{5,13},{6,4},{7,15},{8,10},{9,1},{1... | collective-permute-start | bytes 983048 | tf_op jit(solution)/shard_map/ppermute | solution.py:52
  54.1 7.1 %collective-permute-start.17 = (bf16[128,1280]{1,0:T(8,128)(2,1)S(1)}, bf16[128,1280]{1,0:T(8,128)(2,1)S(1)}, u32[]{:S(2)}, u32[]{:S(2)}) collective-permute-start(bf16[128,1280]{1,0:T(8,128)(2,1)S(1)} %get-tuple-element.71), channel_id=1, source_target_pairs={{0,2},{1,9},{2,0},{3,11},{4,6},{5,13},{6,4},{7,15},{8,10},{9,1},{1... | collective-permute-start | bytes 983048 | tf_op jit(solution)/shard_map/ppermute | solution.py:52
  55.7 8.9 %collective-permute-start.21 = (bf16[128,1280]{1,0:T(8,128)(2,1)S(1)}, bf16[128,1280]{1,0:T(8,128)(2,1)S(1)}, u32[]{:S(2)}, u32[]{:S(2)}) collective-permute-start(bf16[128,1280]{1,0:T(8,128)(2,1)S(1)} %get-tuple-element.76), channel_id=1, source_target_pairs={{0,4},{1,5},{2,6},{3,7},{4,0},{5,1},{6,2},{7,3},{8,12},{9,13},{10,... | collective-permute-start | bytes 983048 | tf_op jit(solution)/shard_map/ppermute | solution.py:52
  61.4 5.4 %collective-permute-start.18 = (bf16[64,1280]{1,0:T(8,128)(2,1)S(1)}, bf16[64,1280]{1,0:T(8,128)(2,1)S(1)}, u32[]{:S(2)}, u32[]{:S(2)}) collective-permute-start(bf16[64,1280]{1,0:T(8,128)(2,1)S(1)} %slice.87), channel_id=1, source_target_pairs={{0,4},{1,5},{2,6},{3,7},{4,0},{5,1},{6,2},{7,3},{8,12},{9,13},{10,... | collective-permute-start | bytes 491528 | tf_op jit(solution)/shard_map/ppermute | solution.py:52
  64.7 5.4 %collective-permute-start.22 = (bf16[64,1280]{1,0:T(8,128)(2,1)S(1)}, bf16[64,1280]{1,0:T(8,128)(2,1)S(1)}, u32[]{:S(2)}, u32[]{:S(2)}) collective-permute-start(bf16[64,1280]{1,0:T(8,128)(2,1)S(1)} %slice.86), channel_id=1, source_target_pairs={{0,2},{1,9},{2,0},{3,11},{4,6},{5,13},{6,4},{7,15},{8,10},{9,1},{1... | collective-permute-start | bytes 491528 | tf_op jit(solution)/shard_map/ppermute | solution.py:52
  66.8 6.3 %collective-permute-start.19 = (bf16[32,1280]{1,0:T(8,128)(2,1)S(1)}, bf16[32,1280]{1,0:T(8,128)(2,1)S(1)}, u32[]{:S(2)}, u32[]{:S(2)}) collective-permute-start(bf16[32,1280]{1,0:T(8,128)(2,1)S(1)} %slice.89), channel_id=1, source_target_pairs={{0,16},{1,17},{2,18},{3,19},{4,20},{5,21},{6,22},{7,23},{8,24},{9,... | collective-permute-start | bytes 245768 | tf_op jit(solution)/shard_map/ppermute | solution.py:52
  70.1 6.3 %collective-permute-start.23 = (bf16[32,1280]{1,0:T(8,128)(2,1)S(1)}, bf16[32,1280]{1,0:T(8,128)(2,1)S(1)}, u32[]{:S(2)}, u32[]{:S(2)}) collective-permute-start(bf16[32,1280]{1,0:T(8,128)(2,1)S(1)} %slice.88), channel_id=1, source_target_pairs={{0,16},{1,17},{2,18},{3,19},{4,20},{5,21},{6,22},{7,23},{8,24},{9,... | collective-permute-start | bytes 245768 | tf_op jit(solution)/shard_map/ppermute | solution.py:52
  73.1 4.1 %collective-permute-start.20 = (bf16[16,1280]{1,0:T(8,128)(2,1)S(1)}, bf16[16,1280]{1,0:T(8,128)(2,1)S(1)}, u32[]{:S(2)}, u32[]{:S(2)}) collective-permute-start(bf16[16,1280]{1,0:T(8,128)(2,1)S(1)} %slice.91), channel_id=1, source_target_pairs={{0,8},{1,3},{2,10},{3,1},{4,12},{5,7},{6,14},{7,5},{8,0},{9,11},{1... | collective-permute-start | bytes 122888 | tf_op jit(solution)/shard_map/ppermute | solution.py:52
  76.4 4.1 %collective-permute-start.24 = (bf16[16,1280]{1,0:T(8,128)(2,1)S(1)}, bf16[16,1280]{1,0:T(8,128)(2,1)S(1)}, u32[]{:S(2)}, u32[]{:S(2)}) collective-permute-start(bf16[16,1280]{1,0:T(8,128)(2,1)S(1)} %slice.90), channel_id=1, source_target_pairs={{0,8},{1,3},{2,10},{3,1},{4,12},{5,7},{6,14},{7,5},{8,0},{9,11},{1... | collective-permute-start | bytes 122888 | tf_op jit(solution)/shard_map/ppermute | solution.py:52

commit v6 on v5

--- a/solution.py
+++ b/solution.py
@@ -122,9 +122,11 @@
     queries_ref,
     keys_ref,
     values_ref,
+    gain_ref,
     query_ref,
     near_keys_ref,
     near_values_ref,
+    near_gain_ref,
     arrived,
 ):
     group_size = queries_ref.shape[0] // row_count
@@ -134,6 +136,7 @@
     copies = [
         pltpu.make_async_copy(keys_ref, near_keys_ref, arrived.at[0]),
         pltpu.make_async_copy(values_ref, near_values_ref, arrived.at[1]),
+        pltpu.make_async_copy(gain_ref, near_gain_ref, arrived.at[2]),
     ]
     for slot, (even_mask, odd_mask) in enumerate(zip(*masks)):
         block = own_block ^ jnp.where(odd, odd_mask, even_mask)
@@ -142,7 +145,7 @@
             pltpu.make_async_copy(
                 queries_ref.at[pl.ds(start, row_count), :],
                 query_ref.at[slot * row_count : (slot + 1) * row_count, :],
-                arrived.at[2 + slot],
+                arrived.at[3 + slot],
             )
         )
     for copy in copies:
@@ -279,7 +282,7 @@
         ).astype(jnp.bfloat16)
 
 
-def hidden_units(expert_ref, gain_ref, row_refs, gate_ref, up_ref, turned, hidden, ready):
+def normed_rows(device_ref, gain_ref, row_refs, turned):
     width = row_refs[1].shape[1]
     model_width = width * len(row_refs)
     square = jnp.zeros((row_refs[0].shape[0], LANES), jnp.float32)
@@ -298,79 +301,102 @@
     turned[model_width:, :] = row_refs[0][:, width:].T
     scores = turned[model_width:, :].astype(jnp.float32)
     lane = lax.broadcasted_iota(jnp.int32, scores.shape, 0)
-    chosen = jnp.where(lane == expert_ref[0] + TABLE_LANE, scores, 0.0)
-    share = jnp.sum(chosen, axis=0, keepdims=True) / jnp.sum(scores, axis=0, keepdims=True)
-    rows = turned[:model_width, :]
-    for chunk in range(gate_ref.shape[0] // UNITS):
-        ready(chunk)
-        units = slice(chunk * UNITS, (chunk + 1) * UNITS)
-        gate_part = jnp.dot(gate_ref[units, :], rows, preferred_element_type=jnp.float32)
-        up_part = jnp.dot(up_ref[units, :], rows, preferred_element_type=jnp.float32)
-        silu = gate_part / (1.0 + jnp.exp(-gate_part))
-        hidden[:, units] = (silu * up_part * share).T.astype(jnp.bfloat16)
-
-
-def down_product(hidden_ref, down_ref, out_ref, start):
+    chosen = jnp.where(lane == lax.div(device_ref[0], 2) + TABLE_LANE, scores, 0.0)
+    return jnp.sum(chosen, axis=0, keepdims=True) / jnp.sum(scores, axis=0, keepdims=True)
+
+
+def down_product(hidden_ref, down_refs, out_ref, start):
     width = out_ref.shape[1]
+    units = down_refs[0].shape[0]
     step = width // 2 if width % (4 * LANES) else 4 * LANES
     for low in range(0, width, step):
-        out_ref[:, low : low + step] = jnp.dot(
-            hidden_ref[...],
-            down_ref[:, start + low : start + low + step],
-            preferred_element_type=jnp.float32,
+        columns = slice(start + low, start + low + step)
+        out_ref[:, low : low + step] = sum(
+            jnp.dot(
+                hidden_ref[:, half * units : (half + 1) * units],
+                down_ref[:, columns],
+                preferred_element_type=jnp.float32,
+            )
+            for half, down_ref in enumerate(down_refs)
         ).astype(out_ref.dtype)
 
 
+def fetch_kernel(*refs):
+    count = (len(refs) - 1) // 2
+    arrived = refs[-1]
+    copies = [
+        pltpu.make_async_copy(refs[i], refs[count + i], arrived.at[i]) for i in range(count)
+    ]
+    for copy in copies:
+        copy.start()
+    for copy in copies:
+        copy.wait()
+
+
+def fetched(arrays):
+    return pl.pallas_call(
+        fetch_kernel,
+        compiler_params=pltpu.CompilerParams(vmem_limit_bytes=1 << 20),
+        out_shape=tuple(near_shape(array.shape, array.dtype) for array in arrays),
+        in_specs=[pl.BlockSpec(memory_space=pltpu.HBM)] * len(arrays),
+        out_specs=(pl.BlockSpec(memory_space=pltpu.VMEM),) * len(arrays),
+        scratch_shapes=[pltpu.SemaphoreType.DMA((len(arrays),))],
+    )(*[far(array) for array in arrays])
+
+
+def joined_kernel(own_ref, came_ref, *refs):
+    out_ref = refs[len(refs) // 2]
+    half = own_ref.shape[0]
+    out_ref[:half, :] = own_ref[...]
+    out_ref[half:, :] = came_ref[...]
+
+
+def joined(own, came, passed=()):
+    rows, width = own.shape
+    whole = pl.BlockSpec(memory_space=pltpu.VMEM)
+    out, *passed = pl.pallas_call(
+        joined_kernel,
+        compiler_params=pltpu.CompilerParams(vmem_limit_bytes=12 << 20),
+        out_shape=(near_shape((2 * rows, width), own.dtype),)
+        + tuple(near_shape(array.shape, array.dtype) for array in passed),
+        in_specs=[whole] * (2 + len(passed)),
+        out_specs=(whole,) * (1 + len(passed)),
+        input_output_aliases={2 + i: 1 + i for i in range(len(passed))},
+    )(near(own), near(came), *[near(array) for array in passed])
+    return out, passed
+
+
 def first_expert_kernel(
-    expert_ref,
+    device_ref,
     gain_ref,
     rows_a,
     rows_b,
     gate_a,
+    up_a,
+    down_a,
     gate_b,
-    up_a,
     up_b,
-    down_a,
     down_b,
     out_a,
     out_b,
-    gate_ref,
-    up_ref,
-    down_ref,
     turned,
     hidden,
-    arrived,
 ):
-    per_half = gate_a.shape[0] // UNITS
-    chunks = 2 * per_half
-    pairs = ((gate_a, gate_b), (up_a, up_b), (down_a, down_b))
-    targets = (gate_ref, up_ref, down_ref)
-
-    def copy_of(part, chunk):
-        low = chunk % per_half * UNITS
-        return pltpu.make_async_copy(
-            pairs[part][chunk // per_half].at[low : low + UNITS, :],
-            targets[part].at[chunk * UNITS : (chunk + 1) * UNITS, :],
-            arrived.at[part, chunk],
-        )
-
-    for chunk in range(chunks):
-        for part in range(2):
-            copy_of(part, chunk).start()
-    for chunk in range(chunks):
-        copy_of(2, chunk).start()
-
-    def ready(chunk):
-        copy_of(0, chunk).wait()
-        copy_of(1, chunk).wait()
-
-    hidden_units(
-        expert_ref, gain_ref, (rows_a, rows_b), gate_ref, up_ref, turned, hidden, ready
-    )
-    for chunk in range(chunks):
-        copy_of(2, chunk).wait()
-    down_product(hidden, down_ref, out_a, 0)
-    down_product(hidden, down_ref, out_b, out_a.shape[1])
+    units = gate_a.shape[0]
+    share = normed_rows(device_ref, gain_ref, (rows_a, rows_b), turned)
+    model_width = gain_ref.shape[1]
+    rows = turned[:model_width, :]
+    for half, (gate_ref, up_ref) in enumerate(((gate_a, up_a), (gate_b, up_b))):
+        for low in range(0, units, UNITS):
+            chunk = slice(low, low + UNITS)
+            gate_part = jnp.dot(gate_ref[chunk, :], rows, preferred_element_type=jnp.float32)
+            up_part = jnp.dot(up_ref[chunk, :], rows, preferred_element_type=jnp.float32)
+            silu = gate_part / (1.0 + jnp.exp(-gate_part))
+            hidden[:, half * units + low : half * units + low + UNITS] = (
+                (silu * up_part * share).T.astype(jnp.bfloat16)
+            )
+    down_product(hidden, (down_a, down_b), out_a, 0)
+    down_product(hidden, (down_a, down_b), out_b, out_a.shape[1])
 
 
 def turned_half(rows_ref, gain_ref, start, width, turned):
@@ -384,19 +410,37 @@
 
 
 def half_expert_kernel(
-    expert_ref, gain_ref, rows_ref, gate_ref, up_ref, gates_ref, ups_ref, stats_ref, turned
+    device_ref,
+    gain_ref,
+    rows_ref,
+    gate_a,
+    gate_b,
+    up_a,
+    up_b,
+    gates_ref,
+    ups_ref,
+    stats_ref,
+    turned,
 ):
     width = turned.shape[0]
     stats_ref[0:1, :] = turned_half(rows_ref, gain_ref, 0, width, turned)
     scores = rows_ref[:, width:].astype(jnp.float32).T
     lane = lax.broadcasted_iota(jnp.int32, scores.shape, 0)
-    chosen = jnp.where(lane == expert_ref[0] + TABLE_LANE, scores, 0.0)
+    chosen = jnp.where(lane == lax.div(device_ref[0], 2) + TABLE_LANE, scores, 0.0)
     stats_ref[1:2, :] = jnp.sum(chosen, axis=0, keepdims=True) / jnp.sum(
         scores, axis=0, keepdims=True
     )
     rows = turned[...]
-    gates_ref[...] = jnp.dot(gate_ref[:, :width], rows, preferred_element_type=jnp.float32)
-    ups_ref[...] = jnp.dot(up_ref[:, :width], rows, preferred_element_type=jnp.float32)
+    units = gate_a.shape[0]
+    for weight_ref, low, out_ref in (
+        (gate_a, 0, gates_ref),
+        (gate_b, units, gates_ref),
+        (up_a, 0, ups_ref),
+        (up_b, units, ups_ref),
+    ):
+        out_ref[low : low + units, :] = jnp.dot(
+            weight_ref[:, :width], rows, preferred_element_type=jnp.float32
+        )
 
 
 def second_expert_kernel(
@@ -405,9 +449,12 @@
     gates_ref,
     ups_ref,
     stats_ref,
-    gate_ref,
-    up_ref,
-    down_ref,
+    gate_a,
+    gate_b,
+    up_a,
+    up_b,
+    down_a,
+    down_b,
     out_ref,
     hidden,
     turned,
@@ -417,23 +464,28 @@
     inverse = lax.rsqrt(square / (2 * width) + 1e-06)
     share = stats_ref[1:2, :]
     rows = turned[...]
-    for low in range(0, gate_ref.shape[0], UNITS):
-        units = slice(low, low + UNITS)
-        gate_part = inverse * (
-            gates_ref[units, :]
-            + jnp.dot(gate_ref[units, width:], rows, preferred_element_type=jnp.float32)
-        )
-        up_part = inverse * (
-            ups_ref[units, :]
-            + jnp.dot(up_ref[units, width:], rows, preferred_element_type=jnp.float32)
-        )
-        silu = gate_part / (1.0 + jnp.exp(-gate_part))
-        hidden[:, units] = (silu * up_part * share).T.astype(jnp.bfloat16)
-    down_product(hidden, down_ref, out_ref, 0)
-
-
-def rest_expert_kernel(start, hidden_ref, down_ref, first_ref, sent_ref, kept_ref, value_ref):
-    down_product(hidden_ref, down_ref, value_ref, start)
+    units = gate_a.shape[0]
+    for half, (gate_ref, up_ref) in enumerate(((gate_a, up_a), (gate_b, up_b))):
+        for low in range(0, units, UNITS):
+            chunk = slice(low, low + UNITS)
+            at = slice(half * units + low, half * units + low + UNITS)
+            gate_part = inverse * (
+                gates_ref[at, :]
+                + jnp.dot(gate_ref[chunk, width:], rows, preferred_element_type=jnp.float32)
+            )
+            up_part = inverse * (
+                ups_ref[at, :]
+                + jnp.dot(up_ref[chunk, width:], rows, preferred_element_type=jnp.float32)
+            )
+            silu = gate_part / (1.0 + jnp.exp(-gate_part))
+            hidden[:, at] = (silu * up_part * share).T.astype(jnp.bfloat16)
+    down_product(hidden, (down_a, down_b), out_ref, 0)
+
+
+def rest_expert_kernel(
+    start, hidden_ref, down_a, down_b, first_ref, sent_ref, kept_ref, value_ref
+):
+    down_product(hidden_ref, (down_a, down_b), value_ref, start)
     half = first_ref.shape[0] // 2
     sent_ref[:half, :] = first_ref[half:, :].astype(sent_ref.dtype)
     sent_ref[half:, :] = value_ref[half:, :].astype(sent_ref.dtype)
@@ -441,24 +493,20 @@
     kept_ref[half:, :] = value_ref[:half, :]
 
 
-def first_expert_rows(expert, gain, halves, weights):
+def first_expert_rows(device, gain, halves, weights):
     units, model_width = weights[0].shape
     row_count = halves[0].shape[0]
     whole = pl.BlockSpec(memory_space=pltpu.VMEM)
-    anywhere = pl.BlockSpec(memory_space=pltpu.HBM)
-    chunks = 2 * units // UNITS
     return pl.pallas_call(
         first_expert_kernel,
         name="expert_first",
         compiler_params=pltpu.CompilerParams(vmem_limit_bytes=12 << 20),
-        out_shape=(near_shape((row_count, model_width // 2), jnp.float32),) * 2
-        + (near_shape((2 * units, model_width), jnp.bfloat16),) * 3,
-        in_specs=[pl.BlockSpec(memory_space=pltpu.SMEM)] + [whole] * 3 + [anywhere] * 6,
-        out_specs=(whole,) * 5,
+        out_shape=(near_shape((row_count, model_width // 2), jnp.float32),) * 2,
+        in_specs=[pl.BlockSpec(memory_space=pltpu.SMEM)] + [whole] * 9,
+        out_specs=(whole,) * 2,
         scratch_shapes=[
             pltpu.VMEM((model_width + LANES, row_count), jnp.bfloat16),
             pltpu.VMEM((row_count, 2 * units), jnp.bfloat16),
-            pltpu.SemaphoreType.DMA((3, chunks)),
         ],
         cost_estimate=pl.CostEstimate(
             flops=12 * row_count * model_width * units,
@@ -466,29 +514,29 @@
             bytes_accessed=12 * units * model_width,
         ),
     )(
-        expert,
+        device,
         near(gain),
-        *[near(half) for half in halves],
-        *[far(weight) for weight in weights],
-    )
-
-
-def second_expert_rows(expert, gain, halves, weights, totals):
-    units, model_width = weights[0].shape
+        *[near(part) for part in (*halves, *weights)],
+    )
+
+
+def second_expert_rows(device, gain, halves, gates, ups, downs, totals):
+    units, model_width = gates[0].shape
+    units = 2 * units
     row_count = halves[0].shape[0]
     width = model_width // 2
     whole = pl.BlockSpec(memory_space=pltpu.VMEM)
-    gate, up, down = weights
-    gates, ups, stats = pl.pallas_call(
+    gates, ups, downs = [[near(half) for half in pair] for pair in (gates, ups, downs)]
+    gate_parts, up_parts, stats = pl.pallas_call(
         half_expert_kernel,
         name="expert_half",
         compiler_params=pltpu.CompilerParams(vmem_limit_bytes=12 << 20),
         out_shape=(near_shape((units, row_count), jnp.float32),) * 2
         + (near_shape((8, row_count), jnp.float32),),
-        in_specs=[pl.BlockSpec(memory_space=pltpu.SMEM)] + [whole] * 4,
+        in_specs=[pl.BlockSpec(memory_space=pltpu.SMEM)] + [whole] * 6,
         out_specs=(whole,) * 3,
         scratch_shapes=[pltpu.VMEM((width, row_count), jnp.bfloat16)],
-    )(expert, near(gain), near(halves[0]), near(gate), near(up))
+    )(device, near(gain), near(halves[0]), *gates, *ups)
     first, hidden = pl.pallas_call(
         second_expert_kernel,
         name="expert_second",
@@ -497,10 +545,19 @@
             near_shape((row_count, width), jnp.bfloat16),
             near_shape((row_count, units), jnp.bfloat16),
         ),
-        in_specs=[whole] * 8,
+        in_specs=[whole] * 11,
         out_specs=(whole, whole),
         scratch_shapes=[pltpu.VMEM((width, row_count), jnp.bfloat16)],
-    )(near(gain), near(halves[1]), near(gates), near(ups), near(stats), near(gate), near(up), near(down))
+    )(
+        near(gain),
+        near(halves[1]),
+        near(gate_parts),
+        near(up_parts),
+        near(stats),
+        *gates,
+        *ups,
+        *downs,
+    )
     sent, kept = pl.pallas_call(
         functools.partial(rest_expert_kernel, width),
         name="expert_rest",
@@ -509,15 +566,15 @@
             near_shape((row_count, width), jnp.bfloat16),
             near_shape((row_count, width), jnp.float32),
         ),
-        in_specs=[whole] * 3,
+        in_specs=[whole] * 4,
         out_specs=(whole, whole),
         scratch_shapes=[pltpu.VMEM((row_count, width), jnp.float32)],
-    )(near(hidden), near(weights[2]), near(totals[1]))
+    )(near(hidden), *downs, near(totals[1]))
     return [(first, totals[0]), (sent, kept)]
 
 
 def attention_rows(
-    queries, patch_keys, patch_values, other_keys, other_values, table, row_count, orders
+    queries, patch_keys, patch_values, other_keys, other_values, gain, table, row_count, orders
 ):
     model_width = patch_values.shape[1]
     part_width = model_width // PARTS + LANES
@@ -545,7 +602,7 @@
         )
 
     anywhere = pl.BlockSpec(memory_space=pltpu.HBM)
-    query_rows, own_keys, own_values = pl.pallas_call(
+    query_rows, own_keys, own_values, gain = pl.pallas_call(
         functools.partial(stage_kernel, row_count, masks),
         name="stage_in",
         compiler_params=pltpu.CompilerParams(vmem_limit_bytes=4 << 20),
@@ -553,11 +610,12 @@
             near_shape((rows, queries.shape[1]), jnp.bfloat16),
             near_shape(patch_keys.shape, jnp.bfloat16),
             near_shape(patch_values.shape, jnp.bfloat16),
+            near_shape(gain.shape, jnp.float32),
         ),
-        in_specs=[pl.BlockSpec(memory_space=pltpu.SMEM)] + [anywhere] * 3,
-        out_specs=(whole,) * 3,
-        scratch_shapes=[pltpu.SemaphoreType.DMA((2 + (1 << stages),))],
-    )(device_index.reshape(1), far(queries), far(patch_keys), far(patch_values))
+        in_specs=[pl.BlockSpec(memory_space=pltpu.SMEM)] + [anywhere] * 4,
+        out_specs=(whole,) * 4,
+        scratch_shapes=[pltpu.SemaphoreType.DMA((3 + (1 << stages),))],
+    )(device_index.reshape(1), far(queries), far(patch_keys), far(patch_values), far(gain))
     operands = (query_rows, own_keys, other_keys, own_values, other_values)
     chains = []
     for part in range(PARTS):
@@ -600,7 +658,7 @@
             out_specs=(whole, whole),
         )(*operands)
         finished.append((block, projected))
-    return finished
+    return finished, gain
 
 
 def on_device(
@@ -629,30 +687,44 @@
     weights = []
     for own in halves:
         weights += [own, partner(own, "wide", 0)]
-    finished = attention_rows(
+    gain = norm_gain.reshape(1, model_width)
+    finished, gain = attention_rows(
         queries,
         patch_keys,
         patch_values,
         other_keys,
         other_values,
+        gain,
         score_table,
         row_count,
         merge_order,
     )
     blocks = [block for block, _ in finished]
-    gain = norm_gain.reshape(1, model_width)
     stages = len(gather_order[0])
-    came = []
-    for part in range(PARTS):
-        for stage in range(stages - 1):
-            arrived = exchange(blocks[part], gather_order, stage)
-            blocks[part] = jnp.concatenate([blocks[part], arrived], axis=0)
-        came.append(exchange(blocks[part], gather_order, stages - 1))
-    expert = (device_index // 2).reshape(1)
-    *totals, gate, up, down = first_expert_rows(expert, gain, blocks, weights)
+    own_weights = fetched(weights[::2])
+    arrived = {}
+    for stage in range(stages):
+        for part in range(PARTS):
+            arrived[part] = exchange(blocks[part], gather_order, stage)
+            if stage < stages - 1:
+                last = stage == stages - 2
+                blocks[part], passed = joined(
+                    blocks[part], arrived[part], own_weights if last else ()
+                )
+                own_weights = passed if last else own_weights
+    came = [arrived[part] for part in range(PARTS)]
+    device = device_index.reshape(1)
+    gate_a, up_a, down_a = own_weights
+    gate_b, up_b, down_b = weights[1::2]
+    totals = first_expert_rows(
+        device, gain, blocks, (*own_weights, gate_b, up_b, down_b)
+    )
+    gates = (gate_a, gate_b)
     outputs = []
     for part, (sent, kept) in enumerate(
-        second_expert_rows(expert, gain, came, (gate, up, down), totals)
+        second_expert_rows(
+            device, gain, came, gates, (up_a, up_b), (down_a, down_b), totals
+        )
     ):
         for stage in range(stages + 1):
             arrived = exchange(sent, scatter_order[part], stage)

time: 81.3 us -> 96.2 us (1.18)
  Pallas kernels: 16.3 us -> 24.9 us
  starting transfers between devices: 26.2 us -> 32.5 us
  waiting for transfers between devices: 37.2 us -> 34.1 us
  local copies, waits for them, and re-layouts: 0.17 us -> 3.14 us
    ppermute x20, starting transfers between devices: 24.8 us -> 31.1 us  [exchange(): return lax.ppermute(value, 'wide', pairs)]
    pallas_call x0 -> x5, Pallas kernels: none -> 3.42 us  [the longest x1 3.34 us: fetched(): pl.pallas_call(fetch_kernel, compiler_params=pltpu.CompilerParams(vmem_li...]
    ppermute x20, waiting for transfers between devices: 34.8 us -> 31.7 us  [exchange(): return lax.ppermute(value, 'wide', pairs)]
    pallas_call x1, Pallas kernels: 2.1 us -> 4.72 us  [second_expert_rows(): pl.pallas_call(second_expert_kernel, name='expert_second', compiler_param...]
    pallas_call x1, Pallas kernels: 1.6 us -> 4.13 us  [second_expert_rows(): pl.pallas_call(half_expert_kernel, name='expert_half', compiler_params=pl...]
    unnamed x10, local copies, waits for them, and re-layouts: 0.05 us -> 1.7 us
    reshape x1, local copies, waits for them, and re-layouts: 0.01 us -> 1.36 us  [on_device(): gain = norm_gain.reshape(1, model_width)]
  transfers between devices with their start and end apart: 25 -> 25, of which waited for: 17 -> 14; matrix products, arithmetic and copies ran while one was open for 1% -> 2% of each run, Pallas kernels for 18% -> 20%
where the time goes in v6:
time: 96.2 us; the launch traced here: 95.9 us
  waiting for transfers between devices  34.1 us (35%)
  starting transfers between devices  32.5 us (34%)
  Pallas kernels  24.9 us (26%)
  local copies, waits for them, and re-layouts  3.14 us (3%)
  other arithmetic  1.01 us (1%)
    ppermute x20, waiting for transfers between devices, exchange(): return lax.ppermute(value, 'wide', pairs)  31.7 us
    ppermute x20, starting transfers between devices, exchange(): return lax.ppermute(value, 'wide', pairs)  31.1 us
    pallas_call x1, Pallas kernels, first_expert_rows(): pl.pallas_call(first_expert_kernel, name='expert_first', compiler_params=...  6.7 us
    pallas_call x1, Pallas kernels, second_expert_rows(): pl.pallas_call(second_expert_kernel, name='expert_second', compiler_param...  4.72 us
    pallas_call x1, Pallas kernels, second_expert_rows(): pl.pallas_call(half_expert_kernel, name='expert_half', compiler_params=pl...  4.13 us
    pallas_call x1, Pallas kernels, fetched(): pl.pallas_call(fetch_kernel, compiler_params=pltpu.CompilerParams(vmem_li...  3.34 us
    pallas_call x2, Pallas kernels, attention_rows(): pl.pallas_call(functools.partial(attend_kernel, HEADS, part, part_heads),...  2.74 us
    ppermute x5, waiting for transfers between devices, partner(): return lax.ppermute(value, axis, pairs)  2.35 us
  transfers between devices with their start and end apart: 25, of which 14 were waited for; matrix products, arithmetic and copies ran while one was open for 2% of the time, Pallas kernels for 20%

profile of v6, /device:TPU:0, one launch (start us, length us, event | category | flops | bytes accessed | tf_op | source)
XLA Modules:
  0.0 95.9 jit_solution(14660137330374243193)
XLA Ops:
  0.5 2.3 %collective-permute-done.keys_b = bf16[128,1152]{1,0:T(8,128)(2,1)S(1)} collective-permute-done((bf16[128,1152]{1,0:T(8,128)(2,1)}, bf16[128,1152]{1,0:T(8,128)(2,1)S(1)}, u32[]{:S(2)}, u32[]{:S(2)}) %collective-permute-start) | collective-permute-done | bytes 294944 | tf_op jit(solution)/shard_map/ppermute | solution.py:33
  4.5 1.4 %reshape.14.gain_ref = f32[1,2560]{1,0:T(1,128)} reshape(f32[2560]{0:T(1024)} %param.12) | data formatting | bytes 20480 | tf_op jit(solution)/shard_map/reshape | solution.py:690
  5.8 1.3 %stage_in.1 = (bf16[128,1152]{1,0:T(8,128)(2,1)S(1)}, bf16[128,1152]{1,0:T(8,128)(2,1)S(1)}, bf16[128,2560]{1,0:T(8,128)(2,1)S(1)}, f32[1,2560]{1,0:T(1,128)S(1)}) custom-call(s32[1]{0:T(128)} %bitcast.device_ref, bf16[256,1152]{1,0:T(8,128)(2,1)} %queries_ref.1, bf16[128,1152]{1,0:T(8,128)(2,1)} %keys_ref.1, bf16[128,2560]{1,0:T(8,128)(2,1)} %values_ref.1, ...), custom_call_target="tpu_custom_call" | custom-call | tf_op jit(solution)/shard_map/stage_in/pallas_call | solution.py:605
  8.1 1.2 %shard_map.91 = (bf16[64,1408]{1,0:T(8,128)(2,1)S(1)}, f32[64,1408]{1,0:T(8,128)S(1)}) custom-call(bf16[128,1152]{1,0:T(8,128)(2,1)S(1)} %get-tuple-element.50.query_ref, bf16[128,1152]{1,0:T(8,128)(2,1)S(1)} %get-tuple-element.51.keys_a, bf16[128,1152]{1,0:T(8,128)(2,1)S(1)} %copy-done.1, bf16[128,2560]{1,0:T(8,128)(2,1)S(1)} %get-tuple-element.53.values_a, ...), custom_call_target="tpu_custom_call" | custom-call | tf_op jit(solution)/shard_map/pallas_call | solution.py:622
  9.3 2.7 %collective-permute-start.2 = (bf16[64,1408]{1,0:T(8,128)(2,1)S(1)}, bf16[64,1408]{1,0:T(8,128)(2,1)S(1)}, u32[]{:S(2)}, u32[]{:S(2)}) collective-permute-start(bf16[64,1408]{1,0:T(8,128)(2,1)S(1)} %get-tuple-element.56), channel_id=1, source_target_pairs={{0,2},{1,5},{2,0},{3,7},{4,6},{5,1},{6,4},{7,3},{8,10},{9,13},{10,... | collective-permute-start | bytes 540680 | tf_op jit(solution)/shard_map/ppermute | solution.py:52
  12.0 1.5 %shard_map.98 = (bf16[64,1408]{1,0:T(8,128)(2,1)S(1)}, f32[64,1408]{1,0:T(8,128)S(1)}) custom-call(bf16[128,1152]{1,0:T(8,128)(2,1)S(1)} %get-tuple-element.50.query_ref, bf16[128,1152]{1,0:T(8,128)(2,1)S(1)} %get-tuple-element.51.keys_a, bf16[128,1152]{1,0:T(8,128)(2,1)S(1)} %copy-done.2, bf16[128,2560]{1,0:T(8,128)(2,1)S(1)} %get-tuple-element.53.values_a, ...), custom_call_target="tpu_custom_call" | custom-call | tf_op jit(solution)/shard_map/pallas_call | solution.py:622
  13.7 1.8 %collective-permute-done.2.came_ref = bf16[64,1408]{1,0:T(8,128)(2,1)S(1)} collective-permute-done((bf16[64,1408]{1,0:T(8,128)(2,1)S(1)}, bf16[64,1408]{1,0:T(8,128)(2,1)S(1)}, u32[]{:S(2)}, u32[]{:S(2)}) %collective-permute-start.2) | collective-permute-done | bytes 180256 | tf_op jit(solution)/shard_map/ppermute | solution.py:52
  15.7 2.1 %collective-permute-start.3 = (bf16[32,1408]{1,0:T(8,128)(2,1)S(1)}, bf16[32,1408]{1,0:T(8,128)(2,1)S(1)}, u32[]{:S(2)}, u32[]{:S(2)}) collective-permute-start(bf16[32,1408]{1,0:T(8,128)(2,1)S(1)} %get-tuple-element.58), channel_id=1, source_target_pairs={{0,4},{1,9},{2,6},{3,11},{4,0},{5,13},{6,2},{7,15},{8,12},{9,1},{1... | collective-permute-start | bytes 270344 | tf_op jit(solution)/shard_map/ppermute | solution.py:52
  18.0 2.4 %collective-permute-done.3.came_ref = bf16[32,1408]{1,0:T(8,128)(2,1)S(1)} collective-permute-done((bf16[32,1408]{1,0:T(8,128)(2,1)S(1)}, bf16[32,1408]{1,0:T(8,128)(2,1)S(1)}, u32[]{:S(2)}, u32[]{:S(2)}) %collective-permute-start.3) | collective-permute-done | bytes 90144 | tf_op jit(solution)/shard_map/ppermute | solution.py:52
  20.5 2.1 %collective-permute-start.4 = (bf16[32,1408]{1,0:T(8,128)(2,1)S(1)}, bf16[32,1408]{1,0:T(8,128)(2,1)S(1)}, u32[]{:S(2)}, u32[]{:S(2)}) collective-permute-start(bf16[32,1408]{1,0:T(8,128)(2,1)S(1)} %get-tuple-element.60), channel_id=1, source_target_pairs={{0,8},{1,3},{2,10},{3,1},{4,12},{5,7},{6,14},{7,5},{8,0},{9,11},{1... | collective-permute-start | bytes 270344 | tf_op jit(solution)/shard_map/ppermute | solution.py:52
  22.7 2.5 %collective-permute-done.4.came_ref = bf16[32,1408]{1,0:T(8,128)(2,1)S(1)} collective-permute-done((bf16[32,1408]{1,0:T(8,128)(2,1)S(1)}, bf16[32,1408]{1,0:T(8,128)(2,1)S(1)}, u32[]{:S(2)}, u32[]{:S(2)}) %collective-permute-start.4) | collective-permute-done | bytes 90144 | tf_op jit(solution)/shard_map/ppermute | solution.py:52
  25.4 3.1 %collective-permute-start.5 = (bf16[32,1408]{1,0:T(8,128)(2,1)S(1)}, bf16[32,1408]{1,0:T(8,128)(2,1)S(1)}, u32[]{:S(2)}, u32[]{:S(2)}) collective-permute-start(bf16[32,1408]{1,0:T(8,128)(2,1)S(1)} %get-tuple-element.63.own_ref), channel_id=1, source_target_pairs={{0,16},{1,17},{2,18},{3,19},{4,20},{5,21},{6,22},{7,23},{8,24},{9,... | collective-permute-start | bytes 270344 | tf_op jit(solution)/shard_map/ppermute | solution.py:52
  28.8 1.6 %collective-permute-start.8 = (bf16[32,1408]{1,0:T(8,128)(2,1)S(1)}, bf16[32,1408]{1,0:T(8,128)(2,1)S(1)}, u32[]{:S(2)}, u32[]{:S(2)}) collective-permute-start(bf16[32,1408]{1,0:T(8,128)(2,1)S(1)} %get-tuple-element.74), channel_id=1, source_target_pairs={{0,4},{1,9},{2,6},{3,11},{4,0},{5,13},{6,2},{7,15},{8,12},{9,1},{1... | collective-permute-start | bytes 270344 | tf_op jit(solution)/shard_map/ppermute | solution.py:52
  31.1 1.9 %collective-permute-start.6 = (bf16[64,1408]{1,0:T(8,128)(2,1)S(1)}, bf16[64,1408]{1,0:T(8,128)(2,1)S(1)}, u32[]{:S(2)}, u32[]{:S(2)}) collective-permute-start(bf16[64,1408]{1,0:T(8,128)(2,1)S(1)} %shard_map.95.own_ref), channel_id=1, source_target_pairs={{0,4},{1,5},{2,6},{3,7},{4,0},{5,1},{6,2},{7,3},{8,12},{9,13},{10,... | collective-permute-start | bytes 540680 | tf_op jit(solution)/shard_map/ppermute | solution.py:52
  33.6 1.6 %collective-permute-start.9 = (bf16[32,1408]{1,0:T(8,128)(2,1)S(1)}, bf16[32,1408]{1,0:T(8,128)(2,1)S(1)}, u32[]{:S(2)}, u32[]{:S(2)}) collective-permute-start(bf16[32,1408]{1,0:T(8,128)(2,1)S(1)} %get-tuple-element.76), channel_id=1, source_target_pairs={{0,8},{1,3},{2,10},{3,1},{4,12},{5,7},{6,14},{7,5},{8,0},{9,11},{1... | collective-permute-start | bytes 270344 | tf_op jit(solution)/shard_map/ppermute | solution.py:52
  35.2 3.5 %collective-permute-done.9.came_ref = bf16[32,1408]{1,0:T(8,128)(2,1)S(1)} collective-permute-done((bf16[32,1408]{1,0:T(8,128)(2,1)S(1)}, bf16[32,1408]{1,0:T(8,128)(2,1)S(1)}, u32[]{:S(2)}, u32[]{:S(2)}) %collective-permute-start.9) | collective-permute-done | bytes 90144 | tf_op jit(solution)/shard_map/ppermute | solution.py:52
  39.0 2.1 %collective-permute-start.10 = (bf16[32,1280]{1,0:T(8,128)(2,1)S(1)}, bf16[32,1280]{1,0:T(8,128)(2,1)S(1)}, u32[]{:S(2)}, u32[]{:S(2)}) collective-permute-start(bf16[32,1280]{1,0:T(8,128)(2,1)S(1)} %get-tuple-element.77.own_ref), channel_id=1, source_target_pairs={{0,16},{1,17},{2,18},{3,19},{4,20},{5,21},{6,22},{7,23},{8,24},{9,... | collective-permute-start | bytes 245768 | tf_op jit(solution)/shard_map/ppermute | solution.py:52
  41.1 3.3 %shard_map.96 = (bf16[512,2560]{1,0:T(8,128)(2,1)S(1)}, bf16[512,2560]{1,0:T(8,128)(2,1)S(1)}, bf16[512,2560]{1,0:T(8,128)(2,1)S(1)}) custom-call(bf16[512,2560]{1,0:T(8,128)(2,1)} %refs_0_, bf16[512,2560]{1,0:T(8,128)(2,1)} %refs_1_, bf16[512,2560]{1,0:T(8,128)(2,1)} %refs_2_), custom_call_target="tpu_custom_call" | custom-call | tf_op jit(solution)/shard_map/pallas_call | solution.py:337
  44.5 1.6 %collective-permute-start.16 = (bf16[128,1408]{1,0:T(8,128)(2,1)S(1)}, bf16[128,1408]{1,0:T(8,128)(2,1)S(1)}, u32[]{:S(2)}, u32[]{:S(2)}) collective-permute-start(bf16[128,1408]{1,0:T(8,128)(2,1)S(1)} %get-tuple-element.70.rows_a), channel_id=1, source_target_pairs={{0,2},{1,9},{2,0},{3,11},{4,6},{5,13},{6,4},{7,15},{8,10},{9,1},{1... | collective-permute-start | bytes 1081352 | tf_op jit(solution)/shard_map/ppermute | solution.py:52
  47.2 4.2 %collective-permute-done.11.came_ref = bf16[64,1280]{1,0:T(8,128)(2,1)S(1)} collective-permute-done((bf16[64,1280]{1,0:T(8,128)(2,1)S(1)}, bf16[64,1280]{1,0:T(8,128)(2,1)S(1)}, u32[]{:S(2)}, u32[]{:S(2)}) %collective-permute-start.11) | collective-permute-done | bytes 163872 | tf_op jit(solution)/shard_map/ppermute | solution.py:52
  52.1 4.1 %expert_half.1 = (f32[1024,128]{1,0:T(8,128)S(1)}, f32[1024,128]{1,0:T(8,128)S(1)}, f32[8,128]{1,0:T(8,128)S(1)}) custom-call(s32[1]{0:T(128)} %bitcast.device_ref, f32[1,2560]{1,0:T(1,128)S(1)} %get-tuple-element.62.gain_ref, bf16[128,1408]{1,0:T(8,128)(2,1)S(1)} %collective-permute-done.16.rows_ref, bf16[512,2560]{1,0:T(8,128)(2,1)S(1)} %get-tuple-element.82.gate_a, ...), custom_call_target="tpu_custom_call" | custom-call | tf_op jit(solution)/shard_map/expert_half/pallas_call | solution.py:530
  56.2 6.7 %expert_first.1 = (f32[128,1280]{1,0:T(8,128)S(1)}, f32[128,1280]{1,0:T(8,128)S(1)}) custom-call(s32[1]{0:T(128)} %bitcast.device_ref, f32[1,2560]{1,0:T(1,128)S(1)} %get-tuple-element.62.gain_ref, bf16[128,1408]{1,0:T(8,128)(2,1)S(1)} %get-tuple-element.70.rows_a, bf16[128,1280]{1,0:T(8,128)(2,1)S(1)} %get-tuple-element.81.rows_b, ...), custom_call_target="tpu_custom_call" | custom-call | flops 2013265920 | bytes 15728640 | tf_op jit(solution)/shard_map/expert_first/pallas_call | solution.py:500
  62.9 4.7 %expert_second.1 = (bf16[128,1280]{1,0:T(8,128)(2,1)S(1)}, bf16[128,1024]{1,0:T(8,128)(2,1)S(1)}) custom-call(f32[1,2560]{1,0:T(1,128)S(1)} %get-tuple-element.62.gain_ref, bf16[128,1280]{1,0:T(8,128)(2,1)S(1)} %collective-permute-done.15.rows_ref, f32[1024,128]{1,0:T(8,128)S(1)} %get-tuple-element.86.gates_ref, f32[1024,128]{1,0:T(8,128)S(1)} %get-tuple-element.87.ups_ref, ...), custom_call_target="tpu_custom_call" | custom-call | tf_op jit(solution)/shard_map/expert_second/pallas_call | solution.py:540
  68.2 1.4 %collective-permute-start.21 = (bf16[128,1280]{1,0:T(8,128)(2,1)S(1)}, bf16[128,1280]{1,0:T(8,128)(2,1)S(1)}, u32[]{:S(2)}, u32[]{:S(2)}) collective-permute-start(bf16[128,1280]{1,0:T(8,128)(2,1)S(1)} %get-tuple-element.94), channel_id=1, source_target_pairs={{0,4},{1,5},{2,6},{3,7},{4,0},{5,1},{6,2},{7,3},{8,12},{9,13},{10,... | collective-permute-start | bytes 983048 | tf_op jit(solution)/shard_map/ppermute | solution.py:52
  69.6 1.3 %collective-permute-start.17 = (bf16[128,1280]{1,0:T(8,128)(2,1)S(1)}, bf16[128,1280]{1,0:T(8,128)(2,1)S(1)}, u32[]{:S(2)}, u32[]{:S(2)}) collective-permute-start(bf16[128,1280]{1,0:T(8,128)(2,1)S(1)} %get-tuple-element.89), channel_id=1, source_target_pairs={{0,2},{1,9},{2,0},{3,11},{4,6},{5,13},{6,4},{7,15},{8,10},{9,1},{1... | collective-permute-start | bytes 983048 | tf_op jit(solution)/shard_map/ppermute | solution.py:52
  70.9 6.3 %collective-permute-done.21 = bf16[128,1280]{1,0:T(8,128)(2,1)S(1)} collective-permute-done((bf16[128,1280]{1,0:T(8,128)(2,1)S(1)}, bf16[128,1280]{1,0:T(8,128)(2,1)S(1)}, u32[]{:S(2)}, u32[]{:S(2)}) %collective-permute-start.21) | collective-permute-done | bytes 327712 | tf_op jit(solution)/shard_map/ppermute | solution.py:52
  77.2 1.6 %collective-permute-start.22 = (bf16[64,1280]{1,0:T(8,128)(2,1)S(1)}, bf16[64,1280]{1,0:T(8,128)(2,1)S(1)}, u32[]{:S(2)}, u32[]{:S(2)}) collective-permute-start(bf16[64,1280]{1,0:T(8,128)(2,1)S(1)} %slice.86), channel_id=1, source_target_pairs={{0,2},{1,9},{2,0},{3,11},{4,6},{5,13},{6,4},{7,15},{8,10},{9,1},{1... | collective-permute-start | bytes 491528 | tf_op jit(solution)/shard_map/ppermute | solution.py:52
  80.0 2.6 %collective-permute-done.22 = bf16[64,1280]{1,0:T(8,128)(2,1)S(1)} collective-permute-done((bf16[64,1280]{1,0:T(8,128)(2,1)S(1)}, bf16[64,1280]{1,0:T(8,128)(2,1)S(1)}, u32[]{:S(2)}, u32[]{:S(2)}) %collective-permute-start.22) | collective-permute-done | bytes 163872 | tf_op jit(solution)/shard_map/ppermute | solution.py:52
  82.7 1.9 %collective-permute-start.23 = (bf16[32,1280]{1,0:T(8,128)(2,1)S(1)}, bf16[32,1280]{1,0:T(8,128)(2,1)S(1)}, u32[]{:S(2)}, u32[]{:S(2)}) collective-permute-start(bf16[32,1280]{1,0:T(8,128)(2,1)S(1)} %slice.88), channel_id=1, source_target_pairs={{0,16},{1,17},{2,18},{3,19},{4,20},{5,21},{6,22},{7,23},{8,24},{9,... | collective-permute-start | bytes 245768 | tf_op jit(solution)/shard_map/ppermute | solution.py:52
  85.8 2.3 %collective-permute-done.23 = bf16[32,1280]{1,0:T(8,128)(2,1)S(1)} collective-permute-done((bf16[32,1280]{1,0:T(8,128)(2,1)S(1)}, bf16[32,1280]{1,0:T(8,128)(2,1)S(1)}, u32[]{:S(2)}, u32[]{:S(2)}) %collective-permute-start.23) | collective-permute-done | bytes 81952 | tf_op jit(solution)/shard_map/ppermute | solution.py:52
  88.1 2.0 %collective-permute-start.24 = (bf16[16,1280]{1,0:T(8,128)(2,1)S(1)}, bf16[16,1280]{1,0:T(8,128)(2,1)S(1)}, u32[]{:S(2)}, u32[]{:S(2)}) collective-permute-start(bf16[16,1280]{1,0:T(8,128)(2,1)S(1)} %slice.90), channel_id=1, source_target_pairs={{0,8},{1,3},{2,10},{3,1},{4,12},{5,7},{6,14},{7,5},{8,0},{9,11},{1... | collective-permute-start | bytes 122888 | tf_op jit(solution)/shard_map/ppermute | solution.py:52
  92.2 3.1 %collective-permute-done.20 = bf16[16,1280]{1,0:T(8,128)(2,1)S(1)} collective-permute-done((bf16[16,1280]{1,0:T(8,128)(2,1)S(1)}, bf16[16,1280]{1,0:T(8,128)(2,1)S(1)}, u32[]{:S(2)}, u32[]{:S(2)}) %collective-permute-start.20) | collective-permute-done | bytes 40992 | tf_op jit(solution)/shard_map/ppermute | solution.py:52
  (65 shorter events, 13.5 us)
Async XLA Ops:
  0.0 3.6 %collective-permute-start.1 = (bf16[128,2560]{1,0:T(8,128)(2,1)}, bf16[128,2560]{1,0:T(8,128)(2,1)S(1)}, u32[]{:S(2)}, u32[]{:S(2)}) collective-permute-start(bf16[128,2560]{1,0:T(8,128)(2,1)} %values_ref.1), channel_id=1, source_target_pairs={{0,1},{1,0},{2,3},{3,2},{4,5},{5,4},{6,7},{7,6},{8,9},{9,8},{10,11... | collective-permute-start | bytes 1966088 | tf_op jit(solution)/shard_map/ppermute | solution.py:33
  0.5 2.4 %collective-permute-start = (bf16[128,1152]{1,0:T(8,128)(2,1)}, bf16[128,1152]{1,0:T(8,128)(2,1)S(1)}, u32[]{:S(2)}, u32[]{:S(2)}) collective-permute-start(bf16[128,1152]{1,0:T(8,128)(2,1)} %keys_ref.1), channel_id=1, source_target_pairs={{0,1},{1,0},{2,3},{3,2},{4,5},{5,4},{6,7},{7,6},{8,9},{9,8},{10,11... | collective-permute-start | bytes 884744 | tf_op jit(solution)/shard_map/ppermute | solution.py:33
  2.9 0.7 copy-start
  3.6 48.5 %collective-permute-start.12 = (bf16[512,2560]{1,0:T(8,128)(2,1)}, bf16[512,2560]{1,0:T(8,128)(2,1)}, u32[]{:S(2)}, u32[]{:S(2)}) collective-permute-start(bf16[512,2560]{1,0:T(8,128)(2,1)} %refs_0_), channel_id=1, source_target_pairs={{0,1},{1,0},{2,3},{3,2},{4,5},{5,4},{6,7},{7,6},{8,9},{9,8},{10,11... | collective-permute-start | bytes 7864328 | tf_op jit(solution)/shard_map/ppermute | solution.py:33
  4.0 48.1 %collective-permute-start.13 = (bf16[512,2560]{1,0:T(8,128)(2,1)}, bf16[512,2560]{1,0:T(8,128)(2,1)}, u32[]{:S(2)}, u32[]{:S(2)}) collective-permute-start(bf16[512,2560]{1,0:T(8,128)(2,1)} %refs_1_), channel_id=1, source_target_pairs={{0,1},{1,0},{2,3},{3,2},{4,5},{5,4},{6,7},{7,6},{8,9},{9,8},{10,11... | collective-permute-start | bytes 7864328 | tf_op jit(solution)/shard_map/ppermute | solution.py:33
  4.1 52.1 %collective-permute-start.14 = (bf16[512,2560]{1,0:T(8,128)(2,1)}, bf16[512,2560]{1,0:T(8,128)(2,1)S(1)}, u32[]{:S(2)}, u32[]{:S(2)}) collective-permute-start(bf16[512,2560]{1,0:T(8,128)(2,1)} %refs_2_), channel_id=1, source_target_pairs={{0,1},{1,0},{2,3},{3,2},{4,5},{5,4},{6,7},{7,6},{8,9},{9,8},{10,11... | collective-permute-start | bytes 7864328 | tf_op jit(solution)/shard_map/ppermute | solution.py:33
  4.5 7.6 %copy-start.2 = (bf16[128,1152]{1,0:T(8,128)(2,1)S(1)}, bf16[128,1152]{1,0:T(8,128)(2,1)}, u32[]{:S(2)}) copy-start(bf16[128,1152]{1,0:T(8,128)(2,1)} %copy-done) | copy-start | bytes 884740
  5.8 12.0 %copy-start.4 = (s32[16,6]{0,1:T(8,128)S(1)}, s32[16,6]{0,1:T(8,128)}, u32[]{:S(2)}) copy-start(s32[16,6]{0,1:T(8,128)} %param.13) | copy-start | bytes 1156
  7.1 10.7 %copy-start.3 = (s32[16,6]{0,1:T(8,128)S(1)}, s32[16,6]{0,1:T(8,128)}, u32[]{:S(2)}) copy-start(s32[16,6]{0,1:T(8,128)} %param.14) | copy-start | bytes 1156
  7.2 1.0 %copy-start.1 = (bf16[128,1152]{1,0:T(8,128)(2,1)S(1)}, bf16[128,1152]{1,0:T(8,128)(2,1)}, u32[]{:S(2)}) copy-start(bf16[128,1152]{1,0:T(8,128)(2,1)} %copy-done) | copy-start | bytes 884740
  9.3 6.2 %collective-permute-start.2 = (bf16[64,1408]{1,0:T(8,128)(2,1)S(1)}, bf16[64,1408]{1,0:T(8,128)(2,1)S(1)}, u32[]{:S(2)}, u32[]{:S(2)}) collective-permute-start(bf16[64,1408]{1,0:T(8,128)(2,1)S(1)} %get-tuple-element.56), channel_id=1, source_target_pairs={{0,2},{1,5},{2,0},{3,7},{4,6},{5,1},{6,4},{7,3},{8,10},{9,13},{10,... | collective-permute-start | bytes 540680 | tf_op jit(solution)/shard_map/ppermute | solution.py:52
  13.6 15.0 %collective-permute-start.7 = (bf16[64,1408]{1,0:T(8,128)(2,1)S(1)}, bf16[64,1408]{1,0:T(8,128)(2,1)S(1)}, u32[]{:S(2)}, u32[]{:S(2)}) collective-permute-start(bf16[64,1408]{1,0:T(8,128)(2,1)S(1)} %get-tuple-element.72), channel_id=1, source_target_pairs={{0,2},{1,5},{2,0},{3,7},{4,6},{5,1},{6,4},{7,3},{8,10},{9,13},{10,... | collective-permute-start | bytes 540680 | tf_op jit(solution)/shard_map/ppermute | solution.py:52
  15.7 4.6 %collective-permute-start.3 = (bf16[32,1408]{1,0:T(8,128)(2,1)S(1)}, bf16[32,1408]{1,0:T(8,128)(2,1)S(1)}, u32[]{:S(2)}, u32[]{:S(2)}) collective-permute-start(bf16[32,1408]{1,0:T(8,128)(2,1)S(1)} %get-tuple-element.58), channel_id=1, source_target_pairs={{0,4},{1,9},{2,6},{3,11},{4,0},{5,13},{6,2},{7,15},{8,12},{9,1},{1... | collective-permute-start | bytes 270344 | tf_op jit(solution)/shard_map/ppermute | solution.py:52
  20.5 4.7 %collective-permute-start.4 = (bf16[32,1408]{1,0:T(8,128)(2,1)S(1)}, bf16[32,1408]{1,0:T(8,128)(2,1)S(1)}, u32[]{:S(2)}, u32[]{:S(2)}) collective-permute-start(bf16[32,1408]{1,0:T(8,128)(2,1)S(1)} %get-tuple-element.60), channel_id=1, source_target_pairs={{0,8},{1,3},{2,10},{3,1},{4,12},{5,7},{6,14},{7,5},{8,0},{9,11},{1... | collective-permute-start | bytes 270344 | tf_op jit(solution)/shard_map/ppermute | solution.py:52
  25.4 5.6 %collective-permute-start.5 = (bf16[32,1408]{1,0:T(8,128)(2,1)S(1)}, bf16[32,1408]{1,0:T(8,128)(2,1)S(1)}, u32[]{:S(2)}, u32[]{:S(2)}) collective-permute-start(bf16[32,1408]{1,0:T(8,128)(2,1)S(1)} %get-tuple-element.63.own_ref), channel_id=1, source_target_pairs={{0,16},{1,17},{2,18},{3,19},{4,20},{5,21},{6,22},{7,23},{8,24},{9,... | collective-permute-start | bytes 270344 | tf_op jit(solution)/shard_map/ppermute | solution.py:52
  28.8 4.6 %collective-permute-start.8 = (bf16[32,1408]{1,0:T(8,128)(2,1)S(1)}, bf16[32,1408]{1,0:T(8,128)(2,1)S(1)}, u32[]{:S(2)}, u32[]{:S(2)}) collective-permute-start(bf16[32,1408]{1,0:T(8,128)(2,1)S(1)} %get-tuple-element.74), channel_id=1, source_target_pairs={{0,4},{1,9},{2,6},{3,11},{4,0},{5,13},{6,2},{7,15},{8,12},{9,1},{1... | collective-permute-start | bytes 270344 | tf_op jit(solution)/shard_map/ppermute | solution.py:52
  31.1 13.3 %collective-permute-start.6 = (bf16[64,1408]{1,0:T(8,128)(2,1)S(1)}, bf16[64,1408]{1,0:T(8,128)(2,1)S(1)}, u32[]{:S(2)}, u32[]{:S(2)}) collective-permute-start(bf16[64,1408]{1,0:T(8,128)(2,1)S(1)} %shard_map.95.own_ref), channel_id=1, source_target_pairs={{0,4},{1,5},{2,6},{3,7},{4,0},{5,1},{6,2},{7,3},{8,12},{9,13},{10,... | collective-permute-start | bytes 540680 | tf_op jit(solution)/shard_map/ppermute | solution.py:52
  33.6 5.2 %collective-permute-start.9 = (bf16[32,1408]{1,0:T(8,128)(2,1)S(1)}, bf16[32,1408]{1,0:T(8,128)(2,1)S(1)}, u32[]{:S(2)}, u32[]{:S(2)}) collective-permute-start(bf16[32,1408]{1,0:T(8,128)(2,1)S(1)} %get-tuple-element.76), channel_id=1, source_target_pairs={{0,8},{1,3},{2,10},{3,1},{4,12},{5,7},{6,14},{7,5},{8,0},{9,11},{1... | collective-permute-start | bytes 270344 | tf_op jit(solution)/shard_map/ppermute | solution.py:52
  39.0 7.0 %collective-permute-start.10 = (bf16[32,1280]{1,0:T(8,128)(2,1)S(1)}, bf16[32,1280]{1,0:T(8,128)(2,1)S(1)}, u32[]{:S(2)}, u32[]{:S(2)}) collective-permute-start(bf16[32,1280]{1,0:T(8,128)(2,1)S(1)} %get-tuple-element.77.own_ref), channel_id=1, source_target_pairs={{0,16},{1,17},{2,18},{3,19},{4,20},{5,21},{6,22},{7,23},{8,24},{9,... | collective-permute-start | bytes 245768 | tf_op jit(solution)/shard_map/ppermute | solution.py:52
  44.5 7.6 %collective-permute-start.16 = (bf16[128,1408]{1,0:T(8,128)(2,1)S(1)}, bf16[128,1408]{1,0:T(8,128)(2,1)S(1)}, u32[]{:S(2)}, u32[]{:S(2)}) collective-permute-start(bf16[128,1408]{1,0:T(8,128)(2,1)S(1)} %get-tuple-element.70.rows_a), channel_id=1, source_target_pairs={{0,2},{1,9},{2,0},{3,11},{4,6},{5,13},{6,4},{7,15},{8,10},{9,1},{1... | collective-permute-start | bytes 1081352 | tf_op jit(solution)/shard_map/ppermute | solution.py:52
  46.0 5.4 %collective-permute-start.11 = (bf16[64,1280]{1,0:T(8,128)(2,1)S(1)}, bf16[64,1280]{1,0:T(8,128)(2,1)S(1)}, u32[]{:S(2)}, u32[]{:S(2)}) collective-permute-start(bf16[64,1280]{1,0:T(8,128)(2,1)S(1)} %shard_map.102.own_ref), channel_id=1, source_target_pairs={{0,4},{1,5},{2,6},{3,7},{4,0},{5,1},{6,2},{7,3},{8,12},{9,13},{10,... | collective-permute-start | bytes 491528 | tf_op jit(solution)/shard_map/ppermute | solution.py:52
  51.4 11.5 %collective-permute-start.15 = (bf16[128,1280]{1,0:T(8,128)(2,1)S(1)}, bf16[128,1280]{1,0:T(8,128)(2,1)S(1)}, u32[]{:S(2)}, u32[]{:S(2)}) collective-permute-start(bf16[128,1280]{1,0:T(8,128)(2,1)S(1)} %get-tuple-element.81.rows_b), channel_id=1, source_target_pairs={{0,2},{1,9},{2,0},{3,11},{4,6},{5,13},{6,4},{7,15},{8,10},{9,1},{1... | collective-permute-start | bytes 983048 | tf_op jit(solution)/shard_map/ppermute | solution.py:52
  68.2 8.9 %collective-permute-start.21 = (bf16[128,1280]{1,0:T(8,128)(2,1)S(1)}, bf16[128,1280]{1,0:T(8,128)(2,1)S(1)}, u32[]{:S(2)}, u32[]{:S(2)}) collective-permute-start(bf16[128,1280]{1,0:T(8,128)(2,1)S(1)} %get-tuple-element.94), channel_id=1, source_target_pairs={{0,4},{1,5},{2,6},{3,7},{4,0},{5,1},{6,2},{7,3},{8,12},{9,13},{10,... | collective-permute-start | bytes 983048 | tf_op jit(solution)/shard_map/ppermute | solution.py:52
  69.6 9.2 %collective-permute-start.17 = (bf16[128,1280]{1,0:T(8,128)(2,1)S(1)}, bf16[128,1280]{1,0:T(8,128)(2,1)S(1)}, u32[]{:S(2)}, u32[]{:S(2)}) collective-permute-start(bf16[128,1280]{1,0:T(8,128)(2,1)S(1)} %get-tuple-element.89), channel_id=1, source_target_pairs={{0,2},{1,9},{2,0},{3,11},{4,6},{5,13},{6,4},{7,15},{8,10},{9,1},{1... | collective-permute-start | bytes 983048 | tf_op jit(solution)/shard_map/ppermute | solution.py:52
  77.2 5.4 %collective-permute-start.22 = (bf16[64,1280]{1,0:T(8,128)(2,1)S(1)}, bf16[64,1280]{1,0:T(8,128)(2,1)S(1)}, u32[]{:S(2)}, u32[]{:S(2)}) collective-permute-start(bf16[64,1280]{1,0:T(8,128)(2,1)S(1)} %slice.86), channel_id=1, source_target_pairs={{0,2},{1,9},{2,0},{3,11},{4,6},{5,13},{6,4},{7,15},{8,10},{9,1},{1... | collective-permute-start | bytes 491528 | tf_op jit(solution)/shard_map/ppermute | solution.py:52
  78.9 5.7 %collective-permute-start.18 = (bf16[64,1280]{1,0:T(8,128)(2,1)S(1)}, bf16[64,1280]{1,0:T(8,128)(2,1)S(1)}, u32[]{:S(2)}, u32[]{:S(2)}) collective-permute-start(bf16[64,1280]{1,0:T(8,128)(2,1)S(1)} %slice.87), channel_id=1, source_target_pairs={{0,4},{1,5},{2,6},{3,7},{4,0},{5,1},{6,2},{7,3},{8,12},{9,13},{10,... | collective-permute-start | bytes 491528 | tf_op jit(solution)/shard_map/ppermute | solution.py:52
  82.7 5.4 %collective-permute-start.23 = (bf16[32,1280]{1,0:T(8,128)(2,1)S(1)}, bf16[32,1280]{1,0:T(8,128)(2,1)S(1)}, u32[]{:S(2)}, u32[]{:S(2)}) collective-permute-start(bf16[32,1280]{1,0:T(8,128)(2,1)S(1)} %slice.88), channel_id=1, source_target_pairs={{0,16},{1,17},{2,18},{3,19},{4,20},{5,21},{6,22},{7,23},{8,24},{9,... | collective-permute-start | bytes 245768 | tf_op jit(solution)/shard_map/ppermute | solution.py:52
  84.6 6.6 %collective-permute-start.19 = (bf16[32,1280]{1,0:T(8,128)(2,1)S(1)}, bf16[32,1280]{1,0:T(8,128)(2,1)S(1)}, u32[]{:S(2)}, u32[]{:S(2)}) collective-permute-start(bf16[32,1280]{1,0:T(8,128)(2,1)S(1)} %slice.89), channel_id=1, source_target_pairs={{0,16},{1,17},{2,18},{3,19},{4,20},{5,21},{6,22},{7,23},{8,24},{9,... | collective-permute-start | bytes 245768 | tf_op jit(solution)/shard_map/ppermute | solution.py:52
  88.1 4.1 %collective-permute-start.24 = (bf16[16,1280]{1,0:T(8,128)(2,1)S(1)}, bf16[16,1280]{1,0:T(8,128)(2,1)S(1)}, u32[]{:S(2)}, u32[]{:S(2)}) collective-permute-start(bf16[16,1280]{1,0:T(8,128)(2,1)S(1)} %slice.90), channel_id=1, source_target_pairs={{0,8},{1,3},{2,10},{3,1},{4,12},{5,7},{6,14},{7,5},{8,0},{9,11},{1... | collective-permute-start | bytes 122888 | tf_op jit(solution)/shard_map/ppermute | solution.py:52
  91.2 4.1 %collective-permute-start.20 = (bf16[16,1280]{1,0:T(8,128)(2,1)S(1)}, bf16[16,1280]{1,0:T(8,128)(2,1)S(1)}, u32[]{:S(2)}, u32[]{:S(2)}) collective-permute-start(bf16[16,1280]{1,0:T(8,128)(2,1)S(1)} %slice.91), channel_id=1, source_target_pairs={{0,8},{1,3},{2,10},{3,1},{4,12},{5,7},{6,14},{7,5},{8,0},{9,11},{1... | collective-permute-start | bytes 122888 | tf_op jit(solution)/shard_map/ppermute | solution.py:52

commit v7 on v6

--- a/solution.py
+++ b/solution.py
@@ -122,11 +122,9 @@
     queries_ref,
     keys_ref,
     values_ref,
-    gain_ref,
     query_ref,
     near_keys_ref,
     near_values_ref,
-    near_gain_ref,
     arrived,
 ):
     group_size = queries_ref.shape[0] // row_count
@@ -136,7 +134,6 @@
     copies = [
         pltpu.make_async_copy(keys_ref, near_keys_ref, arrived.at[0]),
         pltpu.make_async_copy(values_ref, near_values_ref, arrived.at[1]),
-        pltpu.make_async_copy(gain_ref, near_gain_ref, arrived.at[2]),
     ]
     for slot, (even_mask, odd_mask) in enumerate(zip(*masks)):
         block = own_block ^ jnp.where(odd, odd_mask, even_mask)
@@ -145,7 +142,7 @@
             pltpu.make_async_copy(
                 queries_ref.at[pl.ds(start, row_count), :],
                 query_ref.at[slot * row_count : (slot + 1) * row_count, :],
-                arrived.at[3 + slot],
+                arrived.at[2 + slot],
             )
         )
     for copy in copies:
@@ -574,7 +571,7 @@
 
 
 def attention_rows(
-    queries, patch_keys, patch_values, other_keys, other_values, gain, table, row_count, orders
+    queries, patch_keys, patch_values, other_keys, other_values, table, row_count, orders
 ):
     model_width = patch_values.shape[1]
     part_width = model_width // PARTS + LANES
@@ -602,7 +599,7 @@
         )
 
     anywhere = pl.BlockSpec(memory_space=pltpu.HBM)
-    query_rows, own_keys, own_values, gain = pl.pallas_call(
+    query_rows, own_keys, own_values = pl.pallas_call(
         functools.partial(stage_kernel, row_count, masks),
         name="stage_in",
         compiler_params=pltpu.CompilerParams(vmem_limit_bytes=4 << 20),
@@ -610,12 +607,11 @@
             near_shape((rows, queries.shape[1]), jnp.bfloat16),
             near_shape(patch_keys.shape, jnp.bfloat16),
             near_shape(patch_values.shape, jnp.bfloat16),
-            near_shape(gain.shape, jnp.float32),
         ),
-        in_specs=[pl.BlockSpec(memory_space=pltpu.SMEM)] + [anywhere] * 4,
-        out_specs=(whole,) * 4,
-        scratch_shapes=[pltpu.SemaphoreType.DMA((3 + (1 << stages),))],
-    )(device_index.reshape(1), far(queries), far(patch_keys), far(patch_values), far(gain))
+        in_specs=[pl.BlockSpec(memory_space=pltpu.SMEM)] + [anywhere] * 3,
+        out_specs=(whole,) * 3,
+        scratch_shapes=[pltpu.SemaphoreType.DMA((2 + (1 << stages),))],
+    )(device_index.reshape(1), far(queries), far(patch_keys), far(patch_values))
     operands = (query_rows, own_keys, other_keys, own_values, other_values)
     chains = []
     for part in range(PARTS):
@@ -658,7 +654,7 @@
             out_specs=(whole, whole),
         )(*operands)
         finished.append((block, projected))
-    return finished, gain
+    return finished
 
 
 def on_device(
@@ -688,13 +684,12 @@
     for own in halves:
         weights += [own, partner(own, "wide", 0)]
     gain = norm_gain.reshape(1, model_width)
-    finished, gain = attention_rows(
+    finished = attention_rows(
         queries,
         patch_keys,
         patch_values,
         other_keys,
         other_values,
-        gain,
         score_table,
         row_count,
         merge_order,

time: 96.2 us -> 94.8 us (0.985)
  local copies, waits for them, and re-layouts: 3.14 us -> 1.86 us
    reshape x1, local copies, waits for them, and re-layouts: 1.36 us -> 0.01 us  [on_device(): gain = norm_gain.reshape(1, model_width)]
  transfers between devices with their start and end apart: 25 -> 25, of which waited for: 14 -> 14; matrix products, arithmetic and copies ran while one was open for 2% -> 0% of each run, Pallas kernels for 20% -> 21%
where the time goes in v7:
time: 94.8 us; the launch traced here: 94.6 us
  waiting for transfers between devices  34.2 us (36%)
  starting transfers between devices  32.3 us (34%)
  Pallas kernels  24.9 us (26%)
  local copies, waits for them, and re-layouts  1.86 us (2%)
  other arithmetic  1.01 us (1%)
    ppermute x20, waiting for transfers between devices, exchange(): return lax.ppermute(value, 'wide', pairs)  31.9 us
    ppermute x20, starting transfers between devices, exchange(): return lax.ppermute(value, 'wide', pairs)  30.9 us
    pallas_call x1, Pallas kernels, first_expert_rows(): pl.pallas_call(first_expert_kernel, name='expert_first', compiler_params=...  6.7 us
    pallas_call x1, Pallas kernels, second_expert_rows(): pl.pallas_call(second_expert_kernel, name='expert_second', compiler_param...  4.73 us
    pallas_call x1, Pallas kernels, second_expert_rows(): pl.pallas_call(half_expert_kernel, name='expert_half', compiler_params=pl...  4.13 us
    pallas_call x1, Pallas kernels, fetched(): pl.pallas_call(fetch_kernel, compiler_params=pltpu.CompilerParams(vmem_li...  3.34 us
    pallas_call x2, Pallas kernels, attention_rows(): pl.pallas_call(functools.partial(attend_kernel, HEADS, part, part_heads),...  2.74 us
    ppermute x5, waiting for transfers between devices, partner(): return lax.ppermute(value, axis, pairs)  2.35 us
  transfers between devices with their start and end apart: 25, of which 14 were waited for; matrix products, arithmetic and copies ran while one was open for 0% of the time, Pallas kernels for 21%

profile of v7, /device:TPU:0, one launch (start us, length us, event | category | flops | bytes accessed | tf_op | source)
XLA Modules:
  0.0 94.6 jit_solution(3610358388459457761)
XLA Ops:
  0.5 2.3 %collective-permute-done.keys_b = bf16[128,1152]{1,0:T(8,128)(2,1)S(1)} collective-permute-done((bf16[128,1152]{1,0:T(8,128)(2,1)}, bf16[128,1152]{1,0:T(8,128)(2,1)S(1)}, u32[]{:S(2)}, u32[]{:S(2)}) %collective-permute-start) | collective-permute-done | bytes 294944 | tf_op jit(solution)/shard_map/ppermute | solution.py:33
  4.5 1.3 %stage_in.1 = (bf16[128,1152]{1,0:T(8,128)(2,1)S(1)}, bf16[128,1152]{1,0:T(8,128)(2,1)S(1)}, bf16[128,2560]{1,0:T(8,128)(2,1)S(1)}) custom-call(s32[1]{0:T(128)} %bitcast.device_ref, bf16[256,1152]{1,0:T(8,128)(2,1)} %queries_ref.1, bf16[128,1152]{1,0:T(8,128)(2,1)} %keys_ref.1, bf16[128,2560]{1,0:T(8,128)(2,1)} %values_ref.1), custom_call_target="tpu_custom_call" | custom-call | tf_op jit(solution)/shard_map/stage_in/pallas_call | solution.py:602
  6.8 1.2 %shard_map.91 = (bf16[64,1408]{1,0:T(8,128)(2,1)S(1)}, f32[64,1408]{1,0:T(8,128)S(1)}) custom-call(bf16[128,1152]{1,0:T(8,128)(2,1)S(1)} %get-tuple-element.49.query_ref, bf16[128,1152]{1,0:T(8,128)(2,1)S(1)} %get-tuple-element.50.keys_a, bf16[128,1152]{1,0:T(8,128)(2,1)S(1)} %copy-done.1, bf16[128,2560]{1,0:T(8,128)(2,1)S(1)} %get-tuple-element.52.values_a, ...), custom_call_target="tpu_custom_call" | custom-call | tf_op jit(solution)/shard_map/pallas_call | solution.py:618
  8.0 2.7 %collective-permute-start.2 = (bf16[64,1408]{1,0:T(8,128)(2,1)S(1)}, bf16[64,1408]{1,0:T(8,128)(2,1)S(1)}, u32[]{:S(2)}, u32[]{:S(2)}) collective-permute-start(bf16[64,1408]{1,0:T(8,128)(2,1)S(1)} %get-tuple-element.55), channel_id=1, source_target_pairs={{0,2},{1,5},{2,0},{3,7},{4,6},{5,1},{6,4},{7,3},{8,10},{9,13},{10,... | collective-permute-start | bytes 540680 | tf_op jit(solution)/shard_map/ppermute | solution.py:52
  10.7 1.5 %shard_map.98 = (bf16[64,1408]{1,0:T(8,128)(2,1)S(1)}, f32[64,1408]{1,0:T(8,128)S(1)}) custom-call(bf16[128,1152]{1,0:T(8,128)(2,1)S(1)} %get-tuple-element.49.query_ref, bf16[128,1152]{1,0:T(8,128)(2,1)S(1)} %get-tuple-element.50.keys_a, bf16[128,1152]{1,0:T(8,128)(2,1)S(1)} %copy-done.2, bf16[128,2560]{1,0:T(8,128)(2,1)S(1)} %get-tuple-element.52.values_a, ...), custom_call_target="tpu_custom_call" | custom-call | tf_op jit(solution)/shard_map/pallas_call | solution.py:618
  12.3 1.8 %collective-permute-done.2.came_ref = bf16[64,1408]{1,0:T(8,128)(2,1)S(1)} collective-permute-done((bf16[64,1408]{1,0:T(8,128)(2,1)S(1)}, bf16[64,1408]{1,0:T(8,128)(2,1)S(1)}, u32[]{:S(2)}, u32[]{:S(2)}) %collective-permute-start.2) | collective-permute-done | bytes 180256 | tf_op jit(solution)/shard_map/ppermute | solution.py:52
  14.4 2.1 %collective-permute-start.3 = (bf16[32,1408]{1,0:T(8,128)(2,1)S(1)}, bf16[32,1408]{1,0:T(8,128)(2,1)S(1)}, u32[]{:S(2)}, u32[]{:S(2)}) collective-permute-start(bf16[32,1408]{1,0:T(8,128)(2,1)S(1)} %get-tuple-element.57), channel_id=1, source_target_pairs={{0,4},{1,9},{2,6},{3,11},{4,0},{5,13},{6,2},{7,15},{8,12},{9,1},{1... | collective-permute-start | bytes 270344 | tf_op jit(solution)/shard_map/ppermute | solution.py:52
  16.6 2.4 %collective-permute-done.3.came_ref = bf16[32,1408]{1,0:T(8,128)(2,1)S(1)} collective-permute-done((bf16[32,1408]{1,0:T(8,128)(2,1)S(1)}, bf16[32,1408]{1,0:T(8,128)(2,1)S(1)}, u32[]{:S(2)}, u32[]{:S(2)}) %collective-permute-start.3) | collective-permute-done | bytes 90144 | tf_op jit(solution)/shard_map/ppermute | solution.py:52
  19.2 2.1 %collective-permute-start.4 = (bf16[32,1408]{1,0:T(8,128)(2,1)S(1)}, bf16[32,1408]{1,0:T(8,128)(2,1)S(1)}, u32[]{:S(2)}, u32[]{:S(2)}) collective-permute-start(bf16[32,1408]{1,0:T(8,128)(2,1)S(1)} %get-tuple-element.59), channel_id=1, source_target_pairs={{0,8},{1,3},{2,10},{3,1},{4,12},{5,7},{6,14},{7,5},{8,0},{9,11},{1... | collective-permute-start | bytes 270344 | tf_op jit(solution)/shard_map/ppermute | solution.py:52
  21.3 2.5 %collective-permute-done.4.came_ref = bf16[32,1408]{1,0:T(8,128)(2,1)S(1)} collective-permute-done((bf16[32,1408]{1,0:T(8,128)(2,1)S(1)}, bf16[32,1408]{1,0:T(8,128)(2,1)S(1)}, u32[]{:S(2)}, u32[]{:S(2)}) %collective-permute-start.4) | collective-permute-done | bytes 90144 | tf_op jit(solution)/shard_map/ppermute | solution.py:52
  24.1 3.1 %collective-permute-start.5 = (bf16[32,1408]{1,0:T(8,128)(2,1)S(1)}, bf16[32,1408]{1,0:T(8,128)(2,1)S(1)}, u32[]{:S(2)}, u32[]{:S(2)}) collective-permute-start(bf16[32,1408]{1,0:T(8,128)(2,1)S(1)} %get-tuple-element.61.own_ref), channel_id=1, source_target_pairs={{0,16},{1,17},{2,18},{3,19},{4,20},{5,21},{6,22},{7,23},{8,24},{9,... | collective-permute-start | bytes 270344 | tf_op jit(solution)/shard_map/ppermute | solution.py:52
  27.5 1.6 %collective-permute-start.8 = (bf16[32,1408]{1,0:T(8,128)(2,1)S(1)}, bf16[32,1408]{1,0:T(8,128)(2,1)S(1)}, u32[]{:S(2)}, u32[]{:S(2)}) collective-permute-start(bf16[32,1408]{1,0:T(8,128)(2,1)S(1)} %get-tuple-element.72), channel_id=1, source_target_pairs={{0,4},{1,9},{2,6},{3,11},{4,0},{5,13},{6,2},{7,15},{8,12},{9,1},{1... | collective-permute-start | bytes 270344 | tf_op jit(solution)/shard_map/ppermute | solution.py:52
  29.7 1.9 %collective-permute-start.6 = (bf16[64,1408]{1,0:T(8,128)(2,1)S(1)}, bf16[64,1408]{1,0:T(8,128)(2,1)S(1)}, u32[]{:S(2)}, u32[]{:S(2)}) collective-permute-start(bf16[64,1408]{1,0:T(8,128)(2,1)S(1)} %shard_map.95.own_ref), channel_id=1, source_target_pairs={{0,4},{1,5},{2,6},{3,7},{4,0},{5,1},{6,2},{7,3},{8,12},{9,13},{10,... | collective-permute-start | bytes 540680 | tf_op jit(solution)/shard_map/ppermute | solution.py:52
  32.2 1.6 %collective-permute-start.9 = (bf16[32,1408]{1,0:T(8,128)(2,1)S(1)}, bf16[32,1408]{1,0:T(8,128)(2,1)S(1)}, u32[]{:S(2)}, u32[]{:S(2)}) collective-permute-start(bf16[32,1408]{1,0:T(8,128)(2,1)S(1)} %get-tuple-element.74), channel_id=1, source_target_pairs={{0,8},{1,3},{2,10},{3,1},{4,12},{5,7},{6,14},{7,5},{8,0},{9,11},{1... | collective-permute-start | bytes 270344 | tf_op jit(solution)/shard_map/ppermute | solution.py:52
  33.9 3.5 %collective-permute-done.9.came_ref = bf16[32,1408]{1,0:T(8,128)(2,1)S(1)} collective-permute-done((bf16[32,1408]{1,0:T(8,128)(2,1)S(1)}, bf16[32,1408]{1,0:T(8,128)(2,1)S(1)}, u32[]{:S(2)}, u32[]{:S(2)}) %collective-permute-start.9) | collective-permute-done | bytes 90144 | tf_op jit(solution)/shard_map/ppermute | solution.py:52
  37.6 2.1 %collective-permute-start.10 = (bf16[32,1280]{1,0:T(8,128)(2,1)S(1)}, bf16[32,1280]{1,0:T(8,128)(2,1)S(1)}, u32[]{:S(2)}, u32[]{:S(2)}) collective-permute-start(bf16[32,1280]{1,0:T(8,128)(2,1)S(1)} %get-tuple-element.75.own_ref), channel_id=1, source_target_pairs={{0,16},{1,17},{2,18},{3,19},{4,20},{5,21},{6,22},{7,23},{8,24},{9,... | collective-permute-start | bytes 245768 | tf_op jit(solution)/shard_map/ppermute | solution.py:52
  39.7 3.3 %shard_map.96 = (bf16[512,2560]{1,0:T(8,128)(2,1)S(1)}, bf16[512,2560]{1,0:T(8,128)(2,1)S(1)}, bf16[512,2560]{1,0:T(8,128)(2,1)S(1)}) custom-call(bf16[512,2560]{1,0:T(8,128)(2,1)} %refs_0_, bf16[512,2560]{1,0:T(8,128)(2,1)} %refs_1_, bf16[512,2560]{1,0:T(8,128)(2,1)} %refs_2_), custom_call_target="tpu_custom_call" | custom-call | tf_op jit(solution)/shard_map/pallas_call | solution.py:334
  43.1 1.6 %collective-permute-start.16 = (bf16[128,1408]{1,0:T(8,128)(2,1)S(1)}, bf16[128,1408]{1,0:T(8,128)(2,1)S(1)}, u32[]{:S(2)}, u32[]{:S(2)}) collective-permute-start(bf16[128,1408]{1,0:T(8,128)(2,1)S(1)} %get-tuple-element.68.rows_a), channel_id=1, source_target_pairs={{0,2},{1,9},{2,0},{3,11},{4,6},{5,13},{6,4},{7,15},{8,10},{9,1},{1... | collective-permute-start | bytes 1081352 | tf_op jit(solution)/shard_map/ppermute | solution.py:52
  45.8 4.2 %collective-permute-done.11.came_ref = bf16[64,1280]{1,0:T(8,128)(2,1)S(1)} collective-permute-done((bf16[64,1280]{1,0:T(8,128)(2,1)S(1)}, bf16[64,1280]{1,0:T(8,128)(2,1)S(1)}, u32[]{:S(2)}, u32[]{:S(2)}) %collective-permute-start.11) | collective-permute-done | bytes 163872 | tf_op jit(solution)/shard_map/ppermute | solution.py:52
  50.8 4.1 %expert_half.1 = (f32[1024,128]{1,0:T(8,128)S(1)}, f32[1024,128]{1,0:T(8,128)S(1)}, f32[8,128]{1,0:T(8,128)S(1)}) custom-call(s32[1]{0:T(128)} %bitcast.device_ref, f32[1,2560]{1,0:T(1,128)S(1)} %reshape.14.gain_ref, bf16[128,1408]{1,0:T(8,128)(2,1)S(1)} %collective-permute-done.16.rows_ref, bf16[512,2560]{1,0:T(8,128)(2,1)S(1)} %get-tuple-element.80.gate_a, ...), custom_call_target="tpu_custom_call" | custom-call | tf_op jit(solution)/shard_map/expert_half/pallas_call | solution.py:527
  55.0 6.7 %expert_first.1 = (f32[128,1280]{1,0:T(8,128)S(1)}, f32[128,1280]{1,0:T(8,128)S(1)}) custom-call(s32[1]{0:T(128)} %bitcast.device_ref, f32[1,2560]{1,0:T(1,128)S(1)} %reshape.14.gain_ref, bf16[128,1408]{1,0:T(8,128)(2,1)S(1)} %get-tuple-element.68.rows_a, bf16[128,1280]{1,0:T(8,128)(2,1)S(1)} %get-tuple-element.79.rows_b, ...), custom_call_target="tpu_custom_call" | custom-call | flops 2013265920 | bytes 15728640 | tf_op jit(solution)/shard_map/expert_first/pallas_call | solution.py:497
  61.7 4.7 %expert_second.1 = (bf16[128,1280]{1,0:T(8,128)(2,1)S(1)}, bf16[128,1024]{1,0:T(8,128)(2,1)S(1)}) custom-call(f32[1,2560]{1,0:T(1,128)S(1)} %reshape.14.gain_ref, bf16[128,1280]{1,0:T(8,128)(2,1)S(1)} %collective-permute-done.15.rows_ref, f32[1024,128]{1,0:T(8,128)S(1)} %get-tuple-element.84.gates_ref, f32[1024,128]{1,0:T(8,128)S(1)} %get-tuple-element.85.ups_ref, ...), custom_call_target="tpu_custom_call" | custom-call | tf_op jit(solution)/shard_map/expert_second/pallas_call | solution.py:537
  67.0 1.3 %collective-permute-start.21 = (bf16[128,1280]{1,0:T(8,128)(2,1)S(1)}, bf16[128,1280]{1,0:T(8,128)(2,1)S(1)}, u32[]{:S(2)}, u32[]{:S(2)}) collective-permute-start(bf16[128,1280]{1,0:T(8,128)(2,1)S(1)} %get-tuple-element.92), channel_id=1, source_target_pairs={{0,4},{1,5},{2,6},{3,7},{4,0},{5,1},{6,2},{7,3},{8,12},{9,13},{10,... | collective-permute-start | bytes 983048 | tf_op jit(solution)/shard_map/ppermute | solution.py:52
  68.3 1.3 %collective-permute-start.17 = (bf16[128,1280]{1,0:T(8,128)(2,1)S(1)}, bf16[128,1280]{1,0:T(8,128)(2,1)S(1)}, u32[]{:S(2)}, u32[]{:S(2)}) collective-permute-start(bf16[128,1280]{1,0:T(8,128)(2,1)S(1)} %get-tuple-element.87), channel_id=1, source_target_pairs={{0,2},{1,9},{2,0},{3,11},{4,6},{5,13},{6,4},{7,15},{8,10},{9,1},{1... | collective-permute-start | bytes 983048 | tf_op jit(solution)/shard_map/ppermute | solution.py:52
  69.6 6.3 %collective-permute-done.21 = bf16[128,1280]{1,0:T(8,128)(2,1)S(1)} collective-permute-done((bf16[128,1280]{1,0:T(8,128)(2,1)S(1)}, bf16[128,1280]{1,0:T(8,128)(2,1)S(1)}, u32[]{:S(2)}, u32[]{:S(2)}) %collective-permute-start.21) | collective-permute-done | bytes 327712 | tf_op jit(solution)/shard_map/ppermute | solution.py:52
  76.0 1.5 %collective-permute-start.22 = (bf16[64,1280]{1,0:T(8,128)(2,1)S(1)}, bf16[64,1280]{1,0:T(8,128)(2,1)S(1)}, u32[]{:S(2)}, u32[]{:S(2)}) collective-permute-start(bf16[64,1280]{1,0:T(8,128)(2,1)S(1)} %slice.86), channel_id=1, source_target_pairs={{0,2},{1,9},{2,0},{3,11},{4,6},{5,13},{6,4},{7,15},{8,10},{9,1},{1... | collective-permute-start | bytes 491528 | tf_op jit(solution)/shard_map/ppermute | solution.py:52
  78.7 2.6 %collective-permute-done.22 = bf16[64,1280]{1,0:T(8,128)(2,1)S(1)} collective-permute-done((bf16[64,1280]{1,0:T(8,128)(2,1)S(1)}, bf16[64,1280]{1,0:T(8,128)(2,1)S(1)}, u32[]{:S(2)}, u32[]{:S(2)}) %collective-permute-start.22) | collective-permute-done | bytes 163872 | tf_op jit(solution)/shard_map/ppermute | solution.py:52
  81.4 1.8 %collective-permute-start.23 = (bf16[32,1280]{1,0:T(8,128)(2,1)S(1)}, bf16[32,1280]{1,0:T(8,128)(2,1)S(1)}, u32[]{:S(2)}, u32[]{:S(2)}) collective-permute-start(bf16[32,1280]{1,0:T(8,128)(2,1)S(1)} %slice.88), channel_id=1, source_target_pairs={{0,16},{1,17},{2,18},{3,19},{4,20},{5,21},{6,22},{7,23},{8,24},{9,... | collective-permute-start | bytes 245768 | tf_op jit(solution)/shard_map/ppermute | solution.py:52
  83.2 1.3 %collective-permute-start.19 = (bf16[32,1280]{1,0:T(8,128)(2,1)S(1)}, bf16[32,1280]{1,0:T(8,128)(2,1)S(1)}, u32[]{:S(2)}, u32[]{:S(2)}) collective-permute-start(bf16[32,1280]{1,0:T(8,128)(2,1)S(1)} %slice.89), channel_id=1, source_target_pairs={{0,16},{1,17},{2,18},{3,19},{4,20},{5,21},{6,22},{7,23},{8,24},{9,... | collective-permute-start | bytes 245768 | tf_op jit(solution)/shard_map/ppermute | solution.py:52
  84.5 2.3 %collective-permute-done.23 = bf16[32,1280]{1,0:T(8,128)(2,1)S(1)} collective-permute-done((bf16[32,1280]{1,0:T(8,128)(2,1)S(1)}, bf16[32,1280]{1,0:T(8,128)(2,1)S(1)}, u32[]{:S(2)}, u32[]{:S(2)}) %collective-permute-start.23) | collective-permute-done | bytes 81952 | tf_op jit(solution)/shard_map/ppermute | solution.py:52
  86.9 1.9 %collective-permute-start.24 = (bf16[16,1280]{1,0:T(8,128)(2,1)S(1)}, bf16[16,1280]{1,0:T(8,128)(2,1)S(1)}, u32[]{:S(2)}, u32[]{:S(2)}) collective-permute-start(bf16[16,1280]{1,0:T(8,128)(2,1)S(1)} %slice.90), channel_id=1, source_target_pairs={{0,8},{1,3},{2,10},{3,1},{4,12},{5,7},{6,14},{7,5},{8,0},{9,11},{1... | collective-permute-start | bytes 122888 | tf_op jit(solution)/shard_map/ppermute | solution.py:52
  91.0 3.0 %collective-permute-done.20 = bf16[16,1280]{1,0:T(8,128)(2,1)S(1)} collective-permute-done((bf16[16,1280]{1,0:T(8,128)(2,1)S(1)}, bf16[16,1280]{1,0:T(8,128)(2,1)S(1)}, u32[]{:S(2)}, u32[]{:S(2)}) %collective-permute-start.20) | collective-permute-done | bytes 40992 | tf_op jit(solution)/shard_map/ppermute | solution.py:52
  (67 shorter events, 12.5 us)
Async XLA Ops:
  0.0 3.6 %collective-permute-start.1 = (bf16[128,2560]{1,0:T(8,128)(2,1)}, bf16[128,2560]{1,0:T(8,128)(2,1)S(1)}, u32[]{:S(2)}, u32[]{:S(2)}) collective-permute-start(bf16[128,2560]{1,0:T(8,128)(2,1)} %values_ref.1), channel_id=1, source_target_pairs={{0,1},{1,0},{2,3},{3,2},{4,5},{5,4},{6,7},{7,6},{8,9},{9,8},{10,11... | collective-permute-start | bytes 1966088 | tf_op jit(solution)/shard_map/ppermute | solution.py:33
  0.5 2.4 %collective-permute-start = (bf16[128,1152]{1,0:T(8,128)(2,1)}, bf16[128,1152]{1,0:T(8,128)(2,1)S(1)}, u32[]{:S(2)}, u32[]{:S(2)}) collective-permute-start(bf16[128,1152]{1,0:T(8,128)(2,1)} %keys_ref.1), channel_id=1, source_target_pairs={{0,1},{1,0},{2,3},{3,2},{4,5},{5,4},{6,7},{7,6},{8,9},{9,8},{10,11... | collective-permute-start | bytes 884744 | tf_op jit(solution)/shard_map/ppermute | solution.py:33
  2.9 0.7 copy-start
  3.6 47.2 %collective-permute-start.12 = (bf16[512,2560]{1,0:T(8,128)(2,1)}, bf16[512,2560]{1,0:T(8,128)(2,1)}, u32[]{:S(2)}, u32[]{:S(2)}) collective-permute-start(bf16[512,2560]{1,0:T(8,128)(2,1)} %refs_0_), channel_id=1, source_target_pairs={{0,1},{1,0},{2,3},{3,2},{4,5},{5,4},{6,7},{7,6},{8,9},{9,8},{10,11... | collective-permute-start | bytes 7864328 | tf_op jit(solution)/shard_map/ppermute | solution.py:33
  4.0 46.9 %collective-permute-start.13 = (bf16[512,2560]{1,0:T(8,128)(2,1)}, bf16[512,2560]{1,0:T(8,128)(2,1)}, u32[]{:S(2)}, u32[]{:S(2)}) collective-permute-start(bf16[512,2560]{1,0:T(8,128)(2,1)} %refs_1_), channel_id=1, source_target_pairs={{0,1},{1,0},{2,3},{3,2},{4,5},{5,4},{6,7},{7,6},{8,9},{9,8},{10,11... | collective-permute-start | bytes 7864328 | tf_op jit(solution)/shard_map/ppermute | solution.py:33
  4.1 50.9 %collective-permute-start.14 = (bf16[512,2560]{1,0:T(8,128)(2,1)}, bf16[512,2560]{1,0:T(8,128)(2,1)S(1)}, u32[]{:S(2)}, u32[]{:S(2)}) collective-permute-start(bf16[512,2560]{1,0:T(8,128)(2,1)} %refs_2_), channel_id=1, source_target_pairs={{0,1},{1,0},{2,3},{3,2},{4,5},{5,4},{6,7},{7,6},{8,9},{9,8},{10,11... | collective-permute-start | bytes 7864328 | tf_op jit(solution)/shard_map/ppermute | solution.py:33
  4.5 6.2 %copy-start.2 = (bf16[128,1152]{1,0:T(8,128)(2,1)S(1)}, bf16[128,1152]{1,0:T(8,128)(2,1)}, u32[]{:S(2)}) copy-start(bf16[128,1152]{1,0:T(8,128)(2,1)} %copy-done) | copy-start | bytes 884740
  4.5 12.1 %copy-start.5 = (s32[16,6]{0,1:T(8,128)S(1)}, s32[16,6]{0,1:T(8,128)}, u32[]{:S(2)}) copy-start(s32[16,6]{0,1:T(8,128)} %param.13) | copy-start | bytes 1156
  5.8 10.7 %copy-start.4 = (s32[16,6]{0,1:T(8,128)S(1)}, s32[16,6]{0,1:T(8,128)}, u32[]{:S(2)}) copy-start(s32[16,6]{0,1:T(8,128)} %param.14) | copy-start | bytes 1156
  5.8 1.0 %copy-start.1 = (bf16[128,1152]{1,0:T(8,128)(2,1)S(1)}, bf16[128,1152]{1,0:T(8,128)(2,1)}, u32[]{:S(2)}) copy-start(bf16[128,1152]{1,0:T(8,128)(2,1)} %copy-done) | copy-start | bytes 884740
  8.0 6.2 %collective-permute-start.2 = (bf16[64,1408]{1,0:T(8,128)(2,1)S(1)}, bf16[64,1408]{1,0:T(8,128)(2,1)S(1)}, u32[]{:S(2)}, u32[]{:S(2)}) collective-permute-start(bf16[64,1408]{1,0:T(8,128)(2,1)S(1)} %get-tuple-element.55), channel_id=1, source_target_pairs={{0,2},{1,5},{2,0},{3,7},{4,6},{5,1},{6,4},{7,3},{8,10},{9,13},{10,... | collective-permute-start | bytes 540680 | tf_op jit(solution)/shard_map/ppermute | solution.py:52
  12.2 15.0 %collective-permute-start.7 = (bf16[64,1408]{1,0:T(8,128)(2,1)S(1)}, bf16[64,1408]{1,0:T(8,128)(2,1)S(1)}, u32[]{:S(2)}, u32[]{:S(2)}) collective-permute-start(bf16[64,1408]{1,0:T(8,128)(2,1)S(1)} %get-tuple-element.70), channel_id=1, source_target_pairs={{0,2},{1,5},{2,0},{3,7},{4,6},{5,1},{6,4},{7,3},{8,10},{9,13},{10,... | collective-permute-start | bytes 540680 | tf_op jit(solution)/shard_map/ppermute | solution.py:52
  14.4 4.6 %collective-permute-start.3 = (bf16[32,1408]{1,0:T(8,128)(2,1)S(1)}, bf16[32,1408]{1,0:T(8,128)(2,1)S(1)}, u32[]{:S(2)}, u32[]{:S(2)}) collective-permute-start(bf16[32,1408]{1,0:T(8,128)(2,1)S(1)} %get-tuple-element.57), channel_id=1, source_target_pairs={{0,4},{1,9},{2,6},{3,11},{4,0},{5,13},{6,2},{7,15},{8,12},{9,1},{1... | collective-permute-start | bytes 270344 | tf_op jit(solution)/shard_map/ppermute | solution.py:52
  19.2 4.7 %collective-permute-start.4 = (bf16[32,1408]{1,0:T(8,128)(2,1)S(1)}, bf16[32,1408]{1,0:T(8,128)(2,1)S(1)}, u32[]{:S(2)}, u32[]{:S(2)}) collective-permute-start(bf16[32,1408]{1,0:T(8,128)(2,1)S(1)} %get-tuple-element.59), channel_id=1, source_target_pairs={{0,8},{1,3},{2,10},{3,1},{4,12},{5,7},{6,14},{7,5},{8,0},{9,11},{1... | collective-permute-start | bytes 270344 | tf_op jit(solution)/shard_map/ppermute | solution.py:52
  24.1 5.6 %collective-permute-start.5 = (bf16[32,1408]{1,0:T(8,128)(2,1)S(1)}, bf16[32,1408]{1,0:T(8,128)(2,1)S(1)}, u32[]{:S(2)}, u32[]{:S(2)}) collective-permute-start(bf16[32,1408]{1,0:T(8,128)(2,1)S(1)} %get-tuple-element.61.own_ref), channel_id=1, source_target_pairs={{0,16},{1,17},{2,18},{3,19},{4,20},{5,21},{6,22},{7,23},{8,24},{9,... | collective-permute-start | bytes 270344 | tf_op jit(solution)/shard_map/ppermute | solution.py:52
  27.5 4.6 %collective-permute-start.8 = (bf16[32,1408]{1,0:T(8,128)(2,1)S(1)}, bf16[32,1408]{1,0:T(8,128)(2,1)S(1)}, u32[]{:S(2)}, u32[]{:S(2)}) collective-permute-start(bf16[32,1408]{1,0:T(8,128)(2,1)S(1)} %get-tuple-element.72), channel_id=1, source_target_pairs={{0,4},{1,9},{2,6},{3,11},{4,0},{5,13},{6,2},{7,15},{8,12},{9,1},{1... | collective-permute-start | bytes 270344 | tf_op jit(solution)/shard_map/ppermute | solution.py:52
  29.7 13.3 %collective-permute-start.6 = (bf16[64,1408]{1,0:T(8,128)(2,1)S(1)}, bf16[64,1408]{1,0:T(8,128)(2,1)S(1)}, u32[]{:S(2)}, u32[]{:S(2)}) collective-permute-start(bf16[64,1408]{1,0:T(8,128)(2,1)S(1)} %shard_map.95.own_ref), channel_id=1, source_target_pairs={{0,4},{1,5},{2,6},{3,7},{4,0},{5,1},{6,2},{7,3},{8,12},{9,13},{10,... | collective-permute-start | bytes 540680 | tf_op jit(solution)/shard_map/ppermute | solution.py:52
  32.2 5.2 %collective-permute-start.9 = (bf16[32,1408]{1,0:T(8,128)(2,1)S(1)}, bf16[32,1408]{1,0:T(8,128)(2,1)S(1)}, u32[]{:S(2)}, u32[]{:S(2)}) collective-permute-start(bf16[32,1408]{1,0:T(8,128)(2,1)S(1)} %get-tuple-element.74), channel_id=1, source_target_pairs={{0,8},{1,3},{2,10},{3,1},{4,12},{5,7},{6,14},{7,5},{8,0},{9,11},{1... | collective-permute-start | bytes 270344 | tf_op jit(solution)/shard_map/ppermute | solution.py:52
  37.6 7.0 %collective-permute-start.10 = (bf16[32,1280]{1,0:T(8,128)(2,1)S(1)}, bf16[32,1280]{1,0:T(8,128)(2,1)S(1)}, u32[]{:S(2)}, u32[]{:S(2)}) collective-permute-start(bf16[32,1280]{1,0:T(8,128)(2,1)S(1)} %get-tuple-element.75.own_ref), channel_id=1, source_target_pairs={{0,16},{1,17},{2,18},{3,19},{4,20},{5,21},{6,22},{7,23},{8,24},{9,... | collective-permute-start | bytes 245768 | tf_op jit(solution)/shard_map/ppermute | solution.py:52
  43.1 7.7 %collective-permute-start.16 = (bf16[128,1408]{1,0:T(8,128)(2,1)S(1)}, bf16[128,1408]{1,0:T(8,128)(2,1)S(1)}, u32[]{:S(2)}, u32[]{:S(2)}) collective-permute-start(bf16[128,1408]{1,0:T(8,128)(2,1)S(1)} %get-tuple-element.68.rows_a), channel_id=1, source_target_pairs={{0,2},{1,9},{2,0},{3,11},{4,6},{5,13},{6,4},{7,15},{8,10},{9,1},{1... | collective-permute-start | bytes 1081352 | tf_op jit(solution)/shard_map/ppermute | solution.py:52
  44.7 5.4 %collective-permute-start.11 = (bf16[64,1280]{1,0:T(8,128)(2,1)S(1)}, bf16[64,1280]{1,0:T(8,128)(2,1)S(1)}, u32[]{:S(2)}, u32[]{:S(2)}) collective-permute-start(bf16[64,1280]{1,0:T(8,128)(2,1)S(1)} %shard_map.102.own_ref), channel_id=1, source_target_pairs={{0,4},{1,5},{2,6},{3,7},{4,0},{5,1},{6,2},{7,3},{8,12},{9,13},{10,... | collective-permute-start | bytes 491528 | tf_op jit(solution)/shard_map/ppermute | solution.py:52
  50.1 0.7 copy-start.3
  50.1 11.6 %collective-permute-start.15 = (bf16[128,1280]{1,0:T(8,128)(2,1)S(1)}, bf16[128,1280]{1,0:T(8,128)(2,1)S(1)}, u32[]{:S(2)}, u32[]{:S(2)}) collective-permute-start(bf16[128,1280]{1,0:T(8,128)(2,1)S(1)} %get-tuple-element.79.rows_b), channel_id=1, source_target_pairs={{0,2},{1,9},{2,0},{3,11},{4,6},{5,13},{6,4},{7,15},{8,10},{9,1},{1... | collective-permute-start | bytes 983048 | tf_op jit(solution)/shard_map/ppermute | solution.py:52
  67.0 8.9 %collective-permute-start.21 = (bf16[128,1280]{1,0:T(8,128)(2,1)S(1)}, bf16[128,1280]{1,0:T(8,128)(2,1)S(1)}, u32[]{:S(2)}, u32[]{:S(2)}) collective-permute-start(bf16[128,1280]{1,0:T(8,128)(2,1)S(1)} %get-tuple-element.92), channel_id=1, source_target_pairs={{0,4},{1,5},{2,6},{3,7},{4,0},{5,1},{6,2},{7,3},{8,12},{9,13},{10,... | collective-permute-start | bytes 983048 | tf_op jit(solution)/shard_map/ppermute | solution.py:52
  68.3 9.2 %collective-permute-start.17 = (bf16[128,1280]{1,0:T(8,128)(2,1)S(1)}, bf16[128,1280]{1,0:T(8,128)(2,1)S(1)}, u32[]{:S(2)}, u32[]{:S(2)}) collective-permute-start(bf16[128,1280]{1,0:T(8,128)(2,1)S(1)} %get-tuple-element.87), channel_id=1, source_target_pairs={{0,2},{1,9},{2,0},{3,11},{4,6},{5,13},{6,4},{7,15},{8,10},{9,1},{1... | collective-permute-start | bytes 983048 | tf_op jit(solution)/shard_map/ppermute | solution.py:52
  76.0 5.4 %collective-permute-start.22 = (bf16[64,1280]{1,0:T(8,128)(2,1)S(1)}, bf16[64,1280]{1,0:T(8,128)(2,1)S(1)}, u32[]{:S(2)}, u32[]{:S(2)}) collective-permute-start(bf16[64,1280]{1,0:T(8,128)(2,1)S(1)} %slice.86), channel_id=1, source_target_pairs={{0,2},{1,9},{2,0},{3,11},{4,6},{5,13},{6,4},{7,15},{8,10},{9,1},{1... | collective-permute-start | bytes 491528 | tf_op jit(solution)/shard_map/ppermute | solution.py:52
  77.6 5.6 %collective-permute-start.18 = (bf16[64,1280]{1,0:T(8,128)(2,1)S(1)}, bf16[64,1280]{1,0:T(8,128)(2,1)S(1)}, u32[]{:S(2)}, u32[]{:S(2)}) collective-permute-start(bf16[64,1280]{1,0:T(8,128)(2,1)S(1)} %slice.87), channel_id=1, source_target_pairs={{0,4},{1,5},{2,6},{3,7},{4,0},{5,1},{6,2},{7,3},{8,12},{9,13},{10,... | collective-permute-start | bytes 491528 | tf_op jit(solution)/shard_map/ppermute | solution.py:52
  81.4 5.4 %collective-permute-start.23 = (bf16[32,1280]{1,0:T(8,128)(2,1)S(1)}, bf16[32,1280]{1,0:T(8,128)(2,1)S(1)}, u32[]{:S(2)}, u32[]{:S(2)}) collective-permute-start(bf16[32,1280]{1,0:T(8,128)(2,1)S(1)} %slice.88), channel_id=1, source_target_pairs={{0,16},{1,17},{2,18},{3,19},{4,20},{5,21},{6,22},{7,23},{8,24},{9,... | collective-permute-start | bytes 245768 | tf_op jit(solution)/shard_map/ppermute | solution.py:52
  83.2 6.6 %collective-permute-start.19 = (bf16[32,1280]{1,0:T(8,128)(2,1)S(1)}, bf16[32,1280]{1,0:T(8,128)(2,1)S(1)}, u32[]{:S(2)}, u32[]{:S(2)}) collective-permute-start(bf16[32,1280]{1,0:T(8,128)(2,1)S(1)} %slice.89), channel_id=1, source_target_pairs={{0,16},{1,17},{2,18},{3,19},{4,20},{5,21},{6,22},{7,23},{8,24},{9,... | collective-permute-start | bytes 245768 | tf_op jit(solution)/shard_map/ppermute | solution.py:52
  86.9 4.1 %collective-permute-start.24 = (bf16[16,1280]{1,0:T(8,128)(2,1)S(1)}, bf16[16,1280]{1,0:T(8,128)(2,1)S(1)}, u32[]{:S(2)}, u32[]{:S(2)}) collective-permute-start(bf16[16,1280]{1,0:T(8,128)(2,1)S(1)} %slice.90), channel_id=1, source_target_pairs={{0,8},{1,3},{2,10},{3,1},{4,12},{5,7},{6,14},{7,5},{8,0},{9,11},{1... | collective-permute-start | bytes 122888 | tf_op jit(solution)/shard_map/ppermute | solution.py:52
  89.9 4.1 %collective-permute-start.20 = (bf16[16,1280]{1,0:T(8,128)(2,1)S(1)}, bf16[16,1280]{1,0:T(8,128)(2,1)S(1)}, u32[]{:S(2)}, u32[]{:S(2)}) collective-permute-start(bf16[16,1280]{1,0:T(8,128)(2,1)S(1)} %slice.91), channel_id=1, source_target_pairs={{0,8},{1,3},{2,10},{3,1},{4,12},{5,7},{6,14},{7,5},{8,0},{9,11},{1... | collective-permute-start | bytes 122888 | tf_op jit(solution)/shard_map/ppermute | solution.py:52

commit v8 on v7

--- a/solution.py
+++ b/solution.py
@@ -39,9 +39,12 @@
     merge = (near_bits, near_bits[1:] + near_bits[:1])
     rest = [[bit for bit in all_bits if bit != order[-1]] for order in merge]
     gather = (rest[0][::-1], rest[1][2:][::-1] + rest[1][:2])
-    scatter = [order[::-1] + kept[-1:] for order, kept in zip(gather, merge)]
-    crossed = [order[1::-1] + order[2:] for order in scatter]
-    return merge, gather, (scatter, crossed)
+    crossed = [order[:-2] + order[-2:][::-1] for order in gather]
+    scatter = [
+        [order[::-1] + kept[-1:] for order, kept in zip(orders, merge)]
+        for orders in (gather, crossed)
+    ]
+    return merge, (gather, crossed), scatter
 
 
 def exchange(value, orders, stage):
@@ -279,29 +282,6 @@
         ).astype(jnp.bfloat16)
 
 
-def normed_rows(device_ref, gain_ref, row_refs, turned):
-    width = row_refs[1].shape[1]
-    model_width = width * len(row_refs)
-    square = jnp.zeros((row_refs[0].shape[0], LANES), jnp.float32)
-    for rows_ref in row_refs:
-        for low in range(0, width, LANES):
-            residual = rows_ref[:, low : low + LANES].astype(jnp.float32)
-            square = square + residual * residual
-    mean = jnp.sum(square, axis=1, keepdims=True) / model_width
-    inverse = jnp.broadcast_to(lax.rsqrt(mean + 1e-06), square.shape)
-    for part, rows_ref in enumerate(row_refs):
-        for low in range(0, width, LANES):
-            at = part * width + low
-            residual = rows_ref[:, low : low + LANES].astype(jnp.float32)
-            normed = residual * inverse * gain_ref[:, at : at + LANES]
-            turned[at : at + LANES, :] = normed.astype(jnp.bfloat16).T
-    turned[model_width:, :] = row_refs[0][:, width:].T
-    scores = turned[model_width:, :].astype(jnp.float32)
-    lane = lax.broadcasted_iota(jnp.int32, scores.shape, 0)
-    chosen = jnp.where(lane == lax.div(device_ref[0], 2) + TABLE_LANE, scores, 0.0)
-    return jnp.sum(chosen, axis=0, keepdims=True) / jnp.sum(scores, axis=0, keepdims=True)
-
-
 def down_product(hidden_ref, down_refs, out_ref, start):
     width = out_ref.shape[1]
     units = down_refs[0].shape[0]
@@ -363,39 +343,6 @@
     return out, passed
 
 
-def first_expert_kernel(
-    device_ref,
-    gain_ref,
-    rows_a,
-    rows_b,
-    gate_a,
-    up_a,
-    down_a,
-    gate_b,
-    up_b,
-    down_b,
-    out_a,
-    out_b,
-    turned,
-    hidden,
-):
-    units = gate_a.shape[0]
-    share = normed_rows(device_ref, gain_ref, (rows_a, rows_b), turned)
-    model_width = gain_ref.shape[1]
-    rows = turned[:model_width, :]
-    for half, (gate_ref, up_ref) in enumerate(((gate_a, up_a), (gate_b, up_b))):
-        for low in range(0, units, UNITS):
-            chunk = slice(low, low + UNITS)
-            gate_part = jnp.dot(gate_ref[chunk, :], rows, preferred_element_type=jnp.float32)
-            up_part = jnp.dot(up_ref[chunk, :], rows, preferred_element_type=jnp.float32)
-            silu = gate_part / (1.0 + jnp.exp(-gate_part))
-            hidden[:, half * units + low : half * units + low + UNITS] = (
-                (silu * up_part * share).T.astype(jnp.bfloat16)
-            )
-    down_product(hidden, (down_a, down_b), out_a, 0)
-    down_product(hidden, (down_a, down_b), out_b, out_a.shape[1])
-
-
 def turned_half(rows_ref, gain_ref, start, width, turned):
     square = jnp.zeros((rows_ref.shape[0], LANES), jnp.float32)
     for low in range(0, width, LANES):
@@ -406,7 +353,8 @@
     return jnp.sum(square.T, axis=0, keepdims=True)
 
 
-def half_expert_kernel(
+def part_expert_kernel(
+    part,
     device_ref,
     gain_ref,
     rows_ref,
@@ -420,13 +368,14 @@
     turned,
 ):
     width = turned.shape[0]
-    stats_ref[0:1, :] = turned_half(rows_ref, gain_ref, 0, width, turned)
-    scores = rows_ref[:, width:].astype(jnp.float32).T
-    lane = lax.broadcasted_iota(jnp.int32, scores.shape, 0)
-    chosen = jnp.where(lane == lax.div(device_ref[0], 2) + TABLE_LANE, scores, 0.0)
-    stats_ref[1:2, :] = jnp.sum(chosen, axis=0, keepdims=True) / jnp.sum(
-        scores, axis=0, keepdims=True
-    )
+    stats_ref[0:1, :] = turned_half(rows_ref, gain_ref, part * width, width, turned)
+    if rows_ref.shape[1] > width:
+        scores = rows_ref[:, width:].astype(jnp.float32).T
+        lane = lax.broadcasted_iota(jnp.int32, scores.shape, 0)
+        chosen = jnp.where(lane == lax.div(device_ref[0], 2) + TABLE_LANE, scores, 0.0)
+        stats_ref[1:2, :] = jnp.sum(chosen, axis=0, keepdims=True) / jnp.sum(
+            scores, axis=0, keepdims=True
+        )
     rows = turned[...]
     units = gate_a.shape[0]
     for weight_ref, low, out_ref in (
@@ -436,8 +385,26 @@
         (up_b, units, ups_ref),
     ):
         out_ref[low : low + units, :] = jnp.dot(
-            weight_ref[:, :width], rows, preferred_element_type=jnp.float32
+            weight_ref[:, part * width : (part + 1) * width],
+            rows,
+            preferred_element_type=jnp.float32,
         )
+
+
+def lower_pair(early, late):
+    half = early.shape[1] // 2
+    return jnp.where(lane_iota(early.shape) < half, early, pltpu.roll(late, half, 1))
+
+
+def upper_pair(early, late):
+    half = early.shape[1] // 2
+    return jnp.where(lane_iota(early.shape) < half, pltpu.roll(early, half, 1), late)
+
+
+def hidden_of(gate_part, up_part, inverse, share):
+    gate_part = inverse * gate_part
+    silu = gate_part / (1.0 + jnp.exp(-gate_part))
+    return (silu * (inverse * up_part) * share).T.astype(jnp.bfloat16)
 
 
 def second_expert_kernel(
@@ -446,6 +413,9 @@
     gates_ref,
     ups_ref,
     stats_ref,
+    early_gates,
+    early_ups,
+    early_stats,
     gate_a,
     gate_b,
     up_a,
@@ -454,11 +424,19 @@
     down_b,
     out_ref,
     hidden,
+    late_gates,
+    late_ups,
+    late_stats,
     turned,
 ):
     width = turned.shape[0]
-    square = stats_ref[0:1, :] + turned_half(rows_ref, gain_ref, width, width, turned)
-    inverse = lax.rsqrt(square / (2 * width) + 1e-06)
+    square = turned_half(rows_ref, gain_ref, width, width, turned)
+    late_stats[0:1, :] = square
+    row = (8, square.shape[1])
+    other = upper_pair(
+        jnp.broadcast_to(early_stats[0:1, :], row), jnp.broadcast_to(square, row)
+    )[0:1, :]
+    inverse = lax.rsqrt((stats_ref[0:1, :] + other) / (2 * width) + 1e-06)
     share = stats_ref[1:2, :]
     rows = turned[...]
     units = gate_a.shape[0]
@@ -466,108 +444,126 @@
         for low in range(0, units, UNITS):
             chunk = slice(low, low + UNITS)
             at = slice(half * units + low, half * units + low + UNITS)
-            gate_part = inverse * (
-                gates_ref[at, :]
-                + jnp.dot(gate_ref[chunk, width:], rows, preferred_element_type=jnp.float32)
+            gate_part = jnp.dot(
+                gate_ref[chunk, width:], rows, preferred_element_type=jnp.float32
             )
-            up_part = inverse * (
-                ups_ref[at, :]
-                + jnp.dot(up_ref[chunk, width:], rows, preferred_element_type=jnp.float32)
+            up_part = jnp.dot(up_ref[chunk, width:], rows, preferred_element_type=jnp.float32)
+            late_gates[at, :] = gate_part
+            late_ups[at, :] = up_part
+            hidden[:, at] = hidden_of(
+                gates_ref[at, :] + upper_pair(early_gates[at, :], gate_part),
+                ups_ref[at, :] + upper_pair(early_ups[at, :], up_part),
+                inverse,
+                share,
             )
-            silu = gate_part / (1.0 + jnp.exp(-gate_part))
-            hidden[:, at] = (silu * up_part * share).T.astype(jnp.bfloat16)
     down_product(hidden, (down_a, down_b), out_ref, 0)
 
 
 def rest_expert_kernel(
-    start, hidden_ref, down_a, down_b, first_ref, sent_ref, kept_ref, value_ref
+    hidden_ref,
+    gates_ref,
+    ups_ref,
+    stats_ref,
+    early_gates,
+    early_ups,
+    early_stats,
+    late_gates,
+    late_ups,
+    late_stats,
+    down_a,
+    down_b,
+    sent_ref,
+    kept_ref,
+    hidden,
+    early_value,
+    late_value,
 ):
-    down_product(hidden_ref, (down_a, down_b), value_ref, start)
-    half = first_ref.shape[0] // 2
-    sent_ref[:half, :] = first_ref[half:, :].astype(sent_ref.dtype)
-    sent_ref[half:, :] = value_ref[half:, :].astype(sent_ref.dtype)
-    kept_ref[:half, :] = first_ref[:half, :]
-    kept_ref[half:, :] = value_ref[:half, :]
-
-
-def first_expert_rows(device, gain, halves, weights):
-    units, model_width = weights[0].shape
-    row_count = halves[0].shape[0]
+    width = sent_ref.shape[1]
+    row = (8, stats_ref.shape[1])
+    other = lower_pair(
+        jnp.broadcast_to(early_stats[0:1, :], row), jnp.broadcast_to(late_stats[0:1, :], row)
+    )[0:1, :]
+    inverse = lax.rsqrt((stats_ref[0:1, :] + other) / (2 * width) + 1e-06)
+    for low in range(0, gates_ref.shape[0], UNITS):
+        at = slice(low, low + UNITS)
+        hidden[:, at] = hidden_of(
+            gates_ref[at, :] + lower_pair(early_gates[at, :], late_gates[at, :]),
+            ups_ref[at, :] + lower_pair(early_ups[at, :], late_ups[at, :]),
+            inverse,
+            stats_ref[1:2, :],
+        )
+    down_product(hidden, (down_a, down_b), early_value, width)
+    down_product(hidden_ref, (down_a, down_b), late_value, width)
+    half = early_value.shape[0] // 2
+    sent_ref[:half, :] = early_value[half:, :].astype(sent_ref.dtype)
+    sent_ref[half:, :] = late_value[half:, :].astype(sent_ref.dtype)
+    kept_ref[:half, :] = early_value[:half, :]
+    kept_ref[half:, :] = late_value[:half, :]
+
+
+def kept_expert_kernel(hidden_ref, down_a, down_b, kept_ref):
+    down_product(hidden_ref, (down_a, down_b), kept_ref, 0)
+
+
+def part_expert_rows(part, device, gain, rows, gates, ups):
+    units, model_width = gates[0].shape
+    row_count = rows.shape[0]
     whole = pl.BlockSpec(memory_space=pltpu.VMEM)
     return pl.pallas_call(
-        first_expert_kernel,
-        name="expert_first",
+        functools.partial(part_expert_kernel, part),
         compiler_params=pltpu.CompilerParams(vmem_limit_bytes=12 << 20),
-        out_shape=(near_shape((row_count, model_width // 2), jnp.float32),) * 2,
-        in_specs=[pl.BlockSpec(memory_space=pltpu.SMEM)] + [whole] * 9,
-        out_specs=(whole,) * 2,
-        scratch_shapes=[
-            pltpu.VMEM((model_width + LANES, row_count), jnp.bfloat16),
-            pltpu.VMEM((row_count, 2 * units), jnp.bfloat16),
-        ],
-        cost_estimate=pl.CostEstimate(
-            flops=12 * row_count * model_width * units,
-            transcendentals=0,
-            bytes_accessed=12 * units * model_width,
-        ),
-    )(
-        device,
-        near(gain),
-        *[near(part) for part in (*halves, *weights)],
-    )
-
-
-def second_expert_rows(device, gain, halves, gates, ups, downs, totals):
-    units, model_width = gates[0].shape
-    units = 2 * units
-    row_count = halves[0].shape[0]
-    width = model_width // 2
-    whole = pl.BlockSpec(memory_space=pltpu.VMEM)
-    gates, ups, downs = [[near(half) for half in pair] for pair in (gates, ups, downs)]
-    gate_parts, up_parts, stats = pl.pallas_call(
-        half_expert_kernel,
-        name="expert_half",
-        compiler_params=pltpu.CompilerParams(vmem_limit_bytes=12 << 20),
-        out_shape=(near_shape((units, row_count), jnp.float32),) * 2
+        out_shape=(near_shape((2 * units, row_count), jnp.float32),) * 2
         + (near_shape((8, row_count), jnp.float32),),
         in_specs=[pl.BlockSpec(memory_space=pltpu.SMEM)] + [whole] * 6,
         out_specs=(whole,) * 3,
-        scratch_shapes=[pltpu.VMEM((width, row_count), jnp.bfloat16)],
-    )(device, near(gain), near(halves[0]), *gates, *ups)
-    first, hidden = pl.pallas_call(
+        scratch_shapes=[pltpu.VMEM((model_width // PARTS, row_count), jnp.bfloat16)],
+    )(device, near(gain), near(rows), *[near(half) for half in (*gates, *ups)])
+
+
+def expert_rows(device, gain, early, late, gates, ups, downs):
+    units, model_width = gates[0].shape
+    row_count = early[0].shape[0]
+    width = model_width // PARTS
+    whole = pl.BlockSpec(memory_space=pltpu.VMEM)
+    first = [part_expert_rows(part, device, gain, early[part], gates, ups) for part in range(PARTS)]
+    half = part_expert_rows(0, device, gain, late[0], gates, ups)
+    products = (near_shape((2 * units, row_count), jnp.float32),) * 2 + (
+        near_shape((8, row_count), jnp.float32),
+    )
+    hidden_shape = near_shape((row_count, 2 * units), jnp.bfloat16)
+    operands = [gain, late[1], *half, *first[1], *gates, *ups, *downs]
+    sent_first, hidden, *rest = pl.pallas_call(
         second_expert_kernel,
         name="expert_second",
         compiler_params=pltpu.CompilerParams(vmem_limit_bytes=12 << 20),
-        out_shape=(
-            near_shape((row_count, width), jnp.bfloat16),
-            near_shape((row_count, units), jnp.bfloat16),
-        ),
-        in_specs=[whole] * 11,
-        out_specs=(whole, whole),
+        out_shape=(near_shape((row_count, width), jnp.bfloat16), hidden_shape) + products,
+        in_specs=[whole] * len(operands),
+        out_specs=(whole,) * 5,
         scratch_shapes=[pltpu.VMEM((width, row_count), jnp.bfloat16)],
-    )(
-        near(gain),
-        near(halves[1]),
-        near(gate_parts),
-        near(up_parts),
-        near(stats),
-        *gates,
-        *ups,
-        *downs,
-    )
-    sent, kept = pl.pallas_call(
-        functools.partial(rest_expert_kernel, width),
+    )(*[near(operand) for operand in operands])
+    operands = [hidden, *first[0], *first[1], *rest, *downs]
+    sent, kept, hidden = pl.pallas_call(
+        rest_expert_kernel,
         name="expert_rest",
         compiler_params=pltpu.CompilerParams(vmem_limit_bytes=12 << 20),
         out_shape=(
             near_shape((row_count, width), jnp.bfloat16),
             near_shape((row_count, width), jnp.float32),
+            hidden_shape,
         ),
-        in_specs=[whole] * 4,
-        out_specs=(whole, whole),
-        scratch_shapes=[pltpu.VMEM((row_count, width), jnp.float32)],
-    )(near(hidden), *downs, near(totals[1]))
-    return [(first, totals[0]), (sent, kept)]
+        in_specs=[whole] * len(operands),
+        out_specs=(whole,) * 3,
+        scratch_shapes=[pltpu.VMEM((row_count, width), jnp.float32)] * 2,
+    )(*[near(operand) for operand in operands])
+    kept_first = pl.pallas_call(
+        kept_expert_kernel,
+        name="expert_kept",
+        compiler_params=pltpu.CompilerParams(vmem_limit_bytes=12 << 20),
+        out_shape=near_shape((row_count, width), jnp.float32),
+        in_specs=[whole] * 3,
+        out_specs=whole,
+    )(*[near(operand) for operand in (hidden, *downs)])
+    return [(sent_first, kept_first), (sent, kept)]
 
 
 def attention_rows(
@@ -695,12 +691,12 @@
         merge_order,
     )
     blocks = [block for block, _ in finished]
-    stages = len(gather_order[0])
+    stages = len(gather_order[0][0])
     own_weights = fetched(weights[::2])
     arrived = {}
     for stage in range(stages):
         for part in range(PARTS):
-            arrived[part] = exchange(blocks[part], gather_order, stage)
+            arrived[part] = exchange(blocks[part], gather_order[part], stage)
             if stage < stages - 1:
                 last = stage == stages - 2
                 blocks[part], passed = joined(
@@ -711,15 +707,10 @@
     device = device_index.reshape(1)
     gate_a, up_a, down_a = own_weights
     gate_b, up_b, down_b = weights[1::2]
-    totals = first_expert_rows(
-        device, gain, blocks, (*own_weights, gate_b, up_b, down_b)
-    )
-    gates = (gate_a, gate_b)
+    gates, ups, downs = (gate_a, gate_b), (up_a, up_b), (down_a, down_b)
     outputs = []
     for part, (sent, kept) in enumerate(
-        second_expert_rows(
-            device, gain, came, gates, (up_a, up_b), (down_a, down_b), totals
-        )
+        expert_rows(device, gain, blocks, came, gates, ups, downs)
     ):
         for stage in range(stages + 1):
             arrived = exchange(sent, scatter_order[part], stage)

time: 94.8 us -> 90.8 us (0.958)
  starting transfers between devices: 32.3 us -> 27.6 us
  Pallas kernels: 24.9 us -> 29.2 us
  waiting for transfers between devices: 34.2 us -> 30.5 us
    ppermute x20, starting transfers between devices: 30.9 us -> 26.2 us  [exchange(): return lax.ppermute(value, 'wide', pairs)]
    pallas_call x4 -> x6, Pallas kernels: 16.1 us -> 20.5 us  [the longest x3 10 us: part_expert_rows(): pl.pallas_call(functools.partial(part_expert_kernel, part), compiler_para...]
    ppermute x20, waiting for transfers between devices: 31.9 us -> 28.1 us  [exchange(): return lax.ppermute(value, 'wide', pairs)]
  transfers between devices with their start and end apart: 25 -> 25, of which waited for: 14 -> 12; matrix products, arithmetic and copies ran while one was open for 0% -> 0% of each run, Pallas kernels for 21% -> 23%
where the time goes in v8:
time: 90.8 us; the launch traced here: 90.4 us
  waiting for transfers between devices  30.5 us (34%)
  Pallas kernels  29.2 us (32%)
  starting transfers between devices  27.6 us (30%)
  local copies, waits for them, and re-layouts  1.77 us (2%)
  other arithmetic  0.99 us (1%)
    ppermute x20, waiting for transfers between devices, exchange(): return lax.ppermute(value, 'wide', pairs)  28.1 us
    ppermute x20, starting transfers between devices, exchange(): return lax.ppermute(value, 'wide', pairs)  26.2 us
    pallas_call x3, Pallas kernels, part_expert_rows(): pl.pallas_call(functools.partial(part_expert_kernel, part), compiler_para...  10 us
    pallas_call x1, Pallas kernels, expert_rows(): pl.pallas_call(second_expert_kernel, name='expert_second', compiler_param...  4.9 us
    pallas_call x1, Pallas kernels, fetched(): pl.pallas_call(fetch_kernel, compiler_params=pltpu.CompilerParams(vmem_li...  3.34 us
    pallas_call x1, Pallas kernels, expert_rows(): pl.pallas_call(rest_expert_kernel, name='expert_rest', compiler_params=pl...  3.27 us
    pallas_call x2, Pallas kernels, attention_rows(): pl.pallas_call(functools.partial(attend_kernel, HEADS, part, part_heads),...  2.74 us
    ppermute x5, waiting for transfers between devices, partner(): return lax.ppermute(value, axis, pairs)  2.35 us
  transfers between devices with their start and end apart: 25, of which 12 were waited for; matrix products, arithmetic and copies ran while one was open for 0% of the time, Pallas kernels for 23%

profile of v8, /device:TPU:0, one launch (start us, length us, event | category | flops | bytes accessed | tf_op | source)
XLA Modules:
  0.0 90.4 jit_solution(9289450994728522431)
XLA Ops:
  0.5 2.3 %collective-permute-done.keys_b = bf16[128,1152]{1,0:T(8,128)(2,1)S(1)} collective-permute-done((bf16[128,1152]{1,0:T(8,128)(2,1)}, bf16[128,1152]{1,0:T(8,128)(2,1)S(1)}, u32[]{:S(2)}, u32[]{:S(2)}) %collective-permute-start) | collective-permute-done | bytes 294944 | tf_op jit(solution)/shard_map/ppermute | solution.py:33
  4.5 1.3 %stage_in.1 = (bf16[128,1152]{1,0:T(8,128)(2,1)S(1)}, bf16[128,1152]{1,0:T(8,128)(2,1)S(1)}, bf16[128,2560]{1,0:T(8,128)(2,1)S(1)}) custom-call(s32[1]{0:T(128)} %bitcast.device_ref, bf16[256,1152]{1,0:T(8,128)(2,1)} %queries_ref.1, bf16[128,1152]{1,0:T(8,128)(2,1)} %keys_ref.1, bf16[128,2560]{1,0:T(8,128)(2,1)} %values_ref.1), custom_call_target="tpu_custom_call" | custom-call | tf_op jit(solution)/shard_map/stage_in/pallas_call | solution.py:598
  5.8 1.0 %copy-done.1 = bf16[128,1152]{1,0:T(8,128)(2,1)S(1)} copy-done((bf16[128,1152]{1,0:T(8,128)(2,1)S(1)}, bf16[128,1152]{1,0:T(8,128)(2,1)}, u32[]{:S(2)}) %copy-start.1) | copy-done | bytes 294936
  6.7 1.5 %shard_map.95 = (bf16[64,1408]{1,0:T(8,128)(2,1)S(1)}, f32[64,1408]{1,0:T(8,128)S(1)}) custom-call(bf16[128,1152]{1,0:T(8,128)(2,1)S(1)} %get-tuple-element.57.query_ref, bf16[128,1152]{1,0:T(8,128)(2,1)S(1)} %get-tuple-element.58.keys_a, bf16[128,1152]{1,0:T(8,128)(2,1)S(1)} %copy-done.1, bf16[128,2560]{1,0:T(8,128)(2,1)S(1)} %get-tuple-element.60.values_a, ...), custom_call_target="tpu_custom_call" | custom-call | tf_op jit(solution)/shard_map/pallas_call | solution.py:614
  8.3 2.7 %collective-permute-start.5 = (bf16[64,1408]{1,0:T(8,128)(2,1)S(1)}, bf16[64,1408]{1,0:T(8,128)(2,1)S(1)}, u32[]{:S(2)}, u32[]{:S(2)}) collective-permute-start(bf16[64,1408]{1,0:T(8,128)(2,1)S(1)} %get-tuple-element.70), channel_id=1, source_target_pairs={{0,2},{1,5},{2,0},{3,7},{4,6},{5,1},{6,4},{7,3},{8,10},{9,13},{10,... | collective-permute-start | bytes 540680 | tf_op jit(solution)/shard_map/ppermute | solution.py:55
  10.9 1.2 %shard_map.91 = (bf16[64,1408]{1,0:T(8,128)(2,1)S(1)}, f32[64,1408]{1,0:T(8,128)S(1)}) custom-call(bf16[128,1152]{1,0:T(8,128)(2,1)S(1)} %get-tuple-element.57.query_ref, bf16[128,1152]{1,0:T(8,128)(2,1)S(1)} %get-tuple-element.58.keys_a, bf16[128,1152]{1,0:T(8,128)(2,1)S(1)} %copy-done.1, bf16[128,2560]{1,0:T(8,128)(2,1)S(1)} %get-tuple-element.60.values_a, ...), custom_call_target="tpu_custom_call" | custom-call | tf_op jit(solution)/shard_map/pallas_call | solution.py:614
  12.2 2.2 %collective-permute-done.5.came_ref = bf16[64,1408]{1,0:T(8,128)(2,1)S(1)} collective-permute-done((bf16[64,1408]{1,0:T(8,128)(2,1)S(1)}, bf16[64,1408]{1,0:T(8,128)(2,1)S(1)}, u32[]{:S(2)}, u32[]{:S(2)}) %collective-permute-start.5) | collective-permute-done | bytes 180256 | tf_op jit(solution)/shard_map/ppermute | solution.py:55
  14.7 2.1 %collective-permute-start.6 = (bf16[32,1408]{1,0:T(8,128)(2,1)S(1)}, bf16[32,1408]{1,0:T(8,128)(2,1)S(1)}, u32[]{:S(2)}, u32[]{:S(2)}) collective-permute-start(bf16[32,1408]{1,0:T(8,128)(2,1)S(1)} %get-tuple-element.72), channel_id=1, source_target_pairs={{0,4},{1,9},{2,6},{3,11},{4,0},{5,13},{6,2},{7,15},{8,12},{9,1},{1... | collective-permute-start | bytes 270344 | tf_op jit(solution)/shard_map/ppermute | solution.py:55
  18.0 1.6 %collective-permute-start.3 = (bf16[32,1408]{1,0:T(8,128)(2,1)S(1)}, bf16[32,1408]{1,0:T(8,128)(2,1)S(1)}, u32[]{:S(2)}, u32[]{:S(2)}) collective-permute-start(bf16[32,1408]{1,0:T(8,128)(2,1)S(1)} %get-tuple-element.65), channel_id=1, source_target_pairs={{0,4},{1,9},{2,6},{3,11},{4,0},{5,13},{6,2},{7,15},{8,12},{9,1},{1... | collective-permute-start | bytes 270344 | tf_op jit(solution)/shard_map/ppermute | solution.py:55
  19.7 2.9 %collective-permute-done.3.came_ref = bf16[32,1408]{1,0:T(8,128)(2,1)S(1)} collective-permute-done((bf16[32,1408]{1,0:T(8,128)(2,1)S(1)}, bf16[32,1408]{1,0:T(8,128)(2,1)S(1)}, u32[]{:S(2)}, u32[]{:S(2)}) %collective-permute-start.3) | collective-permute-done | bytes 90144 | tf_op jit(solution)/shard_map/ppermute | solution.py:55
  22.7 1.6 %collective-permute-start.4 = (bf16[32,1408]{1,0:T(8,128)(2,1)S(1)}, bf16[32,1408]{1,0:T(8,128)(2,1)S(1)}, u32[]{:S(2)}, u32[]{:S(2)}) collective-permute-start(bf16[32,1408]{1,0:T(8,128)(2,1)S(1)} %get-tuple-element.67), channel_id=1, source_target_pairs={{0,8},{1,3},{2,10},{3,1},{4,12},{5,7},{6,14},{7,5},{8,0},{9,11},{1... | collective-permute-start | bytes 270344 | tf_op jit(solution)/shard_map/ppermute | solution.py:55
  25.1 2.3 %collective-permute-done.4.came_ref = bf16[32,1408]{1,0:T(8,128)(2,1)S(1)} collective-permute-done((bf16[32,1408]{1,0:T(8,128)(2,1)S(1)}, bf16[32,1408]{1,0:T(8,128)(2,1)S(1)}, u32[]{:S(2)}, u32[]{:S(2)}) %collective-permute-start.4) | collective-permute-done | bytes 90144 | tf_op jit(solution)/shard_map/ppermute | solution.py:55
  27.6 2.8 %collective-permute-start.10 = (bf16[32,1408]{1,0:T(8,128)(2,1)S(1)}, bf16[32,1408]{1,0:T(8,128)(2,1)S(1)}, u32[]{:S(2)}, u32[]{:S(2)}) collective-permute-start(bf16[32,1408]{1,0:T(8,128)(2,1)S(1)} %get-tuple-element.76.own_ref), channel_id=1, source_target_pairs={{0,16},{1,17},{2,18},{3,19},{4,20},{5,21},{6,22},{7,23},{8,24},{9,... | collective-permute-start | bytes 270344 | tf_op jit(solution)/shard_map/ppermute | solution.py:55
  30.7 1.5 %collective-permute-start.8 = (bf16[32,1280]{1,0:T(8,128)(2,1)S(1)}, bf16[32,1280]{1,0:T(8,128)(2,1)S(1)}, u32[]{:S(2)}, u32[]{:S(2)}) collective-permute-start(bf16[32,1280]{1,0:T(8,128)(2,1)S(1)} %get-tuple-element.75.own_ref), channel_id=1, source_target_pairs={{0,16},{1,17},{2,18},{3,19},{4,20},{5,21},{6,22},{7,23},{8,24},{9,... | collective-permute-start | bytes 245768 | tf_op jit(solution)/shard_map/ppermute | solution.py:55
  32.2 2.5 %collective-permute-done.10.came_ref = bf16[32,1408]{1,0:T(8,128)(2,1)S(1)} collective-permute-done((bf16[32,1408]{1,0:T(8,128)(2,1)S(1)}, bf16[32,1408]{1,0:T(8,128)(2,1)S(1)}, u32[]{:S(2)}, u32[]{:S(2)}) %collective-permute-start.10) | collective-permute-done | bytes 90144 | tf_op jit(solution)/shard_map/ppermute | solution.py:55
  34.7 1.6 %collective-permute-start.11 = (bf16[64,1408]{1,0:T(8,128)(2,1)S(1)}, bf16[64,1408]{1,0:T(8,128)(2,1)S(1)}, u32[]{:S(2)}, u32[]{:S(2)}) collective-permute-start(bf16[64,1408]{1,0:T(8,128)(2,1)S(1)} %shard_map.100.own_ref), channel_id=1, source_target_pairs={{0,4},{1,5},{2,6},{3,7},{4,0},{5,1},{6,2},{7,3},{8,12},{9,13},{10,... | collective-permute-start | bytes 540680 | tf_op jit(solution)/shard_map/ppermute | solution.py:55
  36.3 1.9 %collective-permute-start.9 = (bf16[64,1280]{1,0:T(8,128)(2,1)S(1)}, bf16[64,1280]{1,0:T(8,128)(2,1)S(1)}, u32[]{:S(2)}, u32[]{:S(2)}) collective-permute-start(bf16[64,1280]{1,0:T(8,128)(2,1)S(1)} %shard_map.99.own_ref), channel_id=1, source_target_pairs={{0,2},{1,9},{2,0},{3,11},{4,6},{5,13},{6,4},{7,15},{8,10},{9,1},{1... | collective-permute-start | bytes 491528 | tf_op jit(solution)/shard_map/ppermute | solution.py:55
  38.2 3.3 %shard_map.101 = (bf16[512,2560]{1,0:T(8,128)(2,1)S(1)}, bf16[512,2560]{1,0:T(8,128)(2,1)S(1)}, bf16[512,2560]{1,0:T(8,128)(2,1)S(1)}) custom-call(bf16[512,2560]{1,0:T(8,128)(2,1)} %refs_0_, bf16[512,2560]{1,0:T(8,128)(2,1)} %refs_1_, bf16[512,2560]{1,0:T(8,128)(2,1)} %refs_2_), custom_call_target="tpu_custom_call" | custom-call | tf_op jit(solution)/shard_map/pallas_call | solution.py:314
  42.1 2.5 %collective-permute-start.12 = (bf16[128,1280]{1,0:T(8,128)(2,1)S(1)}, bf16[128,1280]{1,0:T(8,128)(2,1)S(1)}, u32[]{:S(2)}, u32[]{:S(2)}) collective-permute-start(bf16[128,1280]{1,0:T(8,128)(2,1)S(1)} %get-tuple-element.86.rows_ref), channel_id=1, source_target_pairs={{0,4},{1,5},{2,6},{3,7},{4,0},{5,1},{6,2},{7,3},{8,12},{9,13},{10,... | collective-permute-start | bytes 983048 | tf_op jit(solution)/shard_map/ppermute | solution.py:55
  44.6 3.3 %shard_map.105 = (f32[1024,128]{1,0:T(8,128)S(1)}, f32[1024,128]{1,0:T(8,128)S(1)}, f32[8,128]{1,0:T(8,128)S(1)}) custom-call(s32[1]{0:T(128)} %bitcast.device_ref, f32[1,2560]{1,0:T(1,128)S(1)} %reshape.14.gain_ref, bf16[128,1280]{1,0:T(8,128)(2,1)S(1)} %get-tuple-element.86.rows_ref, bf16[512,2560]{1,0:T(8,128)(2,1)S(1)} %get-tuple-element.88.gate_a, ...), custom_call_target="tpu_custom_call" | custom-call | tf_op jit(solution)/shard_map/pallas_call | solution.py:512
  48.0 3.3 %shard_map.106 = (f32[1024,128]{1,0:T(8,128)S(1)}, f32[1024,128]{1,0:T(8,128)S(1)}, f32[8,128]{1,0:T(8,128)S(1)}) custom-call(s32[1]{0:T(128)} %bitcast.device_ref, f32[1,2560]{1,0:T(1,128)S(1)} %reshape.14.gain_ref, bf16[128,1408]{1,0:T(8,128)(2,1)S(1)} %get-tuple-element.87.rows_ref, bf16[512,2560]{1,0:T(8,128)(2,1)S(1)} %get-tuple-element.88.gate_a, ...), custom_call_target="tpu_custom_call" | custom-call | tf_op jit(solution)/shard_map/pallas_call | solution.py:512
  51.4 3.3 %shard_map.104 = (f32[1024,128]{1,0:T(8,128)S(1)}, f32[1024,128]{1,0:T(8,128)S(1)}, f32[8,128]{1,0:T(8,128)S(1)}) custom-call(s32[1]{0:T(128)} %bitcast.device_ref, f32[1,2560]{1,0:T(1,128)S(1)} %reshape.14.gain_ref, bf16[128,1408]{1,0:T(8,128)(2,1)S(1)} %collective-permute-done.13.rows_ref, bf16[512,2560]{1,0:T(8,128)(2,1)S(1)} %get-tuple-element.88.gate_a, ...), custom_call_target="tpu_custom_call" | custom-call | tf_op jit(solution)/shard_map/pallas_call | solution.py:512
  54.7 4.9 %expert_second.1 = (bf16[128,1280]{1,0:T(8,128)(2,1)S(1)}, bf16[128,1024]{1,0:T(8,128)(2,1)S(1)}, f32[1024,128]{1,0:T(8,128)S(1)}, f32[1024,128]{1,0:T(8,128)S(1)}, f32[8,128]{1,0:T(8,128)S(1)}) custom-call(f32[1,2560]{1,0:T(1,128)S(1)} %reshape.14.gain_ref, bf16[128,1280]{1,0:T(8,128)(2,1)S(1)} %collective-permute-done.12.rows_ref, ...), custom_call_target="tpu_custom_call" | custom-call | tf_op jit(solution)/shard_map/expert_second/pallas_call | solution.py:535
  59.6 3.3 %expert_rest.1 = (bf16[128,1280]{1,0:T(8,128)(2,1)S(1)}, f32[128,1280]{1,0:T(8,128)S(1)}, bf16[128,1024]{1,0:T(8,128)(2,1)S(1)}) custom-call(bf16[128,1024]{1,0:T(8,128)(2,1)S(1)} %get-tuple-element.97.hidden_ref, f32[1024,128]{1,0:T(8,128)S(1)} %get-tuple-element.98.gates_ref, f32[1024,128]{1,0:T(8,128)S(1)} %get-tuple-element.99.ups_ref, ...), custom_call_target="tpu_custom_call" | custom-call | tf_op jit(solution)/shard_map/expert_rest/pallas_call | solution.py:545
  64.4 2.3 %expert_kept.1 = f32[128,1280]{1,0:T(8,128)S(1)} custom-call(bf16[128,1024]{1,0:T(8,128)(2,1)S(1)} %get-tuple-element.104.hidden_ref, bf16[512,2560]{1,0:T(8,128)(2,1)S(1)} %get-tuple-element.96.down_a, bf16[512,2560]{1,0:T(8,128)(2,1)} %collective-permute-done.16.down_b), custom_call_target="tpu_custom_call" | custom-call | tf_op jit(solution)/shard_map/expert_kept/pallas_call | solution.py:558
  66.7 5.1 %collective-permute-done.21 = bf16[128,1280]{1,0:T(8,128)(2,1)S(1)} collective-permute-done((bf16[128,1280]{1,0:T(8,128)(2,1)S(1)}, bf16[128,1280]{1,0:T(8,128)(2,1)S(1)}, u32[]{:S(2)}, u32[]{:S(2)}) %collective-permute-start.21) | collective-permute-done | bytes 327712 | tf_op jit(solution)/shard_map/ppermute | solution.py:55
  72.8 4.8 %collective-permute-done.22 = bf16[64,1280]{1,0:T(8,128)(2,1)S(1)} collective-permute-done((bf16[64,1280]{1,0:T(8,128)(2,1)S(1)}, bf16[64,1280]{1,0:T(8,128)(2,1)S(1)}, u32[]{:S(2)}, u32[]{:S(2)}) %collective-permute-start.22) | collective-permute-done | bytes 163872 | tf_op jit(solution)/shard_map/ppermute | solution.py:55
  77.6 1.4 %collective-permute-start.23 = (bf16[32,1280]{1,0:T(8,128)(2,1)S(1)}, bf16[32,1280]{1,0:T(8,128)(2,1)S(1)}, u32[]{:S(2)}, u32[]{:S(2)}) collective-permute-start(bf16[32,1280]{1,0:T(8,128)(2,1)S(1)} %slice.88), channel_id=1, source_target_pairs={{0,16},{1,17},{2,18},{3,19},{4,20},{5,21},{6,22},{7,23},{8,24},{9,... | collective-permute-start | bytes 245768 | tf_op jit(solution)/shard_map/ppermute | solution.py:55
  79.1 1.6 %collective-permute-start.19 = (bf16[32,1280]{1,0:T(8,128)(2,1)S(1)}, bf16[32,1280]{1,0:T(8,128)(2,1)S(1)}, u32[]{:S(2)}, u32[]{:S(2)}) collective-permute-start(bf16[32,1280]{1,0:T(8,128)(2,1)S(1)} %slice.89), channel_id=1, source_target_pairs={{0,16},{1,17},{2,18},{3,19},{4,20},{5,21},{6,22},{7,23},{8,24},{9,... | collective-permute-start | bytes 245768 | tf_op jit(solution)/shard_map/ppermute | solution.py:55
  80.7 4.0 %collective-permute-done.23 = bf16[32,1280]{1,0:T(8,128)(2,1)S(1)} collective-permute-done((bf16[32,1280]{1,0:T(8,128)(2,1)S(1)}, bf16[32,1280]{1,0:T(8,128)(2,1)S(1)}, u32[]{:S(2)}, u32[]{:S(2)}) %collective-permute-start.23) | collective-permute-done | bytes 81952 | tf_op jit(solution)/shard_map/ppermute | solution.py:55
  85.7 1.3 %collective-permute-start.20 = (bf16[16,1280]{1,0:T(8,128)(2,1)S(1)}, bf16[16,1280]{1,0:T(8,128)(2,1)S(1)}, u32[]{:S(2)}, u32[]{:S(2)}) collective-permute-start(bf16[16,1280]{1,0:T(8,128)(2,1)S(1)} %slice.91), channel_id=1, source_target_pairs={{0,8},{1,3},{2,10},{3,1},{4,12},{5,7},{6,14},{7,5},{8,0},{9,11},{1... | collective-permute-start | bytes 122888 | tf_op jit(solution)/shard_map/ppermute | solution.py:55
  87.0 1.9 %collective-permute-done.24 = bf16[16,1280]{1,0:T(8,128)(2,1)S(1)} collective-permute-done((bf16[16,1280]{1,0:T(8,128)(2,1)S(1)}, bf16[16,1280]{1,0:T(8,128)(2,1)S(1)}, u32[]{:S(2)}, u32[]{:S(2)}) %collective-permute-start.24) | collective-permute-done | bytes 40992 | tf_op jit(solution)/shard_map/ppermute | solution.py:55
  (67 shorter events, 10.6 us)
Async XLA Ops:
  0.0 3.6 %collective-permute-start.1 = (bf16[128,2560]{1,0:T(8,128)(2,1)}, bf16[128,2560]{1,0:T(8,128)(2,1)S(1)}, u32[]{:S(2)}, u32[]{:S(2)}) collective-permute-start(bf16[128,2560]{1,0:T(8,128)(2,1)} %values_ref.1), channel_id=1, source_target_pairs={{0,1},{1,0},{2,3},{3,2},{4,5},{5,4},{6,7},{7,6},{8,9},{9,8},{10,11... | collective-permute-start | bytes 1966088 | tf_op jit(solution)/shard_map/ppermute | solution.py:33
  0.5 2.4 %collective-permute-start = (bf16[128,1152]{1,0:T(8,128)(2,1)}, bf16[128,1152]{1,0:T(8,128)(2,1)S(1)}, u32[]{:S(2)}, u32[]{:S(2)}) collective-permute-start(bf16[128,1152]{1,0:T(8,128)(2,1)} %keys_ref.1), channel_id=1, source_target_pairs={{0,1},{1,0},{2,3},{3,2},{4,5},{5,4},{6,7},{7,6},{8,9},{9,8},{10,11... | collective-permute-start | bytes 884744 | tf_op jit(solution)/shard_map/ppermute | solution.py:33
  2.9 0.7 copy-start
  3.6 41.0 %collective-permute-start.14 = (bf16[512,2560]{1,0:T(8,128)(2,1)}, bf16[512,2560]{1,0:T(8,128)(2,1)S(1)}, u32[]{:S(2)}, u32[]{:S(2)}) collective-permute-start(bf16[512,2560]{1,0:T(8,128)(2,1)} %refs_0_), channel_id=1, source_target_pairs={{0,1},{1,0},{2,3},{3,2},{4,5},{5,4},{6,7},{7,6},{8,9},{9,8},{10,11... | collective-permute-start | bytes 7864328 | tf_op jit(solution)/shard_map/ppermute | solution.py:33
  4.0 40.7 %collective-permute-start.15 = (bf16[512,2560]{1,0:T(8,128)(2,1)}, bf16[512,2560]{1,0:T(8,128)(2,1)}, u32[]{:S(2)}, u32[]{:S(2)}) collective-permute-start(bf16[512,2560]{1,0:T(8,128)(2,1)} %refs_1_), channel_id=1, source_target_pairs={{0,1},{1,0},{2,3},{3,2},{4,5},{5,4},{6,7},{7,6},{8,9},{9,8},{10,11... | collective-permute-start | bytes 7864328 | tf_op jit(solution)/shard_map/ppermute | solution.py:33
  4.1 50.6 %collective-permute-start.16 = (bf16[512,2560]{1,0:T(8,128)(2,1)}, bf16[512,2560]{1,0:T(8,128)(2,1)}, u32[]{:S(2)}, u32[]{:S(2)}) collective-permute-start(bf16[512,2560]{1,0:T(8,128)(2,1)} %refs_2_), channel_id=1, source_target_pairs={{0,1},{1,0},{2,3},{3,2},{4,5},{5,4},{6,7},{7,6},{8,9},{9,8},{10,11... | collective-permute-start | bytes 7864328 | tf_op jit(solution)/shard_map/ppermute | solution.py:33
  5.8 1.0 %copy-start.1 = (bf16[128,1152]{1,0:T(8,128)(2,1)S(1)}, bf16[128,1152]{1,0:T(8,128)(2,1)}, u32[]{:S(2)}) copy-start(bf16[128,1152]{1,0:T(8,128)(2,1)} %copy-done) | copy-start | bytes 884740
  6.7 12.8 %copy-start.3 = (s32[16,6]{0,1:T(8,128)S(1)}, s32[16,6]{0,1:T(8,128)}, u32[]{:S(2)}) copy-start(s32[16,6]{0,1:T(8,128)} %param.14) | copy-start | bytes 1156
  6.7 12.8 %copy-start.4 = (s32[16,6]{0,1:T(8,128)S(1)}, s32[16,6]{0,1:T(8,128)}, u32[]{:S(2)}) copy-start(s32[16,6]{0,1:T(8,128)} %param.13) | copy-start | bytes 1156
  8.3 6.1 %collective-permute-start.5 = (bf16[64,1408]{1,0:T(8,128)(2,1)S(1)}, bf16[64,1408]{1,0:T(8,128)(2,1)S(1)}, u32[]{:S(2)}, u32[]{:S(2)}) collective-permute-start(bf16[64,1408]{1,0:T(8,128)(2,1)S(1)} %get-tuple-element.70), channel_id=1, source_target_pairs={{0,2},{1,5},{2,0},{3,7},{4,6},{5,1},{6,4},{7,3},{8,10},{9,13},{10,... | collective-permute-start | bytes 540680 | tf_op jit(solution)/shard_map/ppermute | solution.py:55
  12.1 5.6 %collective-permute-start.2 = (bf16[64,1408]{1,0:T(8,128)(2,1)S(1)}, bf16[64,1408]{1,0:T(8,128)(2,1)S(1)}, u32[]{:S(2)}, u32[]{:S(2)}) collective-permute-start(bf16[64,1408]{1,0:T(8,128)(2,1)S(1)} %get-tuple-element.63), channel_id=1, source_target_pairs={{0,2},{1,5},{2,0},{3,7},{4,6},{5,1},{6,4},{7,3},{8,10},{9,13},{10,... | collective-permute-start | bytes 540680 | tf_op jit(solution)/shard_map/ppermute | solution.py:55
  14.7 9.7 %collective-permute-start.6 = (bf16[32,1408]{1,0:T(8,128)(2,1)S(1)}, bf16[32,1408]{1,0:T(8,128)(2,1)S(1)}, u32[]{:S(2)}, u32[]{:S(2)}) collective-permute-start(bf16[32,1408]{1,0:T(8,128)(2,1)S(1)} %get-tuple-element.72), channel_id=1, source_target_pairs={{0,4},{1,9},{2,6},{3,11},{4,0},{5,13},{6,2},{7,15},{8,12},{9,1},{1... | collective-permute-start | bytes 270344 | tf_op jit(solution)/shard_map/ppermute | solution.py:55
  18.0 4.6 %collective-permute-start.3 = (bf16[32,1408]{1,0:T(8,128)(2,1)S(1)}, bf16[32,1408]{1,0:T(8,128)(2,1)S(1)}, u32[]{:S(2)}, u32[]{:S(2)}) collective-permute-start(bf16[32,1408]{1,0:T(8,128)(2,1)S(1)} %get-tuple-element.65), channel_id=1, source_target_pairs={{0,4},{1,9},{2,6},{3,11},{4,0},{5,13},{6,2},{7,15},{8,12},{9,1},{1... | collective-permute-start | bytes 270344 | tf_op jit(solution)/shard_map/ppermute | solution.py:55
  22.7 4.6 %collective-permute-start.4 = (bf16[32,1408]{1,0:T(8,128)(2,1)S(1)}, bf16[32,1408]{1,0:T(8,128)(2,1)S(1)}, u32[]{:S(2)}, u32[]{:S(2)}) collective-permute-start(bf16[32,1408]{1,0:T(8,128)(2,1)S(1)} %get-tuple-element.67), channel_id=1, source_target_pairs={{0,8},{1,3},{2,10},{3,1},{4,12},{5,7},{6,14},{7,5},{8,0},{9,11},{1... | collective-permute-start | bytes 270344 | tf_op jit(solution)/shard_map/ppermute | solution.py:55
  24.6 5.9 %collective-permute-start.7 = (bf16[32,1408]{1,0:T(8,128)(2,1)S(1)}, bf16[32,1408]{1,0:T(8,128)(2,1)S(1)}, u32[]{:S(2)}, u32[]{:S(2)}) collective-permute-start(bf16[32,1408]{1,0:T(8,128)(2,1)S(1)} %get-tuple-element.74), channel_id=1, source_target_pairs={{0,8},{1,3},{2,10},{3,1},{4,12},{5,7},{6,14},{7,5},{8,0},{9,11},{1... | collective-permute-start | bytes 270344 | tf_op jit(solution)/shard_map/ppermute | solution.py:55
  27.6 7.1 %collective-permute-start.10 = (bf16[32,1408]{1,0:T(8,128)(2,1)S(1)}, bf16[32,1408]{1,0:T(8,128)(2,1)S(1)}, u32[]{:S(2)}, u32[]{:S(2)}) collective-permute-start(bf16[32,1408]{1,0:T(8,128)(2,1)S(1)} %get-tuple-element.76.own_ref), channel_id=1, source_target_pairs={{0,16},{1,17},{2,18},{3,19},{4,20},{5,21},{6,22},{7,23},{8,24},{9,... | collective-permute-start | bytes 270344 | tf_op jit(solution)/shard_map/ppermute | solution.py:55
  30.7 5.6 %collective-permute-start.8 = (bf16[32,1280]{1,0:T(8,128)(2,1)S(1)}, bf16[32,1280]{1,0:T(8,128)(2,1)S(1)}, u32[]{:S(2)}, u32[]{:S(2)}) collective-permute-start(bf16[32,1280]{1,0:T(8,128)(2,1)S(1)} %get-tuple-element.75.own_ref), channel_id=1, source_target_pairs={{0,16},{1,17},{2,18},{3,19},{4,20},{5,21},{6,22},{7,23},{8,24},{9,... | collective-permute-start | bytes 245768 | tf_op jit(solution)/shard_map/ppermute | solution.py:55
  34.7 6.9 %collective-permute-start.11 = (bf16[64,1408]{1,0:T(8,128)(2,1)S(1)}, bf16[64,1408]{1,0:T(8,128)(2,1)S(1)}, u32[]{:S(2)}, u32[]{:S(2)}) collective-permute-start(bf16[64,1408]{1,0:T(8,128)(2,1)S(1)} %shard_map.100.own_ref), channel_id=1, source_target_pairs={{0,4},{1,5},{2,6},{3,7},{4,0},{5,1},{6,2},{7,3},{8,12},{9,13},{10,... | collective-permute-start | bytes 540680 | tf_op jit(solution)/shard_map/ppermute | solution.py:55
  36.3 5.8 %collective-permute-start.9 = (bf16[64,1280]{1,0:T(8,128)(2,1)S(1)}, bf16[64,1280]{1,0:T(8,128)(2,1)S(1)}, u32[]{:S(2)}, u32[]{:S(2)}) collective-permute-start(bf16[64,1280]{1,0:T(8,128)(2,1)S(1)} %shard_map.99.own_ref), channel_id=1, source_target_pairs={{0,2},{1,9},{2,0},{3,11},{4,6},{5,13},{6,4},{7,15},{8,10},{9,1},{1... | collective-permute-start | bytes 491528 | tf_op jit(solution)/shard_map/ppermute | solution.py:55
  41.6 9.7 %collective-permute-start.13 = (bf16[128,1408]{1,0:T(8,128)(2,1)S(1)}, bf16[128,1408]{1,0:T(8,128)(2,1)S(1)}, u32[]{:S(2)}, u32[]{:S(2)}) collective-permute-start(bf16[128,1408]{1,0:T(8,128)(2,1)S(1)} %get-tuple-element.87.rows_ref), channel_id=1, source_target_pairs={{0,2},{1,9},{2,0},{3,11},{4,6},{5,13},{6,4},{7,15},{8,10},{9,1},{1... | collective-permute-start | bytes 1081352 | tf_op jit(solution)/shard_map/ppermute | solution.py:55
  42.0 2.6 %copy-start.2 = (f32[2560]{0:T(1024)S(1)}, f32[2560]{0:T(1024)}, u32[]{:S(2)}) copy-start(f32[2560]{0:T(1024)} %param.12) | copy-start | bytes 30724
  42.1 12.6 %collective-permute-start.12 = (bf16[128,1280]{1,0:T(8,128)(2,1)S(1)}, bf16[128,1280]{1,0:T(8,128)(2,1)S(1)}, u32[]{:S(2)}, u32[]{:S(2)}) collective-permute-start(bf16[128,1280]{1,0:T(8,128)(2,1)S(1)} %get-tuple-element.86.rows_ref), channel_id=1, source_target_pairs={{0,4},{1,5},{2,6},{3,7},{4,0},{5,1},{6,2},{7,3},{8,12},{9,13},{10,... | collective-permute-start | bytes 983048 | tf_op jit(solution)/shard_map/ppermute | solution.py:55
  62.9 8.9 %collective-permute-start.21 = (bf16[128,1280]{1,0:T(8,128)(2,1)S(1)}, bf16[128,1280]{1,0:T(8,128)(2,1)S(1)}, u32[]{:S(2)}, u32[]{:S(2)}) collective-permute-start(bf16[128,1280]{1,0:T(8,128)(2,1)S(1)} %get-tuple-element.108), channel_id=1, source_target_pairs={{0,4},{1,5},{2,6},{3,7},{4,0},{5,1},{6,2},{7,3},{8,12},{9,13},{10,... | collective-permute-start | bytes 983048 | tf_op jit(solution)/shard_map/ppermute | solution.py:55
  63.6 8.5 %collective-permute-start.17 = (bf16[128,1280]{1,0:T(8,128)(2,1)S(1)}, bf16[128,1280]{1,0:T(8,128)(2,1)S(1)}, u32[]{:S(2)}, u32[]{:S(2)}) collective-permute-start(bf16[128,1280]{1,0:T(8,128)(2,1)S(1)} %get-tuple-element.105), channel_id=1, source_target_pairs={{0,2},{1,9},{2,0},{3,11},{4,6},{5,13},{6,4},{7,15},{8,10},{9,1},{1... | collective-permute-start | bytes 983048 | tf_op jit(solution)/shard_map/ppermute | solution.py:55
  71.9 5.7 %collective-permute-start.22 = (bf16[64,1280]{1,0:T(8,128)(2,1)S(1)}, bf16[64,1280]{1,0:T(8,128)(2,1)S(1)}, u32[]{:S(2)}, u32[]{:S(2)}) collective-permute-start(bf16[64,1280]{1,0:T(8,128)(2,1)S(1)} %slice.86), channel_id=1, source_target_pairs={{0,2},{1,9},{2,0},{3,11},{4,6},{5,13},{6,4},{7,15},{8,10},{9,1},{1... | collective-permute-start | bytes 491528 | tf_op jit(solution)/shard_map/ppermute | solution.py:55
  72.2 6.8 %collective-permute-start.18 = (bf16[64,1280]{1,0:T(8,128)(2,1)S(1)}, bf16[64,1280]{1,0:T(8,128)(2,1)S(1)}, u32[]{:S(2)}, u32[]{:S(2)}) collective-permute-start(bf16[64,1280]{1,0:T(8,128)(2,1)S(1)} %slice.87), channel_id=1, source_target_pairs={{0,4},{1,5},{2,6},{3,7},{4,0},{5,1},{6,2},{7,3},{8,12},{9,13},{10,... | collective-permute-start | bytes 491528 | tf_op jit(solution)/shard_map/ppermute | solution.py:55
  77.6 7.2 %collective-permute-start.23 = (bf16[32,1280]{1,0:T(8,128)(2,1)S(1)}, bf16[32,1280]{1,0:T(8,128)(2,1)S(1)}, u32[]{:S(2)}, u32[]{:S(2)}) collective-permute-start(bf16[32,1280]{1,0:T(8,128)(2,1)S(1)} %slice.88), channel_id=1, source_target_pairs={{0,16},{1,17},{2,18},{3,19},{4,20},{5,21},{6,22},{7,23},{8,24},{9,... | collective-permute-start | bytes 245768 | tf_op jit(solution)/shard_map/ppermute | solution.py:55
  79.1 6.6 %collective-permute-start.19 = (bf16[32,1280]{1,0:T(8,128)(2,1)S(1)}, bf16[32,1280]{1,0:T(8,128)(2,1)S(1)}, u32[]{:S(2)}, u32[]{:S(2)}) collective-permute-start(bf16[32,1280]{1,0:T(8,128)(2,1)S(1)} %slice.89), channel_id=1, source_target_pairs={{0,16},{1,17},{2,18},{3,19},{4,20},{5,21},{6,22},{7,23},{8,24},{9,... | collective-permute-start | bytes 245768 | tf_op jit(solution)/shard_map/ppermute | solution.py:55
  84.8 4.1 %collective-permute-start.24 = (bf16[16,1280]{1,0:T(8,128)(2,1)S(1)}, bf16[16,1280]{1,0:T(8,128)(2,1)S(1)}, u32[]{:S(2)}, u32[]{:S(2)}) collective-permute-start(bf16[16,1280]{1,0:T(8,128)(2,1)S(1)} %slice.90), channel_id=1, source_target_pairs={{0,8},{1,3},{2,10},{3,1},{4,12},{5,7},{6,14},{7,5},{8,0},{9,11},{1... | collective-permute-start | bytes 122888 | tf_op jit(solution)/shard_map/ppermute | solution.py:55
  85.7 4.1 %collective-permute-start.20 = (bf16[16,1280]{1,0:T(8,128)(2,1)S(1)}, bf16[16,1280]{1,0:T(8,128)(2,1)S(1)}, u32[]{:S(2)}, u32[]{:S(2)}) collective-permute-start(bf16[16,1280]{1,0:T(8,128)(2,1)S(1)} %slice.91), channel_id=1, source_target_pairs={{0,8},{1,3},{2,10},{3,1},{4,12},{5,7},{6,14},{7,5},{8,0},{9,11},{1... | collective-permute-start | bytes 122888 | tf_op jit(solution)/shard_map/ppermute | solution.py:55

commit v9 on v8

--- a/solution.py
+++ b/solution.py
@@ -298,49 +298,22 @@
         ).astype(out_ref.dtype)
 
 
-def fetch_kernel(*refs):
-    count = (len(refs) - 1) // 2
-    arrived = refs[-1]
-    copies = [
-        pltpu.make_async_copy(refs[i], refs[count + i], arrived.at[i]) for i in range(count)
-    ]
-    for copy in copies:
-        copy.start()
-    for copy in copies:
-        copy.wait()
-
-
-def fetched(arrays):
-    return pl.pallas_call(
-        fetch_kernel,
-        compiler_params=pltpu.CompilerParams(vmem_limit_bytes=1 << 20),
-        out_shape=tuple(near_shape(array.shape, array.dtype) for array in arrays),
-        in_specs=[pl.BlockSpec(memory_space=pltpu.HBM)] * len(arrays),
-        out_specs=(pl.BlockSpec(memory_space=pltpu.VMEM),) * len(arrays),
-        scratch_shapes=[pltpu.SemaphoreType.DMA((len(arrays),))],
-    )(*[far(array) for array in arrays])
-
-
-def joined_kernel(own_ref, came_ref, *refs):
-    out_ref = refs[len(refs) // 2]
+def joined_kernel(own_ref, came_ref, out_ref):
     half = own_ref.shape[0]
     out_ref[:half, :] = own_ref[...]
     out_ref[half:, :] = came_ref[...]
 
 
-def joined(own, came, passed=()):
+def joined(own, came):
     rows, width = own.shape
     whole = pl.BlockSpec(memory_space=pltpu.VMEM)
-    out, *passed = pl.pallas_call(
+    return pl.pallas_call(
         joined_kernel,
         compiler_params=pltpu.CompilerParams(vmem_limit_bytes=12 << 20),
-        out_shape=(near_shape((2 * rows, width), own.dtype),)
-        + tuple(near_shape(array.shape, array.dtype) for array in passed),
-        in_specs=[whole] * (2 + len(passed)),
-        out_specs=(whole,) * (1 + len(passed)),
-        input_output_aliases={2 + i: 1 + i for i in range(len(passed))},
-    )(near(own), near(came), *[near(array) for array in passed])
-    return out, passed
+        out_shape=near_shape((2 * rows, width), own.dtype),
+        in_specs=[whole] * 2,
+        out_specs=whole,
+    )(near(own), near(came))
 
 
 def turned_half(rows_ref, gain_ref, start, width, turned):
@@ -692,17 +665,13 @@
     )
     blocks = [block for block, _ in finished]
     stages = len(gather_order[0][0])
-    own_weights = fetched(weights[::2])
+    own_weights = weights[::2]
     arrived = {}
     for stage in range(stages):
         for part in range(PARTS):
             arrived[part] = exchange(blocks[part], gather_order[part], stage)
             if stage < stages - 1:
-                last = stage == stages - 2
-                blocks[part], passed = joined(
-                    blocks[part], arrived[part], own_weights if last else ()
-                )
-                own_weights = passed if last else own_weights
+                blocks[part] = joined(blocks[part], arrived[part])
     came = [arrived[part] for part in range(PARTS)]
     device = device_index.reshape(1)
     gate_a, up_a, down_a = own_weights

time: 90.8 us -> 88.7 us (0.977)
  Pallas kernels: 29.2 us -> 26.1 us
  starting transfers between devices: 27.6 us -> 30 us
  waiting for transfers between devices: 30.5 us -> 29.2 us
    pallas_call x1 -> x0, Pallas kernels: 3.34 us -> none  [fetched(): pl.pallas_call(fetch_kernel, compiler_params=pltpu.CompilerParams(vmem_li...]
    ppermute x20, starting transfers between devices: 26.2 us -> 28.6 us  [exchange(): return lax.ppermute(value, 'wide', pairs)]
    ppermute x20, waiting for transfers between devices: 28.1 us -> 26.8 us  [exchange(): return lax.ppermute(value, 'wide', pairs)]
  transfers between devices with their start and end apart: 25 -> 25, of which waited for: 12 -> 15; matrix products, arithmetic and copies ran while one was open for 0% -> 0% of each run, Pallas kernels for 23% -> 24%
where the time goes in v9:
time: 88.7 us; the launch traced here: 88.4 us
  starting transfers between devices  30 us (34%)
  waiting for transfers between devices  29.2 us (33%)
  Pallas kernels  26.1 us (29%)
  local copies, waits for them, and re-layouts  1.79 us (2%)
  other arithmetic  1 us (1%)
    ppermute x20, starting transfers between devices, exchange(): return lax.ppermute(value, 'wide', pairs)  28.6 us
    ppermute x20, waiting for transfers between devices, exchange(): return lax.ppermute(value, 'wide', pairs)  26.8 us
    pallas_call x3, Pallas kernels, part_expert_rows(): pl.pallas_call(functools.partial(part_expert_kernel, part), compiler_para...  10.2 us
    pallas_call x1, Pallas kernels, expert_rows(): pl.pallas_call(second_expert_kernel, name='expert_second', compiler_param...  4.92 us
    pallas_call x1, Pallas kernels, expert_rows(): pl.pallas_call(rest_expert_kernel, name='expert_rest', compiler_params=pl...  3.25 us
    pallas_call x2, Pallas kernels, attention_rows(): pl.pallas_call(functools.partial(attend_kernel, HEADS, part, part_heads),...  2.74 us
    ppermute x5, waiting for transfers between devices, partner(): return lax.ppermute(value, axis, pairs)  2.35 us
    pallas_call x1, Pallas kernels, expert_rows(): pl.pallas_call(kept_expert_kernel, name='expert_kept', compiler_params=pl...  2.32 us
  transfers between devices with their start and end apart: 25, of which 15 were waited for; matrix products, arithmetic and copies ran while one was open for 0% of the time, Pallas kernels for 24%

profile of v9, /device:TPU:0, one launch (start us, length us, event | category | flops | bytes accessed | tf_op | source)
XLA Modules:
  0.0 88.4 jit_solution(17141252832586111627)
XLA Ops:
  0.5 2.3 %collective-permute-done.keys_b = bf16[128,1152]{1,0:T(8,128)(2,1)S(1)} collective-permute-done((bf16[128,1152]{1,0:T(8,128)(2,1)}, bf16[128,1152]{1,0:T(8,128)(2,1)S(1)}, u32[]{:S(2)}, u32[]{:S(2)}) %collective-permute-start) | collective-permute-done | bytes 294944 | tf_op jit(solution)/shard_map/ppermute | solution.py:33
  4.5 1.3 %stage_in.1 = (bf16[128,1152]{1,0:T(8,128)(2,1)S(1)}, bf16[128,1152]{1,0:T(8,128)(2,1)S(1)}, bf16[128,2560]{1,0:T(8,128)(2,1)S(1)}) custom-call(s32[1]{0:T(128)} %bitcast.device_ref, bf16[256,1152]{1,0:T(8,128)(2,1)} %queries_ref.1, bf16[128,1152]{1,0:T(8,128)(2,1)} %keys_ref.1, bf16[128,2560]{1,0:T(8,128)(2,1)} %values_ref.1), custom_call_target="tpu_custom_call" | custom-call | tf_op jit(solution)/shard_map/stage_in/pallas_call | solution.py:571
  6.7 1.5 %shard_map.95 = (bf16[64,1408]{1,0:T(8,128)(2,1)S(1)}, f32[64,1408]{1,0:T(8,128)S(1)}) custom-call(bf16[128,1152]{1,0:T(8,128)(2,1)S(1)} %get-tuple-element.46.query_ref, bf16[128,1152]{1,0:T(8,128)(2,1)S(1)} %get-tuple-element.47.keys_a, bf16[128,1152]{1,0:T(8,128)(2,1)S(1)} %copy-done.4, bf16[128,2560]{1,0:T(8,128)(2,1)S(1)} %get-tuple-element.49.values_a, ...), custom_call_target="tpu_custom_call" | custom-call | tf_op jit(solution)/shard_map/pallas_call | solution.py:587
  8.3 2.7 %collective-permute-start.5 = (bf16[64,1408]{1,0:T(8,128)(2,1)S(1)}, bf16[64,1408]{1,0:T(8,128)(2,1)S(1)}, u32[]{:S(2)}, u32[]{:S(2)}) collective-permute-start(bf16[64,1408]{1,0:T(8,128)(2,1)S(1)} %get-tuple-element.59), channel_id=1, source_target_pairs={{0,2},{1,5},{2,0},{3,7},{4,6},{5,1},{6,4},{7,3},{8,10},{9,13},{10,... | collective-permute-start | bytes 540680 | tf_op jit(solution)/shard_map/ppermute | solution.py:55
  10.9 1.2 %shard_map.91 = (bf16[64,1408]{1,0:T(8,128)(2,1)S(1)}, f32[64,1408]{1,0:T(8,128)S(1)}) custom-call(bf16[128,1152]{1,0:T(8,128)(2,1)S(1)} %get-tuple-element.46.query_ref, bf16[128,1152]{1,0:T(8,128)(2,1)S(1)} %get-tuple-element.47.keys_a, bf16[128,1152]{1,0:T(8,128)(2,1)S(1)} %copy-done.4, bf16[128,2560]{1,0:T(8,128)(2,1)S(1)} %get-tuple-element.49.values_a, ...), custom_call_target="tpu_custom_call" | custom-call | tf_op jit(solution)/shard_map/pallas_call | solution.py:587
  12.3 2.1 %collective-permute-done.5.came_ref = bf16[64,1408]{1,0:T(8,128)(2,1)S(1)} collective-permute-done((bf16[64,1408]{1,0:T(8,128)(2,1)S(1)}, bf16[64,1408]{1,0:T(8,128)(2,1)S(1)}, u32[]{:S(2)}, u32[]{:S(2)}) %collective-permute-start.5) | collective-permute-done | bytes 180256 | tf_op jit(solution)/shard_map/ppermute | solution.py:55
  14.7 2.1 %collective-permute-start.6 = (bf16[32,1408]{1,0:T(8,128)(2,1)S(1)}, bf16[32,1408]{1,0:T(8,128)(2,1)S(1)}, u32[]{:S(2)}, u32[]{:S(2)}) collective-permute-start(bf16[32,1408]{1,0:T(8,128)(2,1)S(1)} %get-tuple-element.61), channel_id=1, source_target_pairs={{0,4},{1,9},{2,6},{3,11},{4,0},{5,13},{6,2},{7,15},{8,12},{9,1},{1... | collective-permute-start | bytes 270344 | tf_op jit(solution)/shard_map/ppermute | solution.py:55
  18.0 1.6 %collective-permute-start.3 = (bf16[32,1408]{1,0:T(8,128)(2,1)S(1)}, bf16[32,1408]{1,0:T(8,128)(2,1)S(1)}, u32[]{:S(2)}, u32[]{:S(2)}) collective-permute-start(bf16[32,1408]{1,0:T(8,128)(2,1)S(1)} %get-tuple-element.54), channel_id=1, source_target_pairs={{0,4},{1,9},{2,6},{3,11},{4,0},{5,13},{6,2},{7,15},{8,12},{9,1},{1... | collective-permute-start | bytes 270344 | tf_op jit(solution)/shard_map/ppermute | solution.py:55
  19.7 2.9 %collective-permute-done.3.came_ref = bf16[32,1408]{1,0:T(8,128)(2,1)S(1)} collective-permute-done((bf16[32,1408]{1,0:T(8,128)(2,1)S(1)}, bf16[32,1408]{1,0:T(8,128)(2,1)S(1)}, u32[]{:S(2)}, u32[]{:S(2)}) %collective-permute-start.3) | collective-permute-done | bytes 90144 | tf_op jit(solution)/shard_map/ppermute | solution.py:55
  22.8 1.6 %collective-permute-start.4 = (bf16[32,1408]{1,0:T(8,128)(2,1)S(1)}, bf16[32,1408]{1,0:T(8,128)(2,1)S(1)}, u32[]{:S(2)}, u32[]{:S(2)}) collective-permute-start(bf16[32,1408]{1,0:T(8,128)(2,1)S(1)} %get-tuple-element.56), channel_id=1, source_target_pairs={{0,8},{1,3},{2,10},{3,1},{4,12},{5,7},{6,14},{7,5},{8,0},{9,11},{1... | collective-permute-start | bytes 270344 | tf_op jit(solution)/shard_map/ppermute | solution.py:55
  25.1 2.3 %collective-permute-done.4.came_ref = bf16[32,1408]{1,0:T(8,128)(2,1)S(1)} collective-permute-done((bf16[32,1408]{1,0:T(8,128)(2,1)S(1)}, bf16[32,1408]{1,0:T(8,128)(2,1)S(1)}, u32[]{:S(2)}, u32[]{:S(2)}) %collective-permute-start.4) | collective-permute-done | bytes 90144 | tf_op jit(solution)/shard_map/ppermute | solution.py:55
  27.6 2.9 %collective-permute-start.11 = (bf16[32,1408]{1,0:T(8,128)(2,1)S(1)}, bf16[32,1408]{1,0:T(8,128)(2,1)S(1)}, u32[]{:S(2)}, u32[]{:S(2)}) collective-permute-start(bf16[32,1408]{1,0:T(8,128)(2,1)S(1)} %get-tuple-element.65.own_ref), channel_id=1, source_target_pairs={{0,16},{1,17},{2,18},{3,19},{4,20},{5,21},{6,22},{7,23},{8,24},{9,... | collective-permute-start | bytes 270344 | tf_op jit(solution)/shard_map/ppermute | solution.py:55
  30.7 1.5 %collective-permute-start.8 = (bf16[32,1280]{1,0:T(8,128)(2,1)S(1)}, bf16[32,1280]{1,0:T(8,128)(2,1)S(1)}, u32[]{:S(2)}, u32[]{:S(2)}) collective-permute-start(bf16[32,1280]{1,0:T(8,128)(2,1)S(1)} %get-tuple-element.64.own_ref), channel_id=1, source_target_pairs={{0,16},{1,17},{2,18},{3,19},{4,20},{5,21},{6,22},{7,23},{8,24},{9,... | collective-permute-start | bytes 245768 | tf_op jit(solution)/shard_map/ppermute | solution.py:55
  32.2 2.5 %collective-permute-done.11.came_ref = bf16[32,1408]{1,0:T(8,128)(2,1)S(1)} collective-permute-done((bf16[32,1408]{1,0:T(8,128)(2,1)S(1)}, bf16[32,1408]{1,0:T(8,128)(2,1)S(1)}, u32[]{:S(2)}, u32[]{:S(2)}) %collective-permute-start.11) | collective-permute-done | bytes 90144 | tf_op jit(solution)/shard_map/ppermute | solution.py:55
  34.7 1.6 %collective-permute-start.12 = (bf16[64,1408]{1,0:T(8,128)(2,1)S(1)}, bf16[64,1408]{1,0:T(8,128)(2,1)S(1)}, u32[]{:S(2)}, u32[]{:S(2)}) collective-permute-start(bf16[64,1408]{1,0:T(8,128)(2,1)S(1)} %shard_map.101.own_ref), channel_id=1, source_target_pairs={{0,4},{1,5},{2,6},{3,7},{4,0},{5,1},{6,2},{7,3},{8,12},{9,13},{10,... | collective-permute-start | bytes 540680 | tf_op jit(solution)/shard_map/ppermute | solution.py:55
  36.3 1.9 %collective-permute-start.9 = (bf16[64,1280]{1,0:T(8,128)(2,1)S(1)}, bf16[64,1280]{1,0:T(8,128)(2,1)S(1)}, u32[]{:S(2)}, u32[]{:S(2)}) collective-permute-start(bf16[64,1280]{1,0:T(8,128)(2,1)S(1)} %shard_map.99.own_ref), channel_id=1, source_target_pairs={{0,2},{1,9},{2,0},{3,11},{4,6},{5,13},{6,4},{7,15},{8,10},{9,1},{1... | collective-permute-start | bytes 491528 | tf_op jit(solution)/shard_map/ppermute | solution.py:55
  38.2 2.8 %collective-permute-done.12.came_ref = bf16[64,1408]{1,0:T(8,128)(2,1)S(1)} collective-permute-done((bf16[64,1408]{1,0:T(8,128)(2,1)S(1)}, bf16[64,1408]{1,0:T(8,128)(2,1)S(1)}, u32[]{:S(2)}, u32[]{:S(2)}) %collective-permute-start.12) | collective-permute-done | bytes 180256 | tf_op jit(solution)/shard_map/ppermute | solution.py:55
  42.1 2.4 %collective-permute-start.10 = (bf16[128,1280]{1,0:T(8,128)(2,1)S(1)}, bf16[128,1280]{1,0:T(8,128)(2,1)S(1)}, u32[]{:S(2)}, u32[]{:S(2)}) collective-permute-start(bf16[128,1280]{1,0:T(8,128)(2,1)S(1)} %shard_map.100.rows_ref), channel_id=1, source_target_pairs={{0,4},{1,5},{2,6},{3,7},{4,0},{5,1},{6,2},{7,3},{8,12},{9,13},{10,... | collective-permute-start | bytes 983048 | tf_op jit(solution)/shard_map/ppermute | solution.py:55
  44.6 3.3 %shard_map.104 = (f32[1024,128]{1,0:T(8,128)S(1)}, f32[1024,128]{1,0:T(8,128)S(1)}, f32[8,128]{1,0:T(8,128)S(1)}) custom-call(s32[1]{0:T(128)} %bitcast.device_ref, f32[1,2560]{1,0:T(1,128)S(1)} %reshape.14.gain_ref, bf16[128,1280]{1,0:T(8,128)(2,1)S(1)} %shard_map.100.rows_ref, bf16[512,2560]{1,0:T(8,128)(2,1)S(1)} %copy-done, ...), custom_call_target="tpu_custom_call" | custom-call | tf_op jit(solution)/shard_map/pallas_call | solution.py:485
  48.5 3.5 %shard_map.103 = (f32[1024,128]{1,0:T(8,128)S(1)}, f32[1024,128]{1,0:T(8,128)S(1)}, f32[8,128]{1,0:T(8,128)S(1)}) custom-call(s32[1]{0:T(128)} %bitcast.device_ref, f32[1,2560]{1,0:T(1,128)S(1)} %reshape.14.gain_ref, bf16[128,1408]{1,0:T(8,128)(2,1)S(1)} %collective-permute-done.13.rows_ref, bf16[512,2560]{1,0:T(8,128)(2,1)S(1)} %copy-done, ...), custom_call_target="tpu_custom_call" | custom-call | tf_op jit(solution)/shard_map/pallas_call | solution.py:485
  52.1 4.9 %expert_second.1 = (bf16[128,1280]{1,0:T(8,128)(2,1)S(1)}, bf16[128,1024]{1,0:T(8,128)(2,1)S(1)}, f32[1024,128]{1,0:T(8,128)S(1)}, f32[1024,128]{1,0:T(8,128)S(1)}, f32[8,128]{1,0:T(8,128)S(1)}) custom-call(f32[1,2560]{1,0:T(1,128)S(1)} %reshape.14.gain_ref, bf16[128,1280]{1,0:T(8,128)(2,1)S(1)} %collective-permute-done.10.rows_ref, ...), custom_call_target="tpu_custom_call" | custom-call | tf_op jit(solution)/shard_map/expert_second/pallas_call | solution.py:508
  58.0 3.3 %shard_map.105 = (f32[1024,128]{1,0:T(8,128)S(1)}, f32[1024,128]{1,0:T(8,128)S(1)}, f32[8,128]{1,0:T(8,128)S(1)}) custom-call(s32[1]{0:T(128)} %bitcast.device_ref, f32[1,2560]{1,0:T(1,128)S(1)} %reshape.14.gain_ref, bf16[128,1408]{1,0:T(8,128)(2,1)S(1)} %shard_map.102.rows_ref, bf16[512,2560]{1,0:T(8,128)(2,1)S(1)} %copy-done, ...), custom_call_target="tpu_custom_call" | custom-call | tf_op jit(solution)/shard_map/pallas_call | solution.py:485
  61.4 3.2 %expert_rest.1 = (bf16[128,1280]{1,0:T(8,128)(2,1)S(1)}, f32[128,1280]{1,0:T(8,128)S(1)}, bf16[128,1024]{1,0:T(8,128)(2,1)S(1)}) custom-call(bf16[128,1024]{1,0:T(8,128)(2,1)S(1)} %get-tuple-element.75.hidden_ref, f32[1024,128]{1,0:T(8,128)S(1)} %get-tuple-element.76.gates_ref, f32[1024,128]{1,0:T(8,128)S(1)} %get-tuple-element.77.ups_ref, ...), custom_call_target="tpu_custom_call" | custom-call | tf_op jit(solution)/shard_map/expert_rest/pallas_call | solution.py:518
  64.6 1.4 %collective-permute-start.21 = (bf16[128,1280]{1,0:T(8,128)(2,1)S(1)}, bf16[128,1280]{1,0:T(8,128)(2,1)S(1)}, u32[]{:S(2)}, u32[]{:S(2)}) collective-permute-start(bf16[128,1280]{1,0:T(8,128)(2,1)S(1)} %get-tuple-element.86), channel_id=1, source_target_pairs={{0,4},{1,5},{2,6},{3,7},{4,0},{5,1},{6,2},{7,3},{8,12},{9,13},{10,... | collective-permute-start | bytes 983048 | tf_op jit(solution)/shard_map/ppermute | solution.py:55
  66.0 2.3 %expert_kept.1 = f32[128,1280]{1,0:T(8,128)S(1)} custom-call(bf16[128,1024]{1,0:T(8,128)(2,1)S(1)} %get-tuple-element.82.hidden_ref, bf16[512,2560]{1,0:T(8,128)(2,1)S(1)} %copy-done.2, bf16[512,2560]{1,0:T(8,128)(2,1)} %collective-permute-done.16.down_b), custom_call_target="tpu_custom_call" | custom-call | tf_op jit(solution)/shard_map/expert_kept/pallas_call | solution.py:531
  69.2 2.5 %collective-permute-done.21 = bf16[128,1280]{1,0:T(8,128)(2,1)S(1)} collective-permute-done((bf16[128,1280]{1,0:T(8,128)(2,1)S(1)}, bf16[128,1280]{1,0:T(8,128)(2,1)S(1)}, u32[]{:S(2)}, u32[]{:S(2)}) %collective-permute-start.21) | collective-permute-done | bytes 327712 | tf_op jit(solution)/shard_map/ppermute | solution.py:55
  71.8 1.4 %collective-permute-start.22 = (bf16[64,1280]{1,0:T(8,128)(2,1)S(1)}, bf16[64,1280]{1,0:T(8,128)(2,1)S(1)}, u32[]{:S(2)}, u32[]{:S(2)}) collective-permute-start(bf16[64,1280]{1,0:T(8,128)(2,1)S(1)} %slice.86), channel_id=1, source_target_pairs={{0,2},{1,9},{2,0},{3,11},{4,6},{5,13},{6,4},{7,15},{8,10},{9,1},{1... | collective-permute-start | bytes 491528 | tf_op jit(solution)/shard_map/ppermute | solution.py:55
  73.9 1.7 %collective-permute-start.19 = (bf16[32,1280]{1,0:T(8,128)(2,1)S(1)}, bf16[32,1280]{1,0:T(8,128)(2,1)S(1)}, u32[]{:S(2)}, u32[]{:S(2)}) collective-permute-start(bf16[32,1280]{1,0:T(8,128)(2,1)S(1)} %slice.89), channel_id=1, source_target_pairs={{0,16},{1,17},{2,18},{3,19},{4,20},{5,21},{6,22},{7,23},{8,24},{9,... | collective-permute-start | bytes 245768 | tf_op jit(solution)/shard_map/ppermute | solution.py:55
  75.6 2.1 %collective-permute-done.22 = bf16[64,1280]{1,0:T(8,128)(2,1)S(1)} collective-permute-done((bf16[64,1280]{1,0:T(8,128)(2,1)S(1)}, bf16[64,1280]{1,0:T(8,128)(2,1)S(1)}, u32[]{:S(2)}, u32[]{:S(2)}) %collective-permute-start.22) | collective-permute-done | bytes 163872 | tf_op jit(solution)/shard_map/ppermute | solution.py:55
  79.4 1.5 %collective-permute-start.20 = (bf16[16,1280]{1,0:T(8,128)(2,1)S(1)}, bf16[16,1280]{1,0:T(8,128)(2,1)S(1)}, u32[]{:S(2)}, u32[]{:S(2)}) collective-permute-start(bf16[16,1280]{1,0:T(8,128)(2,1)S(1)} %slice.91), channel_id=1, source_target_pairs={{0,8},{1,3},{2,10},{3,1},{4,12},{5,7},{6,14},{7,5},{8,0},{9,11},{1... | collective-permute-start | bytes 122888 | tf_op jit(solution)/shard_map/ppermute | solution.py:55
  80.9 2.7 %collective-permute-done.23 = bf16[32,1280]{1,0:T(8,128)(2,1)S(1)} collective-permute-done((bf16[32,1280]{1,0:T(8,128)(2,1)S(1)}, bf16[32,1280]{1,0:T(8,128)(2,1)S(1)}, u32[]{:S(2)}, u32[]{:S(2)}) %collective-permute-start.23) | collective-permute-done | bytes 81952 | tf_op jit(solution)/shard_map/ppermute | solution.py:55
  84.0 3.7 %collective-permute-done.24 = bf16[16,1280]{1,0:T(8,128)(2,1)S(1)} collective-permute-done((bf16[16,1280]{1,0:T(8,128)(2,1)S(1)}, bf16[16,1280]{1,0:T(8,128)(2,1)S(1)}, u32[]{:S(2)}, u32[]{:S(2)}) %collective-permute-start.24) | collective-permute-done | bytes 40992 | tf_op jit(solution)/shard_map/ppermute | solution.py:55
  (72 shorter events, 13.2 us)
Async XLA Ops:
  0.0 3.6 %collective-permute-start.1 = (bf16[128,2560]{1,0:T(8,128)(2,1)}, bf16[128,2560]{1,0:T(8,128)(2,1)S(1)}, u32[]{:S(2)}, u32[]{:S(2)}) collective-permute-start(bf16[128,2560]{1,0:T(8,128)(2,1)} %values_ref.1), channel_id=1, source_target_pairs={{0,1},{1,0},{2,3},{3,2},{4,5},{5,4},{6,7},{7,6},{8,9},{9,8},{10,11... | collective-permute-start | bytes 1966088 | tf_op jit(solution)/shard_map/ppermute | solution.py:33
  0.5 2.4 %collective-permute-start = (bf16[128,1152]{1,0:T(8,128)(2,1)}, bf16[128,1152]{1,0:T(8,128)(2,1)S(1)}, u32[]{:S(2)}, u32[]{:S(2)}) collective-permute-start(bf16[128,1152]{1,0:T(8,128)(2,1)} %keys_ref.1), channel_id=1, source_target_pairs={{0,1},{1,0},{2,3},{3,2},{4,5},{5,4},{6,7},{7,6},{8,9},{9,8},{10,11... | collective-permute-start | bytes 884744 | tf_op jit(solution)/shard_map/ppermute | solution.py:33
  3.6 40.9 %collective-permute-start.14 = (bf16[512,2560]{1,0:T(8,128)(2,1)}, bf16[512,2560]{1,0:T(8,128)(2,1)S(1)}, u32[]{:S(2)}, u32[]{:S(2)}) collective-permute-start(bf16[512,2560]{1,0:T(8,128)(2,1)} %gate_a.3), channel_id=1, source_target_pairs={{0,1},{1,0},{2,3},{3,2},{4,5},{5,4},{6,7},{7,6},{8,9},{9,8},{10,11... | collective-permute-start | bytes 7864328 | tf_op jit(solution)/shard_map/ppermute | solution.py:33
  4.0 40.6 %collective-permute-start.15 = (bf16[512,2560]{1,0:T(8,128)(2,1)}, bf16[512,2560]{1,0:T(8,128)(2,1)}, u32[]{:S(2)}, u32[]{:S(2)}) collective-permute-start(bf16[512,2560]{1,0:T(8,128)(2,1)} %up_a.3), channel_id=1, source_target_pairs={{0,1},{1,0},{2,3},{3,2},{4,5},{5,4},{6,7},{7,6},{8,9},{9,8},{10,11... | collective-permute-start | bytes 7864328 | tf_op jit(solution)/shard_map/ppermute | solution.py:33
  4.1 48.0 %collective-permute-start.16 = (bf16[512,2560]{1,0:T(8,128)(2,1)}, bf16[512,2560]{1,0:T(8,128)(2,1)}, u32[]{:S(2)}, u32[]{:S(2)}) collective-permute-start(bf16[512,2560]{1,0:T(8,128)(2,1)} %down_a.2), channel_id=1, source_target_pairs={{0,1},{1,0},{2,3},{3,2},{4,5},{5,4},{6,7},{7,6},{8,9},{9,8},{10,11... | collective-permute-start | bytes 7864328 | tf_op jit(solution)/shard_map/ppermute | solution.py:33
  5.8 1.0 %copy-start.4 = (bf16[128,1152]{1,0:T(8,128)(2,1)S(1)}, bf16[128,1152]{1,0:T(8,128)(2,1)}, u32[]{:S(2)}) copy-start(bf16[128,1152]{1,0:T(8,128)(2,1)} %copy-done.3) | copy-start | bytes 884740
  6.7 12.9 %copy-start.6 = (s32[16,6]{0,1:T(8,128)S(1)}, s32[16,6]{0,1:T(8,128)}, u32[]{:S(2)}) copy-start(s32[16,6]{0,1:T(8,128)} %param.14) | copy-start | bytes 1156
  6.7 12.9 %copy-start.7 = (s32[16,6]{0,1:T(8,128)S(1)}, s32[16,6]{0,1:T(8,128)}, u32[]{:S(2)}) copy-start(s32[16,6]{0,1:T(8,128)} %param.13) | copy-start | bytes 1156
  8.3 6.1 %collective-permute-start.5 = (bf16[64,1408]{1,0:T(8,128)(2,1)S(1)}, bf16[64,1408]{1,0:T(8,128)(2,1)S(1)}, u32[]{:S(2)}, u32[]{:S(2)}) collective-permute-start(bf16[64,1408]{1,0:T(8,128)(2,1)S(1)} %get-tuple-element.59), channel_id=1, source_target_pairs={{0,2},{1,5},{2,0},{3,7},{4,6},{5,1},{6,4},{7,3},{8,10},{9,13},{10,... | collective-permute-start | bytes 540680 | tf_op jit(solution)/shard_map/ppermute | solution.py:55
  10.9 33.6 %copy-start.1 = (bf16[512,2560]{1,0:T(8,128)(2,1)S(1)}, bf16[512,2560]{1,0:T(8,128)(2,1)}, u32[]{:S(2)}) copy-start(bf16[512,2560]{1,0:T(8,128)(2,1)} %up_a.3) | copy-start | bytes 7864324
  12.2 32.4 %copy-start.5 = (f32[2560]{0:T(1024)S(1)}, f32[2560]{0:T(1024)}, u32[]{:S(2)}) copy-start(f32[2560]{0:T(1024)} %param.12) | copy-start | bytes 30724
  12.2 32.4 %copy-start = (bf16[512,2560]{1,0:T(8,128)(2,1)S(1)}, bf16[512,2560]{1,0:T(8,128)(2,1)}, u32[]{:S(2)}) copy-start(bf16[512,2560]{1,0:T(8,128)(2,1)} %gate_a.3) | copy-start | bytes 7864324
  12.2 5.6 %collective-permute-start.2 = (bf16[64,1408]{1,0:T(8,128)(2,1)S(1)}, bf16[64,1408]{1,0:T(8,128)(2,1)S(1)}, u32[]{:S(2)}, u32[]{:S(2)}) collective-permute-start(bf16[64,1408]{1,0:T(8,128)(2,1)S(1)} %get-tuple-element.52), channel_id=1, source_target_pairs={{0,2},{1,5},{2,0},{3,7},{4,6},{5,1},{6,4},{7,3},{8,10},{9,13},{10,... | collective-permute-start | bytes 540680 | tf_op jit(solution)/shard_map/ppermute | solution.py:55
  14.7 9.7 %collective-permute-start.6 = (bf16[32,1408]{1,0:T(8,128)(2,1)S(1)}, bf16[32,1408]{1,0:T(8,128)(2,1)S(1)}, u32[]{:S(2)}, u32[]{:S(2)}) collective-permute-start(bf16[32,1408]{1,0:T(8,128)(2,1)S(1)} %get-tuple-element.61), channel_id=1, source_target_pairs={{0,4},{1,9},{2,6},{3,11},{4,0},{5,13},{6,2},{7,15},{8,12},{9,1},{1... | collective-permute-start | bytes 270344 | tf_op jit(solution)/shard_map/ppermute | solution.py:55
  18.0 4.6 %collective-permute-start.3 = (bf16[32,1408]{1,0:T(8,128)(2,1)S(1)}, bf16[32,1408]{1,0:T(8,128)(2,1)S(1)}, u32[]{:S(2)}, u32[]{:S(2)}) collective-permute-start(bf16[32,1408]{1,0:T(8,128)(2,1)S(1)} %get-tuple-element.54), channel_id=1, source_target_pairs={{0,4},{1,9},{2,6},{3,11},{4,0},{5,13},{6,2},{7,15},{8,12},{9,1},{1... | collective-permute-start | bytes 270344 | tf_op jit(solution)/shard_map/ppermute | solution.py:55
  22.8 4.6 %collective-permute-start.4 = (bf16[32,1408]{1,0:T(8,128)(2,1)S(1)}, bf16[32,1408]{1,0:T(8,128)(2,1)S(1)}, u32[]{:S(2)}, u32[]{:S(2)}) collective-permute-start(bf16[32,1408]{1,0:T(8,128)(2,1)S(1)} %get-tuple-element.56), channel_id=1, source_target_pairs={{0,8},{1,3},{2,10},{3,1},{4,12},{5,7},{6,14},{7,5},{8,0},{9,11},{1... | collective-permute-start | bytes 270344 | tf_op jit(solution)/shard_map/ppermute | solution.py:55
  24.6 5.9 %collective-permute-start.7 = (bf16[32,1408]{1,0:T(8,128)(2,1)S(1)}, bf16[32,1408]{1,0:T(8,128)(2,1)S(1)}, u32[]{:S(2)}, u32[]{:S(2)}) collective-permute-start(bf16[32,1408]{1,0:T(8,128)(2,1)S(1)} %get-tuple-element.63), channel_id=1, source_target_pairs={{0,8},{1,3},{2,10},{3,1},{4,12},{5,7},{6,14},{7,5},{8,0},{9,11},{1... | collective-permute-start | bytes 270344 | tf_op jit(solution)/shard_map/ppermute | solution.py:55
  27.6 7.0 %collective-permute-start.11 = (bf16[32,1408]{1,0:T(8,128)(2,1)S(1)}, bf16[32,1408]{1,0:T(8,128)(2,1)S(1)}, u32[]{:S(2)}, u32[]{:S(2)}) collective-permute-start(bf16[32,1408]{1,0:T(8,128)(2,1)S(1)} %get-tuple-element.65.own_ref), channel_id=1, source_target_pairs={{0,16},{1,17},{2,18},{3,19},{4,20},{5,21},{6,22},{7,23},{8,24},{9,... | collective-permute-start | bytes 270344 | tf_op jit(solution)/shard_map/ppermute | solution.py:55
  30.7 5.6 %collective-permute-start.8 = (bf16[32,1280]{1,0:T(8,128)(2,1)S(1)}, bf16[32,1280]{1,0:T(8,128)(2,1)S(1)}, u32[]{:S(2)}, u32[]{:S(2)}) collective-permute-start(bf16[32,1280]{1,0:T(8,128)(2,1)S(1)} %get-tuple-element.64.own_ref), channel_id=1, source_target_pairs={{0,16},{1,17},{2,18},{3,19},{4,20},{5,21},{6,22},{7,23},{8,24},{9,... | collective-permute-start | bytes 245768 | tf_op jit(solution)/shard_map/ppermute | solution.py:55
  34.7 6.3 %collective-permute-start.12 = (bf16[64,1408]{1,0:T(8,128)(2,1)S(1)}, bf16[64,1408]{1,0:T(8,128)(2,1)S(1)}, u32[]{:S(2)}, u32[]{:S(2)}) collective-permute-start(bf16[64,1408]{1,0:T(8,128)(2,1)S(1)} %shard_map.101.own_ref), channel_id=1, source_target_pairs={{0,4},{1,5},{2,6},{3,7},{4,0},{5,1},{6,2},{7,3},{8,12},{9,13},{10,... | collective-permute-start | bytes 540680 | tf_op jit(solution)/shard_map/ppermute | solution.py:55
  36.3 5.7 %collective-permute-start.9 = (bf16[64,1280]{1,0:T(8,128)(2,1)S(1)}, bf16[64,1280]{1,0:T(8,128)(2,1)S(1)}, u32[]{:S(2)}, u32[]{:S(2)}) collective-permute-start(bf16[64,1280]{1,0:T(8,128)(2,1)S(1)} %shard_map.99.own_ref), channel_id=1, source_target_pairs={{0,2},{1,9},{2,0},{3,11},{4,6},{5,13},{6,4},{7,15},{8,10},{9,1},{1... | collective-permute-start | bytes 491528 | tf_op jit(solution)/shard_map/ppermute | solution.py:55
  41.0 7.5 %collective-permute-start.13 = (bf16[128,1408]{1,0:T(8,128)(2,1)S(1)}, bf16[128,1408]{1,0:T(8,128)(2,1)S(1)}, u32[]{:S(2)}, u32[]{:S(2)}) collective-permute-start(bf16[128,1408]{1,0:T(8,128)(2,1)S(1)} %shard_map.102.rows_ref), channel_id=1, source_target_pairs={{0,2},{1,9},{2,0},{3,11},{4,6},{5,13},{6,4},{7,15},{8,10},{9,1},{1... | collective-permute-start | bytes 1081352 | tf_op jit(solution)/shard_map/ppermute | solution.py:55
  42.1 10.0 %collective-permute-start.10 = (bf16[128,1280]{1,0:T(8,128)(2,1)S(1)}, bf16[128,1280]{1,0:T(8,128)(2,1)S(1)}, u32[]{:S(2)}, u32[]{:S(2)}) collective-permute-start(bf16[128,1280]{1,0:T(8,128)(2,1)S(1)} %shard_map.100.rows_ref), channel_id=1, source_target_pairs={{0,4},{1,5},{2,6},{3,7},{4,0},{5,1},{6,2},{7,3},{8,12},{9,13},{10,... | collective-permute-start | bytes 983048 | tf_op jit(solution)/shard_map/ppermute | solution.py:55
  47.9 4.2 %copy-start.2 = (bf16[512,2560]{1,0:T(8,128)(2,1)S(1)}, bf16[512,2560]{1,0:T(8,128)(2,1)}, u32[]{:S(2)}) copy-start(bf16[512,2560]{1,0:T(8,128)(2,1)} %down_a.2) | copy-start | bytes 7864324
  57.0 11.4 %collective-permute-start.17 = (bf16[128,1280]{1,0:T(8,128)(2,1)S(1)}, bf16[128,1280]{1,0:T(8,128)(2,1)S(1)}, u32[]{:S(2)}, u32[]{:S(2)}) collective-permute-start(bf16[128,1280]{1,0:T(8,128)(2,1)S(1)} %get-tuple-element.83), channel_id=1, source_target_pairs={{0,2},{1,9},{2,0},{3,11},{4,6},{5,13},{6,4},{7,15},{8,10},{9,1},{1... | collective-permute-start | bytes 983048 | tf_op jit(solution)/shard_map/ppermute | solution.py:55
  64.6 7.1 %collective-permute-start.21 = (bf16[128,1280]{1,0:T(8,128)(2,1)S(1)}, bf16[128,1280]{1,0:T(8,128)(2,1)S(1)}, u32[]{:S(2)}, u32[]{:S(2)}) collective-permute-start(bf16[128,1280]{1,0:T(8,128)(2,1)S(1)} %get-tuple-element.86), channel_id=1, source_target_pairs={{0,4},{1,5},{2,6},{3,7},{4,0},{5,1},{6,2},{7,3},{8,12},{9,13},{10,... | collective-permute-start | bytes 983048 | tf_op jit(solution)/shard_map/ppermute | solution.py:55
  68.4 5.4 %collective-permute-start.18 = (bf16[64,1280]{1,0:T(8,128)(2,1)S(1)}, bf16[64,1280]{1,0:T(8,128)(2,1)S(1)}, u32[]{:S(2)}, u32[]{:S(2)}) collective-permute-start(bf16[64,1280]{1,0:T(8,128)(2,1)S(1)} %slice.87), channel_id=1, source_target_pairs={{0,4},{1,5},{2,6},{3,7},{4,0},{5,1},{6,2},{7,3},{8,12},{9,13},{10,... | collective-permute-start | bytes 491528 | tf_op jit(solution)/shard_map/ppermute | solution.py:55
  71.8 5.8 %collective-permute-start.22 = (bf16[64,1280]{1,0:T(8,128)(2,1)S(1)}, bf16[64,1280]{1,0:T(8,128)(2,1)S(1)}, u32[]{:S(2)}, u32[]{:S(2)}) collective-permute-start(bf16[64,1280]{1,0:T(8,128)(2,1)S(1)} %slice.86), channel_id=1, source_target_pairs={{0,2},{1,9},{2,0},{3,11},{4,6},{5,13},{6,4},{7,15},{8,10},{9,1},{1... | collective-permute-start | bytes 491528 | tf_op jit(solution)/shard_map/ppermute | solution.py:55
  73.9 5.5 %collective-permute-start.19 = (bf16[32,1280]{1,0:T(8,128)(2,1)S(1)}, bf16[32,1280]{1,0:T(8,128)(2,1)S(1)}, u32[]{:S(2)}, u32[]{:S(2)}) collective-permute-start(bf16[32,1280]{1,0:T(8,128)(2,1)S(1)} %slice.89), channel_id=1, source_target_pairs={{0,16},{1,17},{2,18},{3,19},{4,20},{5,21},{6,22},{7,23},{8,24},{9,... | collective-permute-start | bytes 245768 | tf_op jit(solution)/shard_map/ppermute | solution.py:55
  77.7 5.9 %collective-permute-start.23 = (bf16[32,1280]{1,0:T(8,128)(2,1)S(1)}, bf16[32,1280]{1,0:T(8,128)(2,1)S(1)}, u32[]{:S(2)}, u32[]{:S(2)}) collective-permute-start(bf16[32,1280]{1,0:T(8,128)(2,1)S(1)} %slice.88), channel_id=1, source_target_pairs={{0,16},{1,17},{2,18},{3,19},{4,20},{5,21},{6,22},{7,23},{8,24},{9,... | collective-permute-start | bytes 245768 | tf_op jit(solution)/shard_map/ppermute | solution.py:55
  79.4 4.6 %collective-permute-start.20 = (bf16[16,1280]{1,0:T(8,128)(2,1)S(1)}, bf16[16,1280]{1,0:T(8,128)(2,1)S(1)}, u32[]{:S(2)}, u32[]{:S(2)}) collective-permute-start(bf16[16,1280]{1,0:T(8,128)(2,1)S(1)} %slice.91), channel_id=1, source_target_pairs={{0,8},{1,3},{2,10},{3,1},{4,12},{5,7},{6,14},{7,5},{8,0},{9,11},{1... | collective-permute-start | bytes 122888 | tf_op jit(solution)/shard_map/ppermute | solution.py:55
  83.6 4.1 %collective-permute-start.24 = (bf16[16,1280]{1,0:T(8,128)(2,1)S(1)}, bf16[16,1280]{1,0:T(8,128)(2,1)S(1)}, u32[]{:S(2)}, u32[]{:S(2)}) collective-permute-start(bf16[16,1280]{1,0:T(8,128)(2,1)S(1)} %slice.90), channel_id=1, source_target_pairs={{0,8},{1,3},{2,10},{3,1},{4,12},{5,7},{6,14},{7,5},{8,0},{9,11},{1... | collective-permute-start | bytes 122888 | tf_op jit(solution)/shard_map/ppermute | solution.py:55
  (1 other events, 0.7 us)

commit v10 on v9

--- a/solution.py
+++ b/solution.py
@@ -44,6 +44,7 @@
         [order[::-1] + kept[-1:] for order, kept in zip(orders, merge)]
         for orders in (gather, crossed)
     ]
+    scatter[0] = [order[:-2] + order[-2:][::-1] for order in scatter[0]]
     return merge, (gather, crossed), scatter
 
 
@@ -685,7 +686,11 @@
             arrived = exchange(sent, scatter_order[part], stage)
             kept = kept + arrived.astype(jnp.float32)
             half_rows = kept.shape[0] // 2
-            if stage < stages:
+            if part == 0 and stage == stages - 2:
+                quarters = kept.reshape(2, 2, half_rows // 2, -1)
+                sent = quarters[:, 1].reshape(half_rows, -1).astype(jnp.bfloat16)
+                kept = quarters[:, 0].reshape(half_rows, -1)
+            elif stage < stages:
                 sent = kept[half_rows:].astype(jnp.bfloat16)
                 kept = kept[:half_rows]
         outputs.append((finished[part][1].astype(jnp.float32) + kept).astype(jnp.bfloat16))

time: 88.7 us -> 88.7 us (level)
  starting transfers between devices: 30 us -> 29.1 us
  transfers between devices with their start and end apart: 25 -> 25, of which waited for: 15 -> 14; matrix products, arithmetic and copies ran while one was open for 0% -> 0% of each run, Pallas kernels for 24% -> 24%
where the time goes in v10:
time: 88.7 us; the launch traced here: 88.3 us
  waiting for transfers between devices  30 us (34%)
  starting transfers between devices  29.1 us (33%)
  Pallas kernels  26.1 us (29%)
  local copies, waits for them, and re-layouts  1.8 us (2%)
  other arithmetic  1 us (1%)
    ppermute x20, starting transfers between devices, exchange(): return lax.ppermute(value, 'wide', pairs)  27.7 us
    ppermute x20, waiting for transfers between devices, exchange(): return lax.ppermute(value, 'wide', pairs)  27.6 us
    pallas_call x3, Pallas kernels, part_expert_rows(): pl.pallas_call(functools.partial(part_expert_kernel, part), compiler_para...  10.2 us
    pallas_call x1, Pallas kernels, expert_rows(): pl.pallas_call(second_expert_kernel, name='expert_second', compiler_param...  4.92 us
    pallas_call x1, Pallas kernels, expert_rows(): pl.pallas_call(rest_expert_kernel, name='expert_rest', compiler_params=pl...  3.25 us
    pallas_call x2, Pallas kernels, attention_rows(): pl.pallas_call(functools.partial(attend_kernel, HEADS, part, part_heads),...  2.74 us
    ppermute x5, waiting for transfers between devices, partner(): return lax.ppermute(value, axis, pairs)  2.35 us
    pallas_call x1, Pallas kernels, expert_rows(): pl.pallas_call(kept_expert_kernel, name='expert_kept', compiler_params=pl...  2.32 us
  transfers between devices with their start and end apart: 25, of which 14 were waited for; matrix products, arithmetic and copies ran while one was open for 0% of the time, Pallas kernels for 24%

profile of v10, /device:TPU:0, one launch (start us, length us, event | category | flops | bytes accessed | tf_op | source)
XLA Modules:
  0.0 88.3 jit_solution(13095879824650854662)
XLA Ops:
  0.5 2.3 %collective-permute-done.keys_b = bf16[128,1152]{1,0:T(8,128)(2,1)S(1)} collective-permute-done((bf16[128,1152]{1,0:T(8,128)(2,1)}, bf16[128,1152]{1,0:T(8,128)(2,1)S(1)}, u32[]{:S(2)}, u32[]{:S(2)}) %collective-permute-start) | collective-permute-done | bytes 294944 | tf_op jit(solution)/shard_map/ppermute | solution.py:33
  4.5 1.3 %stage_in.1 = (bf16[128,1152]{1,0:T(8,128)(2,1)S(1)}, bf16[128,1152]{1,0:T(8,128)(2,1)S(1)}, bf16[128,2560]{1,0:T(8,128)(2,1)S(1)}) custom-call(s32[1]{0:T(128)} %bitcast.device_ref, bf16[256,1152]{1,0:T(8,128)(2,1)} %queries_ref.1, bf16[128,1152]{1,0:T(8,128)(2,1)} %keys_ref.1, bf16[128,2560]{1,0:T(8,128)(2,1)} %values_ref.1), custom_call_target="tpu_custom_call" | custom-call | tf_op jit(solution)/shard_map/stage_in/pallas_call | solution.py:572
  6.7 1.5 %shard_map.95 = (bf16[64,1408]{1,0:T(8,128)(2,1)S(1)}, f32[64,1408]{1,0:T(8,128)S(1)}) custom-call(bf16[128,1152]{1,0:T(8,128)(2,1)S(1)} %get-tuple-element.46.query_ref, bf16[128,1152]{1,0:T(8,128)(2,1)S(1)} %get-tuple-element.47.keys_a, bf16[128,1152]{1,0:T(8,128)(2,1)S(1)} %copy-done.4, bf16[128,2560]{1,0:T(8,128)(2,1)S(1)} %get-tuple-element.49.values_a, ...), custom_call_target="tpu_custom_call" | custom-call | tf_op jit(solution)/shard_map/pallas_call | solution.py:588
  8.3 2.7 %collective-permute-start.5 = (bf16[64,1408]{1,0:T(8,128)(2,1)S(1)}, bf16[64,1408]{1,0:T(8,128)(2,1)S(1)}, u32[]{:S(2)}, u32[]{:S(2)}) collective-permute-start(bf16[64,1408]{1,0:T(8,128)(2,1)S(1)} %get-tuple-element.59), channel_id=1, source_target_pairs={{0,2},{1,5},{2,0},{3,7},{4,6},{5,1},{6,4},{7,3},{8,10},{9,13},{10,... | collective-permute-start | bytes 540680 | tf_op jit(solution)/shard_map/ppermute | solution.py:56
  10.9 1.2 %shard_map.91 = (bf16[64,1408]{1,0:T(8,128)(2,1)S(1)}, f32[64,1408]{1,0:T(8,128)S(1)}) custom-call(bf16[128,1152]{1,0:T(8,128)(2,1)S(1)} %get-tuple-element.46.query_ref, bf16[128,1152]{1,0:T(8,128)(2,1)S(1)} %get-tuple-element.47.keys_a, bf16[128,1152]{1,0:T(8,128)(2,1)S(1)} %copy-done.4, bf16[128,2560]{1,0:T(8,128)(2,1)S(1)} %get-tuple-element.49.values_a, ...), custom_call_target="tpu_custom_call" | custom-call | tf_op jit(solution)/shard_map/pallas_call | solution.py:588
  12.3 2.1 %collective-permute-done.5.came_ref = bf16[64,1408]{1,0:T(8,128)(2,1)S(1)} collective-permute-done((bf16[64,1408]{1,0:T(8,128)(2,1)S(1)}, bf16[64,1408]{1,0:T(8,128)(2,1)S(1)}, u32[]{:S(2)}, u32[]{:S(2)}) %collective-permute-start.5) | collective-permute-done | bytes 180256 | tf_op jit(solution)/shard_map/ppermute | solution.py:56
  14.7 2.1 %collective-permute-start.6 = (bf16[32,1408]{1,0:T(8,128)(2,1)S(1)}, bf16[32,1408]{1,0:T(8,128)(2,1)S(1)}, u32[]{:S(2)}, u32[]{:S(2)}) collective-permute-start(bf16[32,1408]{1,0:T(8,128)(2,1)S(1)} %get-tuple-element.61), channel_id=1, source_target_pairs={{0,4},{1,9},{2,6},{3,11},{4,0},{5,13},{6,2},{7,15},{8,12},{9,1},{1... | collective-permute-start | bytes 270344 | tf_op jit(solution)/shard_map/ppermute | solution.py:56
  18.0 1.6 %collective-permute-start.3 = (bf16[32,1408]{1,0:T(8,128)(2,1)S(1)}, bf16[32,1408]{1,0:T(8,128)(2,1)S(1)}, u32[]{:S(2)}, u32[]{:S(2)}) collective-permute-start(bf16[32,1408]{1,0:T(8,128)(2,1)S(1)} %get-tuple-element.54), channel_id=1, source_target_pairs={{0,4},{1,9},{2,6},{3,11},{4,0},{5,13},{6,2},{7,15},{8,12},{9,1},{1... | collective-permute-start | bytes 270344 | tf_op jit(solution)/shard_map/ppermute | solution.py:56
  19.7 2.9 %collective-permute-done.3.came_ref = bf16[32,1408]{1,0:T(8,128)(2,1)S(1)} collective-permute-done((bf16[32,1408]{1,0:T(8,128)(2,1)S(1)}, bf16[32,1408]{1,0:T(8,128)(2,1)S(1)}, u32[]{:S(2)}, u32[]{:S(2)}) %collective-permute-start.3) | collective-permute-done | bytes 90144 | tf_op jit(solution)/shard_map/ppermute | solution.py:56
  22.8 1.6 %collective-permute-start.4 = (bf16[32,1408]{1,0:T(8,128)(2,1)S(1)}, bf16[32,1408]{1,0:T(8,128)(2,1)S(1)}, u32[]{:S(2)}, u32[]{:S(2)}) collective-permute-start(bf16[32,1408]{1,0:T(8,128)(2,1)S(1)} %get-tuple-element.56), channel_id=1, source_target_pairs={{0,8},{1,3},{2,10},{3,1},{4,12},{5,7},{6,14},{7,5},{8,0},{9,11},{1... | collective-permute-start | bytes 270344 | tf_op jit(solution)/shard_map/ppermute | solution.py:56
  25.1 2.3 %collective-permute-done.4.came_ref = bf16[32,1408]{1,0:T(8,128)(2,1)S(1)} collective-permute-done((bf16[32,1408]{1,0:T(8,128)(2,1)S(1)}, bf16[32,1408]{1,0:T(8,128)(2,1)S(1)}, u32[]{:S(2)}, u32[]{:S(2)}) %collective-permute-start.4) | collective-permute-done | bytes 90144 | tf_op jit(solution)/shard_map/ppermute | solution.py:56
  27.6 2.9 %collective-permute-start.11 = (bf16[32,1408]{1,0:T(8,128)(2,1)S(1)}, bf16[32,1408]{1,0:T(8,128)(2,1)S(1)}, u32[]{:S(2)}, u32[]{:S(2)}) collective-permute-start(bf16[32,1408]{1,0:T(8,128)(2,1)S(1)} %get-tuple-element.65.own_ref), channel_id=1, source_target_pairs={{0,16},{1,17},{2,18},{3,19},{4,20},{5,21},{6,22},{7,23},{8,24},{9,... | collective-permute-start | bytes 270344 | tf_op jit(solution)/shard_map/ppermute | solution.py:56
  30.7 1.5 %collective-permute-start.8 = (bf16[32,1280]{1,0:T(8,128)(2,1)S(1)}, bf16[32,1280]{1,0:T(8,128)(2,1)S(1)}, u32[]{:S(2)}, u32[]{:S(2)}) collective-permute-start(bf16[32,1280]{1,0:T(8,128)(2,1)S(1)} %get-tuple-element.64.own_ref), channel_id=1, source_target_pairs={{0,16},{1,17},{2,18},{3,19},{4,20},{5,21},{6,22},{7,23},{8,24},{9,... | collective-permute-start | bytes 245768 | tf_op jit(solution)/shard_map/ppermute | solution.py:56
  32.2 2.5 %collective-permute-done.11.came_ref = bf16[32,1408]{1,0:T(8,128)(2,1)S(1)} collective-permute-done((bf16[32,1408]{1,0:T(8,128)(2,1)S(1)}, bf16[32,1408]{1,0:T(8,128)(2,1)S(1)}, u32[]{:S(2)}, u32[]{:S(2)}) %collective-permute-start.11) | collective-permute-done | bytes 90144 | tf_op jit(solution)/shard_map/ppermute | solution.py:56
  34.7 1.6 %collective-permute-start.12 = (bf16[64,1408]{1,0:T(8,128)(2,1)S(1)}, bf16[64,1408]{1,0:T(8,128)(2,1)S(1)}, u32[]{:S(2)}, u32[]{:S(2)}) collective-permute-start(bf16[64,1408]{1,0:T(8,128)(2,1)S(1)} %shard_map.101.own_ref), channel_id=1, source_target_pairs={{0,4},{1,5},{2,6},{3,7},{4,0},{5,1},{6,2},{7,3},{8,12},{9,13},{10,... | collective-permute-start | bytes 540680 | tf_op jit(solution)/shard_map/ppermute | solution.py:56
  36.3 1.9 %collective-permute-start.9 = (bf16[64,1280]{1,0:T(8,128)(2,1)S(1)}, bf16[64,1280]{1,0:T(8,128)(2,1)S(1)}, u32[]{:S(2)}, u32[]{:S(2)}) collective-permute-start(bf16[64,1280]{1,0:T(8,128)(2,1)S(1)} %shard_map.99.own_ref), channel_id=1, source_target_pairs={{0,2},{1,9},{2,0},{3,11},{4,6},{5,13},{6,4},{7,15},{8,10},{9,1},{1... | collective-permute-start | bytes 491528 | tf_op jit(solution)/shard_map/ppermute | solution.py:56
  38.2 2.8 %collective-permute-done.12.came_ref = bf16[64,1408]{1,0:T(8,128)(2,1)S(1)} collective-permute-done((bf16[64,1408]{1,0:T(8,128)(2,1)S(1)}, bf16[64,1408]{1,0:T(8,128)(2,1)S(1)}, u32[]{:S(2)}, u32[]{:S(2)}) %collective-permute-start.12) | collective-permute-done | bytes 180256 | tf_op jit(solution)/shard_map/ppermute | solution.py:56
  41.0 1.0 %collective-permute-start.13 = (bf16[128,1408]{1,0:T(8,128)(2,1)S(1)}, bf16[128,1408]{1,0:T(8,128)(2,1)S(1)}, u32[]{:S(2)}, u32[]{:S(2)}) collective-permute-start(bf16[128,1408]{1,0:T(8,128)(2,1)S(1)} %shard_map.102.rows_ref), channel_id=1, source_target_pairs={{0,2},{1,9},{2,0},{3,11},{4,6},{5,13},{6,4},{7,15},{8,10},{9,1},{1... | collective-permute-start | bytes 1081352 | tf_op jit(solution)/shard_map/ppermute | solution.py:56
  42.1 2.4 %collective-permute-start.10 = (bf16[128,1280]{1,0:T(8,128)(2,1)S(1)}, bf16[128,1280]{1,0:T(8,128)(2,1)S(1)}, u32[]{:S(2)}, u32[]{:S(2)}) collective-permute-start(bf16[128,1280]{1,0:T(8,128)(2,1)S(1)} %shard_map.100.rows_ref), channel_id=1, source_target_pairs={{0,4},{1,5},{2,6},{3,7},{4,0},{5,1},{6,2},{7,3},{8,12},{9,13},{10,... | collective-permute-start | bytes 983048 | tf_op jit(solution)/shard_map/ppermute | solution.py:56
  44.6 3.3 %shard_map.104 = (f32[1024,128]{1,0:T(8,128)S(1)}, f32[1024,128]{1,0:T(8,128)S(1)}, f32[8,128]{1,0:T(8,128)S(1)}) custom-call(s32[1]{0:T(128)} %bitcast.device_ref, f32[1,2560]{1,0:T(1,128)S(1)} %reshape.18.gain_ref, bf16[128,1280]{1,0:T(8,128)(2,1)S(1)} %shard_map.100.rows_ref, bf16[512,2560]{1,0:T(8,128)(2,1)S(1)} %copy-done, ...), custom_call_target="tpu_custom_call" | custom-call | tf_op jit(solution)/shard_map/pallas_call | solution.py:486
  48.5 3.5 %shard_map.103 = (f32[1024,128]{1,0:T(8,128)S(1)}, f32[1024,128]{1,0:T(8,128)S(1)}, f32[8,128]{1,0:T(8,128)S(1)}) custom-call(s32[1]{0:T(128)} %bitcast.device_ref, f32[1,2560]{1,0:T(1,128)S(1)} %reshape.18.gain_ref, bf16[128,1408]{1,0:T(8,128)(2,1)S(1)} %collective-permute-done.13.rows_ref, bf16[512,2560]{1,0:T(8,128)(2,1)S(1)} %copy-done, ...), custom_call_target="tpu_custom_call" | custom-call | tf_op jit(solution)/shard_map/pallas_call | solution.py:486
  52.1 4.9 %expert_second.1 = (bf16[128,1280]{1,0:T(8,128)(2,1)S(1)}, bf16[128,1024]{1,0:T(8,128)(2,1)S(1)}, f32[1024,128]{1,0:T(8,128)S(1)}, f32[1024,128]{1,0:T(8,128)S(1)}, f32[8,128]{1,0:T(8,128)S(1)}) custom-call(f32[1,2560]{1,0:T(1,128)S(1)} %reshape.18.gain_ref, bf16[128,1280]{1,0:T(8,128)(2,1)S(1)} %collective-permute-done.10.rows_ref, ...), custom_call_target="tpu_custom_call" | custom-call | tf_op jit(solution)/shard_map/expert_second/pallas_call | solution.py:509
  58.0 3.3 %shard_map.105 = (f32[1024,128]{1,0:T(8,128)S(1)}, f32[1024,128]{1,0:T(8,128)S(1)}, f32[8,128]{1,0:T(8,128)S(1)}) custom-call(s32[1]{0:T(128)} %bitcast.device_ref, f32[1,2560]{1,0:T(1,128)S(1)} %reshape.18.gain_ref, bf16[128,1408]{1,0:T(8,128)(2,1)S(1)} %shard_map.102.rows_ref, bf16[512,2560]{1,0:T(8,128)(2,1)S(1)} %copy-done, ...), custom_call_target="tpu_custom_call" | custom-call | tf_op jit(solution)/shard_map/pallas_call | solution.py:486
  61.4 3.2 %expert_rest.1 = (bf16[128,1280]{1,0:T(8,128)(2,1)S(1)}, f32[128,1280]{1,0:T(8,128)S(1)}, bf16[128,1024]{1,0:T(8,128)(2,1)S(1)}) custom-call(bf16[128,1024]{1,0:T(8,128)(2,1)S(1)} %get-tuple-element.75.hidden_ref, f32[1024,128]{1,0:T(8,128)S(1)} %get-tuple-element.76.gates_ref, f32[1024,128]{1,0:T(8,128)S(1)} %get-tuple-element.77.ups_ref, ...), custom_call_target="tpu_custom_call" | custom-call | tf_op jit(solution)/shard_map/expert_rest/pallas_call | solution.py:519
  64.6 1.4 %collective-permute-start.21 = (bf16[128,1280]{1,0:T(8,128)(2,1)S(1)}, bf16[128,1280]{1,0:T(8,128)(2,1)S(1)}, u32[]{:S(2)}, u32[]{:S(2)}) collective-permute-start(bf16[128,1280]{1,0:T(8,128)(2,1)S(1)} %get-tuple-element.86), channel_id=1, source_target_pairs={{0,4},{1,5},{2,6},{3,7},{4,0},{5,1},{6,2},{7,3},{8,12},{9,13},{10,... | collective-permute-start | bytes 983048 | tf_op jit(solution)/shard_map/ppermute | solution.py:56
  66.0 2.3 %expert_kept.1 = f32[128,1280]{1,0:T(8,128)S(1)} custom-call(bf16[128,1024]{1,0:T(8,128)(2,1)S(1)} %get-tuple-element.82.hidden_ref, bf16[512,2560]{1,0:T(8,128)(2,1)S(1)} %copy-done.2, bf16[512,2560]{1,0:T(8,128)(2,1)} %collective-permute-done.16.down_b), custom_call_target="tpu_custom_call" | custom-call | tf_op jit(solution)/shard_map/expert_kept/pallas_call | solution.py:532
  69.2 2.5 %collective-permute-done.21 = bf16[128,1280]{1,0:T(8,128)(2,1)S(1)} collective-permute-done((bf16[128,1280]{1,0:T(8,128)(2,1)S(1)}, bf16[128,1280]{1,0:T(8,128)(2,1)S(1)}, u32[]{:S(2)}, u32[]{:S(2)}) %collective-permute-start.21) | collective-permute-done | bytes 327712 | tf_op jit(solution)/shard_map/ppermute | solution.py:56
  71.8 1.4 %collective-permute-start.22 = (bf16[64,1280]{1,0:T(8,128)(2,1)S(1)}, bf16[64,1280]{1,0:T(8,128)(2,1)S(1)}, u32[]{:S(2)}, u32[]{:S(2)}) collective-permute-start(bf16[64,1280]{1,0:T(8,128)(2,1)S(1)} %slice.85), channel_id=1, source_target_pairs={{0,2},{1,9},{2,0},{3,11},{4,6},{5,13},{6,4},{7,15},{8,10},{9,1},{1... | collective-permute-start | bytes 491528 | tf_op jit(solution)/shard_map/ppermute | solution.py:56
  74.0 3.7 %collective-permute-done.22 = bf16[64,1280]{1,0:T(8,128)(2,1)S(1)} collective-permute-done((bf16[64,1280]{1,0:T(8,128)(2,1)S(1)}, bf16[64,1280]{1,0:T(8,128)(2,1)S(1)}, u32[]{:S(2)}, u32[]{:S(2)}) %collective-permute-start.22) | collective-permute-done | bytes 163872 | tf_op jit(solution)/shard_map/ppermute | solution.py:56
  78.6 2.3 %collective-permute-start.20 = (bf16[16,1280]{1,0:T(8,128)(2,1)S(1)}, bf16[16,1280]{1,0:T(8,128)(2,1)S(1)}, u32[]{:S(2)}, u32[]{:S(2)}) collective-permute-start(bf16[16,1280]{1,0:T(8,128)(2,1)S(1)} %slice.90), channel_id=1, source_target_pairs={{0,16},{1,17},{2,18},{3,19},{4,20},{5,21},{6,22},{7,23},{8,24},{9,... | collective-permute-start | bytes 122888 | tf_op jit(solution)/shard_map/ppermute | solution.py:56
  80.8 2.7 %collective-permute-done.23 = bf16[32,1280]{1,0:T(8,128)(2,1)S(1)} collective-permute-done((bf16[32,1280]{1,0:T(8,128)(2,1)S(1)}, bf16[32,1280]{1,0:T(8,128)(2,1)S(1)}, u32[]{:S(2)}, u32[]{:S(2)}) %collective-permute-start.23) | collective-permute-done | bytes 81952 | tf_op jit(solution)/shard_map/ppermute | solution.py:56
  84.0 3.6 %collective-permute-done.24 = bf16[16,1280]{1,0:T(8,128)(2,1)S(1)} collective-permute-done((bf16[16,1280]{1,0:T(8,128)(2,1)S(1)}, bf16[16,1280]{1,0:T(8,128)(2,1)S(1)}, u32[]{:S(2)}, u32[]{:S(2)}) %collective-permute-start.24) | collective-permute-done | bytes 40992 | tf_op jit(solution)/shard_map/ppermute | solution.py:56
  (73 shorter events, 11.4 us)
Async XLA Ops:
  0.0 3.6 %collective-permute-start.1 = (bf16[128,2560]{1,0:T(8,128)(2,1)}, bf16[128,2560]{1,0:T(8,128)(2,1)S(1)}, u32[]{:S(2)}, u32[]{:S(2)}) collective-permute-start(bf16[128,2560]{1,0:T(8,128)(2,1)} %values_ref.1), channel_id=1, source_target_pairs={{0,1},{1,0},{2,3},{3,2},{4,5},{5,4},{6,7},{7,6},{8,9},{9,8},{10,11... | collective-permute-start | bytes 1966088 | tf_op jit(solution)/shard_map/ppermute | solution.py:33
  0.5 2.4 %collective-permute-start = (bf16[128,1152]{1,0:T(8,128)(2,1)}, bf16[128,1152]{1,0:T(8,128)(2,1)S(1)}, u32[]{:S(2)}, u32[]{:S(2)}) collective-permute-start(bf16[128,1152]{1,0:T(8,128)(2,1)} %keys_ref.1), channel_id=1, source_target_pairs={{0,1},{1,0},{2,3},{3,2},{4,5},{5,4},{6,7},{7,6},{8,9},{9,8},{10,11... | collective-permute-start | bytes 884744 | tf_op jit(solution)/shard_map/ppermute | solution.py:33
  3.6 40.9 %collective-permute-start.14 = (bf16[512,2560]{1,0:T(8,128)(2,1)}, bf16[512,2560]{1,0:T(8,128)(2,1)S(1)}, u32[]{:S(2)}, u32[]{:S(2)}) collective-permute-start(bf16[512,2560]{1,0:T(8,128)(2,1)} %gate_a.3), channel_id=1, source_target_pairs={{0,1},{1,0},{2,3},{3,2},{4,5},{5,4},{6,7},{7,6},{8,9},{9,8},{10,11... | collective-permute-start | bytes 7864328 | tf_op jit(solution)/shard_map/ppermute | solution.py:33
  4.0 40.6 %collective-permute-start.15 = (bf16[512,2560]{1,0:T(8,128)(2,1)}, bf16[512,2560]{1,0:T(8,128)(2,1)}, u32[]{:S(2)}, u32[]{:S(2)}) collective-permute-start(bf16[512,2560]{1,0:T(8,128)(2,1)} %up_a.3), channel_id=1, source_target_pairs={{0,1},{1,0},{2,3},{3,2},{4,5},{5,4},{6,7},{7,6},{8,9},{9,8},{10,11... | collective-permute-start | bytes 7864328 | tf_op jit(solution)/shard_map/ppermute | solution.py:33
  4.1 48.0 %collective-permute-start.16 = (bf16[512,2560]{1,0:T(8,128)(2,1)}, bf16[512,2560]{1,0:T(8,128)(2,1)}, u32[]{:S(2)}, u32[]{:S(2)}) collective-permute-start(bf16[512,2560]{1,0:T(8,128)(2,1)} %down_a.2), channel_id=1, source_target_pairs={{0,1},{1,0},{2,3},{3,2},{4,5},{5,4},{6,7},{7,6},{8,9},{9,8},{10,11... | collective-permute-start | bytes 7864328 | tf_op jit(solution)/shard_map/ppermute | solution.py:33
  5.8 1.0 %copy-start.4 = (bf16[128,1152]{1,0:T(8,128)(2,1)S(1)}, bf16[128,1152]{1,0:T(8,128)(2,1)}, u32[]{:S(2)}) copy-start(bf16[128,1152]{1,0:T(8,128)(2,1)} %copy-done.3) | copy-start | bytes 884740
  6.7 12.9 %copy-start.6 = (s32[16,6]{0,1:T(8,128)S(1)}, s32[16,6]{0,1:T(8,128)}, u32[]{:S(2)}) copy-start(s32[16,6]{0,1:T(8,128)} %param.14) | copy-start | bytes 1156
  6.7 12.9 %copy-start.7 = (s32[16,6]{0,1:T(8,128)S(1)}, s32[16,6]{0,1:T(8,128)}, u32[]{:S(2)}) copy-start(s32[16,6]{0,1:T(8,128)} %param.13) | copy-start | bytes 1156
  8.3 6.1 %collective-permute-start.5 = (bf16[64,1408]{1,0:T(8,128)(2,1)S(1)}, bf16[64,1408]{1,0:T(8,128)(2,1)S(1)}, u32[]{:S(2)}, u32[]{:S(2)}) collective-permute-start(bf16[64,1408]{1,0:T(8,128)(2,1)S(1)} %get-tuple-element.59), channel_id=1, source_target_pairs={{0,2},{1,5},{2,0},{3,7},{4,6},{5,1},{6,4},{7,3},{8,10},{9,13},{10,... | collective-permute-start | bytes 540680 | tf_op jit(solution)/shard_map/ppermute | solution.py:56
  10.9 33.6 %copy-start.1 = (bf16[512,2560]{1,0:T(8,128)(2,1)S(1)}, bf16[512,2560]{1,0:T(8,128)(2,1)}, u32[]{:S(2)}) copy-start(bf16[512,2560]{1,0:T(8,128)(2,1)} %up_a.3) | copy-start | bytes 7864324
  12.2 32.4 %copy-start.5 = (f32[2560]{0:T(1024)S(1)}, f32[2560]{0:T(1024)}, u32[]{:S(2)}) copy-start(f32[2560]{0:T(1024)} %param.12) | copy-start | bytes 30724
  12.2 32.4 %copy-start = (bf16[512,2560]{1,0:T(8,128)(2,1)S(1)}, bf16[512,2560]{1,0:T(8,128)(2,1)}, u32[]{:S(2)}) copy-start(bf16[512,2560]{1,0:T(8,128)(2,1)} %gate_a.3) | copy-start | bytes 7864324
  12.2 5.6 %collective-permute-start.2 = (bf16[64,1408]{1,0:T(8,128)(2,1)S(1)}, bf16[64,1408]{1,0:T(8,128)(2,1)S(1)}, u32[]{:S(2)}, u32[]{:S(2)}) collective-permute-start(bf16[64,1408]{1,0:T(8,128)(2,1)S(1)} %get-tuple-element.52), channel_id=1, source_target_pairs={{0,2},{1,5},{2,0},{3,7},{4,6},{5,1},{6,4},{7,3},{8,10},{9,13},{10,... | collective-permute-start | bytes 540680 | tf_op jit(solution)/shard_map/ppermute | solution.py:56
  14.7 9.7 %collective-permute-start.6 = (bf16[32,1408]{1,0:T(8,128)(2,1)S(1)}, bf16[32,1408]{1,0:T(8,128)(2,1)S(1)}, u32[]{:S(2)}, u32[]{:S(2)}) collective-permute-start(bf16[32,1408]{1,0:T(8,128)(2,1)S(1)} %get-tuple-element.61), channel_id=1, source_target_pairs={{0,4},{1,9},{2,6},{3,11},{4,0},{5,13},{6,2},{7,15},{8,12},{9,1},{1... | collective-permute-start | bytes 270344 | tf_op jit(solution)/shard_map/ppermute | solution.py:56
  18.0 4.6 %collective-permute-start.3 = (bf16[32,1408]{1,0:T(8,128)(2,1)S(1)}, bf16[32,1408]{1,0:T(8,128)(2,1)S(1)}, u32[]{:S(2)}, u32[]{:S(2)}) collective-permute-start(bf16[32,1408]{1,0:T(8,128)(2,1)S(1)} %get-tuple-element.54), channel_id=1, source_target_pairs={{0,4},{1,9},{2,6},{3,11},{4,0},{5,13},{6,2},{7,15},{8,12},{9,1},{1... | collective-permute-start | bytes 270344 | tf_op jit(solution)/shard_map/ppermute | solution.py:56
  22.8 4.6 %collective-permute-start.4 = (bf16[32,1408]{1,0:T(8,128)(2,1)S(1)}, bf16[32,1408]{1,0:T(8,128)(2,1)S(1)}, u32[]{:S(2)}, u32[]{:S(2)}) collective-permute-start(bf16[32,1408]{1,0:T(8,128)(2,1)S(1)} %get-tuple-element.56), channel_id=1, source_target_pairs={{0,8},{1,3},{2,10},{3,1},{4,12},{5,7},{6,14},{7,5},{8,0},{9,11},{1... | collective-permute-start | bytes 270344 | tf_op jit(solution)/shard_map/ppermute | solution.py:56
  24.6 5.9 %collective-permute-start.7 = (bf16[32,1408]{1,0:T(8,128)(2,1)S(1)}, bf16[32,1408]{1,0:T(8,128)(2,1)S(1)}, u32[]{:S(2)}, u32[]{:S(2)}) collective-permute-start(bf16[32,1408]{1,0:T(8,128)(2,1)S(1)} %get-tuple-element.63), channel_id=1, source_target_pairs={{0,8},{1,3},{2,10},{3,1},{4,12},{5,7},{6,14},{7,5},{8,0},{9,11},{1... | collective-permute-start | bytes 270344 | tf_op jit(solution)/shard_map/ppermute | solution.py:56
  27.6 7.0 %collective-permute-start.11 = (bf16[32,1408]{1,0:T(8,128)(2,1)S(1)}, bf16[32,1408]{1,0:T(8,128)(2,1)S(1)}, u32[]{:S(2)}, u32[]{:S(2)}) collective-permute-start(bf16[32,1408]{1,0:T(8,128)(2,1)S(1)} %get-tuple-element.65.own_ref), channel_id=1, source_target_pairs={{0,16},{1,17},{2,18},{3,19},{4,20},{5,21},{6,22},{7,23},{8,24},{9,... | collective-permute-start | bytes 270344 | tf_op jit(solution)/shard_map/ppermute | solution.py:56
  30.7 5.6 %collective-permute-start.8 = (bf16[32,1280]{1,0:T(8,128)(2,1)S(1)}, bf16[32,1280]{1,0:T(8,128)(2,1)S(1)}, u32[]{:S(2)}, u32[]{:S(2)}) collective-permute-start(bf16[32,1280]{1,0:T(8,128)(2,1)S(1)} %get-tuple-element.64.own_ref), channel_id=1, source_target_pairs={{0,16},{1,17},{2,18},{3,19},{4,20},{5,21},{6,22},{7,23},{8,24},{9,... | collective-permute-start | bytes 245768 | tf_op jit(solution)/shard_map/ppermute | solution.py:56
  34.7 6.3 %collective-permute-start.12 = (bf16[64,1408]{1,0:T(8,128)(2,1)S(1)}, bf16[64,1408]{1,0:T(8,128)(2,1)S(1)}, u32[]{:S(2)}, u32[]{:S(2)}) collective-permute-start(bf16[64,1408]{1,0:T(8,128)(2,1)S(1)} %shard_map.101.own_ref), channel_id=1, source_target_pairs={{0,4},{1,5},{2,6},{3,7},{4,0},{5,1},{6,2},{7,3},{8,12},{9,13},{10,... | collective-permute-start | bytes 540680 | tf_op jit(solution)/shard_map/ppermute | solution.py:56
  36.3 5.7 %collective-permute-start.9 = (bf16[64,1280]{1,0:T(8,128)(2,1)S(1)}, bf16[64,1280]{1,0:T(8,128)(2,1)S(1)}, u32[]{:S(2)}, u32[]{:S(2)}) collective-permute-start(bf16[64,1280]{1,0:T(8,128)(2,1)S(1)} %shard_map.99.own_ref), channel_id=1, source_target_pairs={{0,2},{1,9},{2,0},{3,11},{4,6},{5,13},{6,4},{7,15},{8,10},{9,1},{1... | collective-permute-start | bytes 491528 | tf_op jit(solution)/shard_map/ppermute | solution.py:56
  41.0 7.5 %collective-permute-start.13 = (bf16[128,1408]{1,0:T(8,128)(2,1)S(1)}, bf16[128,1408]{1,0:T(8,128)(2,1)S(1)}, u32[]{:S(2)}, u32[]{:S(2)}) collective-permute-start(bf16[128,1408]{1,0:T(8,128)(2,1)S(1)} %shard_map.102.rows_ref), channel_id=1, source_target_pairs={{0,2},{1,9},{2,0},{3,11},{4,6},{5,13},{6,4},{7,15},{8,10},{9,1},{1... | collective-permute-start | bytes 1081352 | tf_op jit(solution)/shard_map/ppermute | solution.py:56
  42.1 10.0 %collective-permute-start.10 = (bf16[128,1280]{1,0:T(8,128)(2,1)S(1)}, bf16[128,1280]{1,0:T(8,128)(2,1)S(1)}, u32[]{:S(2)}, u32[]{:S(2)}) collective-permute-start(bf16[128,1280]{1,0:T(8,128)(2,1)S(1)} %shard_map.100.rows_ref), channel_id=1, source_target_pairs={{0,4},{1,5},{2,6},{3,7},{4,0},{5,1},{6,2},{7,3},{8,12},{9,13},{10,... | collective-permute-start | bytes 983048 | tf_op jit(solution)/shard_map/ppermute | solution.py:56
  47.9 4.2 %copy-start.2 = (bf16[512,2560]{1,0:T(8,128)(2,1)S(1)}, bf16[512,2560]{1,0:T(8,128)(2,1)}, u32[]{:S(2)}) copy-start(bf16[512,2560]{1,0:T(8,128)(2,1)} %down_a.2) | copy-start | bytes 7864324
  57.0 11.4 %collective-permute-start.17 = (bf16[128,1280]{1,0:T(8,128)(2,1)S(1)}, bf16[128,1280]{1,0:T(8,128)(2,1)S(1)}, u32[]{:S(2)}, u32[]{:S(2)}) collective-permute-start(bf16[128,1280]{1,0:T(8,128)(2,1)S(1)} %get-tuple-element.83), channel_id=1, source_target_pairs={{0,2},{1,9},{2,0},{3,11},{4,6},{5,13},{6,4},{7,15},{8,10},{9,1},{1... | collective-permute-start | bytes 983048 | tf_op jit(solution)/shard_map/ppermute | solution.py:56
  64.6 7.1 %collective-permute-start.21 = (bf16[128,1280]{1,0:T(8,128)(2,1)S(1)}, bf16[128,1280]{1,0:T(8,128)(2,1)S(1)}, u32[]{:S(2)}, u32[]{:S(2)}) collective-permute-start(bf16[128,1280]{1,0:T(8,128)(2,1)S(1)} %get-tuple-element.86), channel_id=1, source_target_pairs={{0,4},{1,5},{2,6},{3,7},{4,0},{5,1},{6,2},{7,3},{8,12},{9,13},{10,... | collective-permute-start | bytes 983048 | tf_op jit(solution)/shard_map/ppermute | solution.py:56
  68.4 5.4 %collective-permute-start.18 = (bf16[64,1280]{1,0:T(8,128)(2,1)S(1)}, bf16[64,1280]{1,0:T(8,128)(2,1)S(1)}, u32[]{:S(2)}, u32[]{:S(2)}) collective-permute-start(bf16[64,1280]{1,0:T(8,128)(2,1)S(1)} %slice.86), channel_id=1, source_target_pairs={{0,4},{1,5},{2,6},{3,7},{4,0},{5,1},{6,2},{7,3},{8,12},{9,13},{10,... | collective-permute-start | bytes 491528 | tf_op jit(solution)/shard_map/ppermute | solution.py:56
  71.8 5.8 %collective-permute-start.22 = (bf16[64,1280]{1,0:T(8,128)(2,1)S(1)}, bf16[64,1280]{1,0:T(8,128)(2,1)S(1)}, u32[]{:S(2)}, u32[]{:S(2)}) collective-permute-start(bf16[64,1280]{1,0:T(8,128)(2,1)S(1)} %slice.85), channel_id=1, source_target_pairs={{0,2},{1,9},{2,0},{3,11},{4,6},{5,13},{6,4},{7,15},{8,10},{9,1},{1... | collective-permute-start | bytes 491528 | tf_op jit(solution)/shard_map/ppermute | solution.py:56
  73.9 4.7 %collective-permute-start.19 = (bf16[32,1280]{1,0:T(8,128)(2,1)S(1)}, bf16[32,1280]{1,0:T(8,128)(2,1)S(1)}, u32[]{:S(2)}, u32[]{:S(2)}) collective-permute-start(bf16[32,1280]{1,0:T(8,128)(2,1)S(1)} %bitcast.7), channel_id=1, source_target_pairs={{0,8},{1,3},{2,10},{3,1},{4,12},{5,7},{6,14},{7,5},{8,0},{9,11},{1... | collective-permute-start | bytes 245768 | tf_op jit(solution)/shard_map/ppermute | solution.py:56
  77.7 5.8 %collective-permute-start.23 = (bf16[32,1280]{1,0:T(8,128)(2,1)S(1)}, bf16[32,1280]{1,0:T(8,128)(2,1)S(1)}, u32[]{:S(2)}, u32[]{:S(2)}) collective-permute-start(bf16[32,1280]{1,0:T(8,128)(2,1)S(1)} %slice.87), channel_id=1, source_target_pairs={{0,16},{1,17},{2,18},{3,19},{4,20},{5,21},{6,22},{7,23},{8,24},{9,... | collective-permute-start | bytes 245768 | tf_op jit(solution)/shard_map/ppermute | solution.py:56
  78.6 5.4 %collective-permute-start.20 = (bf16[16,1280]{1,0:T(8,128)(2,1)S(1)}, bf16[16,1280]{1,0:T(8,128)(2,1)S(1)}, u32[]{:S(2)}, u32[]{:S(2)}) collective-permute-start(bf16[16,1280]{1,0:T(8,128)(2,1)S(1)} %slice.90), channel_id=1, source_target_pairs={{0,16},{1,17},{2,18},{3,19},{4,20},{5,21},{6,22},{7,23},{8,24},{9,... | collective-permute-start | bytes 122888 | tf_op jit(solution)/shard_map/ppermute | solution.py:56
  83.6 4.1 %collective-permute-start.24 = (bf16[16,1280]{1,0:T(8,128)(2,1)S(1)}, bf16[16,1280]{1,0:T(8,128)(2,1)S(1)}, u32[]{:S(2)}, u32[]{:S(2)}) collective-permute-start(bf16[16,1280]{1,0:T(8,128)(2,1)S(1)} %slice.89), channel_id=1, source_target_pairs={{0,8},{1,3},{2,10},{3,1},{4,12},{5,7},{6,14},{7,5},{8,0},{9,11},{1... | collective-permute-start | bytes 122888 | tf_op jit(solution)/shard_map/ppermute | solution.py:56
  (1 other events, 0.7 us)

commit v11 on v9

--- a/solution.py
+++ b/solution.py
@@ -446,10 +446,8 @@
     down_a,
     down_b,
     sent_ref,
-    kept_ref,
     hidden,
-    early_value,
-    late_value,
+    leaving,
 ):
     width = sent_ref.shape[1]
     row = (8, stats_ref.shape[1])
@@ -465,17 +463,18 @@
             inverse,
             stats_ref[1:2, :],
         )
-    down_product(hidden, (down_a, down_b), early_value, width)
-    down_product(hidden_ref, (down_a, down_b), late_value, width)
-    half = early_value.shape[0] // 2
-    sent_ref[:half, :] = early_value[half:, :].astype(sent_ref.dtype)
-    sent_ref[half:, :] = late_value[half:, :].astype(sent_ref.dtype)
-    kept_ref[:half, :] = early_value[:half, :]
-    kept_ref[half:, :] = late_value[:half, :]
-
-
-def kept_expert_kernel(hidden_ref, down_a, down_b, kept_ref):
-    down_product(hidden_ref, (down_a, down_b), kept_ref, 0)
+    half = leaving.shape[0] // 2
+    leaving[:half, :] = hidden[half:, :]
+    leaving[half:, :] = hidden_ref[half:, :]
+    down_product(leaving, (down_a, down_b), sent_ref, width)
+
+
+def kept_expert_kernel(early_ref, late_ref, down_a, down_b, first_ref, second_ref, staying):
+    half = staying.shape[0] // 2
+    down_product(early_ref, (down_a, down_b), first_ref, 0)
+    staying[:half, :] = early_ref[:half, :]
+    staying[half:, :] = late_ref[:half, :]
+    down_product(staying, (down_a, down_b), second_ref, first_ref.shape[1])
 
 
 def part_expert_rows(part, device, gain, rows, gates, ups):
@@ -515,27 +514,24 @@
         scratch_shapes=[pltpu.VMEM((width, row_count), jnp.bfloat16)],
     )(*[near(operand) for operand in operands])
     operands = [hidden, *first[0], *first[1], *rest, *downs]
-    sent, kept, hidden = pl.pallas_call(
+    sent, early_hidden = pl.pallas_call(
         rest_expert_kernel,
         name="expert_rest",
         compiler_params=pltpu.CompilerParams(vmem_limit_bytes=12 << 20),
-        out_shape=(
-            near_shape((row_count, width), jnp.bfloat16),
-            near_shape((row_count, width), jnp.float32),
-            hidden_shape,
-        ),
+        out_shape=(near_shape((row_count, width), jnp.bfloat16), hidden_shape),
         in_specs=[whole] * len(operands),
-        out_specs=(whole,) * 3,
-        scratch_shapes=[pltpu.VMEM((row_count, width), jnp.float32)] * 2,
+        out_specs=(whole,) * 2,
+        scratch_shapes=[pltpu.VMEM((row_count, 2 * units), jnp.bfloat16)],
     )(*[near(operand) for operand in operands])
-    kept_first = pl.pallas_call(
+    kept_first, kept = pl.pallas_call(
         kept_expert_kernel,
         name="expert_kept",
         compiler_params=pltpu.CompilerParams(vmem_limit_bytes=12 << 20),
-        out_shape=near_shape((row_count, width), jnp.float32),
-        in_specs=[whole] * 3,
-        out_specs=whole,
-    )(*[near(operand) for operand in (hidden, *downs)])
+        out_shape=(near_shape((row_count, width), jnp.float32),) * 2,
+        in_specs=[whole] * 4,
+        out_specs=(whole,) * 2,
+        scratch_shapes=[pltpu.VMEM((row_count, 2 * units), jnp.bfloat16)],
+    )(*[near(operand) for operand in (early_hidden, hidden, *downs)])
     return [(sent_first, kept_first), (sent, kept)]
 
 
@@ -693,7 +689,10 @@
 
 
 def solution(mesh):
-    return mapped(mesh)
+    def step(queries, *rest):
+        return mapped(mesh)(queries, *rest)
+
+    return step
 
 
 def mapped(mesh):

time: 88.7 us -> 88.2 us (level)
  no operation moved by 1% of the time
where the time goes in v11:
time: 88.2 us; the launch traced here: 87.9 us
  starting transfers between devices  29.9 us (34%)
  waiting for transfers between devices  28.7 us (33%)
  Pallas kernels  26.1 us (30%)
  local copies, waits for them, and re-layouts  1.79 us (2%)
  other arithmetic  1.01 us (1%)
    ppermute x20, starting transfers between devices, exchange(): return lax.ppermute(value, 'wide', pairs)  28.5 us
    ppermute x20, waiting for transfers between devices, exchange(): return lax.ppermute(value, 'wide', pairs)  26.4 us
    pallas_call x3, Pallas kernels, part_expert_rows(): pl.pallas_call(functools.partial(part_expert_kernel, part), compiler_para...  10.2 us
    pallas_call x1, Pallas kernels, expert_rows(): pl.pallas_call(second_expert_kernel, name='expert_second', compiler_param...  4.9 us
    pallas_call x1, Pallas kernels, expert_rows(): pl.pallas_call(rest_expert_kernel, name='expert_rest', compiler_params=pl...  2.86 us
    pallas_call x1, Pallas kernels, expert_rows(): pl.pallas_call(kept_expert_kernel, name='expert_kept', compiler_params=pl...  2.75 us
    pallas_call x2, Pallas kernels, attention_rows(): pl.pallas_call(functools.partial(attend_kernel, HEADS, part, part_heads),...  2.74 us
    ppermute x5, waiting for transfers between devices, partner(): return lax.ppermute(value, axis, pairs)  2.35 us
  transfers between devices with their start and end apart: 25, of which 15 were waited for; matrix products, arithmetic and copies ran while one was open for 0% of the time, Pallas kernels for 24%

profile of v11, /device:TPU:0, one launch (start us, length us, event | category | flops | bytes accessed | tf_op | source)
XLA Modules:
  0.0 87.9 jit_solution(16591254820659440754)
XLA Ops:
  0.5 2.3 %collective-permute-done.keys_b = bf16[128,1152]{1,0:T(8,128)(2,1)S(1)} collective-permute-done((bf16[128,1152]{1,0:T(8,128)(2,1)}, bf16[128,1152]{1,0:T(8,128)(2,1)S(1)}, u32[]{:S(2)}, u32[]{:S(2)}) %collective-permute-start) | collective-permute-done | bytes 294944 | tf_op jit(solution)/shard_map/ppermute | solution.py:33
  4.5 1.3 %stage_in.1 = (bf16[128,1152]{1,0:T(8,128)(2,1)S(1)}, bf16[128,1152]{1,0:T(8,128)(2,1)S(1)}, bf16[128,2560]{1,0:T(8,128)(2,1)S(1)}) custom-call(s32[1]{0:T(128)} %bitcast.device_ref, bf16[256,1152]{1,0:T(8,128)(2,1)} %queries_ref.1, bf16[128,1152]{1,0:T(8,128)(2,1)} %keys_ref.1, bf16[128,2560]{1,0:T(8,128)(2,1)} %values_ref.1), custom_call_target="tpu_custom_call" | custom-call | tf_op jit(solution)/shard_map/stage_in/pallas_call | solution.py:567
  6.7 1.5 %shard_map.95 = (bf16[64,1408]{1,0:T(8,128)(2,1)S(1)}, f32[64,1408]{1,0:T(8,128)S(1)}) custom-call(bf16[128,1152]{1,0:T(8,128)(2,1)S(1)} %get-tuple-element.47.query_ref, bf16[128,1152]{1,0:T(8,128)(2,1)S(1)} %get-tuple-element.48.keys_a, bf16[128,1152]{1,0:T(8,128)(2,1)S(1)} %copy-done.4, bf16[128,2560]{1,0:T(8,128)(2,1)S(1)} %get-tuple-element.50.values_a, ...), custom_call_target="tpu_custom_call" | custom-call | tf_op jit(solution)/shard_map/pallas_call | solution.py:583
  8.3 2.7 %collective-permute-start.5 = (bf16[64,1408]{1,0:T(8,128)(2,1)S(1)}, bf16[64,1408]{1,0:T(8,128)(2,1)S(1)}, u32[]{:S(2)}, u32[]{:S(2)}) collective-permute-start(bf16[64,1408]{1,0:T(8,128)(2,1)S(1)} %get-tuple-element.60), channel_id=1, source_target_pairs={{0,2},{1,5},{2,0},{3,7},{4,6},{5,1},{6,4},{7,3},{8,10},{9,13},{10,... | collective-permute-start | bytes 540680 | tf_op jit(solution)/shard_map/ppermute | solution.py:55
  10.9 1.2 %shard_map.91 = (bf16[64,1408]{1,0:T(8,128)(2,1)S(1)}, f32[64,1408]{1,0:T(8,128)S(1)}) custom-call(bf16[128,1152]{1,0:T(8,128)(2,1)S(1)} %get-tuple-element.47.query_ref, bf16[128,1152]{1,0:T(8,128)(2,1)S(1)} %get-tuple-element.48.keys_a, bf16[128,1152]{1,0:T(8,128)(2,1)S(1)} %copy-done.4, bf16[128,2560]{1,0:T(8,128)(2,1)S(1)} %get-tuple-element.50.values_a, ...), custom_call_target="tpu_custom_call" | custom-call | tf_op jit(solution)/shard_map/pallas_call | solution.py:583
  12.3 2.1 %collective-permute-done.5.came_ref = bf16[64,1408]{1,0:T(8,128)(2,1)S(1)} collective-permute-done((bf16[64,1408]{1,0:T(8,128)(2,1)S(1)}, bf16[64,1408]{1,0:T(8,128)(2,1)S(1)}, u32[]{:S(2)}, u32[]{:S(2)}) %collective-permute-start.5) | collective-permute-done | bytes 180256 | tf_op jit(solution)/shard_map/ppermute | solution.py:55
  14.7 2.1 %collective-permute-start.6 = (bf16[32,1408]{1,0:T(8,128)(2,1)S(1)}, bf16[32,1408]{1,0:T(8,128)(2,1)S(1)}, u32[]{:S(2)}, u32[]{:S(2)}) collective-permute-start(bf16[32,1408]{1,0:T(8,128)(2,1)S(1)} %get-tuple-element.62), channel_id=1, source_target_pairs={{0,4},{1,9},{2,6},{3,11},{4,0},{5,13},{6,2},{7,15},{8,12},{9,1},{1... | collective-permute-start | bytes 270344 | tf_op jit(solution)/shard_map/ppermute | solution.py:55
  18.0 1.6 %collective-permute-start.3 = (bf16[32,1408]{1,0:T(8,128)(2,1)S(1)}, bf16[32,1408]{1,0:T(8,128)(2,1)S(1)}, u32[]{:S(2)}, u32[]{:S(2)}) collective-permute-start(bf16[32,1408]{1,0:T(8,128)(2,1)S(1)} %get-tuple-element.55), channel_id=1, source_target_pairs={{0,4},{1,9},{2,6},{3,11},{4,0},{5,13},{6,2},{7,15},{8,12},{9,1},{1... | collective-permute-start | bytes 270344 | tf_op jit(solution)/shard_map/ppermute | solution.py:55
  19.7 2.9 %collective-permute-done.3.came_ref = bf16[32,1408]{1,0:T(8,128)(2,1)S(1)} collective-permute-done((bf16[32,1408]{1,0:T(8,128)(2,1)S(1)}, bf16[32,1408]{1,0:T(8,128)(2,1)S(1)}, u32[]{:S(2)}, u32[]{:S(2)}) %collective-permute-start.3) | collective-permute-done | bytes 90144 | tf_op jit(solution)/shard_map/ppermute | solution.py:55
  22.8 1.6 %collective-permute-start.4 = (bf16[32,1408]{1,0:T(8,128)(2,1)S(1)}, bf16[32,1408]{1,0:T(8,128)(2,1)S(1)}, u32[]{:S(2)}, u32[]{:S(2)}) collective-permute-start(bf16[32,1408]{1,0:T(8,128)(2,1)S(1)} %get-tuple-element.57), channel_id=1, source_target_pairs={{0,8},{1,3},{2,10},{3,1},{4,12},{5,7},{6,14},{7,5},{8,0},{9,11},{1... | collective-permute-start | bytes 270344 | tf_op jit(solution)/shard_map/ppermute | solution.py:55
  25.1 2.3 %collective-permute-done.4.came_ref = bf16[32,1408]{1,0:T(8,128)(2,1)S(1)} collective-permute-done((bf16[32,1408]{1,0:T(8,128)(2,1)S(1)}, bf16[32,1408]{1,0:T(8,128)(2,1)S(1)}, u32[]{:S(2)}, u32[]{:S(2)}) %collective-permute-start.4) | collective-permute-done | bytes 90144 | tf_op jit(solution)/shard_map/ppermute | solution.py:55
  27.6 2.9 %collective-permute-start.11 = (bf16[32,1408]{1,0:T(8,128)(2,1)S(1)}, bf16[32,1408]{1,0:T(8,128)(2,1)S(1)}, u32[]{:S(2)}, u32[]{:S(2)}) collective-permute-start(bf16[32,1408]{1,0:T(8,128)(2,1)S(1)} %get-tuple-element.66.own_ref), channel_id=1, source_target_pairs={{0,16},{1,17},{2,18},{3,19},{4,20},{5,21},{6,22},{7,23},{8,24},{9,... | collective-permute-start | bytes 270344 | tf_op jit(solution)/shard_map/ppermute | solution.py:55
  30.7 1.5 %collective-permute-start.8 = (bf16[32,1280]{1,0:T(8,128)(2,1)S(1)}, bf16[32,1280]{1,0:T(8,128)(2,1)S(1)}, u32[]{:S(2)}, u32[]{:S(2)}) collective-permute-start(bf16[32,1280]{1,0:T(8,128)(2,1)S(1)} %get-tuple-element.65.own_ref), channel_id=1, source_target_pairs={{0,16},{1,17},{2,18},{3,19},{4,20},{5,21},{6,22},{7,23},{8,24},{9,... | collective-permute-start | bytes 245768 | tf_op jit(solution)/shard_map/ppermute | solution.py:55
  32.2 2.5 %collective-permute-done.11.came_ref = bf16[32,1408]{1,0:T(8,128)(2,1)S(1)} collective-permute-done((bf16[32,1408]{1,0:T(8,128)(2,1)S(1)}, bf16[32,1408]{1,0:T(8,128)(2,1)S(1)}, u32[]{:S(2)}, u32[]{:S(2)}) %collective-permute-start.11) | collective-permute-done | bytes 90144 | tf_op jit(solution)/shard_map/ppermute | solution.py:55
  34.7 1.6 %collective-permute-start.12 = (bf16[64,1408]{1,0:T(8,128)(2,1)S(1)}, bf16[64,1408]{1,0:T(8,128)(2,1)S(1)}, u32[]{:S(2)}, u32[]{:S(2)}) collective-permute-start(bf16[64,1408]{1,0:T(8,128)(2,1)S(1)} %shard_map.101.own_ref), channel_id=1, source_target_pairs={{0,4},{1,5},{2,6},{3,7},{4,0},{5,1},{6,2},{7,3},{8,12},{9,13},{10,... | collective-permute-start | bytes 540680 | tf_op jit(solution)/shard_map/ppermute | solution.py:55
  36.3 1.9 %collective-permute-start.9 = (bf16[64,1280]{1,0:T(8,128)(2,1)S(1)}, bf16[64,1280]{1,0:T(8,128)(2,1)S(1)}, u32[]{:S(2)}, u32[]{:S(2)}) collective-permute-start(bf16[64,1280]{1,0:T(8,128)(2,1)S(1)} %shard_map.99.own_ref), channel_id=1, source_target_pairs={{0,2},{1,9},{2,0},{3,11},{4,6},{5,13},{6,4},{7,15},{8,10},{9,1},{1... | collective-permute-start | bytes 491528 | tf_op jit(solution)/shard_map/ppermute | solution.py:55
  38.2 2.8 %collective-permute-done.12.came_ref = bf16[64,1408]{1,0:T(8,128)(2,1)S(1)} collective-permute-done((bf16[64,1408]{1,0:T(8,128)(2,1)S(1)}, bf16[64,1408]{1,0:T(8,128)(2,1)S(1)}, u32[]{:S(2)}, u32[]{:S(2)}) %collective-permute-start.12) | collective-permute-done | bytes 180256 | tf_op jit(solution)/shard_map/ppermute | solution.py:55
  42.1 2.4 %collective-permute-start.10 = (bf16[128,1280]{1,0:T(8,128)(2,1)S(1)}, bf16[128,1280]{1,0:T(8,128)(2,1)S(1)}, u32[]{:S(2)}, u32[]{:S(2)}) collective-permute-start(bf16[128,1280]{1,0:T(8,128)(2,1)S(1)} %shard_map.100.rows_ref), channel_id=1, source_target_pairs={{0,4},{1,5},{2,6},{3,7},{4,0},{5,1},{6,2},{7,3},{8,12},{9,13},{10,... | collective-permute-start | bytes 983048 | tf_op jit(solution)/shard_map/ppermute | solution.py:55
  44.6 3.3 %shard_map.104 = (f32[1024,128]{1,0:T(8,128)S(1)}, f32[1024,128]{1,0:T(8,128)S(1)}, f32[8,128]{1,0:T(8,128)S(1)}) custom-call(s32[1]{0:T(128)} %bitcast.device_ref, f32[1,2560]{1,0:T(1,128)S(1)} %reshape.14.gain_ref, bf16[128,1280]{1,0:T(8,128)(2,1)S(1)} %shard_map.100.rows_ref, bf16[512,2560]{1,0:T(8,128)(2,1)S(1)} %copy-done, ...), custom_call_target="tpu_custom_call" | custom-call | tf_op jit(solution)/shard_map/pallas_call | solution.py:484
  48.5 3.5 %shard_map.103 = (f32[1024,128]{1,0:T(8,128)S(1)}, f32[1024,128]{1,0:T(8,128)S(1)}, f32[8,128]{1,0:T(8,128)S(1)}) custom-call(s32[1]{0:T(128)} %bitcast.device_ref, f32[1,2560]{1,0:T(1,128)S(1)} %reshape.14.gain_ref, bf16[128,1408]{1,0:T(8,128)(2,1)S(1)} %collective-permute-done.13.rows_ref, bf16[512,2560]{1,0:T(8,128)(2,1)S(1)} %copy-done, ...), custom_call_target="tpu_custom_call" | custom-call | tf_op jit(solution)/shard_map/pallas_call | solution.py:484
  52.1 4.9 %expert_second.1 = (bf16[128,1280]{1,0:T(8,128)(2,1)S(1)}, bf16[128,1024]{1,0:T(8,128)(2,1)S(1)}, f32[1024,128]{1,0:T(8,128)S(1)}, f32[1024,128]{1,0:T(8,128)S(1)}, f32[8,128]{1,0:T(8,128)S(1)}) custom-call(f32[1,2560]{1,0:T(1,128)S(1)} %reshape.14.gain_ref, bf16[128,1280]{1,0:T(8,128)(2,1)S(1)} %collective-permute-done.10.rows_ref, ...), custom_call_target="tpu_custom_call" | custom-call | tf_op jit(solution)/shard_map/expert_second/pallas_call | solution.py:507
  58.0 3.3 %shard_map.105 = (f32[1024,128]{1,0:T(8,128)S(1)}, f32[1024,128]{1,0:T(8,128)S(1)}, f32[8,128]{1,0:T(8,128)S(1)}) custom-call(s32[1]{0:T(128)} %bitcast.device_ref, f32[1,2560]{1,0:T(1,128)S(1)} %reshape.14.gain_ref, bf16[128,1408]{1,0:T(8,128)(2,1)S(1)} %shard_map.102.rows_ref, bf16[512,2560]{1,0:T(8,128)(2,1)S(1)} %copy-done, ...), custom_call_target="tpu_custom_call" | custom-call | tf_op jit(solution)/shard_map/pallas_call | solution.py:484
  61.3 2.9 %expert_rest.1 = (bf16[128,1280]{1,0:T(8,128)(2,1)S(1)}, bf16[128,1024]{1,0:T(8,128)(2,1)S(1)}) custom-call(bf16[128,1024]{1,0:T(8,128)(2,1)S(1)} %get-tuple-element.76.hidden_ref.late_ref, f32[1024,128]{1,0:T(8,128)S(1)} %get-tuple-element.77.gates_ref, f32[1024,128]{1,0:T(8,128)S(1)} %get-tuple-element.78.ups_ref, ...), custom_call_target="tpu_custom_call" | custom-call | tf_op jit(solution)/shard_map/expert_rest/pallas_call | solution.py:517
  64.2 1.4 %collective-permute-start.21 = (bf16[128,1280]{1,0:T(8,128)(2,1)S(1)}, bf16[128,1280]{1,0:T(8,128)(2,1)S(1)}, u32[]{:S(2)}, u32[]{:S(2)}) collective-permute-start(bf16[128,1280]{1,0:T(8,128)(2,1)S(1)} %get-tuple-element.88), channel_id=1, source_target_pairs={{0,4},{1,5},{2,6},{3,7},{4,0},{5,1},{6,2},{7,3},{8,12},{9,13},{10,... | collective-permute-start | bytes 983048 | tf_op jit(solution)/shard_map/ppermute | solution.py:55
  65.6 2.7 %expert_kept.1 = (f32[128,1280]{1,0:T(8,128)S(1)}, f32[128,1280]{1,0:T(8,128)S(1)}) custom-call(bf16[128,1024]{1,0:T(8,128)(2,1)S(1)} %get-tuple-element.83.early_ref, bf16[128,1024]{1,0:T(8,128)(2,1)S(1)} %get-tuple-element.76.hidden_ref.late_ref, bf16[512,2560]{1,0:T(8,128)(2,1)S(1)} %copy-done.2, bf16[512,2560]{1,0:T(8,128)(2,1)} %collective-permute-done.16.down_b), custom_call_target="tpu_custom_call" | custom-call | tf_op jit(solution)/shard_map/expert_kept/pallas_call | solution.py:526
  69.2 2.1 %collective-permute-done.21 = bf16[128,1280]{1,0:T(8,128)(2,1)S(1)} collective-permute-done((bf16[128,1280]{1,0:T(8,128)(2,1)S(1)}, bf16[128,1280]{1,0:T(8,128)(2,1)S(1)}, u32[]{:S(2)}, u32[]{:S(2)}) %collective-permute-start.21) | collective-permute-done | bytes 327712 | tf_op jit(solution)/shard_map/ppermute | solution.py:55
  71.4 1.4 %collective-permute-start.22 = (bf16[64,1280]{1,0:T(8,128)(2,1)S(1)}, bf16[64,1280]{1,0:T(8,128)(2,1)S(1)}, u32[]{:S(2)}, u32[]{:S(2)}) collective-permute-start(bf16[64,1280]{1,0:T(8,128)(2,1)S(1)} %slice.86), channel_id=1, source_target_pairs={{0,2},{1,9},{2,0},{3,11},{4,6},{5,13},{6,4},{7,15},{8,10},{9,1},{1... | collective-permute-start | bytes 491528 | tf_op jit(solution)/shard_map/ppermute | solution.py:55
  73.9 1.7 %collective-permute-start.19 = (bf16[32,1280]{1,0:T(8,128)(2,1)S(1)}, bf16[32,1280]{1,0:T(8,128)(2,1)S(1)}, u32[]{:S(2)}, u32[]{:S(2)}) collective-permute-start(bf16[32,1280]{1,0:T(8,128)(2,1)S(1)} %slice.89), channel_id=1, source_target_pairs={{0,16},{1,17},{2,18},{3,19},{4,20},{5,21},{6,22},{7,23},{8,24},{9,... | collective-permute-start | bytes 245768 | tf_op jit(solution)/shard_map/ppermute | solution.py:55
  75.6 1.4 %collective-permute-done.22 = bf16[64,1280]{1,0:T(8,128)(2,1)S(1)} collective-permute-done((bf16[64,1280]{1,0:T(8,128)(2,1)S(1)}, bf16[64,1280]{1,0:T(8,128)(2,1)S(1)}, u32[]{:S(2)}, u32[]{:S(2)}) %collective-permute-start.22) | collective-permute-done | bytes 163872 | tf_op jit(solution)/shard_map/ppermute | solution.py:55
  78.2 1.1 %collective-permute-done.19 = bf16[32,1280]{1,0:T(8,128)(2,1)S(1)} collective-permute-done((bf16[32,1280]{1,0:T(8,128)(2,1)S(1)}, bf16[32,1280]{1,0:T(8,128)(2,1)S(1)}, u32[]{:S(2)}, u32[]{:S(2)}) %collective-permute-start.19) | collective-permute-done | bytes 81952 | tf_op jit(solution)/shard_map/ppermute | solution.py:55
  80.5 2.6 %collective-permute-done.23 = bf16[32,1280]{1,0:T(8,128)(2,1)S(1)} collective-permute-done((bf16[32,1280]{1,0:T(8,128)(2,1)S(1)}, bf16[32,1280]{1,0:T(8,128)(2,1)S(1)}, u32[]{:S(2)}, u32[]{:S(2)}) %collective-permute-start.23) | collective-permute-done | bytes 81952 | tf_op jit(solution)/shard_map/ppermute | solution.py:55
  83.5 3.6 %collective-permute-done.24 = bf16[16,1280]{1,0:T(8,128)(2,1)S(1)} collective-permute-done((bf16[16,1280]{1,0:T(8,128)(2,1)S(1)}, bf16[16,1280]{1,0:T(8,128)(2,1)S(1)}, u32[]{:S(2)}, u32[]{:S(2)}) %collective-permute-start.24) | collective-permute-done | bytes 40992 | tf_op jit(solution)/shard_map/ppermute | solution.py:55
  (72 shorter events, 14.1 us)
Async XLA Ops:
  0.0 3.6 %collective-permute-start.1 = (bf16[128,2560]{1,0:T(8,128)(2,1)}, bf16[128,2560]{1,0:T(8,128)(2,1)S(1)}, u32[]{:S(2)}, u32[]{:S(2)}) collective-permute-start(bf16[128,2560]{1,0:T(8,128)(2,1)} %values_ref.1), channel_id=1, source_target_pairs={{0,1},{1,0},{2,3},{3,2},{4,5},{5,4},{6,7},{7,6},{8,9},{9,8},{10,11... | collective-permute-start | bytes 1966088 | tf_op jit(solution)/shard_map/ppermute | solution.py:33
  0.5 2.4 %collective-permute-start = (bf16[128,1152]{1,0:T(8,128)(2,1)}, bf16[128,1152]{1,0:T(8,128)(2,1)S(1)}, u32[]{:S(2)}, u32[]{:S(2)}) collective-permute-start(bf16[128,1152]{1,0:T(8,128)(2,1)} %keys_ref.1), channel_id=1, source_target_pairs={{0,1},{1,0},{2,3},{3,2},{4,5},{5,4},{6,7},{7,6},{8,9},{9,8},{10,11... | collective-permute-start | bytes 884744 | tf_op jit(solution)/shard_map/ppermute | solution.py:33
  3.6 41.0 %collective-permute-start.14 = (bf16[512,2560]{1,0:T(8,128)(2,1)}, bf16[512,2560]{1,0:T(8,128)(2,1)S(1)}, u32[]{:S(2)}, u32[]{:S(2)}) collective-permute-start(bf16[512,2560]{1,0:T(8,128)(2,1)} %gate_a.3), channel_id=1, source_target_pairs={{0,1},{1,0},{2,3},{3,2},{4,5},{5,4},{6,7},{7,6},{8,9},{9,8},{10,11... | collective-permute-start | bytes 7864328 | tf_op jit(solution)/shard_map/ppermute | solution.py:33
  3.9 40.6 %collective-permute-start.15 = (bf16[512,2560]{1,0:T(8,128)(2,1)}, bf16[512,2560]{1,0:T(8,128)(2,1)}, u32[]{:S(2)}, u32[]{:S(2)}) collective-permute-start(bf16[512,2560]{1,0:T(8,128)(2,1)} %up_a.3), channel_id=1, source_target_pairs={{0,1},{1,0},{2,3},{3,2},{4,5},{5,4},{6,7},{7,6},{8,9},{9,8},{10,11... | collective-permute-start | bytes 7864328 | tf_op jit(solution)/shard_map/ppermute | solution.py:33
  4.1 48.0 %collective-permute-start.16 = (bf16[512,2560]{1,0:T(8,128)(2,1)}, bf16[512,2560]{1,0:T(8,128)(2,1)}, u32[]{:S(2)}, u32[]{:S(2)}) collective-permute-start(bf16[512,2560]{1,0:T(8,128)(2,1)} %down_a.2), channel_id=1, source_target_pairs={{0,1},{1,0},{2,3},{3,2},{4,5},{5,4},{6,7},{7,6},{8,9},{9,8},{10,11... | collective-permute-start | bytes 7864328 | tf_op jit(solution)/shard_map/ppermute | solution.py:33
  5.7 1.0 %copy-start.4 = (bf16[128,1152]{1,0:T(8,128)(2,1)S(1)}, bf16[128,1152]{1,0:T(8,128)(2,1)}, u32[]{:S(2)}) copy-start(bf16[128,1152]{1,0:T(8,128)(2,1)} %copy-done.3) | copy-start | bytes 884740
  6.7 12.9 %copy-start.6 = (s32[16,6]{0,1:T(8,128)S(1)}, s32[16,6]{0,1:T(8,128)}, u32[]{:S(2)}) copy-start(s32[16,6]{0,1:T(8,128)} %param.14) | copy-start | bytes 1156
  6.7 12.9 %copy-start.7 = (s32[16,6]{0,1:T(8,128)S(1)}, s32[16,6]{0,1:T(8,128)}, u32[]{:S(2)}) copy-start(s32[16,6]{0,1:T(8,128)} %param.13) | copy-start | bytes 1156
  8.3 6.2 %collective-permute-start.5 = (bf16[64,1408]{1,0:T(8,128)(2,1)S(1)}, bf16[64,1408]{1,0:T(8,128)(2,1)S(1)}, u32[]{:S(2)}, u32[]{:S(2)}) collective-permute-start(bf16[64,1408]{1,0:T(8,128)(2,1)S(1)} %get-tuple-element.60), channel_id=1, source_target_pairs={{0,2},{1,5},{2,0},{3,7},{4,6},{5,1},{6,4},{7,3},{8,10},{9,13},{10,... | collective-permute-start | bytes 540680 | tf_op jit(solution)/shard_map/ppermute | solution.py:55
  10.9 33.6 %copy-start.1 = (bf16[512,2560]{1,0:T(8,128)(2,1)S(1)}, bf16[512,2560]{1,0:T(8,128)(2,1)}, u32[]{:S(2)}) copy-start(bf16[512,2560]{1,0:T(8,128)(2,1)} %up_a.3) | copy-start | bytes 7864324
  12.2 32.4 %copy-start.5 = (f32[2560]{0:T(1024)S(1)}, f32[2560]{0:T(1024)}, u32[]{:S(2)}) copy-start(f32[2560]{0:T(1024)} %param.12) | copy-start | bytes 30724
  12.2 32.4 %copy-start = (bf16[512,2560]{1,0:T(8,128)(2,1)S(1)}, bf16[512,2560]{1,0:T(8,128)(2,1)}, u32[]{:S(2)}) copy-start(bf16[512,2560]{1,0:T(8,128)(2,1)} %gate_a.3) | copy-start | bytes 7864324
  12.2 5.6 %collective-permute-start.2 = (bf16[64,1408]{1,0:T(8,128)(2,1)S(1)}, bf16[64,1408]{1,0:T(8,128)(2,1)S(1)}, u32[]{:S(2)}, u32[]{:S(2)}) collective-permute-start(bf16[64,1408]{1,0:T(8,128)(2,1)S(1)} %get-tuple-element.53), channel_id=1, source_target_pairs={{0,2},{1,5},{2,0},{3,7},{4,6},{5,1},{6,4},{7,3},{8,10},{9,13},{10,... | collective-permute-start | bytes 540680 | tf_op jit(solution)/shard_map/ppermute | solution.py:55
  14.7 9.8 %collective-permute-start.6 = (bf16[32,1408]{1,0:T(8,128)(2,1)S(1)}, bf16[32,1408]{1,0:T(8,128)(2,1)S(1)}, u32[]{:S(2)}, u32[]{:S(2)}) collective-permute-start(bf16[32,1408]{1,0:T(8,128)(2,1)S(1)} %get-tuple-element.62), channel_id=1, source_target_pairs={{0,4},{1,9},{2,6},{3,11},{4,0},{5,13},{6,2},{7,15},{8,12},{9,1},{1... | collective-permute-start | bytes 270344 | tf_op jit(solution)/shard_map/ppermute | solution.py:55
  18.0 4.6 %collective-permute-start.3 = (bf16[32,1408]{1,0:T(8,128)(2,1)S(1)}, bf16[32,1408]{1,0:T(8,128)(2,1)S(1)}, u32[]{:S(2)}, u32[]{:S(2)}) collective-permute-start(bf16[32,1408]{1,0:T(8,128)(2,1)S(1)} %get-tuple-element.55), channel_id=1, source_target_pairs={{0,4},{1,9},{2,6},{3,11},{4,0},{5,13},{6,2},{7,15},{8,12},{9,1},{1... | collective-permute-start | bytes 270344 | tf_op jit(solution)/shard_map/ppermute | solution.py:55
  22.8 4.6 %collective-permute-start.4 = (bf16[32,1408]{1,0:T(8,128)(2,1)S(1)}, bf16[32,1408]{1,0:T(8,128)(2,1)S(1)}, u32[]{:S(2)}, u32[]{:S(2)}) collective-permute-start(bf16[32,1408]{1,0:T(8,128)(2,1)S(1)} %get-tuple-element.57), channel_id=1, source_target_pairs={{0,8},{1,3},{2,10},{3,1},{4,12},{5,7},{6,14},{7,5},{8,0},{9,11},{1... | collective-permute-start | bytes 270344 | tf_op jit(solution)/shard_map/ppermute | solution.py:55
  24.6 5.9 %collective-permute-start.7 = (bf16[32,1408]{1,0:T(8,128)(2,1)S(1)}, bf16[32,1408]{1,0:T(8,128)(2,1)S(1)}, u32[]{:S(2)}, u32[]{:S(2)}) collective-permute-start(bf16[32,1408]{1,0:T(8,128)(2,1)S(1)} %get-tuple-element.64), channel_id=1, source_target_pairs={{0,8},{1,3},{2,10},{3,1},{4,12},{5,7},{6,14},{7,5},{8,0},{9,11},{1... | collective-permute-start | bytes 270344 | tf_op jit(solution)/shard_map/ppermute | solution.py:55
  27.6 7.0 %collective-permute-start.11 = (bf16[32,1408]{1,0:T(8,128)(2,1)S(1)}, bf16[32,1408]{1,0:T(8,128)(2,1)S(1)}, u32[]{:S(2)}, u32[]{:S(2)}) collective-permute-start(bf16[32,1408]{1,0:T(8,128)(2,1)S(1)} %get-tuple-element.66.own_ref), channel_id=1, source_target_pairs={{0,16},{1,17},{2,18},{3,19},{4,20},{5,21},{6,22},{7,23},{8,24},{9,... | collective-permute-start | bytes 270344 | tf_op jit(solution)/shard_map/ppermute | solution.py:55
  30.7 5.6 %collective-permute-start.8 = (bf16[32,1280]{1,0:T(8,128)(2,1)S(1)}, bf16[32,1280]{1,0:T(8,128)(2,1)S(1)}, u32[]{:S(2)}, u32[]{:S(2)}) collective-permute-start(bf16[32,1280]{1,0:T(8,128)(2,1)S(1)} %get-tuple-element.65.own_ref), channel_id=1, source_target_pairs={{0,16},{1,17},{2,18},{3,19},{4,20},{5,21},{6,22},{7,23},{8,24},{9,... | collective-permute-start | bytes 245768 | tf_op jit(solution)/shard_map/ppermute | solution.py:55
  34.7 6.3 %collective-permute-start.12 = (bf16[64,1408]{1,0:T(8,128)(2,1)S(1)}, bf16[64,1408]{1,0:T(8,128)(2,1)S(1)}, u32[]{:S(2)}, u32[]{:S(2)}) collective-permute-start(bf16[64,1408]{1,0:T(8,128)(2,1)S(1)} %shard_map.101.own_ref), channel_id=1, source_target_pairs={{0,4},{1,5},{2,6},{3,7},{4,0},{5,1},{6,2},{7,3},{8,12},{9,13},{10,... | collective-permute-start | bytes 540680 | tf_op jit(solution)/shard_map/ppermute | solution.py:55
  36.3 5.7 %collective-permute-start.9 = (bf16[64,1280]{1,0:T(8,128)(2,1)S(1)}, bf16[64,1280]{1,0:T(8,128)(2,1)S(1)}, u32[]{:S(2)}, u32[]{:S(2)}) collective-permute-start(bf16[64,1280]{1,0:T(8,128)(2,1)S(1)} %shard_map.99.own_ref), channel_id=1, source_target_pairs={{0,2},{1,9},{2,0},{3,11},{4,6},{5,13},{6,4},{7,15},{8,10},{9,1},{1... | collective-permute-start | bytes 491528 | tf_op jit(solution)/shard_map/ppermute | solution.py:55
  41.0 7.5 %collective-permute-start.13 = (bf16[128,1408]{1,0:T(8,128)(2,1)S(1)}, bf16[128,1408]{1,0:T(8,128)(2,1)S(1)}, u32[]{:S(2)}, u32[]{:S(2)}) collective-permute-start(bf16[128,1408]{1,0:T(8,128)(2,1)S(1)} %shard_map.102.rows_ref), channel_id=1, source_target_pairs={{0,2},{1,9},{2,0},{3,11},{4,6},{5,13},{6,4},{7,15},{8,10},{9,1},{1... | collective-permute-start | bytes 1081352 | tf_op jit(solution)/shard_map/ppermute | solution.py:55
  42.1 10.0 %collective-permute-start.10 = (bf16[128,1280]{1,0:T(8,128)(2,1)S(1)}, bf16[128,1280]{1,0:T(8,128)(2,1)S(1)}, u32[]{:S(2)}, u32[]{:S(2)}) collective-permute-start(bf16[128,1280]{1,0:T(8,128)(2,1)S(1)} %shard_map.100.rows_ref), channel_id=1, source_target_pairs={{0,4},{1,5},{2,6},{3,7},{4,0},{5,1},{6,2},{7,3},{8,12},{9,13},{10,... | collective-permute-start | bytes 983048 | tf_op jit(solution)/shard_map/ppermute | solution.py:55
  47.9 4.2 %copy-start.2 = (bf16[512,2560]{1,0:T(8,128)(2,1)S(1)}, bf16[512,2560]{1,0:T(8,128)(2,1)}, u32[]{:S(2)}) copy-start(bf16[512,2560]{1,0:T(8,128)(2,1)} %down_a.2) | copy-start | bytes 7864324
  57.0 11.4 %collective-permute-start.17 = (bf16[128,1280]{1,0:T(8,128)(2,1)S(1)}, bf16[128,1280]{1,0:T(8,128)(2,1)S(1)}, u32[]{:S(2)}, u32[]{:S(2)}) collective-permute-start(bf16[128,1280]{1,0:T(8,128)(2,1)S(1)} %get-tuple-element.85), channel_id=1, source_target_pairs={{0,2},{1,9},{2,0},{3,11},{4,6},{5,13},{6,4},{7,15},{8,10},{9,1},{1... | collective-permute-start | bytes 983048 | tf_op jit(solution)/shard_map/ppermute | solution.py:55
  64.2 7.1 %collective-permute-start.21 = (bf16[128,1280]{1,0:T(8,128)(2,1)S(1)}, bf16[128,1280]{1,0:T(8,128)(2,1)S(1)}, u32[]{:S(2)}, u32[]{:S(2)}) collective-permute-start(bf16[128,1280]{1,0:T(8,128)(2,1)S(1)} %get-tuple-element.88), channel_id=1, source_target_pairs={{0,4},{1,5},{2,6},{3,7},{4,0},{5,1},{6,2},{7,3},{8,12},{9,13},{10,... | collective-permute-start | bytes 983048 | tf_op jit(solution)/shard_map/ppermute | solution.py:55
  68.5 5.4 %collective-permute-start.18 = (bf16[64,1280]{1,0:T(8,128)(2,1)S(1)}, bf16[64,1280]{1,0:T(8,128)(2,1)S(1)}, u32[]{:S(2)}, u32[]{:S(2)}) collective-permute-start(bf16[64,1280]{1,0:T(8,128)(2,1)S(1)} %slice.87), channel_id=1, source_target_pairs={{0,4},{1,5},{2,6},{3,7},{4,0},{5,1},{6,2},{7,3},{8,12},{9,13},{10,... | collective-permute-start | bytes 491528 | tf_op jit(solution)/shard_map/ppermute | solution.py:55
  71.4 5.6 %collective-permute-start.22 = (bf16[64,1280]{1,0:T(8,128)(2,1)S(1)}, bf16[64,1280]{1,0:T(8,128)(2,1)S(1)}, u32[]{:S(2)}, u32[]{:S(2)}) collective-permute-start(bf16[64,1280]{1,0:T(8,128)(2,1)S(1)} %slice.86), channel_id=1, source_target_pairs={{0,2},{1,9},{2,0},{3,11},{4,6},{5,13},{6,4},{7,15},{8,10},{9,1},{1... | collective-permute-start | bytes 491528 | tf_op jit(solution)/shard_map/ppermute | solution.py:55
  73.9 5.4 %collective-permute-start.19 = (bf16[32,1280]{1,0:T(8,128)(2,1)S(1)}, bf16[32,1280]{1,0:T(8,128)(2,1)S(1)}, u32[]{:S(2)}, u32[]{:S(2)}) collective-permute-start(bf16[32,1280]{1,0:T(8,128)(2,1)S(1)} %slice.89), channel_id=1, source_target_pairs={{0,16},{1,17},{2,18},{3,19},{4,20},{5,21},{6,22},{7,23},{8,24},{9,... | collective-permute-start | bytes 245768 | tf_op jit(solution)/shard_map/ppermute | solution.py:55
  77.1 6.0 %collective-permute-start.23 = (bf16[32,1280]{1,0:T(8,128)(2,1)S(1)}, bf16[32,1280]{1,0:T(8,128)(2,1)S(1)}, u32[]{:S(2)}, u32[]{:S(2)}) collective-permute-start(bf16[32,1280]{1,0:T(8,128)(2,1)S(1)} %slice.88), channel_id=1, source_target_pairs={{0,16},{1,17},{2,18},{3,19},{4,20},{5,21},{6,22},{7,23},{8,24},{9,... | collective-permute-start | bytes 245768 | tf_op jit(solution)/shard_map/ppermute | solution.py:55
  79.4 4.2 %collective-permute-start.20 = (bf16[16,1280]{1,0:T(8,128)(2,1)S(1)}, bf16[16,1280]{1,0:T(8,128)(2,1)S(1)}, u32[]{:S(2)}, u32[]{:S(2)}) collective-permute-start(bf16[16,1280]{1,0:T(8,128)(2,1)S(1)} %slice.91), channel_id=1, source_target_pairs={{0,8},{1,3},{2,10},{3,1},{4,12},{5,7},{6,14},{7,5},{8,0},{9,11},{1... | collective-permute-start | bytes 122888 | tf_op jit(solution)/shard_map/ppermute | solution.py:55
  83.1 4.1 %collective-permute-start.24 = (bf16[16,1280]{1,0:T(8,128)(2,1)S(1)}, bf16[16,1280]{1,0:T(8,128)(2,1)S(1)}, u32[]{:S(2)}, u32[]{:S(2)}) collective-permute-start(bf16[16,1280]{1,0:T(8,128)(2,1)S(1)} %slice.90), channel_id=1, source_target_pairs={{0,8},{1,3},{2,10},{3,1},{4,12},{5,7},{6,14},{7,5},{8,0},{9,11},{1... | collective-permute-start | bytes 122888 | tf_op jit(solution)/shard_map/ppermute | solution.py:55
  (1 other events, 0.7 us)
